TPU v7x, 256 devices: a whole 4x4x8 slice. The times are simulated.
256 devices in a mesh: frame: 16 (over z_hi, x), bx: 4 (over y), by: 4 (over z_lo, core).
Axes of the slice: x: 4, y: 4, z: 8 (z_hi: 4, z_lo: 2; z = z_hi * 2 + z_lo), core: 2. Of those that a mesh axis runs over, the one named last changes fastest.
Arguments:
- features: bfloat16 [64, 16, 64, 32, 512], P('frame', None, None, 'bx', 'by'), may hold values from -26 to 26
- voxel_embed: bfloat16 [16, 64, 32, 512], P(None, None, 'bx', 'by'), may hold values from -26 to 26
- visible: int32 [64, 16, 32, 512], P('frame', None, 'bx', 'by'), may hold values from 0 to 1, as said below
- w_query: bfloat16 [64, 64], replicated, may hold values from -0.75 to 0.75
- w_key: bfloat16 [64, 64], replicated, may hold values from -0.75 to 0.75
- w_value: bfloat16 [64, 64], replicated, may hold values from -0.75 to 0.75
- w_out: bfloat16 [64, 64], replicated, may hold values from -0.75 to 0.75
- conv_weight: bfloat16 [4, 3, 3, 3, 64, 64], replicated, may hold values from -0.21875 to 0.21875
- conv_bias: float32 [4, 64], replicated, may hold values from -1.2 to 1.2
Outputs:
- volume: bfloat16 [16, 64, 32, 512], P('frame', None, 'bx', 'by')
Inputs may be any that keep to these rules, and one draw needn't show every extreme that they name: Every voxel has visible = 1 in at least one of the 64 frames.
All inputs are finite; a program needn't handle non-finite values.
Results may differ from a plain program's by a relative error of at most 0.025.
Values may be sent and summed in bfloat16 or wider, within the bound.
No kernel may reach another device: no remote copies, remote signals or barrier semaphores. Data moves between devices by JAX's collectives and lax.ppermute only.
A program may use at most 64 MiB of HBM per device.

v0:
```python
import math

import jax
import jax.numpy as jnp
from jax import lax
from jax.sharding import PartitionSpec as P

absent_score = -1e30
conv_layout = ("NDCHW", "DHWIO", "NDCHW")


def padded_2(array, sides, width):
    for axis, dim in sides:
        peers, length = (lax.axis_size(axis), array.shape[dim])
        up = [(i, (i + 1) % peers) for i in range(peers - 1)]
        down = [(j, i) for i, j in up]
        last = lax.slice_in_dim(array, length - width, length, axis=dim)
        initial = lax.slice_in_dim(array, 0, width, axis=dim)
        before = lax.ppermute(last, axis, up)
        after = lax.ppermute(initial, axis, down)
        array = jnp.concatenate([before, array, after], axis=dim)
    return array


def shards(features, voxel_embed, visible, w_query, w_key, w_value, w_out, conv_weight, conv_bias):
    width = w_key.shape[0]
    query_data = jnp.einsum(
        "zcxy,cd->zdxy", voxel_embed, w_query, preferred_element_type=jnp.float32
    ).astype(jnp.bfloat16)
    key_data = jnp.einsum(
        "fzcxy,cd->fzdxy", features, w_key, preferred_element_type=jnp.float32
    ).astype(jnp.bfloat16)
    value_data = jnp.einsum(
        "fzcxy,cd->fzdxy", features, w_value, preferred_element_type=jnp.float32
    ).astype(jnp.bfloat16)
    scores = jnp.einsum(
        "zdxy,fzdxy->fzxy", query_data, key_data, preferred_element_type=jnp.float32
    ) / math.sqrt(width)
    is_seen = visible > 0
    highest = jnp.max(jnp.where(is_seen, scores, absent_score), axis=0)
    weights = jnp.where(is_seen, jnp.exp(scores - highest[None]), 0.0)
    weighted = jnp.sum(weights[:, :, None] * value_data, axis=0).astype(jnp.bfloat16)
    totals = jnp.sum(weights, axis=0).astype(jnp.bfloat16)
    overall = lax.pmax(highest.astype(jnp.bfloat16), "frame").astype(highest.dtype)
    factor = jnp.exp(highest - overall)
    merged, norm_sum = (
        lax.psum_scatter(
            (factor[:, None] * weighted.astype(jnp.float32)).astype(jnp.bfloat16),
            "frame",
            scatter_dimension=0,
            tiled=True,
        ).astype(jnp.float32),
        lax.psum_scatter(
            (factor * totals.astype(jnp.float32)).astype(jnp.bfloat16),
            "frame",
            scatter_dimension=0,
            tiled=True,
        ).astype(jnp.float32),
    )
    attended = (merged / norm_sum[:, None]).astype(jnp.bfloat16)
    hidden = jnp.einsum(
        "zcxy,cd->zdxy", attended, w_out, preferred_element_type=jnp.float32
    ).astype(jnp.bfloat16)
    layer_count = conv_weight.shape[0]
    for layer_no in range(layer_count):
        padded = padded_2(hidden, (("frame", 0), ("bx", 2), ("by", 3)), 1)
        result = lax.conv_general_dilated(
            padded[None],
            conv_weight[layer_no],
            (1, 1, 1),
            "VALID",
            dimension_numbers=conv_layout,
            preferred_element_type=jnp.float32,
        )[0]
        result = result + conv_bias[layer_no][None, :, None, None]
        if layer_no + 1 < layer_count:
            result = jnp.maximum(result, 0.0)
        hidden = result.astype(jnp.bfloat16)
    return hidden


def solution(mesh):
    return jax.shard_map(
        shards,
        mesh=mesh,
        in_specs=(
            P("frame", None, None, "bx", "by"),
            P(None, None, "bx", "by"),
            P("frame", None, "bx", "by"),
            P(),
            P(),
            P(),
            P(),
            P(),
            P(),
        ),
        out_specs=P("frame", None, "bx", "by"),
        check_vma=False,
    )
```

profile of v0, /device:TPU:7, one launch (start us, length us, event | category | flops | bytes accessed | tf_op | source)
XLA Modules:
  0.0 375.3 jit_solution(8921618250973270979)
XLA Ops:
  9.6 5.9 %multiply_reduce_fusion = f32[16,8,128,4]{2,1,0,3:T(8,128)S(1)} fusion(f32[16,8,128,64]{2,3,1,0:T(8,128)S(1)} %bitcast_convert_fusion, bf16[4,16,64,8,128]{4,3,2,1,0:T(8,128)(2,1)} %param.9, bf16[64,64]{1,0:T(8,128)(2,1)S(1)} %copy-done.3), kind=kOutput, calls=%fused_computation | convolution fusion | flops 553582592 | bytes 12853248 | tf_op jit(solution)/shard_map/fzcxy,cd->fzdxy/dot_general | solution.py:30
  15.7 60.4 %pmax.7 = bf16[16,8,128]{2,1,0:T(8,128)(2,1)S(1)} all-reduce(bf16[16,8,128]{2,1,0:T(8,128)(2,1)S(1)} %convert_element_type.111), channel_id=1, replica_groups=mesh['frame'=16,'bx'=4,'by'=4] {'frame'}, use_global_device_ids=true, to_apply=%region_1.2 | all-reduce | flops 16384 | bytes 65536 | tf_op jit(solution)/shard_map/pmax | solution.py:44
  76.1 6.2 %multiply_reduce_fusion.1 = bf16[64,16,8,128]{3,0,2,1:T(8,128)(2,1)S(1)} fusion(f32[4,16,8,128]{3,2,1,0:T(8,128)S(1)} %get-tuple-element.8, bf16[4,16,64,8,128]{4,3,2,1,0:T(8,128)(2,1)} %param.9, bf16[64,64]{1,0:T(8,128)(2,1)S(1)} %copy-done.5), kind=kOutput, calls=%fused_computation.1 | convolution fusion | flops 552599552 | bytes 10756096 | tf_op jit(solution)/shard_map/fzcxy,cd->fzdxy/dot_general | solution.py:33
  85.6 66.4 %all-reduce = bf16[16,8,128]{2,1,0:T(8,128)(2,1)S(1)} all-reduce(bf16[16,8,128]{2,1,0:T(8,128)(2,1)S(1)} %get-tuple-element.5), channel_id=3, replica_groups=mesh['frame'=16,'bx'=4,'by'=4] {'frame'}, use_global_device_ids=true, to_apply=%region_5.6.clone | all-reduce | flops 16384 | bytes 65536
  152.6 37.2 %reduce-scatter.2.cloned.1.call-done = bf16[1,64,8,128]{3,1,2,0:T(8,128)(2,1)} async-done(((bf16[16,64,8,128]{3,1,2,0:T(8,128)(2,1)}), bf16[1,64,8,128]{3,1,2,0:T(8,128)(2,1)}) %reduce-scatter.2.cloned.1.call-update) | async-done | bytes 131088 | tf_op jit(solution)/shard_map/reduce_scatter | solution.py:47
  191.0 4.6 %collective-permute-start = (bf16[1,64,8,128]{3,1,2,0:T(8,128)(2,1)S(1)}, bf16[1,64,8,128]{3,1,2,0:T(8,128)(2,1)S(1)}, u32[]{:S(2)}, u32[]{:S(2)}) collective-permute-start(bf16[1,64,8,128]{3,1,2,0:T(8,128)(2,1)S(1)} %fusion.41), channel_id=1, source_target_pairs={{0,16},{16,32},{32,48},{48,64},{64,80},{80,96},{96,112},{112,128},... | collective-permute-start | bytes 393224 | tf_op jit(solution)/shard_map/ppermute | solution.py:19
  197.6 8.2 %collective-permute-done.1 = bf16[1,64,8,128]{3,1,2,0:T(8,128)(2,1)S(1)} collective-permute-done((bf16[1,64,8,128]{3,1,2,0:T(8,128)(2,1)S(1)}, bf16[1,64,8,128]{3,1,2,0:T(8,128)(2,1)S(1)}, u32[]{:S(2)}, u32[]{:S(2)}) %collective-permute-start.1) | collective-permute-done | bytes 131104 | tf_op jit(solution)/shard_map/ppermute | solution.py:20
  205.8 3.1 collective-permute-start.2
  210.2 3.5 collective-permute-done.3
  214.0 7.3 %collective-permute-start.4 = (bf16[3,64,10,1]{3,1,2,0:T(8,128)(2,1)S(1)}, bf16[3,64,10,1]{3,1,2,0:T(8,128)(2,1)S(1)}, u32[]{:S(2)}, u32[]{:S(2)}) collective-permute-start(bf16[3,64,10,1]{3,1,2,0:T(8,128)(2,1)S(1)} %get-tuple-element.23), channel_id=1, source_target_pairs={{0,1},{1,2},{2,3},{4,5},{5,6},{6,7},{8,9},{9,10},{10,11},{12,13},{... | collective-permute-start | bytes 11528 | tf_op jit(solution)/shard_map/ppermute | solution.py:19
  223.2 3.8 %collective-permute-done.4 = bf16[3,64,10,1]{3,1,2,0:T(8,128)(2,1)S(1)} collective-permute-done((bf16[3,64,10,1]{3,1,2,0:T(8,128)(2,1)S(1)}, bf16[3,64,10,1]{3,1,2,0:T(8,128)(2,1)S(1)}, u32[]{:S(2)}, u32[]{:S(2)}) %collective-permute-start.4) | collective-permute-done | bytes 3872 | tf_op jit(solution)/shard_map/ppermute | solution.py:19
  227.0 4.4 %collective-permute-done.5 = bf16[3,64,10,1]{3,1,2,0:T(8,128)(2,1)S(1)} collective-permute-done((bf16[3,64,10,1]{3,1,2,0:T(8,128)(2,1)S(1)}, bf16[3,64,10,1]{3,1,2,0:T(8,128)(2,1)S(1)}, u32[]{:S(2)}, u32[]{:S(2)}) %collective-permute-start.5) | collective-permute-done | bytes 3872 | tf_op jit(solution)/shard_map/ppermute | solution.py:20
  238.6 3.5 collective-permute-start.7
  244.1 7.5 %collective-permute-done.7 = bf16[1,64,8,128]{1,2,3,0:T(8,128)(2,1)S(1)} collective-permute-done((bf16[1,64,8,128]{1,2,3,0:T(8,128)(2,1)S(1)}, bf16[1,64,8,128]{1,2,3,0:T(8,128)(2,1)S(1)}, u32[]{:S(2)}, u32[]{:S(2)}) %collective-permute-start.7) | collective-permute-done | bytes 131104 | tf_op jit(solution)/shard_map/ppermute | solution.py:20
  252.0 3.0 collective-permute-start.8
  257.7 3.7 collective-permute-done.9
  261.9 3.3 collective-permute-start.10
  267.1 3.8 %collective-permute-done.10 = bf16[3,64,10,1]{3,1,2,0:T(8,128)(2,1)S(1)} collective-permute-done((bf16[3,64,10,1]{3,1,2,0:T(8,128)(2,1)S(1)}, bf16[3,64,10,1]{3,1,2,0:T(8,128)(2,1)S(1)}, u32[]{:S(2)}, u32[]{:S(2)}) %collective-permute-start.10) | collective-permute-done | bytes 3872 | tf_op jit(solution)/shard_map/ppermute | solution.py:19
  271.0 4.4 %collective-permute-done.11 = bf16[3,64,10,1]{3,1,2,0:T(8,128)(2,1)S(1)} collective-permute-done((bf16[3,64,10,1]{3,1,2,0:T(8,128)(2,1)S(1)}, bf16[3,64,10,1]{3,1,2,0:T(8,128)(2,1)S(1)}, u32[]{:S(2)}, u32[]{:S(2)}) %collective-permute-start.11) | collective-permute-done | bytes 3872 | tf_op jit(solution)/shard_map/ppermute | solution.py:20
  282.0 3.4 collective-permute-start.13
  287.5 6.7 %collective-permute-done.13 = bf16[1,64,8,128]{1,2,3,0:T(8,128)(2,1)S(1)} collective-permute-done((bf16[1,64,8,128]{1,2,3,0:T(8,128)(2,1)S(1)}, bf16[1,64,8,128]{1,2,3,0:T(8,128)(2,1)S(1)}, u32[]{:S(2)}, u32[]{:S(2)}) %collective-permute-start.13) | collective-permute-done | bytes 131104 | tf_op jit(solution)/shard_map/ppermute | solution.py:20
  294.6 2.9 collective-permute-start.14
  300.3 3.7 collective-permute-done.15
  304.4 4.8 %collective-permute-start.16 = (bf16[3,64,10,1]{3,1,2,0:T(8,128)(2,1)S(1)}, bf16[3,64,10,1]{3,1,2,0:T(8,128)(2,1)S(1)}, u32[]{:S(2)}, u32[]{:S(2)}) collective-permute-start(bf16[3,64,10,1]{3,1,2,0:T(8,128)(2,1)S(1)} %get-tuple-element.19), channel_id=1, source_target_pairs={{0,1},{1,2},{2,3},{4,5},{5,6},{6,7},{8,9},{9,10},{10,11},{12,13},{... | collective-permute-start | bytes 11528 | tf_op jit(solution)/shard_map/ppermute | solution.py:19
  311.1 3.8 %collective-permute-done.16 = bf16[3,64,10,1]{3,1,2,0:T(8,128)(2,1)S(1)} collective-permute-done((bf16[3,64,10,1]{3,1,2,0:T(8,128)(2,1)S(1)}, bf16[3,64,10,1]{3,1,2,0:T(8,128)(2,1)S(1)}, u32[]{:S(2)}, u32[]{:S(2)}) %collective-permute-start.16) | collective-permute-done | bytes 3872 | tf_op jit(solution)/shard_map/ppermute | solution.py:19
  314.9 4.4 %collective-permute-done.17 = bf16[3,64,10,1]{3,1,2,0:T(8,128)(2,1)S(1)} collective-permute-done((bf16[3,64,10,1]{3,1,2,0:T(8,128)(2,1)S(1)}, bf16[3,64,10,1]{3,1,2,0:T(8,128)(2,1)S(1)}, u32[]{:S(2)}, u32[]{:S(2)}) %collective-permute-start.17) | collective-permute-done | bytes 3872 | tf_op jit(solution)/shard_map/ppermute | solution.py:20
  326.0 3.4 collective-permute-start.19
  331.4 5.5 %collective-permute-done.19 = bf16[1,64,8,128]{1,2,3,0:T(8,128)(2,1)S(1)} collective-permute-done((bf16[1,64,8,128]{1,2,3,0:T(8,128)(2,1)S(1)}, bf16[1,64,8,128]{1,2,3,0:T(8,128)(2,1)S(1)}, u32[]{:S(2)}, u32[]{:S(2)}) %collective-permute-start.19) | collective-permute-done | bytes 131104 | tf_op jit(solution)/shard_map/ppermute | solution.py:20
  342.1 3.7 collective-permute-done.21
  346.2 6.4 %collective-permute-start.22 = (bf16[3,64,10,1]{3,1,2,0:T(8,128)(2,1)S(1)}, bf16[3,64,10,1]{3,1,2,0:T(8,128)(2,1)S(1)}, u32[]{:S(2)}, u32[]{:S(2)}) collective-permute-start(bf16[3,64,10,1]{3,1,2,0:T(8,128)(2,1)S(1)} %get-tuple-element.17), channel_id=1, source_target_pairs={{0,1},{1,2},{2,3},{4,5},{5,6},{6,7},{8,9},{9,10},{10,11},{12,13},{... | collective-permute-start | bytes 11528 | tf_op jit(solution)/shard_map/ppermute | solution.py:19
  354.8 3.6 collective-permute-done.22
  358.4 4.4 %collective-permute-done.23 = bf16[3,64,10,1]{3,1,2,0:T(8,128)(2,1)S(1)} collective-permute-done((bf16[3,64,10,1]{3,1,2,0:T(8,128)(2,1)S(1)}, bf16[3,64,10,1]{3,1,2,0:T(8,128)(2,1)S(1)}, u32[]{:S(2)}, u32[]{:S(2)}) %collective-permute-start.23) | collective-permute-done | bytes 3872 | tf_op jit(solution)/shard_map/ppermute | solution.py:20
  (112 shorter events, 64.2 us)
Async XLA Ops:
  6.5 1.6 copy-start
  6.5 3.0 copy-start.3
  6.5 183.3 %reduce-scatter.2.cloned.1.call-start = ((), (), s32[]{:S(2)}) async-start(), calls=%async_computation.1 | async-start | bytes 2228224 | tf_op jit(solution)/shard_map/reduce_scatter | solution.py:47
  9.6 6.0 %copy-start.2 = (s32[4,16,8,128]{3,2,1,0:T(8,128)S(1)}, s32[4,16,8,128]{3,2,1,0:T(8,128)}, u32[]{:S(2)}) copy-start(s32[4,16,8,128]{3,2,1,0:T(8,128)} %param.11) | copy-start | bytes 786436
  9.6 66.5 %copy-start.5 = (bf16[64,64]{1,0:T(8,128)(2,1)S(1)}, bf16[64,64]{1,0:T(8,128)(2,1)}, u32[]{:S(2)}) copy-start(bf16[64,64]{1,0:T(8,128)(2,1)} %param.14) | copy-start | bytes 24580
  84.3 105.6 %copy-start.6 = (bf16[64,64]{1,0:T(8,128)(2,1)S(1)}, bf16[64,64]{1,0:T(8,128)(2,1)}, u32[]{:S(2)}) copy-start(bf16[64,64]{1,0:T(8,128)(2,1)} %param.15) | copy-start | bytes 24580
  191.0 32.2 %copy-start.4 = (f32[4,64]{1,0:T(4,128)S(1)}, f32[4,64]{1,0:T(4,128)}, u32[]{:S(2)}) copy-start(f32[4,64]{1,0:T(4,128)} %param.17) | copy-start | bytes 3076
  191.0 6.5 %collective-permute-start = (bf16[1,64,8,128]{3,1,2,0:T(8,128)(2,1)S(1)}, bf16[1,64,8,128]{3,1,2,0:T(8,128)(2,1)S(1)}, u32[]{:S(2)}, u32[]{:S(2)}) collective-permute-start(bf16[1,64,8,128]{3,1,2,0:T(8,128)(2,1)S(1)} %fusion.41), channel_id=1, source_target_pairs={{0,16},{16,32},{32,48},{48,64},{64,80},{80,96},{96,112},{112,128},... | collective-permute-start | bytes 393224 | tf_op jit(solution)/shard_map/ppermute | solution.py:19
  195.6 10.1 %collective-permute-start.1 = (bf16[1,64,8,128]{3,1,2,0:T(8,128)(2,1)S(1)}, bf16[1,64,8,128]{3,1,2,0:T(8,128)(2,1)S(1)}, u32[]{:S(2)}, u32[]{:S(2)}) collective-permute-start(bf16[1,64,8,128]{3,1,2,0:T(8,128)(2,1)S(1)} %fusion.41), channel_id=1, source_target_pairs={{16,0},{32,16},{48,32},{64,48},{80,64},{96,80},{112,96},{128,112},... | collective-permute-start | bytes 393224 | tf_op jit(solution)/shard_map/ppermute | solution.py:20
  205.8 4.4 %collective-permute-start.2 = (bf16[3,64,1,128]{3,1,2,0:T(8,128)(2,1)S(1)}, bf16[3,64,1,128]{3,1,2,0:T(8,128)(2,1)S(1)}, u32[]{:S(2)}, u32[]{:S(2)}) collective-permute-start(bf16[3,64,1,128]{3,1,2,0:T(8,128)(2,1)S(1)} %get-tuple-element.25), channel_id=1, source_target_pairs={{0,4},{4,8},{8,12},{1,5},{5,9},{9,13},{2,6},{6,10},{10,14},{3,7},{... | collective-permute-start | bytes 147464 | tf_op jit(solution)/shard_map/ppermute | solution.py:19
  208.8 4.8 %collective-permute-start.3 = (bf16[3,64,1,128]{3,1,2,0:T(8,128)(2,1)S(1)}, bf16[3,64,1,128]{3,1,2,0:T(8,128)(2,1)S(1)}, u32[]{:S(2)}, u32[]{:S(2)}) collective-permute-start(bf16[3,64,1,128]{3,1,2,0:T(8,128)(2,1)S(1)} %get-tuple-element.26), channel_id=1, source_target_pairs={{4,0},{8,4},{12,8},{5,1},{9,5},{13,9},{6,2},{10,6},{14,10},{7,3},{... | collective-permute-start | bytes 147464 | tf_op jit(solution)/shard_map/ppermute | solution.py:20
  214.0 13.0 %collective-permute-start.4 = (bf16[3,64,10,1]{3,1,2,0:T(8,128)(2,1)S(1)}, bf16[3,64,10,1]{3,1,2,0:T(8,128)(2,1)S(1)}, u32[]{:S(2)}, u32[]{:S(2)}) collective-permute-start(bf16[3,64,10,1]{3,1,2,0:T(8,128)(2,1)S(1)} %get-tuple-element.23), channel_id=1, source_target_pairs={{0,1},{1,2},{2,3},{4,5},{5,6},{6,7},{8,9},{9,10},{10,11},{12,13},{... | collective-permute-start | bytes 11528 | tf_op jit(solution)/shard_map/ppermute | solution.py:19
  221.3 10.1 %collective-permute-start.5 = (bf16[3,64,10,1]{3,1,2,0:T(8,128)(2,1)S(1)}, bf16[3,64,10,1]{3,1,2,0:T(8,128)(2,1)S(1)}, u32[]{:S(2)}, u32[]{:S(2)}) collective-permute-start(bf16[3,64,10,1]{3,1,2,0:T(8,128)(2,1)S(1)} %get-tuple-element.24), channel_id=1, source_target_pairs={{1,0},{2,1},{3,2},{5,4},{6,5},{7,6},{9,8},{10,9},{11,10},{13,12},{... | collective-permute-start | bytes 11528 | tf_op jit(solution)/shard_map/ppermute | solution.py:20
  236.6 7.4 %collective-permute-start.6 = (bf16[1,64,8,128]{1,2,3,0:T(8,128)(2,1)S(1)}, bf16[1,64,8,128]{1,2,3,0:T(8,128)(2,1)S(1)}, u32[]{:S(2)}, u32[]{:S(2)}) collective-permute-start(bf16[1,64,8,128]{1,2,3,0:T(8,128)(2,1)S(1)} %fusion.56), channel_id=1, source_target_pairs={{0,16},{16,32},{32,48},{48,64},{64,80},{80,96},{96,112},{112,128},... | collective-permute-start | bytes 393224 | tf_op jit(solution)/shard_map/ppermute | solution.py:19
  238.6 12.9 %collective-permute-start.7 = (bf16[1,64,8,128]{1,2,3,0:T(8,128)(2,1)S(1)}, bf16[1,64,8,128]{1,2,3,0:T(8,128)(2,1)S(1)}, u32[]{:S(2)}, u32[]{:S(2)}) collective-permute-start(bf16[1,64,8,128]{1,2,3,0:T(8,128)(2,1)S(1)} %fusion.56), channel_id=1, source_target_pairs={{16,0},{32,16},{48,32},{64,48},{80,64},{96,80},{112,96},{128,112},... | collective-permute-start | bytes 393224 | tf_op jit(solution)/shard_map/ppermute | solution.py:20
  252.0 5.6 %collective-permute-start.8 = (bf16[3,64,1,128]{1,2,3,0:T(2,128)(2,1)S(1)}, bf16[3,64,1,128]{1,2,3,0:T(2,128)(2,1)S(1)}, u32[]{:S(2)}, u32[]{:S(2)}) collective-permute-start(bf16[3,64,1,128]{1,2,3,0:T(2,128)(2,1)S(1)} %get-tuple-element.15), channel_id=1, source_target_pairs={{0,4},{4,8},{8,12},{1,5},{5,9},{9,13},{2,6},{6,10},{10,14},{3,7},{... | collective-permute-start | bytes 147464 | tf_op jit(solution)/shard_map/ppermute | solution.py:19
  255.0 6.4 %collective-permute-start.9 = (bf16[3,64,1,128]{1,2,3,0:T(2,128)(2,1)S(1)}, bf16[3,64,1,128]{1,2,3,0:T(2,128)(2,1)S(1)}, u32[]{:S(2)}, u32[]{:S(2)}) collective-permute-start(bf16[3,64,1,128]{1,2,3,0:T(2,128)(2,1)S(1)} %get-tuple-element.16), channel_id=1, source_target_pairs={{4,0},{8,4},{12,8},{5,1},{9,5},{13,9},{6,2},{10,6},{14,10},{7,3},{... | collective-permute-start | bytes 147464 | tf_op jit(solution)/shard_map/ppermute | solution.py:20
  261.9 9.1 %collective-permute-start.10 = (bf16[3,64,10,1]{3,1,2,0:T(8,128)(2,1)S(1)}, bf16[3,64,10,1]{3,1,2,0:T(8,128)(2,1)S(1)}, u32[]{:S(2)}, u32[]{:S(2)}) collective-permute-start(bf16[3,64,10,1]{3,1,2,0:T(8,128)(2,1)S(1)} %get-tuple-element.21), channel_id=1, source_target_pairs={{0,1},{1,2},{2,3},{4,5},{5,6},{6,7},{8,9},{9,10},{10,11},{12,13},{... | collective-permute-start | bytes 11528 | tf_op jit(solution)/shard_map/ppermute | solution.py:19
  265.2 10.1 %collective-permute-start.11 = (bf16[3,64,10,1]{3,1,2,0:T(8,128)(2,1)S(1)}, bf16[3,64,10,1]{3,1,2,0:T(8,128)(2,1)S(1)}, u32[]{:S(2)}, u32[]{:S(2)}) collective-permute-start(bf16[3,64,10,1]{3,1,2,0:T(8,128)(2,1)S(1)} %get-tuple-element.22), channel_id=1, source_target_pairs={{1,0},{2,1},{3,2},{5,4},{6,5},{7,6},{9,8},{10,9},{11,10},{13,12},{... | collective-permute-start | bytes 11528 | tf_op jit(solution)/shard_map/ppermute | solution.py:20
  280.1 7.4 %collective-permute-start.12 = (bf16[1,64,8,128]{1,2,3,0:T(8,128)(2,1)S(1)}, bf16[1,64,8,128]{1,2,3,0:T(8,128)(2,1)S(1)}, u32[]{:S(2)}, u32[]{:S(2)}) collective-permute-start(bf16[1,64,8,128]{1,2,3,0:T(8,128)(2,1)S(1)} %fusion.53), channel_id=1, source_target_pairs={{0,16},{16,32},{32,48},{48,64},{64,80},{80,96},{96,112},{112,128},... | collective-permute-start | bytes 393224 | tf_op jit(solution)/shard_map/ppermute | solution.py:19
  282.0 12.2 %collective-permute-start.13 = (bf16[1,64,8,128]{1,2,3,0:T(8,128)(2,1)S(1)}, bf16[1,64,8,128]{1,2,3,0:T(8,128)(2,1)S(1)}, u32[]{:S(2)}, u32[]{:S(2)}) collective-permute-start(bf16[1,64,8,128]{1,2,3,0:T(8,128)(2,1)S(1)} %fusion.53), channel_id=1, source_target_pairs={{16,0},{32,16},{48,32},{64,48},{80,64},{96,80},{112,96},{128,112},... | collective-permute-start | bytes 393224 | tf_op jit(solution)/shard_map/ppermute | solution.py:20
  294.6 5.5 %collective-permute-start.14 = (bf16[3,64,1,128]{1,2,3,0:T(2,128)(2,1)S(1)}, bf16[3,64,1,128]{1,2,3,0:T(2,128)(2,1)S(1)}, u32[]{:S(2)}, u32[]{:S(2)}) collective-permute-start(bf16[3,64,1,128]{1,2,3,0:T(2,128)(2,1)S(1)} %get-tuple-element.13), channel_id=1, source_target_pairs={{0,4},{4,8},{8,12},{1,5},{5,9},{9,13},{2,6},{6,10},{10,14},{3,7},{... | collective-permute-start | bytes 147464 | tf_op jit(solution)/shard_map/ppermute | solution.py:19
  297.6 6.4 %collective-permute-start.15 = (bf16[3,64,1,128]{1,2,3,0:T(2,128)(2,1)S(1)}, bf16[3,64,1,128]{1,2,3,0:T(2,128)(2,1)S(1)}, u32[]{:S(2)}, u32[]{:S(2)}) collective-permute-start(bf16[3,64,1,128]{1,2,3,0:T(2,128)(2,1)S(1)} %get-tuple-element.14), channel_id=1, source_target_pairs={{4,0},{8,4},{12,8},{5,1},{9,5},{13,9},{6,2},{10,6},{14,10},{7,3},{... | collective-permute-start | bytes 147464 | tf_op jit(solution)/shard_map/ppermute | solution.py:20
  304.4 10.5 %collective-permute-start.16 = (bf16[3,64,10,1]{3,1,2,0:T(8,128)(2,1)S(1)}, bf16[3,64,10,1]{3,1,2,0:T(8,128)(2,1)S(1)}, u32[]{:S(2)}, u32[]{:S(2)}) collective-permute-start(bf16[3,64,10,1]{3,1,2,0:T(8,128)(2,1)S(1)} %get-tuple-element.19), channel_id=1, source_target_pairs={{0,1},{1,2},{2,3},{4,5},{5,6},{6,7},{8,9},{9,10},{10,11},{12,13},{... | collective-permute-start | bytes 11528 | tf_op jit(solution)/shard_map/ppermute | solution.py:19
  309.2 10.1 %collective-permute-start.17 = (bf16[3,64,10,1]{3,1,2,0:T(8,128)(2,1)S(1)}, bf16[3,64,10,1]{3,1,2,0:T(8,128)(2,1)S(1)}, u32[]{:S(2)}, u32[]{:S(2)}) collective-permute-start(bf16[3,64,10,1]{3,1,2,0:T(8,128)(2,1)S(1)} %get-tuple-element.20), channel_id=1, source_target_pairs={{1,0},{2,1},{3,2},{5,4},{6,5},{7,6},{9,8},{10,9},{11,10},{13,12},{... | collective-permute-start | bytes 11528 | tf_op jit(solution)/shard_map/ppermute | solution.py:20
  324.0 7.4 %collective-permute-start.18 = (bf16[1,64,8,128]{1,2,3,0:T(8,128)(2,1)S(1)}, bf16[1,64,8,128]{1,2,3,0:T(8,128)(2,1)S(1)}, u32[]{:S(2)}, u32[]{:S(2)}) collective-permute-start(bf16[1,64,8,128]{1,2,3,0:T(8,128)(2,1)S(1)} %fusion.50), channel_id=1, source_target_pairs={{0,16},{16,32},{32,48},{48,64},{64,80},{80,96},{96,112},{112,128},... | collective-permute-start | bytes 393224 | tf_op jit(solution)/shard_map/ppermute | solution.py:19
  326.0 11.0 %collective-permute-start.19 = (bf16[1,64,8,128]{1,2,3,0:T(8,128)(2,1)S(1)}, bf16[1,64,8,128]{1,2,3,0:T(8,128)(2,1)S(1)}, u32[]{:S(2)}, u32[]{:S(2)}) collective-permute-start(bf16[1,64,8,128]{1,2,3,0:T(8,128)(2,1)S(1)} %fusion.50), channel_id=1, source_target_pairs={{16,0},{32,16},{48,32},{64,48},{80,64},{96,80},{112,96},{128,112},... | collective-permute-start | bytes 393224 | tf_op jit(solution)/shard_map/ppermute | solution.py:20
  337.5 4.5 %collective-permute-start.20 = (bf16[3,64,1,128]{1,2,3,0:T(2,128)(2,1)S(1)}, bf16[3,64,1,128]{1,2,3,0:T(2,128)(2,1)S(1)}, u32[]{:S(2)}, u32[]{:S(2)}) collective-permute-start(bf16[3,64,1,128]{1,2,3,0:T(2,128)(2,1)S(1)} %get-tuple-element.11), channel_id=1, source_target_pairs={{0,4},{4,8},{8,12},{1,5},{5,9},{9,13},{2,6},{6,10},{10,14},{3,7},{... | collective-permute-start | bytes 147464 | tf_op jit(solution)/shard_map/ppermute | solution.py:19
  339.4 6.4 %collective-permute-start.21 = (bf16[3,64,1,128]{1,2,3,0:T(2,128)(2,1)S(1)}, bf16[3,64,1,128]{1,2,3,0:T(2,128)(2,1)S(1)}, u32[]{:S(2)}, u32[]{:S(2)}) collective-permute-start(bf16[3,64,1,128]{1,2,3,0:T(2,128)(2,1)S(1)} %get-tuple-element.12), channel_id=1, source_target_pairs={{4,0},{8,4},{12,8},{5,1},{9,5},{13,9},{6,2},{10,6},{14,10},{7,3},{... | collective-permute-start | bytes 147464 | tf_op jit(solution)/shard_map/ppermute | solution.py:20
  346.2 12.2 %collective-permute-start.22 = (bf16[3,64,10,1]{3,1,2,0:T(8,128)(2,1)S(1)}, bf16[3,64,10,1]{3,1,2,0:T(8,128)(2,1)S(1)}, u32[]{:S(2)}, u32[]{:S(2)}) collective-permute-start(bf16[3,64,10,1]{3,1,2,0:T(8,128)(2,1)S(1)} %get-tuple-element.17), channel_id=1, source_target_pairs={{0,1},{1,2},{2,3},{4,5},{5,6},{6,7},{8,9},{9,10},{10,11},{12,13},{... | collective-permute-start | bytes 11528 | tf_op jit(solution)/shard_map/ppermute | solution.py:19
  352.6 10.1 %collective-permute-start.23 = (bf16[3,64,10,1]{3,1,2,0:T(8,128)(2,1)S(1)}, bf16[3,64,10,1]{3,1,2,0:T(8,128)(2,1)S(1)}, u32[]{:S(2)}, u32[]{:S(2)}) collective-permute-start(bf16[3,64,10,1]{3,1,2,0:T(8,128)(2,1)S(1)} %get-tuple-element.18), channel_id=1, source_target_pairs={{1,0},{2,1},{3,2},{5,4},{6,5},{7,6},{9,8},{10,9},{11,10},{13,12},{... | collective-permute-start | bytes 11528 | tf_op jit(solution)/shard_map/ppermute | solution.py:20
  365.0 3.4 copy-start.1
  (2 other events, 1.4 us)
Sparse Core Ops, SparseCore 0:
  84.4 105.3 reduce-scatter.1
where the time goes:
time: 376 us; the launch traced here: 375 us
  blocking collectives  127 us (34%)
  waiting for transfers between devices  121 us (32%)
  starting transfers between devices  68.3 us (18%)
  matrix products  23.8 us (6%)
  local copies, waits for them, and re-layouts  15 us (4%)
  between operations  14.1 us (4%)
  other arithmetic  6.26 us (2%)
    unnamed x1, blocking collectives  66.4 us
    pmax x1, blocking collectives, shards(): lax.pmax(highest.astype(jnp.bfloat16), 'frame').astype(highest.dtype)  60.4 us
    ppermute x12, waiting for transfers between devices, padded_2(): after = lax.ppermute(initial, axis, down)  60.1 us
    ppermute x12, starting transfers between devices, padded_2(): before = lax.ppermute(last, axis, up)  43 us
    reduce_scatter x1, waiting for transfers between devices, shards(): lax.psum_scatter((factor[:, None] * weighted.astype(jnp.float32)).astype(...  37.2 us
    ppermute x12, starting transfers between devices, padded_2(): after = lax.ppermute(initial, axis, down)  25.3 us
    ppermute x12, waiting for transfers between devices, padded_2(): before = lax.ppermute(last, axis, up)  23.6 us
    conv_general_dilated x4, matrix products, shards(): lax.conv_general_dilated(padded[None], conv_weight[layer_no], (1, 1, 1),...  9.17 us
  transfers between devices with their start and end apart: 25, of which 23 were waited for; matrix products, arithmetic and copies ran while one was open for 1% of the time, Pallas kernels for 0%

commit v1 on v0

v1 whole, which is shorter than its diff:
```python
import functools

import jax
import jax.numpy as jnp
from jax import lax
from jax.experimental import pallas as pl
from jax.experimental.pallas import tpu as pltpu
from jax.sharding import PartitionSpec as P

absent_score = -1e30
halo = 4


def lane_blocks(v):
    lane = lax.broadcasted_iota(jnp.int32, (8, 128), 1)
    low = lane < 64
    even = (lane & 63) < 32
    t = [None] * 4
    for i in (0, 1):
        t[i] = jnp.where(low, v[i], pltpu.roll(v[i + 2], 64, 1))
        t[i + 2] = jnp.where(low, pltpu.roll(v[i], 64, 1), v[i + 2])
    o = [None] * 4
    for i in (0, 2):
        o[i] = jnp.where(even, t[i], pltpu.roll(t[i + 1], 32, 1))
        o[i + 1] = jnp.where(even, pltpu.roll(t[i], 96, 1), t[i + 1])
    return o


def three_terms(m):
    hi = m.astype(jnp.bfloat16).astype(jnp.float32)
    mid = (m - hi).astype(jnp.bfloat16).astype(jnp.float32)
    return hi, mid, m - hi - mid


def attend_kernel(place, feat, embed, seen, wq_t, wk, out, tmp):
    frames = feat.shape[0]
    tmp[...] = embed[0].astype(jnp.float32)
    cols = [tmp[pl.ds(i, 64, stride=8), :] for i in range(8)]
    wide = jnp.concatenate(cols, axis=1).astype(jnp.bfloat16)
    q = jnp.dot(wq_t[...], wide, preferred_element_type=jnp.float32).astype(jnp.bfloat16)
    qk = jnp.dot(wk[...], q, preferred_element_type=jnp.float32) * 0.125
    for i in range(8):
        tmp[pl.ds(i, 64, stride=8), :] = qk[:, i * 128 : (i + 1) * 128]
    sums = [jnp.zeros((8, 128), jnp.float32) for _ in range(frames)]
    for g in range(16):
        rows = slice(32 * g, 32 * g + 32)
        key = tmp[rows, :]
        for f in range(frames):
            prod = (key * feat[f, 0, rows, :].astype(jnp.float32)).reshape(4, 8, 128)
            sums[f] = sums[f] + jnp.sum(prod, axis=0)
    ok = [seen[f, 0] > 0 for f in range(frames)]
    m = jnp.full((8, 128), absent_score, jnp.float32)
    for f in range(frames):
        m = jnp.maximum(m, jnp.where(ok[f], sums[f], absent_score))
    e = [jnp.where(ok[f], jnp.exp(sums[f] - m), 0.0) for f in range(frames)]
    total = e[0]
    for f in range(1, frames):
        total = total + e[f]
    mine = place[0]

    def put(g, tiles):
        for k, tile in enumerate(lane_blocks(tiles)):
            slot = (k - mine) & 3
            out[slot, 0, 8 * g : 8 * g + 8, :] = tile.astype(jnp.bfloat16)

    for g in range(16):
        rows = slice(32 * g, 32 * g + 32)
        acc = jnp.zeros((4, 8, 128), jnp.float32)
        for f in range(frames):
            acc = acc + e[f][None] * feat[f, 0, rows, :].astype(jnp.float32).reshape(4, 8, 128)
        put(g, [acc[i] for i in range(4)])
    put(16, [*three_terms(m), total])


def attend(place, features, voxel_embed, visible, w_query, w_key):
    frames, planes, c = features.shape[:3]
    feat = features.reshape(frames, planes, c * 8, 128)
    embed = voxel_embed.reshape(planes, c * 8, 128)

    def out_map(z, place):
        return (0, ((z // 4 - place[1]) & 3) * 4 + z % 4, 0, 0)

    return pl.pallas_call(
        attend_kernel,
        out_shape=jax.ShapeDtypeStruct((4, planes, 136, 128), jnp.bfloat16),
        grid_spec=pltpu.PrefetchScalarGridSpec(
            num_scalar_prefetch=1,
            grid=(planes,),
            in_specs=[
                pl.BlockSpec((frames, 1, c * 8, 128), lambda z, p: (0, z, 0, 0)),
                pl.BlockSpec((1, c * 8, 128), lambda z, p: (z, 0, 0)),
                pl.BlockSpec((frames, 1, 8, 128), lambda z, p: (0, z, 0, 0)),
                pl.BlockSpec((c, c), lambda z, p: (0, 0)),
                pl.BlockSpec((c, c), lambda z, p: (0, 0)),
            ],
            out_specs=pl.BlockSpec((4, 1, 136, 128), out_map),
            scratch_shapes=[pltpu.VMEM((c * 8, 128), jnp.float32)],
        ),
        compiler_params=pltpu.CompilerParams(dimension_semantics=("arbitrary",)),
        name="attend",
    )(place, feat, embed, visible, w_query.T, w_key)


def spread(v):
    u = v + pltpu.roll(v, 64, 1)
    return u + pltpu.roll(u, 32, 1)


def merge_kernel(last, *refs):
    parts, out = refs[:-1], refs[-1]
    lane = lax.broadcasted_iota(jnp.int32, (8, 128), 1)
    tail = lane >= 96
    for p in range(out.shape[0]):
        stats = [r[p, 128:136, :].astype(jnp.float32) for r in parts]
        ms = [spread(jnp.where(tail, 0.0, s)) for s in stats]
        ls = [spread(jnp.where(tail, s, 0.0)) for s in stats]
        m = functools.reduce(jnp.maximum, ms)
        ws = [jnp.exp(v - m) for v in ms]
        total = sum(w * v for w, v in zip(ws, ls))
        if last:
            inv = 1.0 / total
            ws = [w * inv for w in ws]
        acc = None
        for r, w in zip(parts, ws):
            term = r[p, 0:128, :].astype(jnp.float32).reshape(16, 8, 128) * w[None]
            acc = term if acc is None else acc + term
        out[p, 0:128, :] = acc.reshape(128, 128).astype(jnp.bfloat16)
        if not last:
            hi, mid, low = three_terms(m)
            packed = jnp.where(
                lane < 32, hi, jnp.where(lane < 64, mid, jnp.where(tail, total, low))
            )
            out[p, 128:136, :] = packed.astype(jnp.bfloat16)


def merge(parts, last=False):
    n = parts[0].shape[0]
    step = min(n, 2)
    spec = pl.BlockSpec((step, 136, 128), lambda i: (i, 0, 0))
    rows = 128 if last else 136
    return pl.pallas_call(
        functools.partial(merge_kernel, last),
        out_shape=jax.ShapeDtypeStruct((n, rows, 128), jnp.bfloat16),
        grid=(n // step,),
        in_specs=[spec] * len(parts),
        out_specs=pl.BlockSpec((step, rows, 128), lambda i: (i, 0, 0)),
        name="merge",
    )(*parts)


def ring_reduce(slots, up, down, last=False):
    half = slots[0].shape[0] // 2
    from_low = lax.ppermute(slots[2][:half], "frame", up)
    from_high = lax.ppermute(slots[2][half:], "frame", down)
    first = jnp.concatenate([merge([slots[1][:half], from_low]), slots[1][half:]])
    third = jnp.concatenate([slots[3][:half], merge([slots[3][half:], from_high])])
    from_low = lax.ppermute(first, "frame", up)
    from_high = lax.ppermute(third, "frame", down)
    return merge([slots[0], from_low, from_high], last)


def banded(w):
    c, o = w.shape[-2:]
    blocks = jnp.zeros((3, 3, 6, c, 4, o), w.dtype)
    for j in range(4):
        for a in range(3):
            blocks = blocks.at[:, :, j + a, :, j, :].set(w[a])
    return blocks.reshape(3, 3, 6 * c, 4 * o)


def shards(features, voxel_embed, visible, w_query, w_key, w_value, w_out, conv_weight, conv_bias):
    me = lax.axis_index("frame")
    zh, xi = me // 4, me % 4
    place = jnp.stack([xi, zh]).astype(jnp.int32)
    x_up = [(4 * z + x, 4 * z + (x + 1) % 4) for z in range(4) for x in range(4)]
    x_down = [(j, i) for i, j in x_up]
    z_up = [(4 * z + x, 4 * ((z + 1) % 4) + x) for z in range(4) for x in range(4)]
    z_down = [(j, i) for i, j in z_up]
    slots = attend(place, features, voxel_embed, visible, w_query, w_key)
    mixed = ring_reduce([slots[r] for r in range(4)], x_up, x_down)
    mixed = ring_reduce([mixed[4 * r : 4 * r + 4] for r in range(4)], z_up, z_down, True)
    mixed = mixed.reshape(4, 16, 8, 4, 32).transpose(2, 4, 0, 1, 3).reshape(8, 32, 4, 64)
    attended = jnp.einsum(
        "xyzc,cd->xyzd", mixed, w_value, preferred_element_type=jnp.float32
    ).astype(jnp.bfloat16)
    hidden = jnp.einsum(
        "xyzc,cd->xyzd", attended, w_out, preferred_element_type=jnp.float32
    ).astype(jnp.bfloat16).reshape(8, 32, 256)

    z_next = [(i, i + 4) for i in range(12)]
    z_prev = [(j, i) for i, j in z_next]
    below = lax.ppermute(hidden, "frame", z_next)
    above = lax.ppermute(hidden, "frame", z_prev)
    hidden = jnp.concatenate([below, hidden, above], axis=2)

    def where_is(z, chunk):
        return (4 * z + chunk % 4) * 4 + chunk // 4

    y_next = [(where_is(z, k), where_is(z, k + 1)) for z in range(4) for k in range(15)]
    y_prev = [(j, i) for i, j in y_next]
    left = lax.ppermute(hidden[:, -halo:], ("frame", "by"), y_next)
    right = lax.ppermute(hidden[:, :halo], ("frame", "by"), y_prev)
    hidden = jnp.concatenate([left, hidden, right], axis=1)
    x_next = [(0, 1), (1, 2), (2, 3)]
    x_prev = [(j, i) for i, j in x_next]
    front = lax.ppermute(hidden[-halo:], "bx", x_next)
    back = lax.ppermute(hidden[:halo], "bx", x_prev)
    hidden = jnp.concatenate([front, hidden, back], axis=0)

    x0 = lax.axis_index("bx") * 8
    y0 = lax.axis_index("by") * 128 + xi * 32
    z0 = zh * 4
    layers = conv_weight.shape[0]
    for layer in range(layers):
        w = banded(conv_weight[layer])
        width = halo - 1 - layer
        planes = 4 + 2 * width
        pieces = []
        for start in range(0, planes, 4):
            count = min(4, planes - start)
            part = hidden[:, :, start * 64 : (start + count + 2) * 64]
            pieces.append(
                lax.conv_general_dilated(
                    part[None],
                    w[:, :, : (count + 2) * 64, : count * 64],
                    (1, 1),
                    "VALID",
                    dimension_numbers=("NHWC", "HWIO", "NHWC"),
                    preferred_element_type=jnp.float32,
                )[0]
            )
        h = jnp.concatenate(pieces, axis=2) + jnp.tile(conv_bias[layer], planes)
        if layer + 1 < layers:
            h = jnp.maximum(h, 0.0)
            xs = x0 - width + jnp.arange(h.shape[0])
            ys = y0 - width + jnp.arange(h.shape[1])
            zs = z0 - width + jnp.arange(planes * 64) // 64
            inside = (
                ((xs >= 0) & (xs < 32))[:, None, None]
                & ((ys >= 0) & (ys < 512))[None, :, None]
                & ((zs >= 0) & (zs < 16))[None, None, :]
            )
            h = jnp.where(inside, h, 0.0)
        hidden = h.astype(jnp.bfloat16)
    groups = [[4 * z + x for x in range(4)] for z in range(4)]
    out = hidden.reshape(256, 256).T.reshape(4, 64, 256)
    out = lax.all_to_all(out, "frame", 0, 0, axis_index_groups=groups, tiled=True)
    out = out.reshape(4, 64, 8, 32).transpose(1, 2, 0, 3).reshape(1, 64, 8, 128)
    return out


def solution(mesh):
    return jax.shard_map(
        shards,
        mesh=mesh,
        in_specs=(
            P("frame", None, None, "bx", "by"),
            P(None, None, "bx", "by"),
            P("frame", None, "bx", "by"),
            P(),
            P(),
            P(),
            P(),
            P(),
            P(),
        ),
        out_specs=P("frame", None, "bx", "by"),
        check_vma=False,
    )
```

time: 376 us -> 242 us (0.64)
  the two profiles are of different devices: /device:TPU:7 before, /device:TPU:1 now
where the time goes in v1:
time: 242 us; the launch traced here: 237 us
  local copies, waits for them, and re-layouts  109 us (45%)
  starting transfers between devices  44.5 us (18%)
  Pallas kernels  35.4 us (15%)
  waiting for transfers between devices  21.1 us (9%)
  other arithmetic  10.6 us (4%)
  matrix products  8.14 us (3%)
  blocking collectives  8.13 us (3%)
    scatter x36, local copies, waits for them, and re-layouts, banded(): blocks = blocks.at[:, :, j + a, :, j, :].set(w[a])  59.1 us
    reshape x4, local copies, waits for them, and re-layouts, banded(): return blocks.reshape(3, 3, 6 * c, 4 * o)  25.6 us
    pallas_call x6, Pallas kernels, merge(): pl.pallas_call(functools.partial(merge_kernel, last), out_shape=jax.Shape...  18.3 us
    pallas_call x1, Pallas kernels, attend(): pl.pallas_call(attend_kernel, out_shape=jax.ShapeDtypeStruct((4, planes,...  17.1 us
    ppermute x1, starting transfers between devices, shards(): right = lax.ppermute(hidden[:, :halo], ('frame', 'by'), y_prev)  11.6 us
    all_to_all x1, blocking collectives, shards(): lax.all_to_all(out, 'frame', 0, 0, axis_index_groups=groups, tiled=True)  8.13 us
    conv_general_dilated x8, matrix products, shards(): lax.conv_general_dilated(part[None], w[:, :, :(count + 2) * 64, :count *...  7.72 us
    ppermute x2, starting transfers between devices, ring_reduce(): from_low = lax.ppermute(slots[2][:half], 'frame', up)  6.88 us
  transfers between devices with their start and end apart: 14, of which 6 were waited for; matrix products, arithmetic and copies ran while one was open for 42% of the time, Pallas kernels for 4%

profile of v1, /device:TPU:1, one launch (start us, length us, event | category | flops | bytes accessed | tf_op | source)
XLA Modules:
  0.0 237.4 jit_solution(16905172368454335708)
XLA Ops:
  2.1 17.1 %attend.1 = bf16[4,16,136,128]{3,2,1,0:T(8,128)(2,1)} custom-call(s32[2]{0:T(128)} %pad_add_fusion.place, bf16[4,16,512,128]{3,2,1,0:T(8,128)(2,1)} %bitcast.194, bf16[16,512,128]{2,1,0:T(8,128)(2,1)} %bitcast.199, s32[4,16,8,128]{3,2,1,0:T(8,128)} %seen.1, bf16[64,64]{1,0:T(8,128)(2,1)} %bitcast.214, bf16[64,64]{1,0:T(8,128)(2,1)} %wk.1), custom_call_target="tpu_custom_call" | custom-call | tf_op jit(solution)/shard_map/attend/pallas_call | solution.py:83
  19.2 2.5 %slice_bitcast_fusion.13 = (bf16[8,136,128]{2,1,0:T(8,128)(2,1)S(1)}, bf16[8,136,128]{2,1,0:T(8,128)(2,1)S(1)}, bf16[8,136,128]{2,1,0:T(8,128)(2,1)}, bf16[8,136...) fusion(bf16[4,16,136,128]{3,2,1,0:T(8,128)(2,1)} %attend.1), kind=kLoop, calls=%fused_computation.101 | loop fusion | bytes 3342336 | tf_op jit(solution)/shard_map/slice | solution.py:156
  21.6 2.0 collective-permute-start
  25.0 2.8 %scatter.160 = bf16[3,3,6,64,4,64]{5,3,1,0,4,2:T(8,128)(2,1)} pad(bf16[3,3,1,64,1,64]{5,3,1,0,4,2:T(8,128)(2,1)S(1)} %get-tuple-element.599, bf16[]{:T(256)} %constant.1236.clone.1), padding=0_0x0_0x0_5x0_0x0_3x0_0 | pad | bytes 1843202 | tf_op jit(solution)/shard_map/scatter | solution.py:167
  33.1 2.6 %scatter.200 = bf16[3,3,6,64,4,64]{5,3,1,0,4,2:T(8,128)(2,1)} pad(bf16[3,3,1,64,1,64]{5,3,1,0,4,2:T(8,128)(2,1)S(1)} %get-tuple-element.601, bf16[]{:T(256)} %constant.1236.clone.1), padding=0_0x0_0x0_5x0_0x0_3x0_0 | pad | bytes 1843202 | tf_op jit(solution)/shard_map/scatter | solution.py:167
  35.7 2.6 %scatter.180 = bf16[3,3,6,64,4,64]{5,3,1,0,4,2:T(8,128)(2,1)} pad(bf16[3,3,1,64,1,64]{5,3,1,0,4,2:T(8,128)(2,1)S(1)} %get-tuple-element.602, bf16[]{:T(256)} %constant.1236.clone.1), padding=0_0x0_0x0_5x0_0x0_3x0_0 | pad | bytes 1843202 | tf_op jit(solution)/shard_map/scatter | solution.py:167
  38.4 2.8 %scatter.220 = bf16[3,3,6,64,4,64]{5,3,1,0,4,2:T(8,128)(2,1)} pad(bf16[3,3,1,64,1,64]{5,3,1,0,4,2:T(8,128)(2,1)S(1)} %get-tuple-element.600, bf16[]{:T(256)} %constant.1236.clone.1), padding=0_0x0_0x0_5x0_0x0_3x0_0 | pad | bytes 1843202 | tf_op jit(solution)/shard_map/scatter | solution.py:167
  56.3 3.4 %merge.6 = bf16[8,136,128]{2,1,0:T(8,128)(2,1)} custom-call(bf16[8,136,128]{2,1,0:T(8,128)(2,1)} %get-tuple-element.586.refs_0_, bf16[8,136,128]{2,1,0:T(8,128)(2,1)} %copy-done.9), custom_call_target="tpu_custom_call" | custom-call | tf_op jit(solution)/shard_map/merge/pallas_call | solution.py:141
  61.0 3.4 %merge.7 = bf16[8,136,128]{2,1,0:T(8,128)(2,1)} custom-call(bf16[8,136,128]{2,1,0:T(8,128)(2,1)} %get-tuple-element.583.refs_0_, bf16[8,136,128]{2,1,0:T(8,128)(2,1)} %collective-permute-done.2.refs_1_), custom_call_target="tpu_custom_call" | custom-call | tf_op jit(solution)/shard_map/merge/pallas_call | solution.py:141
  65.5 2.6 %collective-permute-start.3 = (bf16[16,136,128]{2,1,0:T(8,128)(2,1)S(1)}, bf16[16,136,128]{2,1,0:T(8,128)(2,1)}, u32[]{:S(2)}, u32[]{:S(2)}) collective-permute-start(bf16[16,136,128]{2,1,0:T(8,128)(2,1)S(1)} %pad_maximum_fusion.2), channel_id=1, source_target_pairs={{16,0},{32,16},{48,32},{0,48},{80,64},{96,80},{112,96},{64,112},{1... | collective-permute-start | bytes 1671176 | tf_op jit(solution)/shard_map/ppermute | solution.py:158
  70.6 2.5 %collective-permute-done.1.refs_1_ = bf16[16,136,128]{2,1,0:T(8,128)(2,1)S(1)} collective-permute-done((bf16[16,136,128]{2,1,0:T(8,128)(2,1)S(1)}, bf16[16,136,128]{2,1,0:T(8,128)(2,1)S(1)}, u32[]{:S(2)}, u32[]{:S(2)}) %collective-permute-start.1) | collective-permute-done | bytes 557088 | tf_op jit(solution)/shard_map/ppermute | solution.py:157
  73.1 3.8 %collective-permute-done.3.refs_2_ = bf16[16,136,128]{2,1,0:T(8,128)(2,1)} collective-permute-done((bf16[16,136,128]{2,1,0:T(8,128)(2,1)S(1)}, bf16[16,136,128]{2,1,0:T(8,128)(2,1)}, u32[]{:S(2)}, u32[]{:S(2)}) %collective-permute-start.3) | collective-permute-done | bytes 557088 | tf_op jit(solution)/shard_map/ppermute | solution.py:158
  76.9 6.0 %merge.8 = bf16[16,136,128]{2,1,0:T(8,128)(2,1)} custom-call(bf16[16,136,128]{2,1,0:T(8,128)(2,1)} %slice_bitcast_fusion.4.refs_0_, bf16[16,136,128]{2,1,0:T(8,128)(2,1)} %copy-done.8, bf16[16,136,128]{2,1,0:T(8,128)(2,1)} %collective-permute-done.3.refs_2_), custom_call_target="tpu_custom_call" | custom-call | tf_op jit(solution)/shard_map/merge/pallas_call | solution.py:141
  84.6 4.9 %collective-permute-start.4 = (bf16[2,136,128]{2,1,0:T(8,128)(2,1)S(1)}, bf16[2,136,128]{2,1,0:T(8,128)(2,1)S(1)}, u32[]{:S(2)}, u32[]{:S(2)}) collective-permute-start(bf16[2,136,128]{2,1,0:T(8,128)(2,1)S(1)} %get-tuple-element.623), channel_id=1, source_target_pairs={{0,64},{16,80},{32,96},{48,112},{64,128},{80,144},{96,160},{112,17... | collective-permute-start | bytes 208904 | tf_op jit(solution)/shard_map/ppermute | solution.py:153
  89.4 3.1 %collective-permute-start.6 = (bf16[2,136,128]{2,1,0:T(8,128)(2,1)S(1)}, bf16[2,136,128]{2,1,0:T(8,128)(2,1)S(1)}, u32[]{:S(2)}, u32[]{:S(2)}) collective-permute-start(bf16[2,136,128]{2,1,0:T(8,128)(2,1)S(1)} %get-tuple-element.620), channel_id=1, source_target_pairs={{64,0},{80,16},{96,32},{112,48},{128,64},{144,80},{160,96},{176,11... | collective-permute-start | bytes 208904 | tf_op jit(solution)/shard_map/ppermute | solution.py:154
  101.6 2.9 %collective-permute-start.7 = (bf16[4,136,128]{2,1,0:T(8,128)(2,1)S(1)}, bf16[4,136,128]{2,1,0:T(8,128)(2,1)S(1)}, u32[]{:S(2)}, u32[]{:S(2)}) collective-permute-start(bf16[4,136,128]{2,1,0:T(8,128)(2,1)S(1)} %pad_maximum_fusion.5), channel_id=1, source_target_pairs={{64,0},{80,16},{96,32},{112,48},{128,64},{144,80},{160,96},{176,11... | collective-permute-start | bytes 417800 | tf_op jit(solution)/shard_map/ppermute | solution.py:158
  106.6 3.0 %collective-permute-done.7.refs_2_ = bf16[4,136,128]{2,1,0:T(8,128)(2,1)S(1)} collective-permute-done((bf16[4,136,128]{2,1,0:T(8,128)(2,1)S(1)}, bf16[4,136,128]{2,1,0:T(8,128)(2,1)S(1)}, u32[]{:S(2)}, u32[]{:S(2)}) %collective-permute-start.7) | collective-permute-done | bytes 139296 | tf_op jit(solution)/shard_map/ppermute | solution.py:158
  114.3 5.6 %collective-permute-start.8 = (bf16[8,32,256]{2,1,0:T(8,128)(2,1)S(1)}, bf16[8,32,256]{2,1,0:T(8,128)(2,1)S(1)}, u32[]{:S(2)}, u32[]{:S(2)}) collective-permute-start(bf16[8,32,256]{2,1,0:T(8,128)(2,1)S(1)} %reshape.2337), channel_id=1, source_target_pairs={{0,64},{16,80},{32,96},{48,112},{64,128},{80,144},{96,160},{112,17... | collective-permute-start | bytes 393224 | tf_op jit(solution)/shard_map/ppermute | solution.py:192
  122.4 6.4 %collective-permute-done.9 = bf16[8,32,256]{2,1,0:T(8,128)(2,1)S(1)} collective-permute-done((bf16[8,32,256]{2,1,0:T(8,128)(2,1)S(1)}, bf16[8,32,256]{2,1,0:T(8,128)(2,1)S(1)}, u32[]{:S(2)}, u32[]{:S(2)}) %collective-permute-start.9) | collective-permute-done | bytes 131104 | tf_op jit(solution)/shard_map/ppermute | solution.py:193
  128.9 11.6 %collective-permute-start.11 = (bf16[8,4,768]{2,1,0:T(4,128)(2,1)S(1)}, bf16[8,4,768]{2,1,0:T(4,128)(2,1)S(1)}, u32[]{:S(2)}, u32[]{:S(2)}) collective-permute-start(bf16[8,4,768]{2,1,0:T(4,128)(2,1)S(1)} %get-tuple-element.628), channel_id=1, source_target_pairs={{16,0},{32,16},{48,32},{1,48},{17,1},{33,17},{49,33},{2,49},{18,2}... | collective-permute-start | bytes 147464 | tf_op jit(solution)/shard_map/ppermute | solution.py:202
  140.5 2.2 collective-permute-start.10
  143.3 3.8 %collective-permute-done.10 = bf16[8,4,768]{2,1,0:T(4,128)(2,1)S(1)} collective-permute-done((bf16[8,4,768]{2,1,0:T(4,128)(2,1)S(1)}, bf16[8,4,768]{2,1,0:T(4,128)(2,1)S(1)}, u32[]{:S(2)}, u32[]{:S(2)}) %collective-permute-start.10) | collective-permute-done | bytes 49184 | tf_op jit(solution)/shard_map/ppermute | solution.py:201
  149.4 4.7 %collective-permute-start.12 = (bf16[4,40,768]{2,1,0:T(8,128)(2,1)}, bf16[4,40,768]{2,1,0:T(8,128)(2,1)}, u32[]{:S(2)}, u32[]{:S(2)}) collective-permute-start(bf16[4,40,768]{2,1,0:T(8,128)(2,1)} %get-tuple-element.625), channel_id=1, source_target_pairs={{0,4},{4,8},{8,12},{1,5},{5,9},{9,13},{2,6},{6,10},{10,14},{3,7},{... | collective-permute-start | bytes 737288 | tf_op jit(solution)/shard_map/ppermute | solution.py:206
  154.6 7.2 %copy.83 = bf16[3,3,6,64,4,64]{5,4,3,2,1,0:T(4,128)(2,1)S(1)} copy(bf16[3,3,6,64,4,64]{5,3,1,0,4,2:T(8,128)(2,1)} %bitcast_dynamic-update-slice_fusion) | data formatting | bytes 3538944 | tf_op jit(solution)/shard_map/scatter | solution.py:167
  161.8 3.3 %reshape.2353 = bf16[3,3,384,256]{3,2,1,0:T(8,128)(2,1)} reshape(bf16[3,3,6,64,4,64]{5,4,3,2,1,0:T(4,128)(2,1)S(1)} %copy.83) | data formatting | bytes 3538944 | tf_op jit(solution)/shard_map/reshape | solution.py:168
  165.1 7.2 %copy.76 = bf16[3,3,6,64,4,64]{5,4,3,2,1,0:T(4,128)(2,1)S(1)} copy(bf16[3,3,6,64,4,64]{5,3,1,0,4,2:T(8,128)(2,1)} %get-tuple-element.609) | data formatting | bytes 3538944 | tf_op jit(solution)/shard_map/scatter | solution.py:167
  172.2 3.3 %reshape.2349 = bf16[3,3,384,256]{3,2,1,0:T(8,128)(2,1)} reshape(bf16[3,3,6,64,4,64]{5,4,3,2,1,0:T(4,128)(2,1)S(1)} %copy.76) | data formatting | bytes 3538944 | tf_op jit(solution)/shard_map/reshape | solution.py:168
  175.5 7.2 %copy.69 = bf16[3,3,6,64,4,64]{5,4,3,2,1,0:T(4,128)(2,1)S(1)} copy(bf16[3,3,6,64,4,64]{5,3,1,0,4,2:T(8,128)(2,1)} %get-tuple-element.603) | data formatting | bytes 3538944 | tf_op jit(solution)/shard_map/scatter | solution.py:167
  182.6 15.8 %reshape.2345 = bf16[3,3,384,256]{3,2,1,0:T(8,128)(2,1)} reshape(bf16[3,3,6,64,4,64]{5,4,3,2,1,0:T(4,128)(2,1)S(1)} %copy.69) | data formatting | bytes 3538944 | tf_op jit(solution)/shard_map/reshape | solution.py:168
  198.5 7.2 %copy.57 = bf16[3,3,6,64,4,64]{5,4,3,2,1,0:T(4,128)(2,1)S(1)} copy(bf16[3,3,6,64,4,64]{5,3,1,0,4,2:T(8,128)(2,1)} %get-tuple-element.587) | data formatting | bytes 3538944 | tf_op jit(solution)/shard_map/scatter | solution.py:167
  205.6 3.2 %reshape.2341 = bf16[3,3,384,256]{3,2,1,0:T(8,128)(2,1)} reshape(bf16[3,3,6,64,4,64]{5,4,3,2,1,0:T(4,128)(2,1)S(1)} %copy.57) | data formatting | bytes 3538944 | tf_op jit(solution)/shard_map/reshape | solution.py:168
  228.2 8.1 %all_to_all.5 = bf16[4,64,256]{2,1,0:T(8,128)(2,1)S(1)} all-to-all(bf16[4,64,256]{2,1,0:T(8,128)(2,1)S(1)} %bitcast.213), channel_id=1, replica_groups={{0,16,32,48},{64,80,96,112},{128,144,160,176},{192,208,224,240},{1,17,3..., dimensions={0} | all-to-all | bytes 262144 | tf_op jit(solution)/shard_map/all_to_all | solution.py:247
  (202 shorter events, 72.0 us)
Async XLA Ops:
  0.0 113.5 %copy-start = (bf16[64,64]{1,0:T(8,128)(2,1)S(1)}, bf16[64,64]{1,0:T(8,128)(2,1)}, u32[]{:S(2)}) copy-start(bf16[64,64]{1,0:T(8,128)(2,1)} %param.111) | copy-start | bytes 24580
  19.2 5.8 %copy-start.2 = (bf16[4,3,3,3,64,64]{5,4,3,2,1,0:T(8,128)(2,1)S(1)}, bf16[4,3,3,3,64,64]{5,4,3,2,1,0:T(8,128)(2,1)}, u32[]{:S(2)}) copy-start(bf16[4,3,3,3,64,64]{5,4,3,2,1,0:T(8,128)(2,1)} %param.112) | copy-start | bytes 2654212
  21.6 33.9 %collective-permute-start = (bf16[8,136,128]{2,1,0:T(8,128)(2,1)S(1)}, bf16[8,136,128]{2,1,0:T(8,128)(2,1)S(1)}, u32[]{:S(2)}, u32[]{:S(2)}) collective-permute-start(bf16[8,136,128]{2,1,0:T(8,128)(2,1)S(1)} %get-tuple-element.585), channel_id=1, source_target_pairs={{0,16},{16,32},{32,48},{48,0},{64,80},{80,96},{96,112},{112,64},{1... | collective-permute-start | bytes 835592 | tf_op jit(solution)/shard_map/ppermute | solution.py:153
  23.7 37.4 %collective-permute-start.2 = (bf16[8,136,128]{2,1,0:T(8,128)(2,1)S(1)}, bf16[8,136,128]{2,1,0:T(8,128)(2,1)}, u32[]{:S(2)}, u32[]{:S(2)}) collective-permute-start(bf16[8,136,128]{2,1,0:T(8,128)(2,1)S(1)} %get-tuple-element.582), channel_id=1, source_target_pairs={{16,0},{32,16},{48,32},{0,48},{80,64},{96,80},{112,96},{64,112},{1... | collective-permute-start | bytes 835592 | tf_op jit(solution)/shard_map/ppermute | solution.py:154
  43.7 11.3 %copy-start.17 = (f32[4,64]{1,0:T(4,128)S(1)}, f32[4,64]{1,0:T(4,128)}, u32[]{:S(2)}) copy-start(f32[4,64]{1,0:T(4,128)} %param.113) | copy-start | bytes 3076
  60.7 12.3 %collective-permute-start.1 = (bf16[16,136,128]{2,1,0:T(8,128)(2,1)S(1)}, bf16[16,136,128]{2,1,0:T(8,128)(2,1)S(1)}, u32[]{:S(2)}, u32[]{:S(2)}) collective-permute-start(bf16[16,136,128]{2,1,0:T(8,128)(2,1)S(1)} %pad_maximum_fusion.1), channel_id=1, source_target_pairs={{0,16},{16,32},{32,48},{48,0},{64,80},{80,96},{96,112},{112,64},{1... | collective-permute-start | bytes 1671176 | tf_op jit(solution)/shard_map/ppermute | solution.py:157
  65.5 11.4 %collective-permute-start.3 = (bf16[16,136,128]{2,1,0:T(8,128)(2,1)S(1)}, bf16[16,136,128]{2,1,0:T(8,128)(2,1)}, u32[]{:S(2)}, u32[]{:S(2)}) collective-permute-start(bf16[16,136,128]{2,1,0:T(8,128)(2,1)S(1)} %pad_maximum_fusion.2), channel_id=1, source_target_pairs={{16,0},{32,16},{48,32},{0,48},{80,64},{96,80},{112,96},{64,112},{1... | collective-permute-start | bytes 1671176 | tf_op jit(solution)/shard_map/ppermute | solution.py:158
  70.6 42.9 %copy-start.16 = (bf16[64,64]{1,0:T(8,128)(2,1)S(1)}, bf16[64,64]{1,0:T(8,128)(2,1)}, u32[]{:S(2)}) copy-start(bf16[64,64]{1,0:T(8,128)(2,1)} %param.110) | copy-start | bytes 24580
  73.1 3.8 %copy-start.8 = (bf16[16,136,128]{2,1,0:T(8,128)(2,1)}, bf16[16,136,128]{2,1,0:T(8,128)(2,1)S(1)}, u32[]{:S(2)}) copy-start(bf16[16,136,128]{2,1,0:T(8,128)(2,1)S(1)} %collective-permute-done.1.refs_1_) | copy-start | bytes 1671172
  84.6 9.7 %collective-permute-start.4 = (bf16[2,136,128]{2,1,0:T(8,128)(2,1)S(1)}, bf16[2,136,128]{2,1,0:T(8,128)(2,1)S(1)}, u32[]{:S(2)}, u32[]{:S(2)}) collective-permute-start(bf16[2,136,128]{2,1,0:T(8,128)(2,1)S(1)} %get-tuple-element.623), channel_id=1, source_target_pairs={{0,64},{16,80},{32,96},{48,112},{64,128},{80,144},{96,160},{112,17... | collective-permute-start | bytes 208904 | tf_op jit(solution)/shard_map/ppermute | solution.py:153
  89.4 8.9 %collective-permute-start.6 = (bf16[2,136,128]{2,1,0:T(8,128)(2,1)S(1)}, bf16[2,136,128]{2,1,0:T(8,128)(2,1)S(1)}, u32[]{:S(2)}, u32[]{:S(2)}) collective-permute-start(bf16[2,136,128]{2,1,0:T(8,128)(2,1)S(1)} %get-tuple-element.620), channel_id=1, source_target_pairs={{64,0},{80,16},{96,32},{112,48},{128,64},{144,80},{160,96},{176,11... | collective-permute-start | bytes 208904 | tf_op jit(solution)/shard_map/ppermute | solution.py:154
  97.5 9.1 %collective-permute-start.5 = (bf16[4,136,128]{2,1,0:T(8,128)(2,1)S(1)}, bf16[4,136,128]{2,1,0:T(8,128)(2,1)S(1)}, u32[]{:S(2)}, u32[]{:S(2)}) collective-permute-start(bf16[4,136,128]{2,1,0:T(8,128)(2,1)S(1)} %pad_maximum_fusion.4), channel_id=1, source_target_pairs={{0,64},{16,80},{32,96},{48,112},{64,128},{80,144},{96,160},{112,17... | collective-permute-start | bytes 417800 | tf_op jit(solution)/shard_map/ppermute | solution.py:157
  101.6 8.0 %collective-permute-start.7 = (bf16[4,136,128]{2,1,0:T(8,128)(2,1)S(1)}, bf16[4,136,128]{2,1,0:T(8,128)(2,1)S(1)}, u32[]{:S(2)}, u32[]{:S(2)}) collective-permute-start(bf16[4,136,128]{2,1,0:T(8,128)(2,1)S(1)} %pad_maximum_fusion.5), channel_id=1, source_target_pairs={{64,0},{80,16},{96,32},{112,48},{128,64},{144,80},{160,96},{176,11... | collective-permute-start | bytes 417800 | tf_op jit(solution)/shard_map/ppermute | solution.py:158
  106.6 3.0 %copy-start.12 = (bf16[4,136,128]{2,1,0:T(8,128)(2,1)}, bf16[4,136,128]{2,1,0:T(8,128)(2,1)S(1)}, u32[]{:S(2)}) copy-start(bf16[4,136,128]{2,1,0:T(8,128)(2,1)S(1)} %collective-permute-done.5.refs_1_) | copy-start | bytes 417796
  114.3 8.1 %collective-permute-start.8 = (bf16[8,32,256]{2,1,0:T(8,128)(2,1)S(1)}, bf16[8,32,256]{2,1,0:T(8,128)(2,1)S(1)}, u32[]{:S(2)}, u32[]{:S(2)}) collective-permute-start(bf16[8,32,256]{2,1,0:T(8,128)(2,1)S(1)} %reshape.2337), channel_id=1, source_target_pairs={{0,64},{16,80},{32,96},{48,112},{64,128},{80,144},{96,160},{112,17... | collective-permute-start | bytes 393224 | tf_op jit(solution)/shard_map/ppermute | solution.py:192
  121.1 7.7 %collective-permute-start.9 = (bf16[8,32,256]{2,1,0:T(8,128)(2,1)S(1)}, bf16[8,32,256]{2,1,0:T(8,128)(2,1)S(1)}, u32[]{:S(2)}, u32[]{:S(2)}) collective-permute-start(bf16[8,32,256]{2,1,0:T(8,128)(2,1)S(1)} %reshape.2337), channel_id=1, source_target_pairs={{64,0},{80,16},{96,32},{112,48},{128,64},{144,80},{160,96},{176,11... | collective-permute-start | bytes 393224 | tf_op jit(solution)/shard_map/ppermute | solution.py:193
  128.8 25.3 %copy-start.3 = (bf16[8,32,768]{2,1,0:T(8,128)(2,1)}, bf16[8,32,768]{2,1,0:T(8,128)(2,1)S(1)}, u32[]{:S(2)}) copy-start(bf16[8,32,768]{2,1,0:T(8,128)(2,1)S(1)} %constant_dynamic-update-slice_fusion.12) | copy-start | bytes 1179652
  128.9 14.4 %collective-permute-start.11 = (bf16[8,4,768]{2,1,0:T(4,128)(2,1)S(1)}, bf16[8,4,768]{2,1,0:T(4,128)(2,1)S(1)}, u32[]{:S(2)}, u32[]{:S(2)}) collective-permute-start(bf16[8,4,768]{2,1,0:T(4,128)(2,1)S(1)} %get-tuple-element.628), channel_id=1, source_target_pairs={{16,0},{32,16},{48,32},{1,48},{17,1},{33,17},{49,33},{2,49},{18,2}... | collective-permute-start | bytes 147464 | tf_op jit(solution)/shard_map/ppermute | solution.py:202
  140.5 6.6 %collective-permute-start.10 = (bf16[8,4,768]{2,1,0:T(4,128)(2,1)S(1)}, bf16[8,4,768]{2,1,0:T(4,128)(2,1)S(1)}, u32[]{:S(2)}, u32[]{:S(2)}) collective-permute-start(bf16[8,4,768]{2,1,0:T(4,128)(2,1)S(1)} %get-tuple-element.627), channel_id=1, source_target_pairs={{0,16},{16,32},{32,48},{48,1},{1,17},{17,33},{33,49},{49,2},{2,18}... | collective-permute-start | bytes 147464 | tf_op jit(solution)/shard_map/ppermute | solution.py:201
  143.3 10.8 %copy-start.10 = (bf16[8,4,768]{2,1,0:T(4,128)(2,1)}, bf16[8,4,768]{2,1,0:T(4,128)(2,1)S(1)}, u32[]{:S(2)}) copy-start(bf16[8,4,768]{2,1,0:T(4,128)(2,1)S(1)} %collective-permute-done.11) | copy-start | bytes 147460
  147.1 7.0 %copy-start.11 = (bf16[8,4,768]{2,1,0:T(4,128)(2,1)}, bf16[8,4,768]{2,1,0:T(4,128)(2,1)S(1)}, u32[]{:S(2)}) copy-start(bf16[8,4,768]{2,1,0:T(4,128)(2,1)S(1)} %collective-permute-done.10) | copy-start | bytes 147460
  148.1 63.9 %collective-permute-start.13 = (bf16[4,40,768]{2,1,0:T(8,128)(2,1)}, bf16[4,40,768]{2,1,0:T(8,128)(2,1)}, u32[]{:S(2)}, u32[]{:S(2)}) collective-permute-start(bf16[4,40,768]{2,1,0:T(8,128)(2,1)} %get-tuple-element.626), channel_id=1, source_target_pairs={{4,0},{8,4},{12,8},{5,1},{9,5},{13,9},{6,2},{10,6},{14,10},{7,3},{... | collective-permute-start | bytes 737288 | tf_op jit(solution)/shard_map/ppermute | solution.py:207
  149.4 62.6 %collective-permute-start.12 = (bf16[4,40,768]{2,1,0:T(8,128)(2,1)}, bf16[4,40,768]{2,1,0:T(8,128)(2,1)}, u32[]{:S(2)}, u32[]{:S(2)}) collective-permute-start(bf16[4,40,768]{2,1,0:T(8,128)(2,1)} %get-tuple-element.625), channel_id=1, source_target_pairs={{0,4},{4,8},{8,12},{1,5},{5,9},{9,13},{2,6},{6,10},{10,14},{3,7},{... | collective-permute-start | bytes 737288 | tf_op jit(solution)/shard_map/ppermute | solution.py:206
  208.9 4.9 %copy-start.7 = (bf16[3,3,384,256]{3,2,1,0:T(8,128)(2,1)S(1)}, bf16[3,3,384,256]{3,2,1,0:T(8,128)(2,1)}, u32[]{:S(2)}) copy-start(bf16[3,3,384,256]{3,2,1,0:T(8,128)(2,1)} %reshape.2341) | copy-start | bytes 5308420
  208.9 4.9 %copy-start.24 = (pred[8,5]{0,1:T(8,128)(4,1)S(1)}, pred[8,5]{0,1:T(8,128)(4,1)}, u32[]{:S(2)}) copy-start(pred[8,5]{0,1:T(8,128)(4,1)} %constant.1281) | copy-start | bytes 124
  218.1 1.5 copy-start.6
  218.1 1.5 copy-start.23
  222.2 1.5 copy-start.5
  222.2 1.5 copy-start.22
  225.6 1.5 copy-start.4
  225.6 1.5 copy-start.21
  227.1 10.3 %copy-start.1 = (bf16[64,64]{1,0:T(8,128)(2,1)S(1)}, bf16[64,64]{1,0:T(8,128)(2,1)}, u32[]{:S(2)}) copy-start(bf16[64,64]{1,0:T(8,128)(2,1)} %param.111) | copy-start | bytes 24580
  (7 other events, 5.9 us)

commit v2 on v0

v2 whole, which is shorter than its diff:
```python
import functools

import jax
import jax.numpy as jnp
from jax import lax
from jax.experimental import pallas as pl
from jax.experimental.pallas import tpu as pltpu
from jax.sharding import PartitionSpec as P

absent_score = -1e30
halo = 4
stride = 48
bf16, f32 = jnp.bfloat16, jnp.float32
VM = pl.BlockSpec(memory_space=pltpu.VMEM)


def dot(a, b):
    return jnp.dot(a, b, preferred_element_type=f32)


def lane_blocks(v):
    lane = lax.broadcasted_iota(jnp.int32, (8, 128), 1)
    low = lane < 64
    even = (lane & 63) < 32
    t = [None] * 4
    for i in (0, 1):
        t[i] = jnp.where(low, v[i], pltpu.roll(v[i + 2], 64, 1))
        t[i + 2] = jnp.where(low, pltpu.roll(v[i], 64, 1), v[i + 2])
    o = [None] * 4
    for i in (0, 2):
        o[i] = jnp.where(even, t[i], pltpu.roll(t[i + 1], 32, 1))
        o[i + 1] = jnp.where(even, pltpu.roll(t[i], 96, 1), t[i + 1])
    return o


def three_terms(m):
    hi = m.astype(bf16).astype(f32)
    mid = (m - hi).astype(bf16).astype(f32)
    return hi, mid, m - hi - mid


def attend_kernel(place, feat, embed, seen, wq, wk, *refs):
    outs, tmp = refs[:4], refs[4]
    frames, planes = feat.shape[:2]
    turn = (128 - 32 * place[0]) & 127
    for p in range(planes):
        tmp[p] = embed[p].astype(f32)
    cols = [tmp[p, pl.ds(i, 64, stride=8), :] for p in range(planes) for i in range(8)]
    wide = jnp.concatenate(cols, axis=1).astype(bf16)
    q = lax.dot_general(wq[...], wide, (((0,), (0,)), ((), ())), preferred_element_type=f32)
    qk = dot(wk[...], q.astype(bf16)) * 0.125
    for p in range(planes):
        for i in range(8):
            at = (8 * p + i) * 128
            tmp[p, pl.ds(i, 64, stride=8), :] = qk[:, at : at + 128]
    for p in range(planes):
        sums = [jnp.zeros((8, 128), f32) for _ in range(frames)]
        for g in range(16):
            rows = slice(32 * g, 32 * g + 32)
            key = tmp[p, rows, :]
            for f in range(frames):
                prod = (key * feat[f, p, rows, :].astype(f32)).reshape(4, 8, 128)
                sums[f] = sums[f] + jnp.sum(prod, axis=0)
        ok = [seen[f, p] > 0 for f in range(frames)]
        m = jnp.full((8, 128), absent_score, f32)
        for f in range(frames):
            m = jnp.maximum(m, jnp.where(ok[f], sums[f], absent_score))
        e = [jnp.where(ok[f], jnp.exp(sums[f] - m), 0.0) for f in range(frames)]
        total = e[0]
        for f in range(1, frames):
            total = total + e[f]

        def put(g, tiles):
            tiles = [pltpu.roll(t, turn, 1) for t in tiles]
            for out, tile in zip(outs, lane_blocks(tiles)):
                out[p, 8 * g : 8 * g + 8, :] = tile.astype(bf16)

        for g in range(16):
            rows = slice(32 * g, 32 * g + 32)
            acc = jnp.zeros((4, 8, 128), f32)
            for f in range(frames):
                acc = acc + e[f][None] * feat[f, p, rows, :].astype(f32).reshape(4, 8, 128)
            put(g, [acc[i] for i in range(4)])
        put(16, [*three_terms(m), total])


def attend(half, place, feat, embed, visible, w_query, w_key):
    frames, planes, rows = feat.shape[:3]
    c = w_key.shape[0]
    n = 2
    count = planes // 2

    def block(i, place):
        rel = half * count + i * n
        return (((rel // 4 + place[1]) & 3) * 4 + rel % 4) // n

    return pl.pallas_call(
        attend_kernel,
        out_shape=[jax.ShapeDtypeStruct((count, 136, 128), bf16)] * 4,
        grid_spec=pltpu.PrefetchScalarGridSpec(
            num_scalar_prefetch=1,
            grid=(count // n,),
            in_specs=[
                pl.BlockSpec((frames, n, rows, 128), lambda i, p: (0, block(i, p), 0, 0)),
                pl.BlockSpec((n, rows, 128), lambda i, p: (block(i, p), 0, 0)),
                pl.BlockSpec((frames, n, 8, 128), lambda i, p: (0, block(i, p), 0, 0)),
                pl.BlockSpec((c, c), lambda i, p: (0, 0)),
                pl.BlockSpec((c, c), lambda i, p: (0, 0)),
            ],
            out_specs=[pl.BlockSpec((n, 136, 128), lambda i, p: (i, 0, 0))] * 4,
            scratch_shapes=[pltpu.VMEM((n, rows, 128), f32)],
        ),
        compiler_params=pltpu.CompilerParams(
            dimension_semantics=("arbitrary",), vmem_limit_bytes=12 << 20
        ),
        cost_estimate=pl.CostEstimate(flops=10**8, bytes_accessed=12 << 20, transcendentals=0),
        name="attend",
    )(place, feat, embed, visible, w_query, w_key)


def spread(v):
    u = v + pltpu.roll(v, 64, 1)
    return u + pltpu.roll(u, 32, 1)


def merged_plane(parts):
    lane = lax.broadcasted_iota(jnp.int32, (8, 128), 1)
    tail = lane >= 96
    stats = [r[p, 128:136, :].astype(f32) for r, p in parts]
    ms = [spread(jnp.where(tail, 0.0, s)) for s in stats]
    ls = [spread(jnp.where(tail, s, 0.0)) for s in stats]
    m = functools.reduce(jnp.maximum, ms)
    ws = [jnp.exp(v - m) for v in ms]
    total = sum(w * v for w, v in zip(ws, ls))
    return ws, total, m


def weighted_rows(parts, ws):
    acc = None
    for (r, p), w in zip(parts, ws):
        term = r[p, 0:128, :].astype(f32).reshape(16, 8, 128) * w[None]
        acc = term if acc is None else acc + term
    return acc.reshape(128, 128)


def merge_kernel(n, sizes, *refs):
    ins, outs = refs[:n], refs[n:]
    lane = lax.broadcasted_iota(jnp.int32, (8, 128), 1)
    at = 0
    for out, size in zip(outs, sizes):
        for i in range(size):
            parts = [(r, at) for r in ins]
            ws, total, m = merged_plane(parts)
            out[i, 0:128, :] = weighted_rows(parts, ws).astype(bf16)
            hi, mid, low = three_terms(m)
            packed = jnp.where(
                lane < 32, hi, jnp.where(lane < 64, mid, jnp.where(lane >= 96, total, low))
            )
            out[i, 128:136, :] = packed.astype(bf16)
            at += 1


def merge(parts, sizes):
    n = parts[0].shape[0]
    return pl.pallas_call(
        functools.partial(merge_kernel, len(parts), sizes),
        out_shape=[jax.ShapeDtypeStruct((s, 136, 128), bf16) for s in sizes],
        in_specs=[VM] * len(parts),
        out_specs=[VM] * len(sizes),
        compiler_params=pltpu.CompilerParams(vmem_limit_bytes=6 << 20),
        cost_estimate=pl.CostEstimate(flops=n * 10**5, bytes_accessed=n * 10**5, transcendentals=0),
        name="merge",
    )(*parts)


def finish_kernel(own, low_a, low_b, high_a, high_b, wv, wo, out, rows):
    for p in range(4):
        low, high = (low_a, high_a) if p < 2 else (low_b, high_b)
        parts = [(own, p), (low, p % 2), (high, p % 2)]
        ws, total, _ = merged_plane(parts)
        inv = 1.0 / total
        rows[128 * p : 128 * p + 128, :] = weighted_rows(parts, [w * inv for w in ws])
    lines = []
    for x in range(8):
        t = rows[pl.ds(x, 64, stride=8), :].T
        lines.append(jnp.concatenate([t[32 * i : 32 * i + 32] for i in range(4)], axis=1))
    mixed = jnp.concatenate(lines, axis=0).astype(bf16)
    attended = dot(mixed, wv[...]).astype(bf16)
    out[...] = dot(attended, wo[...]).astype(bf16)


def finish(own, low_a, low_b, high_a, high_b, wv, wo):
    return pl.pallas_call(
        finish_kernel,
        out_shape=jax.ShapeDtypeStruct((256, 256), bf16),
        in_specs=[VM] * 7,
        out_specs=VM,
        scratch_shapes=[pltpu.VMEM((512, 128), f32)],
        compiler_params=pltpu.CompilerParams(vmem_limit_bytes=6 << 20),
        name="finish",
    )(own, low_a, low_b, high_a, high_b, wv, wo)


def weights_kernel(w, wv, wo, band, wide_v, wide_o, tmp):
    zero = jnp.zeros((64, 64), bf16)
    for tap in range(9):
        a = [w[0, 9 * i + tap] for i in range(3)]
        left = jnp.concatenate([a[0], a[1], a[2], zero], axis=0)
        right = jnp.concatenate([zero, a[0], a[1], a[2]], axis=0)
        band[0, tap] = jnp.concatenate([left, right], axis=1)

    @pl.when(pl.program_id(0) == 0)
    def _():
        tmp[...] = wv[...].astype(f32)
        blank = jnp.zeros((16, 64), f32)
        for i in range(4):
            piece = tmp[pl.ds(i, 16, stride=4), :]
            for p in range(4):
                line = jnp.concatenate([piece if j == p else blank for j in range(4)], axis=1)
                at = 64 * i + 16 * p
                wide_v[at : at + 16, :] = line.astype(bf16)
        for p in range(4):
            line = jnp.concatenate([wo[...] if j == p else zero for j in range(4)], axis=1)
            wide_o[64 * p : 64 * p + 64, :] = line


def weights(conv_weight, w_value, w_out):
    layers = conv_weight.shape[0]
    small = pl.BlockSpec((64, 64), lambda i: (0, 0))
    big = pl.BlockSpec((256, 256), lambda i: (0, 0))
    return pl.pallas_call(
        weights_kernel,
        out_shape=[
            jax.ShapeDtypeStruct((layers, 9, 256, 128), bf16),
            jax.ShapeDtypeStruct((256, 256), bf16),
            jax.ShapeDtypeStruct((256, 256), bf16),
        ],
        grid=(layers,),
        in_specs=[pl.BlockSpec((1, 27, 64, 64), lambda i: (i, 0, 0, 0)), small, small],
        out_specs=[pl.BlockSpec((1, 9, 256, 128), lambda i: (i, 0, 0, 0)), big, big],
        scratch_shapes=[pltpu.VMEM((64, 64), f32)],
        compiler_params=pltpu.CompilerParams(
            dimension_semantics=("arbitrary",), vmem_limit_bytes=8 << 20
        ),
        cost_estimate=pl.CostEstimate(flops=10**6, bytes_accessed=8 << 20, transcendentals=0),
        name="weights",
    )(conv_weight.reshape(layers, 27, 64, 64), w_value, w_out)


def conv_kernel(where, block, band, bias, out, buf0, buf1, mask):
    layers = band.shape[0]
    x0, y0, z0 = where[0], where[1], where[2]
    y = lax.broadcasted_iota(jnp.int32, (stride, 128), 0) + (y0 - halo)
    y_ok = (y >= 0) & (y < 512)
    for x in range(16):
        x_at = x0 - halo + x
        line = jnp.where(y_ok & (x_at >= 0) & (x_at < 32), 1.0, 0.0)
        mask[stride * x : stride * x + stride, :] = line
    lane = lax.broadcasted_iota(jnp.int32, (1, 128), 1)

    def spread_rows(buf, value, at, lanes):
        n = value.shape[0]
        buf[1, at : at + n, lanes] = value.astype(bf16)
        buf[0, at : at + n, lanes] = pltpu.roll(value, 1, 0).astype(bf16)
        buf[2, at : at + n, lanes] = pltpu.roll(value, n - 1, 0).astype(bf16)

    for i in range(6):
        lanes = slice(128 * i, 128 * i + 128)
        spread_rows(buf0, block[:, lanes].astype(f32), 0, lanes)
    src, dst = buf0, buf1
    for layer in range(layers):
        first = stride * (layer + 1)
        n = stride * (14 - 2 * layer)
        last = layer + 1 == layers

        def pair(t, carry, src=src, dst=dst, layer=layer, first=first, n=n, last=last):
            lanes_in = pl.ds(pl.multiple_of(128 * t, 128), 256)
            lanes_out = pl.ds(pl.multiple_of(128 * t, 128), 128)
            acc = jnp.zeros((n, 128), f32)
            for b in range(3):
                rows = slice(first + stride * (b - 1), first + stride * (b - 1) + n)
                for e in range(3):
                    acc = acc + dot(src[e, rows, lanes_in], band[layer, 3 * b + e])
            acc = acc + bias[layer : layer + 1, :]
            if last:
                acc = pltpu.roll(acc, n - halo, 0)
                tiles = [acc[stride * x : stride * x + 32] for x in range(8)]
                whole = jnp.concatenate(tiles, axis=0).T
                out[pl.ds(pl.multiple_of(128 * t, 128), 128), :] = whole.astype(bf16)
            else:
                z = z0 - halo + layer + 1 + 2 * t + lane // 64
                ok = jnp.where((z >= 0) & (z < 16), 1.0, 0.0) * mask[first : first + n, :]
                spread_rows(dst, jnp.where(ok > 0, jnp.maximum(acc, 0.0), 0.0), first, lanes_out)
            return carry

        lax.fori_loop(0, 5 - layer, pair, 0)
        src, dst = dst, src


def convolve(where, block, band, bias):
    return pl.pallas_call(
        conv_kernel,
        out_shape=jax.ShapeDtypeStruct((256, 256), bf16),
        in_specs=[pl.BlockSpec(memory_space=pltpu.SMEM), VM, VM, VM],
        out_specs=VM,
        scratch_shapes=[
            pltpu.VMEM((3, 16 * stride, 768), bf16),
            pltpu.VMEM((3, 16 * stride, 640), bf16),
            pltpu.VMEM((16 * stride, 128), f32),
        ],
        compiler_params=pltpu.CompilerParams(vmem_limit_bytes=24 << 20),
        name="convolve",
    )(where, block, band, bias)


def ring_step(s1a, s1b, s2a, s2b, s3a, s3b, up, down):
    send = lambda v, way: lax.ppermute(v, "frame", way)
    from_low, from_high = send(s2a, up), send(s2b, down)
    low_b, high_a = send(s1b, up), send(s3a, down)
    n = s1a.shape[0]
    low_a = send(merge([s1a, from_low], [n])[0], up)
    high_b = send(merge([s3b, from_high], [n])[0], down)
    return low_a, low_b, high_a, high_b


def shards(features, voxel_embed, visible, w_query, w_key, w_value, w_out, conv_weight, conv_bias):
    me = lax.axis_index("frame")
    zh, xi = me // 4, me % 4
    place = jnp.stack([xi, zh]).astype(jnp.int32)
    x_up = [(4 * z + x, 4 * z + (x + 1) % 4) for z in range(4) for x in range(4)]
    x_down = [(j, i) for i, j in x_up]
    z_up = [(4 * z + x, 4 * ((z + 1) % 4) + x) for z in range(4) for x in range(4)]
    z_down = [(j, i) for i, j in z_up]
    frames, planes, c = features.shape[:3]
    feat = features.reshape(frames, planes, c * 8, 128)
    embed = voxel_embed.reshape(planes, c * 8, 128)
    a0, a1, a2, a3 = attend(0, place, feat, embed, visible, w_query, w_key)
    b0, b1, b2, b3 = attend(1, place, feat, embed, visible, w_query, w_key)
    band, wide_v, wide_o = weights(conv_weight, w_value, w_out)
    low_a, low_b, high_a, high_b = ring_step(a1, b1, a2, b2, a3, b3, x_up, x_down)
    z2a, z2b, z3a, z3b = merge([b0, low_b, high_b], [2, 2, 2, 2])
    z0, z1a, z1b = merge([a0, low_a, high_a], [4, 2, 2])
    rest = ring_step(z1a, z1b, z2a, z2b, z3a, z3b, z_up, z_down)
    hidden = finish(z0, *rest, wide_v, wide_o).reshape(8, 32, 256)

    z_next = [(i, i + 4) for i in range(12)]
    z_prev = [(j, i) for i, j in z_next]
    below = lax.ppermute(hidden, "frame", z_next)
    above = lax.ppermute(hidden, "frame", z_prev)
    hidden = jnp.concatenate([below, hidden, above], axis=2)

    def where_is(z, chunk):
        return (4 * z + chunk % 4) * 4 + chunk // 4

    y_next = [(where_is(z, k), where_is(z, k + 1)) for z in range(4) for k in range(15)]
    y_prev = [(j, i) for i, j in y_next]
    left = lax.ppermute(hidden[:, -halo:], ("frame", "by"), y_next)
    right = lax.ppermute(hidden[:, :halo], ("frame", "by"), y_prev)
    pad = jnp.zeros((8, stride - 32 - 2 * halo, 768), bf16)
    hidden = jnp.concatenate([left, hidden, right, pad], axis=1)
    x_next = [(0, 1), (1, 2), (2, 3)]
    x_prev = [(j, i) for i, j in x_next]
    front = lax.ppermute(hidden[-halo:], "bx", x_next)
    back = lax.ppermute(hidden[:halo], "bx", x_prev)
    hidden = jnp.concatenate([front, hidden, back], axis=0)

    where = jnp.stack(
        [lax.axis_index("bx") * 8, lax.axis_index("by") * 128 + xi * 32, zh * 4]
    ).astype(jnp.int32)
    bias = jnp.concatenate([conv_bias, conv_bias], axis=1)
    out = convolve(where, hidden.reshape(16 * stride, 768), band, bias)
    groups = [[4 * z + x for x in range(4)] for z in range(4)]
    out = lax.all_to_all(
        out.reshape(4, 64, 256), "frame", 0, 0, axis_index_groups=groups, tiled=True
    )
    return out.reshape(4, 64, 8, 32).transpose(1, 2, 0, 3).reshape(1, 64, 8, 128)


def solution(mesh):
    return jax.shard_map(
        shards,
        mesh=mesh,
        in_specs=(
            P("frame", None, None, "bx", "by"),
            P(None, None, "bx", "by"),
            P("frame", None, "bx", "by"),
            P(),
            P(),
            P(),
            P(),
            P(),
            P(),
        ),
        out_specs=P("frame", None, "bx", "by"),
        check_vma=False,
    )
```

time: 376 us -> 118 us (0.31)
  the two profiles are of different devices: /device:TPU:7 before, /device:TPU:184 now
where the time goes in v2:
time: 118 us; the launch traced here: 117 us
  starting transfers between devices  38.8 us (33%)
  waiting for transfers between devices  32.5 us (28%)
  Pallas kernels  27.3 us (23%)
  local copies, waits for them, and re-layouts  9.24 us (8%)
  blocking collectives  8.36 us (7%)
    ppermute x12, starting transfers between devices, ring_step(): send = lambda v, way: lax.ppermute(v, 'frame', way)  21.2 us
    pallas_call x1, Pallas kernels, convolve(): pl.pallas_call(conv_kernel, out_shape=jax.ShapeDtypeStruct((256, 256), bf...  13.6 us
    ppermute x12, waiting for transfers between devices, ring_step(): send = lambda v, way: lax.ppermute(v, 'frame', way)  12.4 us
    pallas_call x2, Pallas kernels, attend(): pl.pallas_call(attend_kernel, out_shape=[jax.ShapeDtypeStruct((count, 136...  10.5 us
    all_to_all x1, blocking collectives, shards(): lax.all_to_all(out.reshape(4, 64, 256), 'frame', 0, 0, axis_index_groups=...  8.36 us
    unnamed x20, local copies, waits for them, and re-layouts  7.38 us
    ppermute x1, waiting for transfers between devices, shards(): below = lax.ppermute(hidden, 'frame', z_next)  7.06 us
    ppermute x1, starting transfers between devices, shards(): above = lax.ppermute(hidden, 'frame', z_prev)  5.84 us
  transfers between devices with their start and end apart: 18, of which 9 were waited for; matrix products, arithmetic and copies ran while one was open for 0% of the time, Pallas kernels for 7%

profile of v2, /device:TPU:184, one launch (start us, length us, event | category | flops | bytes accessed | tf_op | source)
XLA Modules:
  0.0 117.1 jit_solution(9782383237454307108)
XLA Ops:
  0.1 3.4 %copy-done = bf16[4,16,64,8,128]{4,3,2,1,0:T(8,128)(2,1)S(1)} copy-done((bf16[4,16,64,8,128]{4,3,2,1,0:T(8,128)(2,1)S(1)}, bf16[4,16,64,8,128]{4,3,2,1,0:T(8,128)(2,1)}, u32[]{:S(2)}) %copy-start) | copy-done | bytes 8388632
  3.5 1.6 %copy-done.1 = bf16[16,64,8,128]{3,2,1,0:T(8,128)(2,1)S(1)} copy-done((bf16[16,64,8,128]{3,2,1,0:T(8,128)(2,1)S(1)}, bf16[16,64,8,128]{3,2,1,0:T(8,128)(2,1)}, u32[]{:S(2)}) %copy-start.1) | copy-done | bytes 2097176
  5.1 0.9 copy-done.3
  7.4 5.3 %attend.3 = (bf16[8,136,128]{2,1,0:T(8,128)(2,1)S(1)}, bf16[8,136,128]{2,1,0:T(8,128)(2,1)S(1)}, bf16[8,136,128]{2,1,0:T(8,128)(2,1)S(1)}, bf16[8,136,128]{2,1,0:T(8,128)(2,1)S(1)}) custom-call(s32[2]{0:T(128)S(1)} %pad_add_fusion.1.place, bf16[4,16,512,128]{3,2,1,0:T(8,128)(2,1)S(1)} %bitcast.15, bf16[16,512,128]{2,1,0:T(8,128)(2,1)S(1)} %bitcast.17, ...), custom_call_target="tpu_custom_call" | custom-call | flops 100000000 | bytes 12582912 | tf_op jit(solution)/shard_map/attend/pallas_call | solution.py:97
  12.7 2.8 %collective-permute-start.4 = (bf16[8,136,128]{2,1,0:T(8,128)(2,1)S(1)}, bf16[8,136,128]{2,1,0:T(8,128)(2,1)S(1)}, u32[]{:S(2)}, u32[]{:S(2)}) collective-permute-start(bf16[8,136,128]{2,1,0:T(8,128)(2,1)S(1)} %get-tuple-element.32), channel_id=1, source_target_pairs={{16,0},{32,16},{48,32},{0,48},{80,64},{96,80},{112,96},{64,112},{1... | collective-permute-start | bytes 835592 | tf_op jit(solution)/shard_map/ppermute | solution.py:317
  15.5 5.3 %attend.2 = (bf16[8,136,128]{2,1,0:T(8,128)(2,1)S(1)}, bf16[8,136,128]{2,1,0:T(8,128)(2,1)S(1)}, bf16[8,136,128]{2,1,0:T(8,128)(2,1)S(1)}, bf16[8,136,128]{2,1,0:T(8,128)(2,1)S(1)}) custom-call(s32[2]{0:T(128)S(1)} %pad_add_fusion.1.place, bf16[4,16,512,128]{3,2,1,0:T(8,128)(2,1)S(1)} %bitcast.16, bf16[16,512,128]{2,1,0:T(8,128)(2,1)S(1)} %bitcast.18, ...), custom_call_target="tpu_custom_call" | custom-call | flops 100000000 | bytes 12582912 | tf_op jit(solution)/shard_map/attend/pallas_call | solution.py:97
  21.9 3.6 %collective-permute-start.5 = (bf16[8,136,128]{2,1,0:T(8,128)(2,1)S(1)}, bf16[8,136,128]{2,1,0:T(8,128)(2,1)S(1)}, u32[]{:S(2)}, u32[]{:S(2)}) collective-permute-start(bf16[8,136,128]{2,1,0:T(8,128)(2,1)S(1)} %merge.8), channel_id=1, source_target_pairs={{16,0},{32,16},{48,32},{0,48},{80,64},{96,80},{112,96},{64,112},{1... | collective-permute-start | bytes 835592 | tf_op jit(solution)/shard_map/ppermute | solution.py:317
  25.5 1.0 collective-permute-start.2
  26.5 5.1 %collective-permute-done.refs_1_ = bf16[8,136,128]{2,1,0:T(8,128)(2,1)S(1)} collective-permute-done((bf16[8,136,128]{2,1,0:T(8,128)(2,1)S(1)}, bf16[8,136,128]{2,1,0:T(8,128)(2,1)S(1)}, u32[]{:S(2)}, u32[]{:S(2)}) %collective-permute-start) | collective-permute-done | bytes 278560 | tf_op jit(solution)/shard_map/ppermute | solution.py:317
  32.0 5.6 %collective-permute-done.3.refs_1_ = bf16[8,136,128]{2,1,0:T(8,128)(2,1)S(1)} collective-permute-done((bf16[8,136,128]{2,1,0:T(8,128)(2,1)S(1)}, bf16[8,136,128]{2,1,0:T(8,128)(2,1)S(1)}, u32[]{:S(2)}, u32[]{:S(2)}) %collective-permute-start.3) | collective-permute-done | bytes 278560 | tf_op jit(solution)/shard_map/ppermute | solution.py:317
  37.9 1.6 %collective-permute-start.6 = (bf16[2,136,128]{2,1,0:T(8,128)(2,1)S(1)}, bf16[2,136,128]{2,1,0:T(8,128)(2,1)S(1)}, u32[]{:S(2)}, u32[]{:S(2)}) collective-permute-start(bf16[2,136,128]{2,1,0:T(8,128)(2,1)S(1)} %get-tuple-element.33), channel_id=1, source_target_pairs={{0,64},{16,80},{32,96},{48,112},{64,128},{80,144},{96,160},{112,17... | collective-permute-start | bytes 208904 | tf_op jit(solution)/shard_map/ppermute | solution.py:317
  39.5 2.7 %collective-permute-start.10 = (bf16[2,136,128]{2,1,0:T(8,128)(2,1)S(1)}, bf16[2,136,128]{2,1,0:T(8,128)(2,1)S(1)}, u32[]{:S(2)}, u32[]{:S(2)}) collective-permute-start(bf16[2,136,128]{2,1,0:T(8,128)(2,1)S(1)} %get-tuple-element.37), channel_id=1, source_target_pairs={{64,0},{80,16},{96,32},{112,48},{128,64},{144,80},{160,96},{176,11... | collective-permute-start | bytes 208904 | tf_op jit(solution)/shard_map/ppermute | solution.py:317
  42.5 1.5 %collective-permute-start.8 = (bf16[2,136,128]{2,1,0:T(8,128)(2,1)S(1)}, bf16[2,136,128]{2,1,0:T(8,128)(2,1)S(1)}, u32[]{:S(2)}, u32[]{:S(2)}) collective-permute-start(bf16[2,136,128]{2,1,0:T(8,128)(2,1)S(1)} %get-tuple-element.34), channel_id=1, source_target_pairs={{0,64},{16,80},{32,96},{48,112},{64,128},{80,144},{96,160},{112,17... | collective-permute-start | bytes 208904 | tf_op jit(solution)/shard_map/ppermute | solution.py:317
  44.1 2.7 %collective-permute-start.9 = (bf16[2,136,128]{2,1,0:T(8,128)(2,1)S(1)}, bf16[2,136,128]{2,1,0:T(8,128)(2,1)S(1)}, u32[]{:S(2)}, u32[]{:S(2)}) collective-permute-start(bf16[2,136,128]{2,1,0:T(8,128)(2,1)S(1)} %get-tuple-element.35), channel_id=1, source_target_pairs={{64,0},{80,16},{96,32},{112,48},{128,64},{144,80},{160,96},{176,11... | collective-permute-start | bytes 208904 | tf_op jit(solution)/shard_map/ppermute | solution.py:317
  47.4 4.1 %collective-permute-start.11 = (bf16[2,136,128]{2,1,0:T(8,128)(2,1)S(1)}, bf16[2,136,128]{2,1,0:T(8,128)(2,1)S(1)}, u32[]{:S(2)}, u32[]{:S(2)}) collective-permute-start(bf16[2,136,128]{2,1,0:T(8,128)(2,1)S(1)} %merge.11), channel_id=1, source_target_pairs={{64,0},{80,16},{96,32},{112,48},{128,64},{144,80},{160,96},{176,11... | collective-permute-start | bytes 208904 | tf_op jit(solution)/shard_map/ppermute | solution.py:317
  51.6 0.9 weights.1
  52.5 1.7 %collective-permute-done.7.low_a = bf16[2,136,128]{2,1,0:T(8,128)(2,1)S(1)} collective-permute-done((bf16[2,136,128]{2,1,0:T(8,128)(2,1)S(1)}, bf16[2,136,128]{2,1,0:T(8,128)(2,1)S(1)}, u32[]{:S(2)}, u32[]{:S(2)}) %collective-permute-start.7) | collective-permute-done | bytes 69664 | tf_op jit(solution)/shard_map/ppermute | solution.py:317
  55.0 5.8 %collective-permute-start.13 = (bf16[8,32,256]{2,1,0:T(8,128)(2,1)S(1)}, bf16[8,32,256]{2,1,0:T(8,128)(2,1)S(1)}, u32[]{:S(2)}, u32[]{:S(2)}) collective-permute-start(bf16[8,32,256]{2,1,0:T(8,128)(2,1)S(1)} %bitcast.20), channel_id=1, source_target_pairs={{64,0},{80,16},{96,32},{112,48},{128,64},{144,80},{160,96},{176,11... | collective-permute-start | bytes 393224 | tf_op jit(solution)/shard_map/ppermute | solution.py:349
  60.8 1.9 %collective-permute-start.12 = (bf16[8,32,256]{2,1,0:T(8,128)(2,1)S(1)}, bf16[8,32,256]{2,1,0:T(8,128)(2,1)S(1)}, u32[]{:S(2)}, u32[]{:S(2)}) collective-permute-start(bf16[8,32,256]{2,1,0:T(8,128)(2,1)S(1)} %bitcast.21), channel_id=1, source_target_pairs={{0,64},{16,80},{32,96},{48,112},{64,128},{80,144},{96,160},{112,17... | collective-permute-start | bytes 393224 | tf_op jit(solution)/shard_map/ppermute | solution.py:348
  62.7 1.4 %collective-permute-done.13 = bf16[8,32,256]{2,1,0:T(8,128)(2,1)S(1)} collective-permute-done((bf16[8,32,256]{2,1,0:T(8,128)(2,1)S(1)}, bf16[8,32,256]{2,1,0:T(8,128)(2,1)S(1)}, u32[]{:S(2)}, u32[]{:S(2)}) %collective-permute-start.13) | collective-permute-done | bytes 131104 | tf_op jit(solution)/shard_map/ppermute | solution.py:349
  64.1 7.1 %collective-permute-done.12 = bf16[8,32,256]{2,1,0:T(8,128)(2,1)S(1)} collective-permute-done((bf16[8,32,256]{2,1,0:T(8,128)(2,1)S(1)}, bf16[8,32,256]{2,1,0:T(8,128)(2,1)S(1)}, u32[]{:S(2)}, u32[]{:S(2)}) %collective-permute-start.12) | collective-permute-done | bytes 131104 | tf_op jit(solution)/shard_map/ppermute | solution.py:348
  71.2 1.9 %collective-permute-start.15 = (bf16[8,4,768]{2,1,0:T(4,128)(2,1)S(1)}, bf16[8,4,768]{2,1,0:T(4,128)(2,1)S(1)}, u32[]{:S(2)}, u32[]{:S(2)}) collective-permute-start(bf16[8,4,768]{2,1,0:T(4,128)(2,1)S(1)} %get-tuple-element.44), channel_id=1, source_target_pairs={{16,0},{32,16},{48,32},{1,48},{17,1},{33,17},{49,33},{2,49},{18,2}... | collective-permute-start | bytes 147464 | tf_op jit(solution)/shard_map/ppermute | solution.py:358
  73.2 3.9 %collective-permute-start.14 = (bf16[8,4,768]{2,1,0:T(4,128)(2,1)S(1)}, bf16[8,4,768]{2,1,0:T(4,128)(2,1)S(1)}, u32[]{:S(2)}, u32[]{:S(2)}) collective-permute-start(bf16[8,4,768]{2,1,0:T(4,128)(2,1)S(1)} %get-tuple-element.43), channel_id=1, source_target_pairs={{0,16},{16,32},{32,48},{48,1},{1,17},{17,33},{33,49},{49,2},{2,18}... | collective-permute-start | bytes 147464 | tf_op jit(solution)/shard_map/ppermute | solution.py:357
  77.2 3.5 %collective-permute-done.14 = bf16[8,4,768]{2,1,0:T(4,128)(2,1)S(1)} collective-permute-done((bf16[8,4,768]{2,1,0:T(4,128)(2,1)S(1)}, bf16[8,4,768]{2,1,0:T(4,128)(2,1)S(1)}, u32[]{:S(2)}, u32[]{:S(2)}) %collective-permute-start.14) | collective-permute-done | bytes 49184 | tf_op jit(solution)/shard_map/ppermute | solution.py:357
  80.9 0.9 fusion
  81.8 2.7 %collective-permute-start.17 = (bf16[4,48,768]{2,1,0:T(8,128)(2,1)}, bf16[4,48,768]{2,1,0:T(8,128)(2,1)S(1)}, u32[]{:S(2)}, u32[]{:S(2)}) collective-permute-start(bf16[4,48,768]{2,1,0:T(8,128)(2,1)} %get-tuple-element.42), channel_id=1, source_target_pairs={{4,0},{8,4},{12,8},{5,1},{9,5},{13,9},{6,2},{10,6},{14,10},{7,3},{... | collective-permute-start | bytes 884744 | tf_op jit(solution)/shard_map/ppermute | solution.py:364
  84.4 1.3 %collective-permute-start.16 = (bf16[4,48,768]{2,1,0:T(8,128)(2,1)}, bf16[4,48,768]{2,1,0:T(8,128)(2,1)S(1)}, u32[]{:S(2)}, u32[]{:S(2)}) collective-permute-start(bf16[4,48,768]{2,1,0:T(8,128)(2,1)} %get-tuple-element.41), channel_id=1, source_target_pairs={{0,4},{4,8},{8,12},{1,5},{5,9},{9,13},{2,6},{6,10},{10,14},{3,7},{... | collective-permute-start | bytes 884744 | tf_op jit(solution)/shard_map/ppermute | solution.py:363
  85.9 4.1 %collective-permute-done.17 = bf16[4,48,768]{2,1,0:T(8,128)(2,1)S(1)} collective-permute-done((bf16[4,48,768]{2,1,0:T(8,128)(2,1)}, bf16[4,48,768]{2,1,0:T(8,128)(2,1)S(1)}, u32[]{:S(2)}, u32[]{:S(2)}) %collective-permute-start.17) | collective-permute-done | bytes 294944 | tf_op jit(solution)/shard_map/ppermute | solution.py:364
  90.0 4.0 %collective-permute-done.16 = bf16[4,48,768]{2,1,0:T(8,128)(2,1)S(1)} collective-permute-done((bf16[4,48,768]{2,1,0:T(8,128)(2,1)}, bf16[4,48,768]{2,1,0:T(8,128)(2,1)S(1)}, u32[]{:S(2)}, u32[]{:S(2)}) %collective-permute-start.16) | collective-permute-done | bytes 294944 | tf_op jit(solution)/shard_map/ppermute | solution.py:363
  94.2 13.6 %convolve.1 = bf16[256,256]{1,0:T(8,128)(2,1)S(1)} custom-call(s32[3]{0:T(128)S(1)} %pad_add_fusion.where, bf16[768,768]{1,0:T(8,128)(2,1)S(1)} %bitcast.19, bf16[4,9,256,128]{3,2,1,0:T(8,128)(2,1)S(1)} %get-tuple-element.40.band, f32[4,128]{1,0:T(4,128)S(1)} %pad_maximum_fusion.5.bias), custom_call_target="tpu_custom_call" | custom-call | tf_op jit(solution)/shard_map/convolve/pallas_call | solution.py:301
  107.7 8.4 %all_to_all.5 = bf16[4,64,256]{2,1,0:T(8,128)(2,1)S(1)} all-to-all(bf16[4,64,256]{2,1,0:T(8,128)(2,1)S(1)} %bitcast.26), channel_id=1, replica_groups={{0,16,32,48},{64,80,96,112},{128,144,160,176},{192,208,224,240},{1,17,3..., dimensions={0} | all-to-all | bytes 262144 | tf_op jit(solution)/shard_map/all_to_all | solution.py:373
  116.3 0.8 copy.16
  (47 shorter events, 6.1 us)
Async XLA Ops:
  0.1 3.4 %copy-start = (bf16[4,16,64,8,128]{4,3,2,1,0:T(8,128)(2,1)S(1)}, bf16[4,16,64,8,128]{4,3,2,1,0:T(8,128)(2,1)}, u32[]{:S(2)}) copy-start(bf16[4,16,64,8,128]{4,3,2,1,0:T(8,128)(2,1)} %param.9) | copy-start | bytes 25165828
  3.5 1.6 %copy-start.1 = (bf16[16,64,8,128]{3,2,1,0:T(8,128)(2,1)S(1)}, bf16[16,64,8,128]{3,2,1,0:T(8,128)(2,1)}, u32[]{:S(2)}) copy-start(bf16[16,64,8,128]{3,2,1,0:T(8,128)(2,1)} %param.10) | copy-start | bytes 6291460
  5.0 0.9 copy-start.3
  6.0 0.7 copy-start.4
  6.7 0.7 copy-start.5
  7.4 8.1 %copy-start.6 = (bf16[64,64]{1,0:T(8,128)(2,1)S(1)}, bf16[64,64]{1,0:T(8,128)(2,1)}, u32[]{:S(2)}) copy-start(bf16[64,64]{1,0:T(8,128)(2,1)} %wk.3) | copy-start | bytes 24580
  12.7 8.9 %collective-permute-start.4 = (bf16[8,136,128]{2,1,0:T(8,128)(2,1)S(1)}, bf16[8,136,128]{2,1,0:T(8,128)(2,1)S(1)}, u32[]{:S(2)}, u32[]{:S(2)}) collective-permute-start(bf16[8,136,128]{2,1,0:T(8,128)(2,1)S(1)} %get-tuple-element.32), channel_id=1, source_target_pairs={{16,0},{32,16},{48,32},{0,48},{80,64},{96,80},{112,96},{64,112},{1... | collective-permute-start | bytes 835592 | tf_op jit(solution)/shard_map/ppermute | solution.py:317
  20.8 10.8 %collective-permute-start = (bf16[8,136,128]{2,1,0:T(8,128)(2,1)S(1)}, bf16[8,136,128]{2,1,0:T(8,128)(2,1)S(1)}, u32[]{:S(2)}, u32[]{:S(2)}) collective-permute-start(bf16[8,136,128]{2,1,0:T(8,128)(2,1)S(1)} %get-tuple-element.25), channel_id=1, source_target_pairs={{0,16},{16,32},{32,48},{48,0},{64,80},{80,96},{96,112},{112,64},{1... | collective-permute-start | bytes 835592 | tf_op jit(solution)/shard_map/ppermute | solution.py:317
  20.9 16.7 %collective-permute-start.3 = (bf16[8,136,128]{2,1,0:T(8,128)(2,1)S(1)}, bf16[8,136,128]{2,1,0:T(8,128)(2,1)S(1)}, u32[]{:S(2)}, u32[]{:S(2)}) collective-permute-start(bf16[8,136,128]{2,1,0:T(8,128)(2,1)S(1)} %get-tuple-element.30), channel_id=1, source_target_pairs={{0,16},{16,32},{32,48},{48,0},{64,80},{80,96},{96,112},{112,64},{1... | collective-permute-start | bytes 835592 | tf_op jit(solution)/shard_map/ppermute | solution.py:317
  21.9 15.7 %collective-permute-start.5 = (bf16[8,136,128]{2,1,0:T(8,128)(2,1)S(1)}, bf16[8,136,128]{2,1,0:T(8,128)(2,1)S(1)}, u32[]{:S(2)}, u32[]{:S(2)}) collective-permute-start(bf16[8,136,128]{2,1,0:T(8,128)(2,1)S(1)} %merge.8), channel_id=1, source_target_pairs={{16,0},{32,16},{48,32},{0,48},{80,64},{96,80},{112,96},{64,112},{1... | collective-permute-start | bytes 835592 | tf_op jit(solution)/shard_map/ppermute | solution.py:317
  25.5 16.7 %collective-permute-start.2 = (bf16[8,136,128]{2,1,0:T(8,128)(2,1)S(1)}, bf16[8,136,128]{2,1,0:T(8,128)(2,1)S(1)}, u32[]{:S(2)}, u32[]{:S(2)}) collective-permute-start(bf16[8,136,128]{2,1,0:T(8,128)(2,1)S(1)} %get-tuple-element.26), channel_id=1, source_target_pairs={{16,0},{32,16},{48,32},{0,48},{80,64},{96,80},{112,96},{64,112},{1... | collective-permute-start | bytes 835592 | tf_op jit(solution)/shard_map/ppermute | solution.py:317
  31.9 19.7 %copy-start.2 = (bf16[4,3,3,3,64,64]{5,4,3,2,1,0:T(8,128)(2,1)S(1)}, bf16[4,3,3,3,64,64]{5,4,3,2,1,0:T(8,128)(2,1)}, u32[]{:S(2)}) copy-start(bf16[4,3,3,3,64,64]{5,4,3,2,1,0:T(8,128)(2,1)} %param.16) | copy-start | bytes 2654212
  31.9 19.7 %copy-start.7 = (bf16[64,64]{1,0:T(8,128)(2,1)S(1)}, bf16[64,64]{1,0:T(8,128)(2,1)}, u32[]{:S(2)}) copy-start(bf16[64,64]{1,0:T(8,128)(2,1)} %wv.1) | copy-start | bytes 24580
  31.9 19.6 %copy-start.8 = (bf16[64,64]{1,0:T(8,128)(2,1)S(1)}, bf16[64,64]{1,0:T(8,128)(2,1)}, u32[]{:S(2)}) copy-start(bf16[64,64]{1,0:T(8,128)(2,1)} %wo.1) | copy-start | bytes 24580
  31.9 10.2 %collective-permute-start.1 = (bf16[8,136,128]{2,1,0:T(8,128)(2,1)S(1)}, bf16[8,136,128]{2,1,0:T(8,128)(2,1)S(1)}, u32[]{:S(2)}, u32[]{:S(2)}) collective-permute-start(bf16[8,136,128]{2,1,0:T(8,128)(2,1)S(1)} %merge.6), channel_id=1, source_target_pairs={{0,16},{16,32},{32,48},{48,0},{64,80},{80,96},{96,112},{112,64},{1... | collective-permute-start | bytes 835592 | tf_op jit(solution)/shard_map/ppermute | solution.py:317
  37.9 8.8 %collective-permute-start.6 = (bf16[2,136,128]{2,1,0:T(8,128)(2,1)S(1)}, bf16[2,136,128]{2,1,0:T(8,128)(2,1)S(1)}, u32[]{:S(2)}, u32[]{:S(2)}) collective-permute-start(bf16[2,136,128]{2,1,0:T(8,128)(2,1)S(1)} %get-tuple-element.33), channel_id=1, source_target_pairs={{0,64},{16,80},{32,96},{48,112},{64,128},{80,144},{96,160},{112,17... | collective-permute-start | bytes 208904 | tf_op jit(solution)/shard_map/ppermute | solution.py:317
  39.5 7.8 %collective-permute-start.10 = (bf16[2,136,128]{2,1,0:T(8,128)(2,1)S(1)}, bf16[2,136,128]{2,1,0:T(8,128)(2,1)S(1)}, u32[]{:S(2)}, u32[]{:S(2)}) collective-permute-start(bf16[2,136,128]{2,1,0:T(8,128)(2,1)S(1)} %get-tuple-element.37), channel_id=1, source_target_pairs={{64,0},{80,16},{96,32},{112,48},{128,64},{144,80},{160,96},{176,11... | collective-permute-start | bytes 208904 | tf_op jit(solution)/shard_map/ppermute | solution.py:317
  42.5 9.9 %collective-permute-start.8 = (bf16[2,136,128]{2,1,0:T(8,128)(2,1)S(1)}, bf16[2,136,128]{2,1,0:T(8,128)(2,1)S(1)}, u32[]{:S(2)}, u32[]{:S(2)}) collective-permute-start(bf16[2,136,128]{2,1,0:T(8,128)(2,1)S(1)} %get-tuple-element.34), channel_id=1, source_target_pairs={{0,64},{16,80},{32,96},{48,112},{64,128},{80,144},{96,160},{112,17... | collective-permute-start | bytes 208904 | tf_op jit(solution)/shard_map/ppermute | solution.py:317
  44.1 8.4 %collective-permute-start.9 = (bf16[2,136,128]{2,1,0:T(8,128)(2,1)S(1)}, bf16[2,136,128]{2,1,0:T(8,128)(2,1)S(1)}, u32[]{:S(2)}, u32[]{:S(2)}) collective-permute-start(bf16[2,136,128]{2,1,0:T(8,128)(2,1)S(1)} %get-tuple-element.35), channel_id=1, source_target_pairs={{64,0},{80,16},{96,32},{112,48},{128,64},{144,80},{160,96},{176,11... | collective-permute-start | bytes 208904 | tf_op jit(solution)/shard_map/ppermute | solution.py:317
  46.9 7.2 %collective-permute-start.7 = (bf16[2,136,128]{2,1,0:T(8,128)(2,1)S(1)}, bf16[2,136,128]{2,1,0:T(8,128)(2,1)S(1)}, u32[]{:S(2)}, u32[]{:S(2)}) collective-permute-start(bf16[2,136,128]{2,1,0:T(8,128)(2,1)S(1)} %merge.10), channel_id=1, source_target_pairs={{0,64},{16,80},{32,96},{48,112},{64,128},{80,144},{96,160},{112,17... | collective-permute-start | bytes 208904 | tf_op jit(solution)/shard_map/ppermute | solution.py:317
  47.4 6.7 %collective-permute-start.11 = (bf16[2,136,128]{2,1,0:T(8,128)(2,1)S(1)}, bf16[2,136,128]{2,1,0:T(8,128)(2,1)S(1)}, u32[]{:S(2)}, u32[]{:S(2)}) collective-permute-start(bf16[2,136,128]{2,1,0:T(8,128)(2,1)S(1)} %merge.11), channel_id=1, source_target_pairs={{64,0},{80,16},{96,32},{112,48},{128,64},{144,80},{160,96},{176,11... | collective-permute-start | bytes 208904 | tf_op jit(solution)/shard_map/ppermute | solution.py:317
  55.0 9.2 %collective-permute-start.13 = (bf16[8,32,256]{2,1,0:T(8,128)(2,1)S(1)}, bf16[8,32,256]{2,1,0:T(8,128)(2,1)S(1)}, u32[]{:S(2)}, u32[]{:S(2)}) collective-permute-start(bf16[8,32,256]{2,1,0:T(8,128)(2,1)S(1)} %bitcast.20), channel_id=1, source_target_pairs={{64,0},{80,16},{96,32},{112,48},{128,64},{144,80},{160,96},{176,11... | collective-permute-start | bytes 393224 | tf_op jit(solution)/shard_map/ppermute | solution.py:349
  60.8 10.4 %collective-permute-start.12 = (bf16[8,32,256]{2,1,0:T(8,128)(2,1)S(1)}, bf16[8,32,256]{2,1,0:T(8,128)(2,1)S(1)}, u32[]{:S(2)}, u32[]{:S(2)}) collective-permute-start(bf16[8,32,256]{2,1,0:T(8,128)(2,1)S(1)} %bitcast.21), channel_id=1, source_target_pairs={{0,64},{16,80},{32,96},{48,112},{64,128},{80,144},{96,160},{112,17... | collective-permute-start | bytes 393224 | tf_op jit(solution)/shard_map/ppermute | solution.py:348
  71.2 6.0 %collective-permute-start.15 = (bf16[8,4,768]{2,1,0:T(4,128)(2,1)S(1)}, bf16[8,4,768]{2,1,0:T(4,128)(2,1)S(1)}, u32[]{:S(2)}, u32[]{:S(2)}) collective-permute-start(bf16[8,4,768]{2,1,0:T(4,128)(2,1)S(1)} %get-tuple-element.44), channel_id=1, source_target_pairs={{16,0},{32,16},{48,32},{1,48},{17,1},{33,17},{49,33},{2,49},{18,2}... | collective-permute-start | bytes 147464 | tf_op jit(solution)/shard_map/ppermute | solution.py:358
  73.2 7.5 %collective-permute-start.14 = (bf16[8,4,768]{2,1,0:T(4,128)(2,1)S(1)}, bf16[8,4,768]{2,1,0:T(4,128)(2,1)S(1)}, u32[]{:S(2)}, u32[]{:S(2)}) collective-permute-start(bf16[8,4,768]{2,1,0:T(4,128)(2,1)S(1)} %get-tuple-element.43), channel_id=1, source_target_pairs={{0,16},{16,32},{32,48},{48,1},{1,17},{17,33},{33,49},{49,2},{2,18}... | collective-permute-start | bytes 147464 | tf_op jit(solution)/shard_map/ppermute | solution.py:357
  80.7 5.1 %copy-start.9 = (f32[4,64]{1,0:T(4,128)S(1)}, f32[4,64]{1,0:T(4,128)}, u32[]{:S(2)}) copy-start(f32[4,64]{1,0:T(4,128)} %param.17) | copy-start | bytes 3076
  81.8 8.2 %collective-permute-start.17 = (bf16[4,48,768]{2,1,0:T(8,128)(2,1)}, bf16[4,48,768]{2,1,0:T(8,128)(2,1)S(1)}, u32[]{:S(2)}, u32[]{:S(2)}) collective-permute-start(bf16[4,48,768]{2,1,0:T(8,128)(2,1)} %get-tuple-element.42), channel_id=1, source_target_pairs={{4,0},{8,4},{12,8},{5,1},{9,5},{13,9},{6,2},{10,6},{14,10},{7,3},{... | collective-permute-start | bytes 884744 | tf_op jit(solution)/shard_map/ppermute | solution.py:364
  84.4 9.6 %collective-permute-start.16 = (bf16[4,48,768]{2,1,0:T(8,128)(2,1)}, bf16[4,48,768]{2,1,0:T(8,128)(2,1)S(1)}, u32[]{:S(2)}, u32[]{:S(2)}) collective-permute-start(bf16[4,48,768]{2,1,0:T(8,128)(2,1)} %get-tuple-element.41), channel_id=1, source_target_pairs={{0,4},{4,8},{8,12},{1,5},{5,9},{9,13},{2,6},{6,10},{10,14},{3,7},{... | collective-permute-start | bytes 884744 | tf_op jit(solution)/shard_map/ppermute | solution.py:363

commit v3 on v2

v3 whole, which is shorter than its diff:
```python
import functools

import jax
import jax.numpy as jnp
from jax import lax
from jax.experimental import pallas as pl
from jax.experimental.pallas import tpu as pltpu
from jax.sharding import PartitionSpec as P


absent_score = -1e30
halo = 4
stride = 48
bf16, f32 = jnp.bfloat16, jnp.float32
VM = pl.BlockSpec(memory_space=pltpu.VMEM)


def dot(a, b):
    return jnp.dot(a, b, preferred_element_type=f32)


def lane_blocks(v):
    lane = lax.broadcasted_iota(jnp.int32, (8, 128), 1)
    low = lane < 64
    even = (lane & 63) < 32
    t = [None] * 4
    for i in (0, 1):
        t[i] = jnp.where(low, v[i], pltpu.roll(v[i + 2], 64, 1))
        t[i + 2] = jnp.where(low, pltpu.roll(v[i], 64, 1), v[i + 2])
    o = [None] * 4
    for i in (0, 2):
        o[i] = jnp.where(even, t[i], pltpu.roll(t[i + 1], 32, 1))
        o[i + 1] = jnp.where(even, pltpu.roll(t[i], 96, 1), t[i + 1])
    return o


def three_terms(m):
    hi = m.astype(bf16).astype(f32)
    mid = (m - hi).astype(bf16).astype(f32)
    return hi, mid, m - hi - mid


def attend_kernel(half, feat_at, embed_at, seen_at, wq_at, wk_at, *refs):
    outs, feat, embed, seen, wq, wk, key0, key1, sems = refs[:4], *refs[4:]
    steps, frames, n = feat.shape[:3]
    me = lax.axis_index("frame")
    zh, xi = me // 4, me % 4
    turn = (128 - 32 * xi) & 127

    def copies(s):
        rel = half * steps * n + s * n
        z = pl.ds(((rel // 4 + zh) & 3) * 4 + rel % 4, n)
        return [
            pltpu.make_async_copy(embed_at.at[z], embed.at[s], sems.at[s, 0]),
            pltpu.make_async_copy(feat_at.at[:, z], feat.at[s], sems.at[s, 1]),
            pltpu.make_async_copy(seen_at.at[:, z], seen.at[s], sems.at[s, 2]),
        ]

    loads = [copies(s) for s in range(steps)]
    small = [
        pltpu.make_async_copy(wq_at, wq, sems.at[steps, 0]),
        pltpu.make_async_copy(wk_at, wk, sems.at[steps, 1]),
    ]
    for c in [loads[0][0], *small, *loads[0][1:], *sum(loads[1:], [])]:
        c.start()
    for c in small:
        c.wait()

    def keys(s):
        key = (key0, key1)[s % 2]
        loads[s][0].wait()
        for p in range(n):
            key[p] = embed[s, p].astype(f32)
        cols = [key[p, pl.ds(i, 64, stride=8), :] for p in range(n) for i in range(8)]
        wide = jnp.concatenate(cols, axis=1).astype(bf16)
        q = lax.dot_general(wq[...], wide, (((0,), (0,)), ((), ())), preferred_element_type=f32)
        qk = dot(wk[...], q.astype(bf16)) * 0.125
        for p in range(n):
            for i in range(8):
                at = (8 * p + i) * 128
                key[p, pl.ds(i, 64, stride=8), :] = qk[:, at : at + 128]

    def plane(s, p):
        key = (key0, key1)[s % 2]
        sums = [jnp.zeros((8, 128), f32) for _ in range(frames)]
        for g in range(16):
            rows = slice(32 * g, 32 * g + 32)
            line = key[p, rows, :]
            for f in range(frames):
                prod = (line * feat[s, f, p, rows, :].astype(f32)).reshape(4, 8, 128)
                sums[f] = sums[f] + jnp.sum(prod, axis=0)
        ok = [seen[s, f, p] > 0 for f in range(frames)]
        m = jnp.full((8, 128), absent_score, f32)
        for f in range(frames):
            m = jnp.maximum(m, jnp.where(ok[f], sums[f], absent_score))
        e = [jnp.where(ok[f], jnp.exp(sums[f] - m), 0.0) for f in range(frames)]
        total = e[0]
        for f in range(1, frames):
            total = total + e[f]

        def put(g, tiles):
            tiles = [pltpu.roll(t, turn, 1) for t in tiles]
            for out, tile in zip(outs, lane_blocks(tiles)):
                out[s * n + p, 8 * g : 8 * g + 8, :] = tile.astype(bf16)

        for g in range(16):
            rows = slice(32 * g, 32 * g + 32)
            acc = None
            for f in range(frames):
                term = e[f][None] * feat[s, f, p, rows, :].astype(f32).reshape(4, 8, 128)
                acc = term if acc is None else acc + term
            put(g, [acc[i] for i in range(4)])
        put(16, [*three_terms(m), total])

    keys(0)
    for s in range(steps):
        loads[s][1].wait()
        loads[s][2].wait()
        if s + 1 < steps:
            keys(s + 1)
        for p in range(n):
            plane(s, p)


def attend(half, feat, embed, visible, w_query, w_key):
    frames, planes, rows = feat.shape[:3]
    c = w_key.shape[0]
    n = 2
    count = planes // 2
    steps = count // n
    hbm = pl.BlockSpec(memory_space=pltpu.HBM)
    return pl.pallas_call(
        functools.partial(attend_kernel, half),
        out_shape=[jax.ShapeDtypeStruct((count, 136, 128), bf16)] * 4,
        in_specs=[hbm] * 5,
        out_specs=[VM] * 4,
        scratch_shapes=[
            pltpu.VMEM((steps, frames, n, rows, 128), bf16),
            pltpu.VMEM((steps, n, rows, 128), bf16),
            pltpu.VMEM((steps, frames, n, 8, 128), jnp.int32),
            pltpu.VMEM((c, c), bf16),
            pltpu.VMEM((c, c), bf16),
            pltpu.VMEM((n, rows, 128), f32),
            pltpu.VMEM((n, rows, 128), f32),
            pltpu.SemaphoreType.DMA((steps + 1, 3)),
        ],
        compiler_params=pltpu.CompilerParams(vmem_limit_bytes=14 << 20),
        cost_estimate=pl.CostEstimate(flops=10**8, bytes_accessed=12 << 20, transcendentals=0),
        name="attend",
    )(feat, embed, visible, w_query, w_key)


def spread(v):
    u = v + pltpu.roll(v, 64, 1)
    return u + pltpu.roll(u, 32, 1)


def merged_plane(parts):
    lane = lax.broadcasted_iota(jnp.int32, (8, 128), 1)
    tail = lane >= 96
    stats = [r[p, 128:136, :].astype(f32) for r, p in parts]
    ms = [spread(jnp.where(tail, 0.0, s)) for s in stats]
    ls = [spread(jnp.where(tail, s, 0.0)) for s in stats]
    m = functools.reduce(jnp.maximum, ms)
    ws = [jnp.exp(v - m) for v in ms]
    total = sum(w * v for w, v in zip(ws, ls))
    return ws, total, m


def weighted_rows(parts, ws):
    acc = None
    for (r, p), w in zip(parts, ws):
        term = r[p, 0:128, :].astype(f32).reshape(16, 8, 128) * w[None]
        acc = term if acc is None else acc + term
    return acc.reshape(128, 128)


def merge_kernel(n, sizes, *refs):
    ins, outs = refs[:n], refs[n:]
    lane = lax.broadcasted_iota(jnp.int32, (8, 128), 1)
    at = 0
    for out, size in zip(outs, sizes):
        for i in range(size):
            parts = [(r, at) for r in ins]
            ws, total, m = merged_plane(parts)
            out[i, 0:128, :] = weighted_rows(parts, ws).astype(bf16)
            hi, mid, low = three_terms(m)
            packed = jnp.where(
                lane < 32, hi, jnp.where(lane < 64, mid, jnp.where(lane >= 96, total, low))
            )
            out[i, 128:136, :] = packed.astype(bf16)
            at += 1


def merge(parts, sizes):
    n = parts[0].shape[0]
    return pl.pallas_call(
        functools.partial(merge_kernel, len(parts), sizes),
        out_shape=[jax.ShapeDtypeStruct((s, 136, 128), bf16) for s in sizes],
        in_specs=[VM] * len(parts),
        out_specs=[VM] * len(sizes),
        compiler_params=pltpu.CompilerParams(vmem_limit_bytes=6 << 20),
        cost_estimate=pl.CostEstimate(flops=n * 10**5, bytes_accessed=n * 10**5, transcendentals=0),
        name="merge",
    )(*parts)


def gather_kernel(*refs):
    ins, out = refs[:6], refs[6]
    lane = lax.broadcasted_iota(jnp.int32, (8, 128), 1)
    zh = lax.axis_index("frame") // 4
    for rel in range(4):
        slot = (zh + rel) & 3
        for i in range(4):
            at = (4 * rel + i) & 7
            parts = [(r, at) for r in ins[3 * (rel // 2) : 3 * (rel // 2) + 3]]
            ws, total, m = merged_plane(parts)
            out[slot, i, 0:128, :] = weighted_rows(parts, ws).astype(bf16)
            hi, mid, low = three_terms(m)
            packed = jnp.where(
                lane < 32, hi, jnp.where(lane < 64, mid, jnp.where(lane >= 96, total, low))
            )
            out[slot, i, 128:136, :] = packed.astype(bf16)


def gather(*parts):
    return pl.pallas_call(
        gather_kernel,
        out_shape=jax.ShapeDtypeStruct((4, 4, 136, 128), bf16),
        in_specs=[VM] * 6,
        out_specs=VM,
        compiler_params=pltpu.CompilerParams(vmem_limit_bytes=6 << 20),
        name="gather",
    )(*parts)


def finish_kernel(part, wv, wo, out, rows):
    for p in range(4):
        parts = [(part.at[i], p) for i in range(4)]
        ws, total, _ = merged_plane(parts)
        inv = 1.0 / total
        rows[128 * p : 128 * p + 128, :] = weighted_rows(parts, [w * inv for w in ws])
    lines = []
    for x in range(8):
        t = rows[pl.ds(x, 64, stride=8), :].T
        lines.append(jnp.concatenate([t[32 * i : 32 * i + 32] for i in range(4)], axis=1))
    mixed = jnp.concatenate(lines, axis=0).astype(bf16)
    attended = dot(mixed, wv[...]).astype(bf16)
    out[...] = dot(attended, wo[...]).astype(bf16)


def finish(part, wv, wo):
    return pl.pallas_call(
        finish_kernel,
        out_shape=jax.ShapeDtypeStruct((256, 256), bf16),
        in_specs=[VM] * 3,
        out_specs=VM,
        scratch_shapes=[pltpu.VMEM((512, 128), f32)],
        compiler_params=pltpu.CompilerParams(vmem_limit_bytes=6 << 20),
        name="finish",
    )(part, wv, wo)


def weights_kernel(w, wv, wo, band, wide_v, wide_o, tmp):
    zero = jnp.zeros((64, 64), bf16)
    for tap in range(9):
        a = [w[0, 9 * i + tap] for i in range(3)]
        left = jnp.concatenate([a[0], a[1], a[2], zero], axis=0)
        right = jnp.concatenate([zero, a[0], a[1], a[2]], axis=0)
        e = tap % 3
        band[0, tap // 3, :, 128 * e : 128 * e + 128] = jnp.concatenate([left, right], axis=1)

    @pl.when(pl.program_id(0) == 0)
    def _():
        tmp[...] = wv[...].astype(f32)
        blank = jnp.zeros((16, 64), f32)
        for i in range(4):
            piece = tmp[pl.ds(i, 16, stride=4), :]
            for p in range(4):
                line = jnp.concatenate([piece if j == p else blank for j in range(4)], axis=1)
                at = 64 * i + 16 * p
                wide_v[at : at + 16, :] = line.astype(bf16)
        for p in range(4):
            line = jnp.concatenate([wo[...] if j == p else zero for j in range(4)], axis=1)
            wide_o[64 * p : 64 * p + 64, :] = line


def weights(conv_weight, w_value, w_out):
    layers = conv_weight.shape[0]
    small = pl.BlockSpec((64, 64), lambda i: (0, 0))
    big = pl.BlockSpec((256, 256), lambda i: (0, 0))
    return pl.pallas_call(
        weights_kernel,
        out_shape=[
            jax.ShapeDtypeStruct((layers, 3, 256, 384), bf16),
            jax.ShapeDtypeStruct((256, 256), bf16),
            jax.ShapeDtypeStruct((256, 256), bf16),
        ],
        grid=(layers,),
        in_specs=[pl.BlockSpec((1, 27, 64, 64), lambda i: (i, 0, 0, 0)), small, small],
        out_specs=[pl.BlockSpec((1, 3, 256, 384), lambda i: (i, 0, 0, 0)), big, big],
        scratch_shapes=[pltpu.VMEM((64, 64), f32)],
        compiler_params=pltpu.CompilerParams(
            dimension_semantics=("arbitrary",), vmem_limit_bytes=8 << 20
        ),
        cost_estimate=pl.CostEstimate(flops=10**6, bytes_accessed=8 << 20, transcendentals=0),
        name="weights",
    )(conv_weight.reshape(layers, 27, 64, 64), w_value, w_out)


def conv_kernel(block, band, bias, out, buf0, buf1, mask):
    layers = band.shape[0]
    me = lax.axis_index("frame")
    xi = me % 4
    x0, z0 = lax.axis_index("bx") * 8, me // 4 * 4
    y0 = lax.axis_index("by") * 128 + xi * 32
    y = lax.broadcasted_iota(jnp.int32, (stride, 128), 0) + (y0 - halo)
    y_ok = (y >= 0) & (y < 512)
    for x in range(16):
        x_at = x0 - halo + x
        line = jnp.where(y_ok & (x_at >= 0) & (x_at < 32), 1.0, 0.0)
        mask[stride * x : stride * x + stride, :] = line
    lane = lax.broadcasted_iota(jnp.int32, (1, 128), 1)
    for layer in range(layers):
        src = (block, buf0, buf1, buf0)[layer]
        dst = (buf0, buf1, buf0, None)[layer]
        first = stride * (layer + 1)
        n = stride * (14 - 2 * layer)

        def pair(t, carry, src=src, dst=dst, layer=layer, first=first, n=n):
            lanes_in = pl.ds(pl.multiple_of(128 * t, 128), 256)
            lanes_out = pl.ds(pl.multiple_of(128 * t, 128), 128)
            acc = None
            for b in range(3):
                rows = slice(first + stride * (b - 1), first + stride * (b - 1) + n)
                term = dot(src[rows, lanes_in], band[layer, b])
                acc = term if acc is None else acc + term
            h = acc[:, 128:256] + bias[layer : layer + 1, :]
            h = h + pltpu.roll(acc[:, 0:128], 1, 0) + pltpu.roll(acc[:, 256:384], n - 1, 0)
            if dst is None:
                h = pltpu.roll(h, n - halo, 0)
                tiles = [h[stride * x : stride * x + 32] for x in range(8)]
                whole = jnp.concatenate(tiles, axis=0).T.astype(bf16)
                for i in range(2):
                    out[(2 * t + i - xi) & 3] = whole[64 * i : 64 * i + 64]
            else:
                z = z0 - halo + layer + 1 + 2 * t + lane // 64
                ok = jnp.where((z >= 0) & (z < 16), 1.0, 0.0) * mask[first : first + n, :]
                dst[first : first + n, lanes_out] = jnp.where(
                    ok > 0, jnp.maximum(h, 0.0), 0.0
                ).astype(bf16)
            return carry

        lax.fori_loop(0, 5 - layer, pair, 0)


def convolve(block, band, bias):
    return pl.pallas_call(
        conv_kernel,
        out_shape=jax.ShapeDtypeStruct((4, 64, 256), bf16),
        in_specs=[VM, VM, VM],
        out_specs=VM,
        scratch_shapes=[
            pltpu.VMEM((16 * stride, 640), bf16),
            pltpu.VMEM((16 * stride, 512), bf16),
            pltpu.VMEM((16 * stride, 128), f32),
        ],
        compiler_params=pltpu.CompilerParams(vmem_limit_bytes=20 << 20),
        name="convolve",
    )(block, band, bias)


def place_kernel(own, high, far, low, out, rows):
    turn = 32 * (lax.axis_index("frame") % 4)
    parts = [r[...].astype(f32) for r in (own, high, far, low)]
    for x in range(8):
        line = jnp.concatenate([p[:, 32 * x : 32 * x + 32] for p in parts], axis=1)
        rows[pl.ds(x, 64, stride=8), :] = pltpu.roll(line, turn, 1)
    out[...] = rows[...].astype(bf16)


def place(own, high, far, low):
    return pl.pallas_call(
        place_kernel,
        out_shape=jax.ShapeDtypeStruct((512, 128), bf16),
        in_specs=[VM] * 4,
        out_specs=VM,
        scratch_shapes=[pltpu.VMEM((512, 128), f32)],
        compiler_params=pltpu.CompilerParams(vmem_limit_bytes=4 << 20),
        name="place",
    )(own, high, far, low)


def send(v, way, axis="frame"):
    return lax.ppermute(v, axis, way)


def joined(features, voxel_embed, visible, w_query, w_key, w_value, w_out, conv_weight, conv_bias):
    around = range(4)
    x_by = lambda k: [(4 * z + x, 4 * z + (x + k) % 4) for z in around for x in around]
    up, down = x_by(1), x_by(3)
    groups = [[4 * z + x for z in around] for x in around]
    frames, planes, c = features.shape[:3]
    feat = features.reshape(frames, planes, c * 8, 128)
    embed = voxel_embed.reshape(planes, c * 8, 128)
    a0, a1, a2, a3 = attend(0, feat, embed, visible, w_query, w_key)
    from_low = send(a2, up)
    high_a = send(a3, down)
    b0, b1, b2, b3 = attend(1, feat, embed, visible, w_query, w_key)
    band, wide_v, wide_o = weights(conv_weight, w_value, w_out)
    from_high = send(b2, down)
    low_b = send(b1, up)
    low_a = send(merge([a1, from_low], [8])[0], up)
    high_b = send(merge([b3, from_high], [8])[0], down)
    part = gather(a0, low_a, high_a, b0, low_b, high_b)
    part = lax.all_to_all(part, "frame", 0, 0, axis_index_groups=groups, tiled=True)
    hidden = finish(part, wide_v, wide_o).reshape(8, 32, 256)

    z_next = [(i, i + 4) for i in range(12)]
    z_prev = [(j, i) for i, j in z_next]
    below = send(hidden, z_next)
    above = send(hidden, z_prev)
    hidden = jnp.concatenate([below, hidden, above], axis=2)

    def where_is(z, chunk):
        return (4 * z + chunk % 4) * 4 + chunk // 4

    y_next = [(where_is(z, k), where_is(z, k + 1)) for z in range(4) for k in range(15)]
    y_prev = [(j, i) for i, j in y_next]
    left = send(hidden[:, -halo:], y_next, ("frame", "by"))
    right = send(hidden[:, :halo], y_prev, ("frame", "by"))
    hidden = jnp.concatenate([left, hidden, right], axis=1)
    x_next = [(0, 1), (1, 2), (2, 3)]
    x_prev = [(j, i) for i, j in x_next]
    front = send(hidden[-halo:], x_next, "bx")
    back = send(hidden[:halo], x_prev, "bx")
    pad = jnp.zeros((16, stride - 32 - 2 * halo, 768), bf16)
    hidden = jnp.concatenate([jnp.concatenate([front, hidden, back], axis=0), pad], axis=1)
    bias = jnp.concatenate([conv_bias, conv_bias], axis=1)
    out = convolve(hidden.reshape(16 * stride, 768), band, bias)
    low = send(out[1], up)
    high = send(out[3], down)
    far = send(out[2], x_by(2))
    return place(out[0], high, far, low).reshape(1, c, 8, 128)


def solution(mesh):
    return jax.shard_map(
        joined,
        mesh=mesh,
        in_specs=(
            P("frame", None, None, "bx", "by"),
            P(None, None, "bx", "by"),
            P("frame", None, "bx", "by"),
            P(),
            P(),
            P(),
            P(),
            P(),
            P(),
        ),
        out_specs=P("frame", None, "bx", "by"),
        check_vma=False,
    )
```

time: 118 us -> 120 us (1.017)
  the two profiles are of different devices: /device:TPU:184 before, /device:TPU:1 now
where the time goes in v3:
time: 120 us; the launch traced here: 119 us
  starting transfers between devices  45 us (38%)
  waiting for transfers between devices  41.8 us (35%)
  Pallas kernels  22.7 us (19%)
  local copies, waits for them, and re-layouts  8.89 us (7%)
    ppermute x15, starting transfers between devices, send(): return lax.ppermute(v, axis, way)  36.8 us
    ppermute x15, waiting for transfers between devices, send(): return lax.ppermute(v, axis, way)  30.5 us
    all_to_all x1, waiting for transfers between devices, joined(): lax.all_to_all(part, 'frame', 0, 0, axis_index_groups=groups, tiled=True)  11.3 us
    pallas_call x2, Pallas kernels, attend(): pl.pallas_call(functools.partial(attend_kernel, half), out_shape=[jax.Sha...  9.01 us
    pallas_call x1, Pallas kernels, convolve(): pl.pallas_call(conv_kernel, out_shape=jax.ShapeDtypeStruct((4, 64, 256),...  8.93 us
    unnamed x20, local copies, waits for them, and re-layouts  8.85 us
    all_to_all x1, starting transfers between devices, joined(): lax.all_to_all(part, 'frame', 0, 0, axis_index_groups=groups, tiled=True)  8.18 us
  transfers between devices with their start and end apart: 16, of which 11 were waited for; matrix products, arithmetic and copies ran while one was open for 0% of the time, Pallas kernels for 5%

profile of v3, /device:TPU:1, one launch (start us, length us, event | category | flops | bytes accessed | tf_op | source)
XLA Modules:
  0.0 119.1 jit_solution(7925050275961549342)
XLA Ops:
  0.0 3.4 %copy-done = bf16[4,16,64,8,128]{4,3,2,1,0:T(8,128)(2,1)S(1)} copy-done((bf16[4,16,64,8,128]{4,3,2,1,0:T(8,128)(2,1)S(1)}, bf16[4,16,64,8,128]{4,3,2,1,0:T(8,128)(2,1)}, u32[]{:S(2)}) %copy-start) | copy-done | bytes 8388632
  3.4 1.6 %copy-done.1 = bf16[16,64,8,128]{3,2,1,0:T(8,128)(2,1)S(1)} copy-done((bf16[16,64,8,128]{3,2,1,0:T(8,128)(2,1)S(1)}, bf16[16,64,8,128]{3,2,1,0:T(8,128)(2,1)}, u32[]{:S(2)}) %copy-start.1) | copy-done | bytes 2097176
  5.0 0.9 copy-done.3
  5.9 0.7 copy-done.4
  7.4 4.5 %attend.3 = (bf16[8,136,128]{2,1,0:T(8,128)(2,1)S(1)}, bf16[8,136,128]{2,1,0:T(8,128)(2,1)S(1)}, bf16[8,136,128]{2,1,0:T(8,128)(2,1)S(1)}, bf16[8,136,128]{2,1,0:T(8,128)(2,1)S(1)}) custom-call(bf16[4,16,512,128]{3,2,1,0:T(8,128)(2,1)S(1)} %bitcast.14, bf16[16,512,128]{2,1,0:T(8,128)(2,1)S(1)} %bitcast.16, s32[4,16,8,128]{3,2,1,0:T(8,128)S(1)} %copy-done.3, ...), custom_call_target="tpu_custom_call" | custom-call | flops 100000000 | bytes 12582912 | tf_op jit(solution)/shard_map/attend/pallas_call | solution.py:132
  11.9 3.4 %collective-permute-start.4 = (bf16[8,136,128]{2,1,0:T(8,128)(2,1)S(1)}, bf16[8,136,128]{2,1,0:T(8,128)(2,1)S(1)}, u32[]{:S(2)}, u32[]{:S(2)}) collective-permute-start(bf16[8,136,128]{2,1,0:T(8,128)(2,1)S(1)} %get-tuple-element.23), channel_id=1, source_target_pairs={{0,48},{16,0},{32,16},{48,32},{64,112},{80,64},{96,80},{112,96},{1... | collective-permute-start | bytes 835592 | tf_op jit(solution)/shard_map/ppermute | solution.py:395
  15.3 4.5 %attend.2 = (bf16[8,136,128]{2,1,0:T(8,128)(2,1)S(1)}, bf16[8,136,128]{2,1,0:T(8,128)(2,1)S(1)}, bf16[8,136,128]{2,1,0:T(8,128)(2,1)S(1)}, bf16[8,136,128]{2,1,0:T(8,128)(2,1)S(1)}) custom-call(bf16[4,16,512,128]{3,2,1,0:T(8,128)(2,1)S(1)} %bitcast.15, bf16[16,512,128]{2,1,0:T(8,128)(2,1)S(1)} %bitcast.17, s32[4,16,8,128]{3,2,1,0:T(8,128)S(1)} %copy-done.3, ...), custom_call_target="tpu_custom_call" | custom-call | flops 100000000 | bytes 12582912 | tf_op jit(solution)/shard_map/attend/pallas_call | solution.py:132
  19.9 2.7 %collective-permute-start.2 = (bf16[8,136,128]{2,1,0:T(8,128)(2,1)S(1)}, bf16[8,136,128]{2,1,0:T(8,128)(2,1)S(1)}, u32[]{:S(2)}, u32[]{:S(2)}) collective-permute-start(bf16[8,136,128]{2,1,0:T(8,128)(2,1)S(1)} %get-tuple-element.19), channel_id=1, source_target_pairs={{0,48},{16,0},{32,16},{48,32},{64,112},{80,64},{96,80},{112,96},{1... | collective-permute-start | bytes 835592 | tf_op jit(solution)/shard_map/ppermute | solution.py:395
  22.8 2.8 %collective-permute-start.5 = (bf16[8,136,128]{2,1,0:T(8,128)(2,1)S(1)}, bf16[8,136,128]{2,1,0:T(8,128)(2,1)S(1)}, u32[]{:S(2)}, u32[]{:S(2)}) collective-permute-start(bf16[8,136,128]{2,1,0:T(8,128)(2,1)S(1)} %merge.3), channel_id=1, source_target_pairs={{0,48},{16,0},{32,16},{48,32},{64,112},{80,64},{96,80},{112,96},{1... | collective-permute-start | bytes 835592 | tf_op jit(solution)/shard_map/ppermute | solution.py:395
  25.6 2.7 %collective-permute-done.refs_1_ = bf16[8,136,128]{2,1,0:T(8,128)(2,1)S(1)} collective-permute-done((bf16[8,136,128]{2,1,0:T(8,128)(2,1)S(1)}, bf16[8,136,128]{2,1,0:T(8,128)(2,1)S(1)}, u32[]{:S(2)}, u32[]{:S(2)}) %collective-permute-start) | collective-permute-done | bytes 278560 | tf_op jit(solution)/shard_map/ppermute | solution.py:395
  28.9 5.4 %collective-permute-done.3.refs_4_ = bf16[8,136,128]{2,1,0:T(8,128)(2,1)S(1)} collective-permute-done((bf16[8,136,128]{2,1,0:T(8,128)(2,1)S(1)}, bf16[8,136,128]{2,1,0:T(8,128)(2,1)S(1)}, u32[]{:S(2)}, u32[]{:S(2)}) %collective-permute-start.3) | collective-permute-done | bytes 278560 | tf_op jit(solution)/shard_map/ppermute | solution.py:395
  34.3 6.0 %collective-permute-done.1.refs_1_ = bf16[8,136,128]{2,1,0:T(8,128)(2,1)S(1)} collective-permute-done((bf16[8,136,128]{2,1,0:T(8,128)(2,1)S(1)}, bf16[8,136,128]{2,1,0:T(8,128)(2,1)S(1)}, u32[]{:S(2)}, u32[]{:S(2)}) %collective-permute-start.1) | collective-permute-done | bytes 278560 | tf_op jit(solution)/shard_map/ppermute | solution.py:395
  40.3 1.5 %gather.1 = bf16[4,4,136,128]{3,2,1,0:T(8,128)(2,1)} custom-call(bf16[8,136,128]{2,1,0:T(8,128)(2,1)S(1)} %get-tuple-element.16.refs_0_, bf16[8,136,128]{2,1,0:T(8,128)(2,1)S(1)} %collective-permute-done.1.refs_1_, bf16[8,136,128]{2,1,0:T(8,128)(2,1)S(1)} %collective-permute-done.2.refs_2_, bf16[8,136,128]{2,1,0:T(8,128)(2,1)S(1)} %get-tuple-element.20.refs_3_, ...), custom_call_target="tpu_custom_call" | custom-call | tf_op jit(solution)/shard_map/gather/pallas_call | solution.py:227
  41.7 8.2 %all-to-all-start = ((bf16[4,4,136,128]{3,2,1,0:T(8,128)(2,1)}), bf16[4,4,136,128]{3,2,1,0:T(8,128)(2,1)S(1)}, u32[]{:S(2)}, u32[]{:S(2)}) async-start(bf16[4,4,136,128]{3,2,1,0:T(8,128)(2,1)} %gather.1), calls=%async_computation | async-start | bytes 1114112 | tf_op jit(solution)/shard_map/all_to_all | solution.py:416
  49.9 1.5 %copy-done.2 = bf16[4,3,3,3,64,64]{5,4,3,2,1,0:T(8,128)(2,1)S(1)} copy-done((bf16[4,3,3,3,64,64]{5,4,3,2,1,0:T(8,128)(2,1)S(1)}, bf16[4,3,3,3,64,64]{5,4,3,2,1,0:T(8,128)(2,1)}, u32[]{:S(2)}) %copy-start.2) | copy-done | bytes 884760
  51.4 0.9 weights.1
  52.3 11.3 %all-to-all-done.part = bf16[4,4,136,128]{3,2,1,0:T(8,128)(2,1)S(1)} async-done(((bf16[4,4,136,128]{3,2,1,0:T(8,128)(2,1)}), bf16[4,4,136,128]{3,2,1,0:T(8,128)(2,1)S(1)}, u32[]{:S(2)}, u32[]{:S(2)}) %all-to-all-start) | async-done | bytes 557088 | tf_op jit(solution)/shard_map/all_to_all | solution.py:416
  63.6 0.8 finish.1
  64.4 3.0 %collective-permute-start.6 = (bf16[8,32,256]{2,1,0:T(8,128)(2,1)S(1)}, bf16[8,32,256]{2,1,0:T(8,128)(2,1)S(1)}, u32[]{:S(2)}, u32[]{:S(2)}) collective-permute-start(bf16[8,32,256]{2,1,0:T(8,128)(2,1)S(1)} %bitcast.19), channel_id=1, source_target_pairs={{0,64},{16,80},{32,96},{48,112},{64,128},{80,144},{96,160},{112,17... | collective-permute-start | bytes 393224 | tf_op jit(solution)/shard_map/ppermute | solution.py:395
  67.5 1.3 %collective-permute-start.7 = (bf16[8,32,256]{2,1,0:T(8,128)(2,1)S(1)}, bf16[8,32,256]{2,1,0:T(8,128)(2,1)S(1)}, u32[]{:S(2)}, u32[]{:S(2)}) collective-permute-start(bf16[8,32,256]{2,1,0:T(8,128)(2,1)S(1)} %bitcast.20), channel_id=1, source_target_pairs={{64,0},{80,16},{96,32},{112,48},{128,64},{144,80},{160,96},{176,11... | collective-permute-start | bytes 393224 | tf_op jit(solution)/shard_map/ppermute | solution.py:395
  69.4 5.2 %collective-permute-done.7 = bf16[8,32,256]{2,1,0:T(8,128)(2,1)S(1)} collective-permute-done((bf16[8,32,256]{2,1,0:T(8,128)(2,1)S(1)}, bf16[8,32,256]{2,1,0:T(8,128)(2,1)S(1)}, u32[]{:S(2)}, u32[]{:S(2)}) %collective-permute-start.7) | collective-permute-done | bytes 131104 | tf_op jit(solution)/shard_map/ppermute | solution.py:395
  74.6 1.9 %collective-permute-start.8 = (bf16[8,4,768]{2,1,0:T(4,128)(2,1)S(1)}, bf16[8,4,768]{2,1,0:T(4,128)(2,1)S(1)}, u32[]{:S(2)}, u32[]{:S(2)}) collective-permute-start(bf16[8,4,768]{2,1,0:T(4,128)(2,1)S(1)} %get-tuple-element.29), channel_id=1, source_target_pairs={{0,16},{16,32},{32,48},{48,1},{1,17},{17,33},{33,49},{49,2},{2,18}... | collective-permute-start | bytes 147464 | tf_op jit(solution)/shard_map/ppermute | solution.py:395
  76.6 7.2 %collective-permute-start.9 = (bf16[8,4,768]{2,1,0:T(4,128)(2,1)S(1)}, bf16[8,4,768]{2,1,0:T(4,128)(2,1)S(1)}, u32[]{:S(2)}, u32[]{:S(2)}) collective-permute-start(bf16[8,4,768]{2,1,0:T(4,128)(2,1)S(1)} %get-tuple-element.30), channel_id=1, source_target_pairs={{16,0},{32,16},{48,32},{1,48},{17,1},{33,17},{49,33},{2,49},{18,2}... | collective-permute-start | bytes 147464 | tf_op jit(solution)/shard_map/ppermute | solution.py:395
  83.7 1.1 collective-permute-done.9
  85.1 3.2 %collective-permute-start.10 = (bf16[4,40,768]{2,1,0:T(8,128)(2,1)S(1)}, bf16[4,40,768]{2,1,0:T(8,128)(2,1)S(1)}, u32[]{:S(2)}, u32[]{:S(2)}) collective-permute-start(bf16[4,40,768]{2,1,0:T(8,128)(2,1)S(1)} %get-tuple-element.27), channel_id=1, source_target_pairs={{0,4},{4,8},{8,12},{1,5},{5,9},{9,13},{2,6},{6,10},{10,14},{3,7},{... | collective-permute-start | bytes 737288 | tf_op jit(solution)/shard_map/ppermute | solution.py:395
  88.3 1.3 %collective-permute-start.11 = (bf16[4,40,768]{2,1,0:T(8,128)(2,1)S(1)}, bf16[4,40,768]{2,1,0:T(8,128)(2,1)S(1)}, u32[]{:S(2)}, u32[]{:S(2)}) collective-permute-start(bf16[4,40,768]{2,1,0:T(8,128)(2,1)S(1)} %get-tuple-element.28), channel_id=1, source_target_pairs={{4,0},{8,4},{12,8},{5,1},{9,5},{13,9},{6,2},{10,6},{14,10},{7,3},{... | collective-permute-start | bytes 737288 | tf_op jit(solution)/shard_map/ppermute | solution.py:395
  89.7 1.7 %collective-permute-done.10 = bf16[4,40,768]{2,1,0:T(8,128)(2,1)S(1)} collective-permute-done((bf16[4,40,768]{2,1,0:T(8,128)(2,1)S(1)}, bf16[4,40,768]{2,1,0:T(8,128)(2,1)S(1)}, u32[]{:S(2)}, u32[]{:S(2)}) %collective-permute-start.10) | collective-permute-done | bytes 245792 | tf_op jit(solution)/shard_map/ppermute | solution.py:395
  91.4 4.0 %collective-permute-done.11 = bf16[4,40,768]{2,1,0:T(8,128)(2,1)S(1)} collective-permute-done((bf16[4,40,768]{2,1,0:T(8,128)(2,1)S(1)}, bf16[4,40,768]{2,1,0:T(8,128)(2,1)S(1)}, u32[]{:S(2)}, u32[]{:S(2)}) %collective-permute-start.11) | collective-permute-done | bytes 245792 | tf_op jit(solution)/shard_map/ppermute | solution.py:395
  95.6 8.9 %convolve.1 = bf16[4,64,256]{2,1,0:T(8,128)(2,1)S(1)} custom-call(bf16[768,768]{1,0:T(8,128)(2,1)S(1)} %bitcast.18, bf16[4,3,256,384]{3,2,1,0:T(8,128)(2,1)S(1)} %get-tuple-element.26.band, f32[4,128]{1,0:T(4,128)S(1)} %pad_maximum_fusion.4.bias), custom_call_target="tpu_custom_call" | custom-call | tf_op jit(solution)/shard_map/convolve/pallas_call | solution.py:358
  104.6 9.1 %collective-permute-start.12 = (bf16[64,256]{1,0:T(8,128)(2,1)S(1)}, bf16[64,256]{1,0:T(8,128)(2,1)S(1)}, u32[]{:S(2)}, u32[]{:S(2)}) collective-permute-start(bf16[64,256]{1,0:T(8,128)(2,1)S(1)} %get-tuple-element.33), channel_id=1, source_target_pairs={{0,48},{16,0},{32,16},{48,32},{64,112},{80,64},{96,80},{112,96},{1... | collective-permute-start | bytes 98312 | tf_op jit(solution)/shard_map/ppermute | solution.py:395
  114.7 3.3 %collective-permute-done.13.far = bf16[64,256]{1,0:T(8,128)(2,1)S(1)} collective-permute-done((bf16[64,256]{1,0:T(8,128)(2,1)S(1)}, bf16[64,256]{1,0:T(8,128)(2,1)S(1)}, u32[]{:S(2)}, u32[]{:S(2)}) %collective-permute-start.13) | collective-permute-done | bytes 32800 | tf_op jit(solution)/shard_map/ppermute | solution.py:395
  118.0 1.1 place.1
  (35 shorter events, 3.8 us)
Async XLA Ops:
  0.0 3.4 %copy-start = (bf16[4,16,64,8,128]{4,3,2,1,0:T(8,128)(2,1)S(1)}, bf16[4,16,64,8,128]{4,3,2,1,0:T(8,128)(2,1)}, u32[]{:S(2)}) copy-start(bf16[4,16,64,8,128]{4,3,2,1,0:T(8,128)(2,1)} %param.9) | copy-start | bytes 25165828
  3.4 1.6 %copy-start.1 = (bf16[16,64,8,128]{3,2,1,0:T(8,128)(2,1)S(1)}, bf16[16,64,8,128]{3,2,1,0:T(8,128)(2,1)}, u32[]{:S(2)}) copy-start(bf16[16,64,8,128]{3,2,1,0:T(8,128)(2,1)} %param.10) | copy-start | bytes 6291460
  5.0 0.9 copy-start.3
  5.9 0.7 copy-start.4
  6.6 0.7 copy-start.5
  7.4 7.9 %copy-start.6 = (bf16[64,64]{1,0:T(8,128)(2,1)S(1)}, bf16[64,64]{1,0:T(8,128)(2,1)}, u32[]{:S(2)}) copy-start(bf16[64,64]{1,0:T(8,128)(2,1)} %wk_at.3) | copy-start | bytes 24580
  11.9 10.7 %collective-permute-start.4 = (bf16[8,136,128]{2,1,0:T(8,128)(2,1)S(1)}, bf16[8,136,128]{2,1,0:T(8,128)(2,1)S(1)}, u32[]{:S(2)}, u32[]{:S(2)}) collective-permute-start(bf16[8,136,128]{2,1,0:T(8,128)(2,1)S(1)} %get-tuple-element.23), channel_id=1, source_target_pairs={{0,48},{16,0},{32,16},{48,32},{64,112},{80,64},{96,80},{112,96},{1... | collective-permute-start | bytes 835592 | tf_op jit(solution)/shard_map/ppermute | solution.py:395
  19.8 8.6 %collective-permute-start = (bf16[8,136,128]{2,1,0:T(8,128)(2,1)S(1)}, bf16[8,136,128]{2,1,0:T(8,128)(2,1)S(1)}, u32[]{:S(2)}, u32[]{:S(2)}) collective-permute-start(bf16[8,136,128]{2,1,0:T(8,128)(2,1)S(1)} %get-tuple-element.18), channel_id=1, source_target_pairs={{0,16},{16,32},{32,48},{48,0},{64,80},{80,96},{96,112},{112,64},{1... | collective-permute-start | bytes 835592 | tf_op jit(solution)/shard_map/ppermute | solution.py:395
  19.9 9.0 %collective-permute-start.2 = (bf16[8,136,128]{2,1,0:T(8,128)(2,1)S(1)}, bf16[8,136,128]{2,1,0:T(8,128)(2,1)S(1)}, u32[]{:S(2)}, u32[]{:S(2)}) collective-permute-start(bf16[8,136,128]{2,1,0:T(8,128)(2,1)S(1)} %get-tuple-element.19), channel_id=1, source_target_pairs={{0,48},{16,0},{32,16},{48,32},{64,112},{80,64},{96,80},{112,96},{1... | collective-permute-start | bytes 835592 | tf_op jit(solution)/shard_map/ppermute | solution.py:395
  22.5 11.8 %collective-permute-start.3 = (bf16[8,136,128]{2,1,0:T(8,128)(2,1)S(1)}, bf16[8,136,128]{2,1,0:T(8,128)(2,1)S(1)}, u32[]{:S(2)}, u32[]{:S(2)}) collective-permute-start(bf16[8,136,128]{2,1,0:T(8,128)(2,1)S(1)} %get-tuple-element.21), channel_id=1, source_target_pairs={{0,16},{16,32},{32,48},{48,0},{64,80},{80,96},{96,112},{112,64},{1... | collective-permute-start | bytes 835592 | tf_op jit(solution)/shard_map/ppermute | solution.py:395
  22.8 27.1 %copy-start.7 = (bf16[64,64]{1,0:T(8,128)(2,1)S(1)}, bf16[64,64]{1,0:T(8,128)(2,1)}, u32[]{:S(2)}) copy-start(bf16[64,64]{1,0:T(8,128)(2,1)} %wv.1) | copy-start | bytes 24580
  22.8 27.1 %copy-start.8 = (bf16[64,64]{1,0:T(8,128)(2,1)S(1)}, bf16[64,64]{1,0:T(8,128)(2,1)}, u32[]{:S(2)}) copy-start(bf16[64,64]{1,0:T(8,128)(2,1)} %wo.1) | copy-start | bytes 24580
  22.8 11.5 %collective-permute-start.5 = (bf16[8,136,128]{2,1,0:T(8,128)(2,1)S(1)}, bf16[8,136,128]{2,1,0:T(8,128)(2,1)S(1)}, u32[]{:S(2)}, u32[]{:S(2)}) collective-permute-start(bf16[8,136,128]{2,1,0:T(8,128)(2,1)S(1)} %merge.3), channel_id=1, source_target_pairs={{0,48},{16,0},{32,16},{48,32},{64,112},{80,64},{96,80},{112,96},{1... | collective-permute-start | bytes 835592 | tf_op jit(solution)/shard_map/ppermute | solution.py:395
  28.6 11.7 %collective-permute-start.1 = (bf16[8,136,128]{2,1,0:T(8,128)(2,1)S(1)}, bf16[8,136,128]{2,1,0:T(8,128)(2,1)S(1)}, u32[]{:S(2)}, u32[]{:S(2)}) collective-permute-start(bf16[8,136,128]{2,1,0:T(8,128)(2,1)S(1)} %merge.2), channel_id=1, source_target_pairs={{0,16},{16,32},{32,48},{48,0},{64,80},{80,96},{96,112},{112,64},{1... | collective-permute-start | bytes 835592 | tf_op jit(solution)/shard_map/ppermute | solution.py:395
  41.7 21.9 %all-to-all-start = ((bf16[4,4,136,128]{3,2,1,0:T(8,128)(2,1)}), bf16[4,4,136,128]{3,2,1,0:T(8,128)(2,1)S(1)}, u32[]{:S(2)}, u32[]{:S(2)}) async-start(bf16[4,4,136,128]{3,2,1,0:T(8,128)(2,1)} %gather.1), calls=%async_computation | async-start | bytes 1114112 | tf_op jit(solution)/shard_map/all_to_all | solution.py:416
  49.9 1.5 %copy-start.2 = (bf16[4,3,3,3,64,64]{5,4,3,2,1,0:T(8,128)(2,1)S(1)}, bf16[4,3,3,3,64,64]{5,4,3,2,1,0:T(8,128)(2,1)}, u32[]{:S(2)}) copy-start(bf16[4,3,3,3,64,64]{5,4,3,2,1,0:T(8,128)(2,1)} %param.16) | copy-start | bytes 2654212
  52.3 37.4 %copy-start.9 = (f32[4,64]{1,0:T(4,128)S(1)}, f32[4,64]{1,0:T(4,128)}, u32[]{:S(2)}) copy-start(f32[4,64]{1,0:T(4,128)} %param.17) | copy-start | bytes 3076
  64.4 5.0 %collective-permute-start.6 = (bf16[8,32,256]{2,1,0:T(8,128)(2,1)S(1)}, bf16[8,32,256]{2,1,0:T(8,128)(2,1)S(1)}, u32[]{:S(2)}, u32[]{:S(2)}) collective-permute-start(bf16[8,32,256]{2,1,0:T(8,128)(2,1)S(1)} %bitcast.19), channel_id=1, source_target_pairs={{0,64},{16,80},{32,96},{48,112},{64,128},{80,144},{96,160},{112,17... | collective-permute-start | bytes 393224 | tf_op jit(solution)/shard_map/ppermute | solution.py:395
  67.5 7.1 %collective-permute-start.7 = (bf16[8,32,256]{2,1,0:T(8,128)(2,1)S(1)}, bf16[8,32,256]{2,1,0:T(8,128)(2,1)S(1)}, u32[]{:S(2)}, u32[]{:S(2)}) collective-permute-start(bf16[8,32,256]{2,1,0:T(8,128)(2,1)S(1)} %bitcast.20), channel_id=1, source_target_pairs={{64,0},{80,16},{96,32},{112,48},{128,64},{144,80},{160,96},{176,11... | collective-permute-start | bytes 393224 | tf_op jit(solution)/shard_map/ppermute | solution.py:395
  74.6 9.1 %collective-permute-start.8 = (bf16[8,4,768]{2,1,0:T(4,128)(2,1)S(1)}, bf16[8,4,768]{2,1,0:T(4,128)(2,1)S(1)}, u32[]{:S(2)}, u32[]{:S(2)}) collective-permute-start(bf16[8,4,768]{2,1,0:T(4,128)(2,1)S(1)} %get-tuple-element.29), channel_id=1, source_target_pairs={{0,16},{16,32},{32,48},{48,1},{1,17},{17,33},{33,49},{49,2},{2,18}... | collective-permute-start | bytes 147464 | tf_op jit(solution)/shard_map/ppermute | solution.py:395
  76.6 8.3 %collective-permute-start.9 = (bf16[8,4,768]{2,1,0:T(4,128)(2,1)S(1)}, bf16[8,4,768]{2,1,0:T(4,128)(2,1)S(1)}, u32[]{:S(2)}, u32[]{:S(2)}) collective-permute-start(bf16[8,4,768]{2,1,0:T(4,128)(2,1)S(1)} %get-tuple-element.30), channel_id=1, source_target_pairs={{16,0},{32,16},{48,32},{1,48},{17,1},{33,17},{49,33},{2,49},{18,2}... | collective-permute-start | bytes 147464 | tf_op jit(solution)/shard_map/ppermute | solution.py:395
  85.1 6.3 %collective-permute-start.10 = (bf16[4,40,768]{2,1,0:T(8,128)(2,1)S(1)}, bf16[4,40,768]{2,1,0:T(8,128)(2,1)S(1)}, u32[]{:S(2)}, u32[]{:S(2)}) collective-permute-start(bf16[4,40,768]{2,1,0:T(8,128)(2,1)S(1)} %get-tuple-element.27), channel_id=1, source_target_pairs={{0,4},{4,8},{8,12},{1,5},{5,9},{9,13},{2,6},{6,10},{10,14},{3,7},{... | collective-permute-start | bytes 737288 | tf_op jit(solution)/shard_map/ppermute | solution.py:395
  88.3 7.1 %collective-permute-start.11 = (bf16[4,40,768]{2,1,0:T(8,128)(2,1)S(1)}, bf16[4,40,768]{2,1,0:T(8,128)(2,1)S(1)}, u32[]{:S(2)}, u32[]{:S(2)}) collective-permute-start(bf16[4,40,768]{2,1,0:T(8,128)(2,1)S(1)} %get-tuple-element.28), channel_id=1, source_target_pairs={{4,0},{8,4},{12,8},{5,1},{9,5},{13,9},{6,2},{10,6},{14,10},{7,3},{... | collective-permute-start | bytes 737288 | tf_op jit(solution)/shard_map/ppermute | solution.py:395
  104.6 10.1 %collective-permute-start.12 = (bf16[64,256]{1,0:T(8,128)(2,1)S(1)}, bf16[64,256]{1,0:T(8,128)(2,1)S(1)}, u32[]{:S(2)}, u32[]{:S(2)}) collective-permute-start(bf16[64,256]{1,0:T(8,128)(2,1)S(1)} %get-tuple-element.33), channel_id=1, source_target_pairs={{0,48},{16,0},{32,16},{48,32},{64,112},{80,64},{96,80},{112,96},{1... | collective-permute-start | bytes 98312 | tf_op jit(solution)/shard_map/ppermute | solution.py:395
  113.7 4.3 %collective-permute-start.13 = (bf16[64,256]{1,0:T(8,128)(2,1)S(1)}, bf16[64,256]{1,0:T(8,128)(2,1)S(1)}, u32[]{:S(2)}, u32[]{:S(2)}) collective-permute-start(bf16[64,256]{1,0:T(8,128)(2,1)S(1)} %get-tuple-element.32), channel_id=1, source_target_pairs={{0,32},{16,48},{32,0},{48,16},{64,96},{80,112},{96,64},{112,80},{1... | collective-permute-start | bytes 98312 | tf_op jit(solution)/shard_map/ppermute | solution.py:395
  113.7 4.3 %collective-permute-start.14 = (bf16[64,256]{1,0:T(8,128)(2,1)S(1)}, bf16[64,256]{1,0:T(8,128)(2,1)S(1)}, u32[]{:S(2)}, u32[]{:S(2)}) collective-permute-start(bf16[64,256]{1,0:T(8,128)(2,1)S(1)} %get-tuple-element.31), channel_id=1, source_target_pairs={{0,16},{16,32},{32,48},{48,0},{64,80},{80,96},{96,112},{112,64},{1... | collective-permute-start | bytes 98312 | tf_op jit(solution)/shard_map/ppermute | solution.py:395

commit v4 on v3

--- a/solution.py
+++ b/solution.py
@@ -48,8 +48,8 @@
     turn = (128 - 32 * xi) & 127
 
     def copies(s):
-        rel = half * steps * n + s * n
-        z = pl.ds(((rel // 4 + zh) & 3) * 4 + rel % 4, n)
+        block = 1 + 2 * half + s * n // 4
+        z = pl.ds(((block + zh) & 3) * 4 + s * n % 4, n)
         return [
             pltpu.make_async_copy(embed_at.at[z], embed.at[s], sems.at[s, 0]),
             pltpu.make_async_copy(feat_at.at[:, z], feat.at[s], sems.at[s, 1]),
@@ -147,7 +147,7 @@
         compiler_params=pltpu.CompilerParams(vmem_limit_bytes=14 << 20),
         cost_estimate=pl.CostEstimate(flops=10**8, bytes_accessed=12 << 20, transcendentals=0),
         name="attend",
-    )(feat, embed, visible, w_query, w_key)
+    )(*[pltpu.with_memory_space_constraint(v, pltpu.HBM) for v in (feat, embed, visible, w_query, w_key)])
 
 
 def spread(v):
@@ -175,20 +175,23 @@
     return acc.reshape(128, 128)
 
 
+def merge_plane(out, i, parts):
+    lane = lax.broadcasted_iota(jnp.int32, (8, 128), 1)
+    ws, total, m = merged_plane(parts)
+    out[i, 0:128, :] = weighted_rows(parts, ws).astype(bf16)
+    hi, mid, low = three_terms(m)
+    packed = jnp.where(
+        lane < 32, hi, jnp.where(lane < 64, mid, jnp.where(lane >= 96, total, low))
+    )
+    out[i, 128:136, :] = packed.astype(bf16)
+
+
 def merge_kernel(n, sizes, *refs):
     ins, outs = refs[:n], refs[n:]
-    lane = lax.broadcasted_iota(jnp.int32, (8, 128), 1)
     at = 0
     for out, size in zip(outs, sizes):
         for i in range(size):
-            parts = [(r, at) for r in ins]
-            ws, total, m = merged_plane(parts)
-            out[i, 0:128, :] = weighted_rows(parts, ws).astype(bf16)
-            hi, mid, low = three_terms(m)
-            packed = jnp.where(
-                lane < 32, hi, jnp.where(lane < 64, mid, jnp.where(lane >= 96, total, low))
-            )
-            out[i, 128:136, :] = packed.astype(bf16)
+            merge_plane(out, i, [(r, at) for r in ins])
             at += 1
 
 
@@ -205,38 +208,28 @@
     )(*parts)
 
 
-def gather_kernel(*refs):
-    ins, out = refs[:6], refs[6]
-    lane = lax.broadcasted_iota(jnp.int32, (8, 128), 1)
-    zh = lax.axis_index("frame") // 4
-    for rel in range(4):
-        slot = (zh + rel) & 3
-        for i in range(4):
-            at = (4 * rel + i) & 7
-            parts = [(r, at) for r in ins[3 * (rel // 2) : 3 * (rel // 2) + 3]]
-            ws, total, m = merged_plane(parts)
-            out[slot, i, 0:128, :] = weighted_rows(parts, ws).astype(bf16)
-            hi, mid, low = three_terms(m)
-            packed = jnp.where(
-                lane < 32, hi, jnp.where(lane < 64, mid, jnp.where(lane >= 96, total, low))
-            )
-            out[slot, i, 128:136, :] = packed.astype(bf16)
-
-
-def gather(*parts):
-    return pl.pallas_call(
-        gather_kernel,
-        out_shape=jax.ShapeDtypeStruct((4, 4, 136, 128), bf16),
-        in_specs=[VM] * 6,
+def lift_kernel(at, slot, came, out):
+    other = 2 - at
+    out[other : other + 2] = slot[other : other + 2]
+    for i in range(2):
+        merge_plane(out, at + i, [(slot, at + i), (came, i)])
+
+
+def lift(at, slot, came):
+    return pl.pallas_call(
+        functools.partial(lift_kernel, at),
+        out_shape=jax.ShapeDtypeStruct(slot.shape, bf16),
+        in_specs=[VM] * 2,
         out_specs=VM,
-        compiler_params=pltpu.CompilerParams(vmem_limit_bytes=6 << 20),
-        name="gather",
-    )(*parts)
-
-
-def finish_kernel(part, wv, wo, out, rows):
+        compiler_params=pltpu.CompilerParams(vmem_limit_bytes=4 << 20),
+        cost_estimate=pl.CostEstimate(flops=10**5, bytes_accessed=10**5, transcendentals=0),
+        name="lift",
+    )(slot, came)
+
+
+def finish_kernel(own, low, high, wv, wo, out, rows):
     for p in range(4):
-        parts = [(part.at[i], p) for i in range(4)]
+        parts = [(own, p), (low, p), (high, p)]
         ws, total, _ = merged_plane(parts)
         inv = 1.0 / total
         rows[128 * p : 128 * p + 128, :] = weighted_rows(parts, [w * inv for w in ws])
@@ -249,16 +242,16 @@
     out[...] = dot(attended, wo[...]).astype(bf16)
 
 
-def finish(part, wv, wo):
+def finish(own, low, high, wv, wo):
     return pl.pallas_call(
         finish_kernel,
         out_shape=jax.ShapeDtypeStruct((256, 256), bf16),
-        in_specs=[VM] * 3,
+        in_specs=[VM] * 5,
         out_specs=VM,
         scratch_shapes=[pltpu.VMEM((512, 128), f32)],
         compiler_params=pltpu.CompilerParams(vmem_limit_bytes=6 << 20),
         name="finish",
-    )(part, wv, wo)
+    )(own, low, high, wv, wo)
 
 
 def weights_kernel(w, wv, wo, band, wide_v, wide_o, tmp):
@@ -399,7 +392,8 @@
     around = range(4)
     x_by = lambda k: [(4 * z + x, 4 * z + (x + k) % 4) for z in around for x in around]
     up, down = x_by(1), x_by(3)
-    groups = [[4 * z + x for z in around] for x in around]
+    z_up = [(i, (i + 4) % 16) for i in range(16)]
+    z_down = [(j, i) for i, j in z_up]
     frames, planes, c = features.shape[:3]
     feat = features.reshape(frames, planes, c * 8, 128)
     embed = voxel_embed.reshape(planes, c * 8, 128)
@@ -412,9 +406,13 @@
     low_b = send(b1, up)
     low_a = send(merge([a1, from_low], [8])[0], up)
     high_b = send(merge([b3, from_high], [8])[0], down)
-    part = gather(a0, low_a, high_a, b0, low_b, high_b)
-    part = lax.all_to_all(part, "frame", 0, 0, axis_index_groups=groups, tiled=True)
-    hidden = finish(part, wide_v, wide_o).reshape(8, 32, 256)
+    z1, z2a, z2b = merge([a0, low_a, high_a], [4, 2, 2])
+    from_low = send(z2a, z_up)
+    from_high = send(z2b, z_down)
+    low = send(lift(0, z1, from_low), z_up)
+    z3, z0 = merge([b0, low_b, high_b], [4, 4])
+    high = send(lift(2, z3, from_high), z_down)
+    hidden = finish(z0, low, high, wide_v, wide_o).reshape(8, 32, 256)
 
     z_next = [(i, i + 4) for i in range(12)]
     z_prev = [(j, i) for i, j in z_next]

time: 120 us -> 104 us (0.87)
  the two profiles are of different devices: /device:TPU:1 before, /device:TPU:8 now
where the time goes in v4:
time: 104 us; the launch traced here: 103 us
  starting transfers between devices  41.8 us (40%)
  waiting for transfers between devices  37.6 us (36%)
  Pallas kernels  23.3 us (22%)
    ppermute x19, starting transfers between devices, send(): return lax.ppermute(v, axis, way)  41.8 us
    ppermute x19, waiting for transfers between devices, send(): return lax.ppermute(v, axis, way)  37.6 us
    pallas_call x2, Pallas kernels, attend(): pl.pallas_call(functools.partial(attend_kernel, half), out_shape=[jax.Sha...  10.1 us
    pallas_call x1, Pallas kernels, convolve(): pl.pallas_call(conv_kernel, out_shape=jax.ShapeDtypeStruct((4, 64, 256),...  8.94 us
  transfers between devices with their start and end apart: 19, of which 14 were waited for; matrix products, arithmetic and copies ran while one was open for 0% of the time, Pallas kernels for 7%

profile of v4, /device:TPU:8, one launch (start us, length us, event | category | flops | bytes accessed | tf_op | source)
XLA Modules:
  0.0 103.4 jit_solution(12451486522645531012)
XLA Ops:
  0.0 5.0 %attend.3 = (bf16[8,136,128]{2,1,0:T(8,128)(2,1)S(1)}, bf16[8,136,128]{2,1,0:T(8,128)(2,1)S(1)}, bf16[8,136,128]{2,1,0:T(8,128)(2,1)S(1)}, bf16[8,136,128]{2,1,0:T(8,128)(2,1)S(1)}) custom-call(bf16[4,16,512,128]{3,2,1,0:T(8,128)(2,1)} %bitcast.21, bf16[16,512,128]{2,1,0:T(8,128)(2,1)} %bitcast.23, s32[4,16,8,128]{3,2,1,0:T(8,128)} %seen_at.3, ...), custom_call_target="tpu_custom_call" | custom-call | flops 100000000 | bytes 12582912 | tf_op jit(solution)/shard_map/attend/pallas_call | solution.py:132
  5.0 1.6 %collective-permute-start.3 = (bf16[8,136,128]{2,1,0:T(8,128)(2,1)S(1)}, bf16[8,136,128]{2,1,0:T(8,128)(2,1)S(1)}, u32[]{:S(2)}, u32[]{:S(2)}) collective-permute-start(bf16[8,136,128]{2,1,0:T(8,128)(2,1)S(1)} %get-tuple-element.28), channel_id=1, source_target_pairs={{0,16},{16,32},{32,48},{48,0},{64,80},{80,96},{96,112},{112,64},{1... | collective-permute-start | bytes 835592 | tf_op jit(solution)/shard_map/ppermute | solution.py:388
  6.6 5.0 %attend.2 = (bf16[8,136,128]{2,1,0:T(8,128)(2,1)S(1)}, bf16[8,136,128]{2,1,0:T(8,128)(2,1)S(1)}, bf16[8,136,128]{2,1,0:T(8,128)(2,1)S(1)}, bf16[8,136,128]{2,1,0:T(8,128)(2,1)S(1)}) custom-call(bf16[4,16,512,128]{3,2,1,0:T(8,128)(2,1)} %bitcast.22, bf16[16,512,128]{2,1,0:T(8,128)(2,1)} %bitcast.24, s32[4,16,8,128]{3,2,1,0:T(8,128)} %seen_at.3, ...), custom_call_target="tpu_custom_call" | custom-call | flops 100000000 | bytes 12582912 | tf_op jit(solution)/shard_map/attend/pallas_call | solution.py:132
  11.7 1.8 %collective-permute-start.1 = (bf16[8,136,128]{2,1,0:T(8,128)(2,1)S(1)}, bf16[8,136,128]{2,1,0:T(8,128)(2,1)S(1)}, u32[]{:S(2)}, u32[]{:S(2)}) collective-permute-start(bf16[8,136,128]{2,1,0:T(8,128)(2,1)S(1)} %get-tuple-element.24), channel_id=1, source_target_pairs={{0,48},{16,0},{32,16},{48,32},{64,112},{80,64},{96,80},{112,96},{1... | collective-permute-start | bytes 835592 | tf_op jit(solution)/shard_map/ppermute | solution.py:388
  13.5 1.5 %collective-permute-start.5 = (bf16[8,136,128]{2,1,0:T(8,128)(2,1)S(1)}, bf16[8,136,128]{2,1,0:T(8,128)(2,1)S(1)}, u32[]{:S(2)}, u32[]{:S(2)}) collective-permute-start(bf16[8,136,128]{2,1,0:T(8,128)(2,1)S(1)} %get-tuple-element.29), channel_id=1, source_target_pairs={{0,48},{16,0},{32,16},{48,32},{64,112},{80,64},{96,80},{112,96},{1... | collective-permute-start | bytes 835592 | tf_op jit(solution)/shard_map/ppermute | solution.py:388
  15.9 0.9 collective-permute-start
  16.8 4.5 %collective-permute-done.1.refs_1_ = bf16[8,136,128]{2,1,0:T(8,128)(2,1)S(1)} collective-permute-done((bf16[8,136,128]{2,1,0:T(8,128)(2,1)S(1)}, bf16[8,136,128]{2,1,0:T(8,128)(2,1)S(1)}, u32[]{:S(2)}, u32[]{:S(2)}) %collective-permute-start.1) | collective-permute-done | bytes 278560 | tf_op jit(solution)/shard_map/ppermute | solution.py:388
  21.6 3.2 %collective-permute-start.2 = (bf16[8,136,128]{2,1,0:T(8,128)(2,1)S(1)}, bf16[8,136,128]{2,1,0:T(8,128)(2,1)S(1)}, u32[]{:S(2)}, u32[]{:S(2)}) collective-permute-start(bf16[8,136,128]{2,1,0:T(8,128)(2,1)S(1)} %merge.4), channel_id=1, source_target_pairs={{0,48},{16,0},{32,16},{48,32},{64,112},{80,64},{96,80},{112,96},{1... | collective-permute-start | bytes 835592 | tf_op jit(solution)/shard_map/ppermute | solution.py:388
  24.8 2.5 %collective-permute-done.5.refs_2_ = bf16[8,136,128]{2,1,0:T(8,128)(2,1)S(1)} collective-permute-done((bf16[8,136,128]{2,1,0:T(8,128)(2,1)S(1)}, bf16[8,136,128]{2,1,0:T(8,128)(2,1)S(1)}, u32[]{:S(2)}, u32[]{:S(2)}) %collective-permute-start.5) | collective-permute-done | bytes 278560 | tf_op jit(solution)/shard_map/ppermute | solution.py:388
  27.6 3.4 %collective-permute-start.6 = (bf16[2,136,128]{2,1,0:T(8,128)(2,1)S(1)}, bf16[2,136,128]{2,1,0:T(8,128)(2,1)S(1)}, u32[]{:S(2)}, u32[]{:S(2)}) collective-permute-start(bf16[2,136,128]{2,1,0:T(8,128)(2,1)S(1)} %get-tuple-element.31), channel_id=1, source_target_pairs={{0,64},{16,80},{32,96},{48,112},{64,128},{80,144},{96,160},{112,17... | collective-permute-start | bytes 208904 | tf_op jit(solution)/shard_map/ppermute | solution.py:388
  31.0 3.1 %collective-permute-start.8 = (bf16[2,136,128]{2,1,0:T(8,128)(2,1)S(1)}, bf16[2,136,128]{2,1,0:T(8,128)(2,1)S(1)}, u32[]{:S(2)}, u32[]{:S(2)}) collective-permute-start(bf16[2,136,128]{2,1,0:T(8,128)(2,1)S(1)} %get-tuple-element.33), channel_id=1, source_target_pairs={{64,0},{80,16},{96,32},{112,48},{128,64},{144,80},{160,96},{176,11... | collective-permute-start | bytes 208904 | tf_op jit(solution)/shard_map/ppermute | solution.py:388
  34.4 1.9 %collective-permute-done.6.came = bf16[2,136,128]{2,1,0:T(8,128)(2,1)S(1)} collective-permute-done((bf16[2,136,128]{2,1,0:T(8,128)(2,1)S(1)}, bf16[2,136,128]{2,1,0:T(8,128)(2,1)S(1)}, u32[]{:S(2)}, u32[]{:S(2)}) %collective-permute-start.6) | collective-permute-done | bytes 69664 | tf_op jit(solution)/shard_map/ppermute | solution.py:388
  36.6 1.1 %collective-permute-start.7 = (bf16[4,136,128]{2,1,0:T(8,128)(2,1)S(1)}, bf16[4,136,128]{2,1,0:T(8,128)(2,1)S(1)}, u32[]{:S(2)}, u32[]{:S(2)}) collective-permute-start(bf16[4,136,128]{2,1,0:T(8,128)(2,1)S(1)} %lift.2), channel_id=1, source_target_pairs={{0,64},{16,80},{32,96},{48,112},{64,128},{80,144},{96,160},{112,17... | collective-permute-start | bytes 417800 | tf_op jit(solution)/shard_map/ppermute | solution.py:388
  38.7 2.5 %collective-permute-start.9 = (bf16[4,136,128]{2,1,0:T(8,128)(2,1)S(1)}, bf16[4,136,128]{2,1,0:T(8,128)(2,1)S(1)}, u32[]{:S(2)}, u32[]{:S(2)}) collective-permute-start(bf16[4,136,128]{2,1,0:T(8,128)(2,1)S(1)} %lift.3), channel_id=1, source_target_pairs={{64,0},{80,16},{96,32},{112,48},{128,64},{144,80},{160,96},{176,11... | collective-permute-start | bytes 417800 | tf_op jit(solution)/shard_map/ppermute | solution.py:388
  42.1 2.4 %collective-permute-done.7.low = bf16[4,136,128]{2,1,0:T(8,128)(2,1)S(1)} collective-permute-done((bf16[4,136,128]{2,1,0:T(8,128)(2,1)S(1)}, bf16[4,136,128]{2,1,0:T(8,128)(2,1)S(1)}, u32[]{:S(2)}, u32[]{:S(2)}) %collective-permute-start.7) | collective-permute-done | bytes 139296 | tf_op jit(solution)/shard_map/ppermute | solution.py:388
  44.5 3.0 %collective-permute-done.9.high = bf16[4,136,128]{2,1,0:T(8,128)(2,1)S(1)} collective-permute-done((bf16[4,136,128]{2,1,0:T(8,128)(2,1)S(1)}, bf16[4,136,128]{2,1,0:T(8,128)(2,1)S(1)}, u32[]{:S(2)}, u32[]{:S(2)}) %collective-permute-start.9) | collective-permute-done | bytes 139296 | tf_op jit(solution)/shard_map/ppermute | solution.py:388
  48.3 6.0 %collective-permute-start.10 = (bf16[8,32,256]{2,1,0:T(8,128)(2,1)S(1)}, bf16[8,32,256]{2,1,0:T(8,128)(2,1)S(1)}, u32[]{:S(2)}, u32[]{:S(2)}) collective-permute-start(bf16[8,32,256]{2,1,0:T(8,128)(2,1)S(1)} %bitcast.15), channel_id=1, source_target_pairs={{0,64},{16,80},{32,96},{48,112},{64,128},{80,144},{96,160},{112,17... | collective-permute-start | bytes 393224 | tf_op jit(solution)/shard_map/ppermute | solution.py:388
  54.4 1.3 %collective-permute-start.11 = (bf16[8,32,256]{2,1,0:T(8,128)(2,1)S(1)}, bf16[8,32,256]{2,1,0:T(8,128)(2,1)S(1)}, u32[]{:S(2)}, u32[]{:S(2)}) collective-permute-start(bf16[8,32,256]{2,1,0:T(8,128)(2,1)S(1)} %bitcast.16), channel_id=1, source_target_pairs={{64,0},{80,16},{96,32},{112,48},{128,64},{144,80},{160,96},{176,11... | collective-permute-start | bytes 393224 | tf_op jit(solution)/shard_map/ppermute | solution.py:388
  55.7 1.2 %collective-permute-done.10 = bf16[8,32,256]{2,1,0:T(8,128)(2,1)S(1)} collective-permute-done((bf16[8,32,256]{2,1,0:T(8,128)(2,1)S(1)}, bf16[8,32,256]{2,1,0:T(8,128)(2,1)S(1)}, u32[]{:S(2)}, u32[]{:S(2)}) %collective-permute-start.10) | collective-permute-done | bytes 131104 | tf_op jit(solution)/shard_map/ppermute | solution.py:388
  56.9 6.0 %collective-permute-done.11 = bf16[8,32,256]{2,1,0:T(8,128)(2,1)S(1)} collective-permute-done((bf16[8,32,256]{2,1,0:T(8,128)(2,1)S(1)}, bf16[8,32,256]{2,1,0:T(8,128)(2,1)S(1)}, u32[]{:S(2)}, u32[]{:S(2)}) %collective-permute-start.11) | collective-permute-done | bytes 131104 | tf_op jit(solution)/shard_map/ppermute | solution.py:388
  62.9 3.4 %collective-permute-start.12 = (bf16[8,4,768]{2,1,0:T(4,128)(2,1)S(1)}, bf16[8,4,768]{2,1,0:T(4,128)(2,1)S(1)}, u32[]{:S(2)}, u32[]{:S(2)}) collective-permute-start(bf16[8,4,768]{2,1,0:T(4,128)(2,1)S(1)} %get-tuple-element.39), channel_id=1, source_target_pairs={{0,16},{16,32},{32,48},{48,1},{1,17},{17,33},{33,49},{49,2},{2,18}... | collective-permute-start | bytes 147464 | tf_op jit(solution)/shard_map/ppermute | solution.py:388
  66.3 1.3 %collective-permute-start.13 = (bf16[8,4,768]{2,1,0:T(4,128)(2,1)S(1)}, bf16[8,4,768]{2,1,0:T(4,128)(2,1)S(1)}, u32[]{:S(2)}, u32[]{:S(2)}) collective-permute-start(bf16[8,4,768]{2,1,0:T(4,128)(2,1)S(1)} %get-tuple-element.40), channel_id=1, source_target_pairs={{16,0},{32,16},{48,32},{1,48},{17,1},{33,17},{49,33},{2,49},{18,2}... | collective-permute-start | bytes 147464 | tf_op jit(solution)/shard_map/ppermute | solution.py:388
  68.0 4.3 %collective-permute-done.13 = bf16[8,4,768]{2,1,0:T(4,128)(2,1)S(1)} collective-permute-done((bf16[8,4,768]{2,1,0:T(4,128)(2,1)S(1)}, bf16[8,4,768]{2,1,0:T(4,128)(2,1)S(1)}, u32[]{:S(2)}, u32[]{:S(2)}) %collective-permute-start.13) | collective-permute-done | bytes 49184 | tf_op jit(solution)/shard_map/ppermute | solution.py:388
  72.5 3.5 %collective-permute-start.14 = (bf16[4,40,768]{2,1,0:T(8,128)(2,1)S(1)}, bf16[4,40,768]{2,1,0:T(8,128)(2,1)S(1)}, u32[]{:S(2)}, u32[]{:S(2)}) collective-permute-start(bf16[4,40,768]{2,1,0:T(8,128)(2,1)S(1)} %get-tuple-element.37), channel_id=1, source_target_pairs={{0,4},{4,8},{8,12},{1,5},{5,9},{9,13},{2,6},{6,10},{10,14},{3,7},{... | collective-permute-start | bytes 737288 | tf_op jit(solution)/shard_map/ppermute | solution.py:388
  76.0 2.4 %collective-permute-start.15 = (bf16[4,40,768]{2,1,0:T(8,128)(2,1)S(1)}, bf16[4,40,768]{2,1,0:T(8,128)(2,1)S(1)}, u32[]{:S(2)}, u32[]{:S(2)}) collective-permute-start(bf16[4,40,768]{2,1,0:T(8,128)(2,1)S(1)} %get-tuple-element.38), channel_id=1, source_target_pairs={{4,0},{8,4},{12,8},{5,1},{9,5},{13,9},{6,2},{10,6},{14,10},{7,3},{... | collective-permute-start | bytes 737288 | tf_op jit(solution)/shard_map/ppermute | solution.py:388
  78.4 2.9 %collective-permute-done.14 = bf16[4,40,768]{2,1,0:T(8,128)(2,1)S(1)} collective-permute-done((bf16[4,40,768]{2,1,0:T(8,128)(2,1)S(1)}, bf16[4,40,768]{2,1,0:T(8,128)(2,1)S(1)}, u32[]{:S(2)}, u32[]{:S(2)}) %collective-permute-start.14) | collective-permute-done | bytes 245792 | tf_op jit(solution)/shard_map/ppermute | solution.py:388
  81.3 3.2 %collective-permute-done.15 = bf16[4,40,768]{2,1,0:T(8,128)(2,1)S(1)} collective-permute-done((bf16[4,40,768]{2,1,0:T(8,128)(2,1)S(1)}, bf16[4,40,768]{2,1,0:T(8,128)(2,1)S(1)}, u32[]{:S(2)}, u32[]{:S(2)}) %collective-permute-start.15) | collective-permute-done | bytes 245792 | tf_op jit(solution)/shard_map/ppermute | solution.py:388
  84.7 8.9 %convolve.1 = bf16[4,64,256]{2,1,0:T(8,128)(2,1)S(1)} custom-call(bf16[768,768]{1,0:T(8,128)(2,1)S(1)} %bitcast.14, bf16[4,3,256,384]{3,2,1,0:T(8,128)(2,1)S(1)} %get-tuple-element.36.band, f32[4,128]{1,0:T(4,128)S(1)} %pad_maximum_fusion.4.bias), custom_call_target="tpu_custom_call" | custom-call | tf_op jit(solution)/shard_map/convolve/pallas_call | solution.py:351
  93.7 3.2 %collective-permute-start.16 = (bf16[64,256]{1,0:T(8,128)(2,1)S(1)}, bf16[64,256]{1,0:T(8,128)(2,1)S(1)}, u32[]{:S(2)}, u32[]{:S(2)}) collective-permute-start(bf16[64,256]{1,0:T(8,128)(2,1)S(1)} %get-tuple-element.43), channel_id=1, source_target_pairs={{0,48},{16,0},{32,16},{48,32},{64,112},{80,64},{96,80},{112,96},{1... | collective-permute-start | bytes 98312 | tf_op jit(solution)/shard_map/ppermute | solution.py:388
  96.8 1.0 collective-permute-start.18
  98.4 3.9 %collective-permute-done.17.far = bf16[64,256]{1,0:T(8,128)(2,1)S(1)} collective-permute-done((bf16[64,256]{1,0:T(8,128)(2,1)S(1)}, bf16[64,256]{1,0:T(8,128)(2,1)S(1)}, u32[]{:S(2)}, u32[]{:S(2)}) %collective-permute-start.17) | collective-permute-done | bytes 32800 | tf_op jit(solution)/shard_map/ppermute | solution.py:388
  102.3 1.1 %place.1 = bf16[512,128]{1,0:T(8,128)(2,1)} custom-call(bf16[64,256]{1,0:T(8,128)(2,1)S(1)} %get-tuple-element.44.own, bf16[64,256]{1,0:T(8,128)(2,1)S(1)} %collective-permute-done.16.high, bf16[64,256]{1,0:T(8,128)(2,1)S(1)} %collective-permute-done.17.far, bf16[64,256]{1,0:T(8,128)(2,1)S(1)} %collective-permute-done.18.low), custom_call_target="tpu_custom_call" | custom-call | tf_op jit(solution)/shard_map/place/pallas_call | solution.py:376
  (32 shorter events, 6.2 us)
Async XLA Ops:
  5.0 10.0 %collective-permute-start.3 = (bf16[8,136,128]{2,1,0:T(8,128)(2,1)S(1)}, bf16[8,136,128]{2,1,0:T(8,128)(2,1)S(1)}, u32[]{:S(2)}, u32[]{:S(2)}) collective-permute-start(bf16[8,136,128]{2,1,0:T(8,128)(2,1)S(1)} %get-tuple-element.28), channel_id=1, source_target_pairs={{0,16},{16,32},{32,48},{48,0},{64,80},{80,96},{96,112},{112,64},{1... | collective-permute-start | bytes 835592 | tf_op jit(solution)/shard_map/ppermute | solution.py:388
  11.7 29.6 %copy-start = (bf16[4,3,3,3,64,64]{5,4,3,2,1,0:T(8,128)(2,1)S(1)}, bf16[4,3,3,3,64,64]{5,4,3,2,1,0:T(8,128)(2,1)}, u32[]{:S(2)}) copy-start(bf16[4,3,3,3,64,64]{5,4,3,2,1,0:T(8,128)(2,1)} %param.16) | copy-start | bytes 2654212
  11.7 29.5 %copy-start.1 = (bf16[64,64]{1,0:T(8,128)(2,1)S(1)}, bf16[64,64]{1,0:T(8,128)(2,1)}, u32[]{:S(2)}) copy-start(bf16[64,64]{1,0:T(8,128)(2,1)} %wv.1) | copy-start | bytes 24580
  11.7 29.5 %copy-start.2 = (bf16[64,64]{1,0:T(8,128)(2,1)S(1)}, bf16[64,64]{1,0:T(8,128)(2,1)}, u32[]{:S(2)}) copy-start(bf16[64,64]{1,0:T(8,128)(2,1)} %wo.1) | copy-start | bytes 24580
  11.7 9.6 %collective-permute-start.1 = (bf16[8,136,128]{2,1,0:T(8,128)(2,1)S(1)}, bf16[8,136,128]{2,1,0:T(8,128)(2,1)S(1)}, u32[]{:S(2)}, u32[]{:S(2)}) collective-permute-start(bf16[8,136,128]{2,1,0:T(8,128)(2,1)S(1)} %get-tuple-element.24), channel_id=1, source_target_pairs={{0,48},{16,0},{32,16},{48,32},{64,112},{80,64},{96,80},{112,96},{1... | collective-permute-start | bytes 835592 | tf_op jit(solution)/shard_map/ppermute | solution.py:388
  13.5 13.7 %collective-permute-start.5 = (bf16[8,136,128]{2,1,0:T(8,128)(2,1)S(1)}, bf16[8,136,128]{2,1,0:T(8,128)(2,1)S(1)}, u32[]{:S(2)}, u32[]{:S(2)}) collective-permute-start(bf16[8,136,128]{2,1,0:T(8,128)(2,1)S(1)} %get-tuple-element.29), channel_id=1, source_target_pairs={{0,48},{16,0},{32,16},{48,32},{64,112},{80,64},{96,80},{112,96},{1... | collective-permute-start | bytes 835592 | tf_op jit(solution)/shard_map/ppermute | solution.py:388
  15.3 11.9 %collective-permute-start.4 = (bf16[8,136,128]{2,1,0:T(8,128)(2,1)S(1)}, bf16[8,136,128]{2,1,0:T(8,128)(2,1)S(1)}, u32[]{:S(2)}, u32[]{:S(2)}) collective-permute-start(bf16[8,136,128]{2,1,0:T(8,128)(2,1)S(1)} %merge.6), channel_id=1, source_target_pairs={{0,16},{16,32},{32,48},{48,0},{64,80},{80,96},{96,112},{112,64},{1... | collective-permute-start | bytes 835592 | tf_op jit(solution)/shard_map/ppermute | solution.py:388
  15.9 18.2 %collective-permute-start = (bf16[8,136,128]{2,1,0:T(8,128)(2,1)S(1)}, bf16[8,136,128]{2,1,0:T(8,128)(2,1)S(1)}, u32[]{:S(2)}, u32[]{:S(2)}) collective-permute-start(bf16[8,136,128]{2,1,0:T(8,128)(2,1)S(1)} %get-tuple-element.22), channel_id=1, source_target_pairs={{0,16},{16,32},{32,48},{48,0},{64,80},{80,96},{96,112},{112,64},{1... | collective-permute-start | bytes 835592 | tf_op jit(solution)/shard_map/ppermute | solution.py:388
  21.6 12.5 %collective-permute-start.2 = (bf16[8,136,128]{2,1,0:T(8,128)(2,1)S(1)}, bf16[8,136,128]{2,1,0:T(8,128)(2,1)S(1)}, u32[]{:S(2)}, u32[]{:S(2)}) collective-permute-start(bf16[8,136,128]{2,1,0:T(8,128)(2,1)S(1)} %merge.4), channel_id=1, source_target_pairs={{0,48},{16,0},{32,16},{48,32},{64,112},{80,64},{96,80},{112,96},{1... | collective-permute-start | bytes 835592 | tf_op jit(solution)/shard_map/ppermute | solution.py:388
  27.6 8.8 %collective-permute-start.6 = (bf16[2,136,128]{2,1,0:T(8,128)(2,1)S(1)}, bf16[2,136,128]{2,1,0:T(8,128)(2,1)S(1)}, u32[]{:S(2)}, u32[]{:S(2)}) collective-permute-start(bf16[2,136,128]{2,1,0:T(8,128)(2,1)S(1)} %get-tuple-element.31), channel_id=1, source_target_pairs={{0,64},{16,80},{32,96},{48,112},{64,128},{80,144},{96,160},{112,17... | collective-permute-start | bytes 208904 | tf_op jit(solution)/shard_map/ppermute | solution.py:388
  31.0 7.5 %collective-permute-start.8 = (bf16[2,136,128]{2,1,0:T(8,128)(2,1)S(1)}, bf16[2,136,128]{2,1,0:T(8,128)(2,1)S(1)}, u32[]{:S(2)}, u32[]{:S(2)}) collective-permute-start(bf16[2,136,128]{2,1,0:T(8,128)(2,1)S(1)} %get-tuple-element.33), channel_id=1, source_target_pairs={{64,0},{80,16},{96,32},{112,48},{128,64},{144,80},{160,96},{176,11... | collective-permute-start | bytes 208904 | tf_op jit(solution)/shard_map/ppermute | solution.py:388
  36.6 7.9 %collective-permute-start.7 = (bf16[4,136,128]{2,1,0:T(8,128)(2,1)S(1)}, bf16[4,136,128]{2,1,0:T(8,128)(2,1)S(1)}, u32[]{:S(2)}, u32[]{:S(2)}) collective-permute-start(bf16[4,136,128]{2,1,0:T(8,128)(2,1)S(1)} %lift.2), channel_id=1, source_target_pairs={{0,64},{16,80},{32,96},{48,112},{64,128},{80,144},{96,160},{112,17... | collective-permute-start | bytes 417800 | tf_op jit(solution)/shard_map/ppermute | solution.py:388
  38.7 8.8 %collective-permute-start.9 = (bf16[4,136,128]{2,1,0:T(8,128)(2,1)S(1)}, bf16[4,136,128]{2,1,0:T(8,128)(2,1)S(1)}, u32[]{:S(2)}, u32[]{:S(2)}) collective-permute-start(bf16[4,136,128]{2,1,0:T(8,128)(2,1)S(1)} %lift.3), channel_id=1, source_target_pairs={{64,0},{80,16},{96,32},{112,48},{128,64},{144,80},{160,96},{176,11... | collective-permute-start | bytes 417800 | tf_op jit(solution)/shard_map/ppermute | solution.py:388
  41.2 37.1 %copy-start.3 = (f32[4,64]{1,0:T(4,128)S(1)}, f32[4,64]{1,0:T(4,128)}, u32[]{:S(2)}) copy-start(f32[4,64]{1,0:T(4,128)} %param.17) | copy-start | bytes 3076
  48.3 8.5 %collective-permute-start.10 = (bf16[8,32,256]{2,1,0:T(8,128)(2,1)S(1)}, bf16[8,32,256]{2,1,0:T(8,128)(2,1)S(1)}, u32[]{:S(2)}, u32[]{:S(2)}) collective-permute-start(bf16[8,32,256]{2,1,0:T(8,128)(2,1)S(1)} %bitcast.15), channel_id=1, source_target_pairs={{0,64},{16,80},{32,96},{48,112},{64,128},{80,144},{96,160},{112,17... | collective-permute-start | bytes 393224 | tf_op jit(solution)/shard_map/ppermute | solution.py:388
  54.4 8.5 %collective-permute-start.11 = (bf16[8,32,256]{2,1,0:T(8,128)(2,1)S(1)}, bf16[8,32,256]{2,1,0:T(8,128)(2,1)S(1)}, u32[]{:S(2)}, u32[]{:S(2)}) collective-permute-start(bf16[8,32,256]{2,1,0:T(8,128)(2,1)S(1)} %bitcast.16), channel_id=1, source_target_pairs={{64,0},{80,16},{96,32},{112,48},{128,64},{144,80},{160,96},{176,11... | collective-permute-start | bytes 393224 | tf_op jit(solution)/shard_map/ppermute | solution.py:388
  62.9 5.1 %collective-permute-start.12 = (bf16[8,4,768]{2,1,0:T(4,128)(2,1)S(1)}, bf16[8,4,768]{2,1,0:T(4,128)(2,1)S(1)}, u32[]{:S(2)}, u32[]{:S(2)}) collective-permute-start(bf16[8,4,768]{2,1,0:T(4,128)(2,1)S(1)} %get-tuple-element.39), channel_id=1, source_target_pairs={{0,16},{16,32},{32,48},{48,1},{1,17},{17,33},{33,49},{49,2},{2,18}... | collective-permute-start | bytes 147464 | tf_op jit(solution)/shard_map/ppermute | solution.py:388
  66.3 6.0 %collective-permute-start.13 = (bf16[8,4,768]{2,1,0:T(4,128)(2,1)S(1)}, bf16[8,4,768]{2,1,0:T(4,128)(2,1)S(1)}, u32[]{:S(2)}, u32[]{:S(2)}) collective-permute-start(bf16[8,4,768]{2,1,0:T(4,128)(2,1)S(1)} %get-tuple-element.40), channel_id=1, source_target_pairs={{16,0},{32,16},{48,32},{1,48},{17,1},{33,17},{49,33},{2,49},{18,2}... | collective-permute-start | bytes 147464 | tf_op jit(solution)/shard_map/ppermute | solution.py:388
  72.5 8.8 %collective-permute-start.14 = (bf16[4,40,768]{2,1,0:T(8,128)(2,1)S(1)}, bf16[4,40,768]{2,1,0:T(8,128)(2,1)S(1)}, u32[]{:S(2)}, u32[]{:S(2)}) collective-permute-start(bf16[4,40,768]{2,1,0:T(8,128)(2,1)S(1)} %get-tuple-element.37), channel_id=1, source_target_pairs={{0,4},{4,8},{8,12},{1,5},{5,9},{9,13},{2,6},{6,10},{10,14},{3,7},{... | collective-permute-start | bytes 737288 | tf_op jit(solution)/shard_map/ppermute | solution.py:388
  76.0 8.5 %collective-permute-start.15 = (bf16[4,40,768]{2,1,0:T(8,128)(2,1)S(1)}, bf16[4,40,768]{2,1,0:T(8,128)(2,1)S(1)}, u32[]{:S(2)}, u32[]{:S(2)}) collective-permute-start(bf16[4,40,768]{2,1,0:T(8,128)(2,1)S(1)} %get-tuple-element.38), channel_id=1, source_target_pairs={{4,0},{8,4},{12,8},{5,1},{9,5},{13,9},{6,2},{10,6},{14,10},{7,3},{... | collective-permute-start | bytes 737288 | tf_op jit(solution)/shard_map/ppermute | solution.py:388
  93.7 4.8 %collective-permute-start.16 = (bf16[64,256]{1,0:T(8,128)(2,1)S(1)}, bf16[64,256]{1,0:T(8,128)(2,1)S(1)}, u32[]{:S(2)}, u32[]{:S(2)}) collective-permute-start(bf16[64,256]{1,0:T(8,128)(2,1)S(1)} %get-tuple-element.43), channel_id=1, source_target_pairs={{0,48},{16,0},{32,16},{48,32},{64,112},{80,64},{96,80},{112,96},{1... | collective-permute-start | bytes 98312 | tf_op jit(solution)/shard_map/ppermute | solution.py:388
  96.8 5.5 %collective-permute-start.17 = (bf16[64,256]{1,0:T(8,128)(2,1)S(1)}, bf16[64,256]{1,0:T(8,128)(2,1)S(1)}, u32[]{:S(2)}, u32[]{:S(2)}) collective-permute-start(bf16[64,256]{1,0:T(8,128)(2,1)S(1)} %get-tuple-element.42), channel_id=1, source_target_pairs={{0,32},{16,48},{32,0},{48,16},{64,96},{80,112},{96,64},{112,80},{1... | collective-permute-start | bytes 98312 | tf_op jit(solution)/shard_map/ppermute | solution.py:388
  96.8 5.5 %collective-permute-start.18 = (bf16[64,256]{1,0:T(8,128)(2,1)S(1)}, bf16[64,256]{1,0:T(8,128)(2,1)S(1)}, u32[]{:S(2)}, u32[]{:S(2)}) collective-permute-start(bf16[64,256]{1,0:T(8,128)(2,1)S(1)} %get-tuple-element.41), channel_id=1, source_target_pairs={{0,16},{16,32},{32,48},{48,0},{64,80},{80,96},{96,112},{112,64},{1... | collective-permute-start | bytes 98312 | tf_op jit(solution)/shard_map/ppermute | solution.py:388

commit v5 on v4

--- a/solution.py
+++ b/solution.py
@@ -320,13 +320,11 @@
         first = stride * (layer + 1)
         n = stride * (14 - 2 * layer)
 
-        def pair(t, carry, src=src, dst=dst, layer=layer, first=first, n=n):
-            lanes_in = pl.ds(pl.multiple_of(128 * t, 128), 256)
-            lanes_out = pl.ds(pl.multiple_of(128 * t, 128), 128)
+        for t in range(5 - layer):
             acc = None
             for b in range(3):
                 rows = slice(first + stride * (b - 1), first + stride * (b - 1) + n)
-                term = dot(src[rows, lanes_in], band[layer, b])
+                term = dot(src[rows, 128 * t : 128 * t + 256], band[layer, b])
                 acc = term if acc is None else acc + term
             h = acc[:, 128:256] + bias[layer : layer + 1, :]
             h = h + pltpu.roll(acc[:, 0:128], 1, 0) + pltpu.roll(acc[:, 256:384], n - 1, 0)
@@ -339,12 +337,9 @@
             else:
                 z = z0 - halo + layer + 1 + 2 * t + lane // 64
                 ok = jnp.where((z >= 0) & (z < 16), 1.0, 0.0) * mask[first : first + n, :]
-                dst[first : first + n, lanes_out] = jnp.where(
+                dst[first : first + n, 128 * t : 128 * t + 128] = jnp.where(
                     ok > 0, jnp.maximum(h, 0.0), 0.0
                 ).astype(bf16)
-            return carry
-
-        lax.fori_loop(0, 5 - layer, pair, 0)
 
 
 def convolve(block, band, bias):
@@ -386,6 +381,10 @@
 
 def send(v, way, axis="frame"):
     return lax.ppermute(v, axis, way)
+
+
+def only(inside, v):
+    return jnp.where(inside, v, jnp.zeros_like(v))
 
 
 def joined(features, voxel_embed, visible, w_query, w_key, w_value, w_out, conv_weight, conv_bias):
@@ -414,24 +413,26 @@
     high = send(lift(2, z3, from_high), z_down)
     hidden = finish(z0, low, high, wide_v, wide_o).reshape(8, 32, 256)
 
-    z_next = [(i, i + 4) for i in range(12)]
-    z_prev = [(j, i) for i, j in z_next]
-    below = send(hidden, z_next)
-    above = send(hidden, z_prev)
+    me = lax.axis_index("frame")
+    zh, xi = me // 4, me % 4
+    below = only(zh > 0, send(hidden, z_up))
+    above = only(zh < 3, send(hidden, z_down))
     hidden = jnp.concatenate([below, hidden, above], axis=2)
 
     def where_is(z, chunk):
         return (4 * z + chunk % 4) * 4 + chunk // 4
 
-    y_next = [(where_is(z, k), where_is(z, k + 1)) for z in range(4) for k in range(15)]
+    y_next = [(where_is(z, k), where_is(z, (k + 1) % 16)) for z in range(4) for k in range(16)]
     y_prev = [(j, i) for i, j in y_next]
-    left = send(hidden[:, -halo:], y_next, ("frame", "by"))
-    right = send(hidden[:, :halo], y_prev, ("frame", "by"))
+    chunk = lax.axis_index("by") * 4 + xi
+    left = only(chunk > 0, send(hidden[:, -halo:], y_next, ("frame", "by")))
+    right = only(chunk < 15, send(hidden[:, :halo], y_prev, ("frame", "by")))
     hidden = jnp.concatenate([left, hidden, right], axis=1)
-    x_next = [(0, 1), (1, 2), (2, 3)]
+    x_next = [(i, (i + 1) % 4) for i in range(4)]
     x_prev = [(j, i) for i, j in x_next]
-    front = send(hidden[-halo:], x_next, "bx")
-    back = send(hidden[:halo], x_prev, "bx")
+    bx = lax.axis_index("bx")
+    front = only(bx > 0, send(hidden[-halo:], x_next, "bx"))
+    back = only(bx < 3, send(hidden[:halo], x_prev, "bx"))
     pad = jnp.zeros((16, stride - 32 - 2 * halo, 768), bf16)
     hidden = jnp.concatenate([jnp.concatenate([front, hidden, back], axis=0), pad], axis=1)
     bias = jnp.concatenate([conv_bias, conv_bias], axis=1)

time: 104 us -> 90.9 us (0.87)
  starting transfers between devices: 41.8 us -> 33.9 us
  waiting for transfers between devices: 37.6 us -> 34.4 us
  Pallas kernels: 23.3 us -> 20.9 us
    ppermute x19, starting transfers between devices: 41.8 us -> 33.9 us  [send(): return lax.ppermute(v, axis, way)]
    ppermute x19, waiting for transfers between devices: 37.6 us -> 34.4 us  [send(): return lax.ppermute(v, axis, way)]
    pallas_call x1, Pallas kernels: 8.94 us -> 6.53 us  [convolve(): pl.pallas_call(conv_kernel, out_shape=jax.ShapeDtypeStruct((4, 64, 256),...]
  transfers between devices with their start and end apart: 19 -> 19, of which waited for: 14 -> 13; matrix products, arithmetic and copies ran while one was open for 0% -> 0% of each run, Pallas kernels for 7% -> 8%
where the time goes in v5:
time: 90.9 us; the launch traced here: 90.8 us
  waiting for transfers between devices  34.4 us (38%)
  starting transfers between devices  33.9 us (37%)
  Pallas kernels  20.9 us (23%)
    ppermute x19, waiting for transfers between devices, send(): return lax.ppermute(v, axis, way)  34.4 us
    ppermute x19, starting transfers between devices, send(): return lax.ppermute(v, axis, way)  33.9 us
    pallas_call x2, Pallas kernels, attend(): pl.pallas_call(functools.partial(attend_kernel, half), out_shape=[jax.Sha...  10.1 us
    pallas_call x1, Pallas kernels, convolve(): pl.pallas_call(conv_kernel, out_shape=jax.ShapeDtypeStruct((4, 64, 256),...  6.53 us
  transfers between devices with their start and end apart: 19, of which 13 were waited for; matrix products, arithmetic and copies ran while one was open for 0% of the time, Pallas kernels for 8%

profile of v5, /device:TPU:8, one launch (start us, length us, event | category | flops | bytes accessed | tf_op | source)
XLA Modules:
  0.0 90.8 jit_solution(18180325641803668666)
XLA Ops:
  0.0 5.0 %attend.3 = (bf16[8,136,128]{2,1,0:T(8,128)(2,1)S(1)}, bf16[8,136,128]{2,1,0:T(8,128)(2,1)S(1)}, bf16[8,136,128]{2,1,0:T(8,128)(2,1)S(1)}, bf16[8,136,128]{2,1,0:T(8,128)(2,1)S(1)}) custom-call(bf16[4,16,512,128]{3,2,1,0:T(8,128)(2,1)} %bitcast.21, bf16[16,512,128]{2,1,0:T(8,128)(2,1)} %bitcast.23, s32[4,16,8,128]{3,2,1,0:T(8,128)} %seen_at.3, ...), custom_call_target="tpu_custom_call" | custom-call | flops 100000000 | bytes 12582912 | tf_op jit(solution)/shard_map/attend/pallas_call | solution.py:132
  5.0 1.6 %collective-permute-start.3 = (bf16[8,136,128]{2,1,0:T(8,128)(2,1)S(1)}, bf16[8,136,128]{2,1,0:T(8,128)(2,1)S(1)}, u32[]{:S(2)}, u32[]{:S(2)}) collective-permute-start(bf16[8,136,128]{2,1,0:T(8,128)(2,1)S(1)} %get-tuple-element.28), channel_id=1, source_target_pairs={{0,16},{16,32},{32,48},{48,0},{64,80},{80,96},{96,112},{112,64},{1... | collective-permute-start | bytes 835592 | tf_op jit(solution)/shard_map/ppermute | solution.py:383
  6.6 5.0 %attend.2 = (bf16[8,136,128]{2,1,0:T(8,128)(2,1)S(1)}, bf16[8,136,128]{2,1,0:T(8,128)(2,1)S(1)}, bf16[8,136,128]{2,1,0:T(8,128)(2,1)S(1)}, bf16[8,136,128]{2,1,0:T(8,128)(2,1)S(1)}) custom-call(bf16[4,16,512,128]{3,2,1,0:T(8,128)(2,1)} %bitcast.22, bf16[16,512,128]{2,1,0:T(8,128)(2,1)} %bitcast.24, s32[4,16,8,128]{3,2,1,0:T(8,128)} %seen_at.3, ...), custom_call_target="tpu_custom_call" | custom-call | flops 100000000 | bytes 12582912 | tf_op jit(solution)/shard_map/attend/pallas_call | solution.py:132
  11.7 1.8 %collective-permute-start.1 = (bf16[8,136,128]{2,1,0:T(8,128)(2,1)S(1)}, bf16[8,136,128]{2,1,0:T(8,128)(2,1)S(1)}, u32[]{:S(2)}, u32[]{:S(2)}) collective-permute-start(bf16[8,136,128]{2,1,0:T(8,128)(2,1)S(1)} %get-tuple-element.24), channel_id=1, source_target_pairs={{0,48},{16,0},{32,16},{48,32},{64,112},{80,64},{96,80},{112,96},{1... | collective-permute-start | bytes 835592 | tf_op jit(solution)/shard_map/ppermute | solution.py:383
  13.5 1.5 %collective-permute-start.5 = (bf16[8,136,128]{2,1,0:T(8,128)(2,1)S(1)}, bf16[8,136,128]{2,1,0:T(8,128)(2,1)S(1)}, u32[]{:S(2)}, u32[]{:S(2)}) collective-permute-start(bf16[8,136,128]{2,1,0:T(8,128)(2,1)S(1)} %get-tuple-element.29), channel_id=1, source_target_pairs={{0,48},{16,0},{32,16},{48,32},{64,112},{80,64},{96,80},{112,96},{1... | collective-permute-start | bytes 835592 | tf_op jit(solution)/shard_map/ppermute | solution.py:383
  15.9 0.9 %collective-permute-start = (bf16[8,136,128]{2,1,0:T(8,128)(2,1)S(1)}, bf16[8,136,128]{2,1,0:T(8,128)(2,1)S(1)}, u32[]{:S(2)}, u32[]{:S(2)}) collective-permute-start(bf16[8,136,128]{2,1,0:T(8,128)(2,1)S(1)} %get-tuple-element.22), channel_id=1, source_target_pairs={{0,16},{16,32},{32,48},{48,0},{64,80},{80,96},{96,112},{112,64},{1... | collective-permute-start | bytes 835592 | tf_op jit(solution)/shard_map/ppermute | solution.py:383
  16.8 4.5 %collective-permute-done.1.refs_1_ = bf16[8,136,128]{2,1,0:T(8,128)(2,1)S(1)} collective-permute-done((bf16[8,136,128]{2,1,0:T(8,128)(2,1)S(1)}, bf16[8,136,128]{2,1,0:T(8,128)(2,1)S(1)}, u32[]{:S(2)}, u32[]{:S(2)}) %collective-permute-start.1) | collective-permute-done | bytes 278560 | tf_op jit(solution)/shard_map/ppermute | solution.py:383
  21.6 3.2 %collective-permute-start.2 = (bf16[8,136,128]{2,1,0:T(8,128)(2,1)S(1)}, bf16[8,136,128]{2,1,0:T(8,128)(2,1)S(1)}, u32[]{:S(2)}, u32[]{:S(2)}) collective-permute-start(bf16[8,136,128]{2,1,0:T(8,128)(2,1)S(1)} %merge.4), channel_id=1, source_target_pairs={{0,48},{16,0},{32,16},{48,32},{64,112},{80,64},{96,80},{112,96},{1... | collective-permute-start | bytes 835592 | tf_op jit(solution)/shard_map/ppermute | solution.py:383
  24.8 2.5 %collective-permute-done.5.refs_2_ = bf16[8,136,128]{2,1,0:T(8,128)(2,1)S(1)} collective-permute-done((bf16[8,136,128]{2,1,0:T(8,128)(2,1)S(1)}, bf16[8,136,128]{2,1,0:T(8,128)(2,1)S(1)}, u32[]{:S(2)}, u32[]{:S(2)}) %collective-permute-start.5) | collective-permute-done | bytes 278560 | tf_op jit(solution)/shard_map/ppermute | solution.py:383
  27.6 3.4 %collective-permute-start.6 = (bf16[2,136,128]{2,1,0:T(8,128)(2,1)S(1)}, bf16[2,136,128]{2,1,0:T(8,128)(2,1)S(1)}, u32[]{:S(2)}, u32[]{:S(2)}) collective-permute-start(bf16[2,136,128]{2,1,0:T(8,128)(2,1)S(1)} %get-tuple-element.31), channel_id=1, source_target_pairs={{0,64},{16,80},{32,96},{48,112},{64,128},{80,144},{96,160},{112,17... | collective-permute-start | bytes 208904 | tf_op jit(solution)/shard_map/ppermute | solution.py:383
  31.0 3.1 %collective-permute-start.8 = (bf16[2,136,128]{2,1,0:T(8,128)(2,1)S(1)}, bf16[2,136,128]{2,1,0:T(8,128)(2,1)S(1)}, u32[]{:S(2)}, u32[]{:S(2)}) collective-permute-start(bf16[2,136,128]{2,1,0:T(8,128)(2,1)S(1)} %get-tuple-element.33), channel_id=1, source_target_pairs={{64,0},{80,16},{96,32},{112,48},{128,64},{144,80},{160,96},{176,11... | collective-permute-start | bytes 208904 | tf_op jit(solution)/shard_map/ppermute | solution.py:383
  34.4 1.9 %collective-permute-done.6.came = bf16[2,136,128]{2,1,0:T(8,128)(2,1)S(1)} collective-permute-done((bf16[2,136,128]{2,1,0:T(8,128)(2,1)S(1)}, bf16[2,136,128]{2,1,0:T(8,128)(2,1)S(1)}, u32[]{:S(2)}, u32[]{:S(2)}) %collective-permute-start.6) | collective-permute-done | bytes 69664 | tf_op jit(solution)/shard_map/ppermute | solution.py:383
  36.6 1.1 %collective-permute-start.7 = (bf16[4,136,128]{2,1,0:T(8,128)(2,1)S(1)}, bf16[4,136,128]{2,1,0:T(8,128)(2,1)S(1)}, u32[]{:S(2)}, u32[]{:S(2)}) collective-permute-start(bf16[4,136,128]{2,1,0:T(8,128)(2,1)S(1)} %lift.2), channel_id=1, source_target_pairs={{0,64},{16,80},{32,96},{48,112},{64,128},{80,144},{96,160},{112,17... | collective-permute-start | bytes 417800 | tf_op jit(solution)/shard_map/ppermute | solution.py:383
  37.7 0.8 collective-permute-done.8.came
  38.7 2.5 %collective-permute-start.9 = (bf16[4,136,128]{2,1,0:T(8,128)(2,1)S(1)}, bf16[4,136,128]{2,1,0:T(8,128)(2,1)S(1)}, u32[]{:S(2)}, u32[]{:S(2)}) collective-permute-start(bf16[4,136,128]{2,1,0:T(8,128)(2,1)S(1)} %lift.3), channel_id=1, source_target_pairs={{64,0},{80,16},{96,32},{112,48},{128,64},{144,80},{160,96},{176,11... | collective-permute-start | bytes 417800 | tf_op jit(solution)/shard_map/ppermute | solution.py:383
  41.2 0.9 weights.1
  42.1 2.4 %collective-permute-done.7.low = bf16[4,136,128]{2,1,0:T(8,128)(2,1)S(1)} collective-permute-done((bf16[4,136,128]{2,1,0:T(8,128)(2,1)S(1)}, bf16[4,136,128]{2,1,0:T(8,128)(2,1)S(1)}, u32[]{:S(2)}, u32[]{:S(2)}) %collective-permute-start.7) | collective-permute-done | bytes 139296 | tf_op jit(solution)/shard_map/ppermute | solution.py:383
  44.5 3.0 %collective-permute-done.9.high = bf16[4,136,128]{2,1,0:T(8,128)(2,1)S(1)} collective-permute-done((bf16[4,136,128]{2,1,0:T(8,128)(2,1)S(1)}, bf16[4,136,128]{2,1,0:T(8,128)(2,1)S(1)}, u32[]{:S(2)}, u32[]{:S(2)}) %collective-permute-start.9) | collective-permute-done | bytes 139296 | tf_op jit(solution)/shard_map/ppermute | solution.py:383
  48.3 4.3 %collective-permute-start.10 = (bf16[8,32,256]{2,1,0:T(8,128)(2,1)S(1)}, bf16[8,32,256]{2,1,0:T(8,128)(2,1)S(1)}, u32[]{:S(2)}, u32[]{:S(2)}) collective-permute-start(bf16[8,32,256]{2,1,0:T(8,128)(2,1)S(1)} %bitcast.15), channel_id=1, source_target_pairs={{0,64},{16,80},{32,96},{48,112},{64,128},{80,144},{96,160},{112,17... | collective-permute-start | bytes 393224 | tf_op jit(solution)/shard_map/ppermute | solution.py:383
  52.6 4.3 %collective-permute-done.10 = bf16[8,32,256]{2,1,0:T(8,128)(2,1)S(1)} collective-permute-done((bf16[8,32,256]{2,1,0:T(8,128)(2,1)S(1)}, bf16[8,32,256]{2,1,0:T(8,128)(2,1)S(1)}, u32[]{:S(2)}, u32[]{:S(2)}) %collective-permute-start.10) | collective-permute-done | bytes 131104 | tf_op jit(solution)/shard_map/ppermute | solution.py:383
  56.9 2.2 %collective-permute-done.11 = bf16[8,32,256]{2,1,0:T(8,128)(2,1)S(1)} collective-permute-done((bf16[8,32,256]{2,1,0:T(8,128)(2,1)S(1)}, bf16[8,32,256]{2,1,0:T(8,128)(2,1)S(1)}, u32[]{:S(2)}, u32[]{:S(2)}) %collective-permute-start.11) | collective-permute-done | bytes 131104 | tf_op jit(solution)/shard_map/ppermute | solution.py:383
  59.2 1.6 %collective-permute-start.12 = (bf16[8,4,768]{2,1,0:T(4,128)(2,1)S(1)}, bf16[8,4,768]{2,1,0:T(4,128)(2,1)S(1)}, u32[]{:S(2)}, u32[]{:S(2)}) collective-permute-start(bf16[8,4,768]{2,1,0:T(4,128)(2,1)S(1)} %get-tuple-element.39), channel_id=1, source_target_pairs={{0,16},{16,32},{32,48},{48,1},{1,17},{17,33},{33,49},{49,2},{2,18}... | collective-permute-start | bytes 147464 | tf_op jit(solution)/shard_map/ppermute | solution.py:383
  60.8 2.4 %collective-permute-start.13 = (bf16[8,4,768]{2,1,0:T(4,128)(2,1)S(1)}, bf16[8,4,768]{2,1,0:T(4,128)(2,1)S(1)}, u32[]{:S(2)}, u32[]{:S(2)}) collective-permute-start(bf16[8,4,768]{2,1,0:T(4,128)(2,1)S(1)} %get-tuple-element.40), channel_id=1, source_target_pairs={{16,0},{32,16},{48,32},{1,48},{17,1},{33,17},{49,33},{2,49},{18,2}... | collective-permute-start | bytes 147464 | tf_op jit(solution)/shard_map/ppermute | solution.py:383
  63.1 1.8 %collective-permute-done.12 = bf16[8,4,768]{2,1,0:T(4,128)(2,1)S(1)} collective-permute-done((bf16[8,4,768]{2,1,0:T(4,128)(2,1)S(1)}, bf16[8,4,768]{2,1,0:T(4,128)(2,1)S(1)}, u32[]{:S(2)}, u32[]{:S(2)}) %collective-permute-start.12) | collective-permute-done | bytes 49184 | tf_op jit(solution)/shard_map/ppermute | solution.py:383
  65.9 1.6 %collective-permute-start.14 = (bf16[4,40,768]{2,1,0:T(8,128)(2,1)}, bf16[4,40,768]{2,1,0:T(8,128)(2,1)S(1)}, u32[]{:S(2)}, u32[]{:S(2)}) collective-permute-start(bf16[4,40,768]{2,1,0:T(8,128)(2,1)} %get-tuple-element.37), channel_id=1, source_target_pairs={{0,4},{4,8},{8,12},{12,0},{1,5},{5,9},{9,13},{13,1},{2,6},{6,10},{... | collective-permute-start | bytes 737288 | tf_op jit(solution)/shard_map/ppermute | solution.py:383
  68.1 5.2 %collective-permute-done.14 = bf16[4,40,768]{2,1,0:T(8,128)(2,1)S(1)} collective-permute-done((bf16[4,40,768]{2,1,0:T(8,128)(2,1)}, bf16[4,40,768]{2,1,0:T(8,128)(2,1)S(1)}, u32[]{:S(2)}, u32[]{:S(2)}) %collective-permute-start.14) | collective-permute-done | bytes 245792 | tf_op jit(solution)/shard_map/ppermute | solution.py:383
  73.3 1.3 %collective-permute-done.15 = bf16[4,40,768]{2,1,0:T(8,128)(2,1)S(1)} collective-permute-done((bf16[4,40,768]{2,1,0:T(8,128)(2,1)}, bf16[4,40,768]{2,1,0:T(8,128)(2,1)S(1)}, u32[]{:S(2)}, u32[]{:S(2)}) %collective-permute-start.15) | collective-permute-done | bytes 245792 | tf_op jit(solution)/shard_map/ppermute | solution.py:383
  74.8 6.5 %convolve.1 = bf16[4,64,256]{2,1,0:T(8,128)(2,1)S(1)} custom-call(bf16[768,768]{1,0:T(8,128)(2,1)S(1)} %bitcast.14, bf16[4,3,256,384]{3,2,1,0:T(8,128)(2,1)S(1)} %get-tuple-element.36.band, f32[4,128]{1,0:T(4,128)S(1)} %pad_maximum_fusion.4.bias), custom_call_target="tpu_custom_call" | custom-call | tf_op jit(solution)/shard_map/convolve/pallas_call | solution.py:346
  81.3 2.9 %collective-permute-start.16 = (bf16[64,256]{1,0:T(8,128)(2,1)S(1)}, bf16[64,256]{1,0:T(8,128)(2,1)S(1)}, u32[]{:S(2)}, u32[]{:S(2)}) collective-permute-start(bf16[64,256]{1,0:T(8,128)(2,1)S(1)} %get-tuple-element.43), channel_id=1, source_target_pairs={{0,48},{16,0},{32,16},{48,32},{64,112},{80,64},{96,80},{112,96},{1... | collective-permute-start | bytes 98312 | tf_op jit(solution)/shard_map/ppermute | solution.py:383
  84.2 1.0 %collective-permute-start.18 = (bf16[64,256]{1,0:T(8,128)(2,1)S(1)}, bf16[64,256]{1,0:T(8,128)(2,1)S(1)}, u32[]{:S(2)}, u32[]{:S(2)}) collective-permute-start(bf16[64,256]{1,0:T(8,128)(2,1)S(1)} %get-tuple-element.41), channel_id=1, source_target_pairs={{0,16},{16,32},{32,48},{48,0},{64,80},{80,96},{96,112},{112,64},{1... | collective-permute-start | bytes 98312 | tf_op jit(solution)/shard_map/ppermute | solution.py:383
  85.8 3.9 %collective-permute-done.17.far = bf16[64,256]{1,0:T(8,128)(2,1)S(1)} collective-permute-done((bf16[64,256]{1,0:T(8,128)(2,1)S(1)}, bf16[64,256]{1,0:T(8,128)(2,1)S(1)}, u32[]{:S(2)}, u32[]{:S(2)}) %collective-permute-start.17) | collective-permute-done | bytes 32800 | tf_op jit(solution)/shard_map/ppermute | solution.py:383
  89.7 1.1 %place.1 = bf16[512,128]{1,0:T(8,128)(2,1)} custom-call(bf16[64,256]{1,0:T(8,128)(2,1)S(1)} %get-tuple-element.44.own, bf16[64,256]{1,0:T(8,128)(2,1)S(1)} %collective-permute-done.16.high, bf16[64,256]{1,0:T(8,128)(2,1)S(1)} %collective-permute-done.17.far, bf16[64,256]{1,0:T(8,128)(2,1)S(1)} %collective-permute-done.18.low), custom_call_target="tpu_custom_call" | custom-call | tf_op jit(solution)/shard_map/place/pallas_call | solution.py:371
  (38 shorter events, 5.5 us)
Async XLA Ops:
  5.0 10.0 %collective-permute-start.3 = (bf16[8,136,128]{2,1,0:T(8,128)(2,1)S(1)}, bf16[8,136,128]{2,1,0:T(8,128)(2,1)S(1)}, u32[]{:S(2)}, u32[]{:S(2)}) collective-permute-start(bf16[8,136,128]{2,1,0:T(8,128)(2,1)S(1)} %get-tuple-element.28), channel_id=1, source_target_pairs={{0,16},{16,32},{32,48},{48,0},{64,80},{80,96},{96,112},{112,64},{1... | collective-permute-start | bytes 835592 | tf_op jit(solution)/shard_map/ppermute | solution.py:383
  11.7 29.6 %copy-start = (bf16[4,3,3,3,64,64]{5,4,3,2,1,0:T(8,128)(2,1)S(1)}, bf16[4,3,3,3,64,64]{5,4,3,2,1,0:T(8,128)(2,1)}, u32[]{:S(2)}) copy-start(bf16[4,3,3,3,64,64]{5,4,3,2,1,0:T(8,128)(2,1)} %param.16) | copy-start | bytes 2654212
  11.7 29.5 %copy-start.1 = (bf16[64,64]{1,0:T(8,128)(2,1)S(1)}, bf16[64,64]{1,0:T(8,128)(2,1)}, u32[]{:S(2)}) copy-start(bf16[64,64]{1,0:T(8,128)(2,1)} %wv.1) | copy-start | bytes 24580
  11.7 29.5 %copy-start.2 = (bf16[64,64]{1,0:T(8,128)(2,1)S(1)}, bf16[64,64]{1,0:T(8,128)(2,1)}, u32[]{:S(2)}) copy-start(bf16[64,64]{1,0:T(8,128)(2,1)} %wo.1) | copy-start | bytes 24580
  11.7 9.6 %collective-permute-start.1 = (bf16[8,136,128]{2,1,0:T(8,128)(2,1)S(1)}, bf16[8,136,128]{2,1,0:T(8,128)(2,1)S(1)}, u32[]{:S(2)}, u32[]{:S(2)}) collective-permute-start(bf16[8,136,128]{2,1,0:T(8,128)(2,1)S(1)} %get-tuple-element.24), channel_id=1, source_target_pairs={{0,48},{16,0},{32,16},{48,32},{64,112},{80,64},{96,80},{112,96},{1... | collective-permute-start | bytes 835592 | tf_op jit(solution)/shard_map/ppermute | solution.py:383
  13.5 13.7 %collective-permute-start.5 = (bf16[8,136,128]{2,1,0:T(8,128)(2,1)S(1)}, bf16[8,136,128]{2,1,0:T(8,128)(2,1)S(1)}, u32[]{:S(2)}, u32[]{:S(2)}) collective-permute-start(bf16[8,136,128]{2,1,0:T(8,128)(2,1)S(1)} %get-tuple-element.29), channel_id=1, source_target_pairs={{0,48},{16,0},{32,16},{48,32},{64,112},{80,64},{96,80},{112,96},{1... | collective-permute-start | bytes 835592 | tf_op jit(solution)/shard_map/ppermute | solution.py:383
  15.3 11.9 %collective-permute-start.4 = (bf16[8,136,128]{2,1,0:T(8,128)(2,1)S(1)}, bf16[8,136,128]{2,1,0:T(8,128)(2,1)S(1)}, u32[]{:S(2)}, u32[]{:S(2)}) collective-permute-start(bf16[8,136,128]{2,1,0:T(8,128)(2,1)S(1)} %merge.6), channel_id=1, source_target_pairs={{0,16},{16,32},{32,48},{48,0},{64,80},{80,96},{96,112},{112,64},{1... | collective-permute-start | bytes 835592 | tf_op jit(solution)/shard_map/ppermute | solution.py:383
  15.9 18.2 %collective-permute-start = (bf16[8,136,128]{2,1,0:T(8,128)(2,1)S(1)}, bf16[8,136,128]{2,1,0:T(8,128)(2,1)S(1)}, u32[]{:S(2)}, u32[]{:S(2)}) collective-permute-start(bf16[8,136,128]{2,1,0:T(8,128)(2,1)S(1)} %get-tuple-element.22), channel_id=1, source_target_pairs={{0,16},{16,32},{32,48},{48,0},{64,80},{80,96},{96,112},{112,64},{1... | collective-permute-start | bytes 835592 | tf_op jit(solution)/shard_map/ppermute | solution.py:383
  21.6 12.5 %collective-permute-start.2 = (bf16[8,136,128]{2,1,0:T(8,128)(2,1)S(1)}, bf16[8,136,128]{2,1,0:T(8,128)(2,1)S(1)}, u32[]{:S(2)}, u32[]{:S(2)}) collective-permute-start(bf16[8,136,128]{2,1,0:T(8,128)(2,1)S(1)} %merge.4), channel_id=1, source_target_pairs={{0,48},{16,0},{32,16},{48,32},{64,112},{80,64},{96,80},{112,96},{1... | collective-permute-start | bytes 835592 | tf_op jit(solution)/shard_map/ppermute | solution.py:383
  27.6 8.8 %collective-permute-start.6 = (bf16[2,136,128]{2,1,0:T(8,128)(2,1)S(1)}, bf16[2,136,128]{2,1,0:T(8,128)(2,1)S(1)}, u32[]{:S(2)}, u32[]{:S(2)}) collective-permute-start(bf16[2,136,128]{2,1,0:T(8,128)(2,1)S(1)} %get-tuple-element.31), channel_id=1, source_target_pairs={{0,64},{16,80},{32,96},{48,112},{64,128},{80,144},{96,160},{112,17... | collective-permute-start | bytes 208904 | tf_op jit(solution)/shard_map/ppermute | solution.py:383
  31.0 7.5 %collective-permute-start.8 = (bf16[2,136,128]{2,1,0:T(8,128)(2,1)S(1)}, bf16[2,136,128]{2,1,0:T(8,128)(2,1)S(1)}, u32[]{:S(2)}, u32[]{:S(2)}) collective-permute-start(bf16[2,136,128]{2,1,0:T(8,128)(2,1)S(1)} %get-tuple-element.33), channel_id=1, source_target_pairs={{64,0},{80,16},{96,32},{112,48},{128,64},{144,80},{160,96},{176,11... | collective-permute-start | bytes 208904 | tf_op jit(solution)/shard_map/ppermute | solution.py:383
  36.6 7.9 %collective-permute-start.7 = (bf16[4,136,128]{2,1,0:T(8,128)(2,1)S(1)}, bf16[4,136,128]{2,1,0:T(8,128)(2,1)S(1)}, u32[]{:S(2)}, u32[]{:S(2)}) collective-permute-start(bf16[4,136,128]{2,1,0:T(8,128)(2,1)S(1)} %lift.2), channel_id=1, source_target_pairs={{0,64},{16,80},{32,96},{48,112},{64,128},{80,144},{96,160},{112,17... | collective-permute-start | bytes 417800 | tf_op jit(solution)/shard_map/ppermute | solution.py:383
  38.7 8.8 %collective-permute-start.9 = (bf16[4,136,128]{2,1,0:T(8,128)(2,1)S(1)}, bf16[4,136,128]{2,1,0:T(8,128)(2,1)S(1)}, u32[]{:S(2)}, u32[]{:S(2)}) collective-permute-start(bf16[4,136,128]{2,1,0:T(8,128)(2,1)S(1)} %lift.3), channel_id=1, source_target_pairs={{64,0},{80,16},{96,32},{112,48},{128,64},{144,80},{160,96},{176,11... | collective-permute-start | bytes 417800 | tf_op jit(solution)/shard_map/ppermute | solution.py:383
  42.1 25.9 %copy-start.3 = (f32[4,64]{1,0:T(4,128)S(1)}, f32[4,64]{1,0:T(4,128)}, u32[]{:S(2)}) copy-start(f32[4,64]{1,0:T(4,128)} %param.17) | copy-start | bytes 3076
  48.3 8.6 %collective-permute-start.10 = (bf16[8,32,256]{2,1,0:T(8,128)(2,1)S(1)}, bf16[8,32,256]{2,1,0:T(8,128)(2,1)S(1)}, u32[]{:S(2)}, u32[]{:S(2)}) collective-permute-start(bf16[8,32,256]{2,1,0:T(8,128)(2,1)S(1)} %bitcast.15), channel_id=1, source_target_pairs={{0,64},{16,80},{32,96},{48,112},{64,128},{80,144},{96,160},{112,17... | collective-permute-start | bytes 393224 | tf_op jit(solution)/shard_map/ppermute | solution.py:383
  52.6 6.5 %collective-permute-start.11 = (bf16[8,32,256]{2,1,0:T(8,128)(2,1)S(1)}, bf16[8,32,256]{2,1,0:T(8,128)(2,1)S(1)}, u32[]{:S(2)}, u32[]{:S(2)}) collective-permute-start(bf16[8,32,256]{2,1,0:T(8,128)(2,1)S(1)} %bitcast.16), channel_id=1, source_target_pairs={{64,0},{80,16},{96,32},{112,48},{128,64},{144,80},{160,96},{176,11... | collective-permute-start | bytes 393224 | tf_op jit(solution)/shard_map/ppermute | solution.py:383
  59.2 5.7 %collective-permute-start.12 = (bf16[8,4,768]{2,1,0:T(4,128)(2,1)S(1)}, bf16[8,4,768]{2,1,0:T(4,128)(2,1)S(1)}, u32[]{:S(2)}, u32[]{:S(2)}) collective-permute-start(bf16[8,4,768]{2,1,0:T(4,128)(2,1)S(1)} %get-tuple-element.39), channel_id=1, source_target_pairs={{0,16},{16,32},{32,48},{48,1},{1,17},{17,33},{33,49},{49,2},{2,18}... | collective-permute-start | bytes 147464 | tf_op jit(solution)/shard_map/ppermute | solution.py:383
  60.8 4.2 %collective-permute-start.13 = (bf16[8,4,768]{2,1,0:T(4,128)(2,1)S(1)}, bf16[8,4,768]{2,1,0:T(4,128)(2,1)S(1)}, u32[]{:S(2)}, u32[]{:S(2)}) collective-permute-start(bf16[8,4,768]{2,1,0:T(4,128)(2,1)S(1)} %get-tuple-element.40), channel_id=1, source_target_pairs={{16,0},{32,16},{48,32},{1,48},{17,1},{33,17},{49,33},{2,49},{18,2}... | collective-permute-start | bytes 147464 | tf_op jit(solution)/shard_map/ppermute | solution.py:383
  65.9 7.3 %collective-permute-start.14 = (bf16[4,40,768]{2,1,0:T(8,128)(2,1)}, bf16[4,40,768]{2,1,0:T(8,128)(2,1)S(1)}, u32[]{:S(2)}, u32[]{:S(2)}) collective-permute-start(bf16[4,40,768]{2,1,0:T(8,128)(2,1)} %get-tuple-element.37), channel_id=1, source_target_pairs={{0,4},{4,8},{8,12},{12,0},{1,5},{5,9},{9,13},{13,1},{2,6},{6,10},{... | collective-permute-start | bytes 737288 | tf_op jit(solution)/shard_map/ppermute | solution.py:383
  67.5 7.0 %collective-permute-start.15 = (bf16[4,40,768]{2,1,0:T(8,128)(2,1)}, bf16[4,40,768]{2,1,0:T(8,128)(2,1)S(1)}, u32[]{:S(2)}, u32[]{:S(2)}) collective-permute-start(bf16[4,40,768]{2,1,0:T(8,128)(2,1)} %get-tuple-element.38), channel_id=1, source_target_pairs={{4,0},{8,4},{12,8},{0,12},{5,1},{9,5},{13,9},{1,13},{6,2},{10,6},{... | collective-permute-start | bytes 737288 | tf_op jit(solution)/shard_map/ppermute | solution.py:383
  81.3 4.5 %collective-permute-start.16 = (bf16[64,256]{1,0:T(8,128)(2,1)S(1)}, bf16[64,256]{1,0:T(8,128)(2,1)S(1)}, u32[]{:S(2)}, u32[]{:S(2)}) collective-permute-start(bf16[64,256]{1,0:T(8,128)(2,1)S(1)} %get-tuple-element.43), channel_id=1, source_target_pairs={{0,48},{16,0},{32,16},{48,32},{64,112},{80,64},{96,80},{112,96},{1... | collective-permute-start | bytes 98312 | tf_op jit(solution)/shard_map/ppermute | solution.py:383
  84.2 5.5 %collective-permute-start.17 = (bf16[64,256]{1,0:T(8,128)(2,1)S(1)}, bf16[64,256]{1,0:T(8,128)(2,1)S(1)}, u32[]{:S(2)}, u32[]{:S(2)}) collective-permute-start(bf16[64,256]{1,0:T(8,128)(2,1)S(1)} %get-tuple-element.42), channel_id=1, source_target_pairs={{0,32},{16,48},{32,0},{48,16},{64,96},{80,112},{96,64},{112,80},{1... | collective-permute-start | bytes 98312 | tf_op jit(solution)/shard_map/ppermute | solution.py:383
  84.2 5.5 %collective-permute-start.18 = (bf16[64,256]{1,0:T(8,128)(2,1)S(1)}, bf16[64,256]{1,0:T(8,128)(2,1)S(1)}, u32[]{:S(2)}, u32[]{:S(2)}) collective-permute-start(bf16[64,256]{1,0:T(8,128)(2,1)S(1)} %get-tuple-element.41), channel_id=1, source_target_pairs={{0,16},{16,32},{32,48},{48,0},{64,80},{80,96},{96,112},{112,64},{1... | collective-permute-start | bytes 98312 | tf_op jit(solution)/shard_map/ppermute | solution.py:383

commit v6 on v5

--- a/solution.py
+++ b/solution.py
@@ -41,7 +41,7 @@
 
 
 def attend_kernel(half, feat_at, embed_at, seen_at, wq_at, wk_at, *refs):
-    outs, feat, embed, seen, wq, wk, key0, key1, sems = refs[:4], *refs[4:]
+    outs, feat, embed, seen, wq, wk, key0, key1, wide0, wide1, sems = refs[:4], *refs[4:]
     steps, frames, n = feat.shape[:3]
     me = lax.axis_index("frame")
     zh, xi = me // 4, me % 4
@@ -74,21 +74,23 @@
         cols = [key[p, pl.ds(i, 64, stride=8), :] for p in range(n) for i in range(8)]
         wide = jnp.concatenate(cols, axis=1).astype(bf16)
         q = lax.dot_general(wq[...], wide, (((0,), (0,)), ((), ())), preferred_element_type=f32)
-        qk = dot(wk[...], q.astype(bf16)) * 0.125
+        qk = dot(wk[...], q.astype(bf16))
         for p in range(n):
             for i in range(8):
                 at = (8 * p + i) * 128
                 key[p, pl.ds(i, 64, stride=8), :] = qk[:, at : at + 128]
 
     def plane(s, p):
-        key = (key0, key1)[s % 2]
+        key, wide = (key0, key1)[s % 2], (wide0, wide1)[p % 2]
         sums = [jnp.zeros((8, 128), f32) for _ in range(frames)]
         for g in range(16):
             rows = slice(32 * g, 32 * g + 32)
             line = key[p, rows, :]
             for f in range(frames):
-                prod = (line * feat[s, f, p, rows, :].astype(f32)).reshape(4, 8, 128)
-                sums[f] = sums[f] + jnp.sum(prod, axis=0)
+                value = feat[s, f, p, rows, :].astype(f32)
+                wide[f, rows, :] = value
+                sums[f] = sums[f] + jnp.sum((line * value).reshape(4, 8, 128), axis=0)
+        sums = [v * 0.125 for v in sums]
         ok = [seen[s, f, p] > 0 for f in range(frames)]
         m = jnp.full((8, 128), absent_score, f32)
         for f in range(frames):
@@ -107,7 +109,7 @@
             rows = slice(32 * g, 32 * g + 32)
             acc = None
             for f in range(frames):
-                term = e[f][None] * feat[s, f, p, rows, :].astype(f32).reshape(4, 8, 128)
+                term = e[f][None] * wide[f, rows, :].reshape(4, 8, 128)
                 acc = term if acc is None else acc + term
             put(g, [acc[i] for i in range(4)])
         put(16, [*three_terms(m), total])
@@ -142,9 +144,11 @@
             pltpu.VMEM((c, c), bf16),
             pltpu.VMEM((n, rows, 128), f32),
             pltpu.VMEM((n, rows, 128), f32),
+            pltpu.VMEM((frames, rows, 128), f32),
+            pltpu.VMEM((frames, rows, 128), f32),
             pltpu.SemaphoreType.DMA((steps + 1, 3)),
         ],
-        compiler_params=pltpu.CompilerParams(vmem_limit_bytes=14 << 20),
+        compiler_params=pltpu.CompilerParams(vmem_limit_bytes=16 << 20),
         cost_estimate=pl.CostEstimate(flops=10**8, bytes_accessed=12 << 20, transcendentals=0),
         name="attend",
     )(*[pltpu.with_memory_space_constraint(v, pltpu.HBM) for v in (feat, embed, visible, w_query, w_key)])
@@ -301,61 +305,106 @@
     )(conv_weight.reshape(layers, 27, 64, 64), w_value, w_out)
 
 
-def conv_kernel(block, band, bias, out, buf0, buf1, mask):
-    layers = band.shape[0]
-    me = lax.axis_index("frame")
-    xi = me % 4
-    x0, z0 = lax.axis_index("bx") * 8, me // 4 * 4
-    y0 = lax.axis_index("by") * 128 + xi * 32
-    y = lax.broadcasted_iota(jnp.int32, (stride, 128), 0) + (y0 - halo)
+def row_mask(mask):
+    xi = lax.axis_index("frame") % 4
+    x0, y0 = lax.axis_index("bx") * 8 - halo, lax.axis_index("by") * 128 + xi * 32 - halo
+    y = lax.broadcasted_iota(jnp.int32, (stride, 128), 0) + y0
     y_ok = (y >= 0) & (y < 512)
     for x in range(16):
-        x_at = x0 - halo + x
-        line = jnp.where(y_ok & (x_at >= 0) & (x_at < 32), 1.0, 0.0)
+        line = jnp.where(y_ok & (x0 + x >= 0) & (x0 + x < 32), 1.0, 0.0)
         mask[stride * x : stride * x + stride, :] = line
+
+
+def pair_rows(src, shift, lines, t, layer, band, bias):
+    acc = None
+    for b in range(3):
+        at = [(stride * (i - shift + b - 1), stride * (j - shift + b - 1)) for i, j in lines]
+        rows = [src[i:j, 128 * t : 128 * t + 256] for i, j in at]
+        rows = rows[0] if len(rows) == 1 else jnp.concatenate(rows, axis=0)
+        term = dot(rows, band[layer, b])
+        acc = term if acc is None else acc + term
+    n = acc.shape[0]
+    h = acc[:, 128:256] + bias[layer : layer + 1, :]
+    return h + pltpu.roll(acc[:, 0:128], 1, 0) + pltpu.roll(acc[:, 256:384], n - 1, 0)
+
+
+def keep(h, dst, shift, lines, t, layer, mask):
+    z0 = lax.axis_index("frame") // 4 * 4 - halo
     lane = lax.broadcasted_iota(jnp.int32, (1, 128), 1)
-    for layer in range(layers):
-        src = (block, buf0, buf1, buf0)[layer]
-        dst = (buf0, buf1, buf0, None)[layer]
-        first = stride * (layer + 1)
-        n = stride * (14 - 2 * layer)
-
+    z = z0 + layer + 1 + 2 * t + lane // 64
+    z_ok = jnp.where((z >= 0) & (z < 16), 1.0, 0.0)
+    at = 0
+    for i, j in lines:
+        n = stride * (j - i)
+        ok = z_ok * mask[stride * i : stride * j, :]
+        part = jnp.where(ok > 0, jnp.maximum(h[at : at + n], 0.0), 0.0)
+        row = stride * (i - shift)
+        dst[row : row + n, 128 * t : 128 * t + 128] = part.astype(bf16)
+        at += n
+
+
+def core_kernel(block, band, bias, out0, out1, out2, mask):
+    row_mask(mask)
+    src, shift = block, 4
+    for layer, dst in enumerate((out0, out1, out2)):
+        lines = [(5 + layer, 11 - layer)]
         for t in range(5 - layer):
-            acc = None
-            for b in range(3):
-                rows = slice(first + stride * (b - 1), first + stride * (b - 1) + n)
-                term = dot(src[rows, 128 * t : 128 * t + 256], band[layer, b])
-                acc = term if acc is None else acc + term
-            h = acc[:, 128:256] + bias[layer : layer + 1, :]
-            h = h + pltpu.roll(acc[:, 0:128], 1, 0) + pltpu.roll(acc[:, 256:384], n - 1, 0)
-            if dst is None:
-                h = pltpu.roll(h, n - halo, 0)
-                tiles = [h[stride * x : stride * x + 32] for x in range(8)]
-                whole = jnp.concatenate(tiles, axis=0).T.astype(bf16)
-                for i in range(2):
-                    out[(2 * t + i - xi) & 3] = whole[64 * i : 64 * i + 64]
-            else:
-                z = z0 - halo + layer + 1 + 2 * t + lane // 64
-                ok = jnp.where((z >= 0) & (z < 16), 1.0, 0.0) * mask[first : first + n, :]
-                dst[first : first + n, 128 * t : 128 * t + 128] = jnp.where(
-                    ok > 0, jnp.maximum(h, 0.0), 0.0
-                ).astype(bf16)
-
-
-def convolve(block, band, bias):
+            h = pair_rows(src, shift, lines, t, layer, band, bias)
+            keep(h, dst, 5 + layer, lines, t, layer, mask)
+        src, shift = dst, 5 + layer
+
+
+def core(block, band, bias):
+    widths = (640, 512, 384)
+    return pl.pallas_call(
+        core_kernel,
+        out_shape=[
+            jax.ShapeDtypeStruct((stride * (6 - 2 * i), w), bf16) for i, w in enumerate(widths)
+        ],
+        in_specs=[VM] * 3,
+        out_specs=[VM] * 3,
+        scratch_shapes=[pltpu.VMEM((16 * stride, 128), f32)],
+        compiler_params=pltpu.CompilerParams(vmem_limit_bytes=8 << 20),
+        cost_estimate=pl.CostEstimate(flops=10**9, bytes_accessed=10**6, transcendentals=0),
+        name="core",
+    )(block, band, bias)
+
+
+def conv_kernel(block, core0, core1, core2, band, bias, out, buf0, buf1, mask):
+    xi = lax.axis_index("frame") % 4
+    row_mask(mask)
+    src = block
+    for layer, (dst, done) in enumerate(((buf0, core0), (buf1, core1), (buf0, core2))):
+        width = done.shape[1]
+        dst[stride * (5 + layer) : stride * (11 - layer), 0:width] = done[...]
+        lines = [(1 + layer, 5 + layer), (11 - layer, 15 - layer)]
+        for t in range(5 - layer):
+            h = pair_rows(src, 0, lines, t, layer, band, bias)
+            keep(h, dst, 0, lines, t, layer, mask)
+        src = dst
+    for t in range(2):
+        h = pair_rows(src, 0, [(4, 12)], t, 3, band, bias)
+        h = pltpu.roll(h, h.shape[0] - halo, 0)
+        tiles = [h[stride * x : stride * x + 32] for x in range(8)]
+        whole = jnp.concatenate(tiles, axis=0).T.astype(bf16)
+        for i in range(2):
+            out[(2 * t + i - xi) & 3] = whole[64 * i : 64 * i + 64]
+
+
+def convolve(block, cores, band, bias):
     return pl.pallas_call(
         conv_kernel,
         out_shape=jax.ShapeDtypeStruct((4, 64, 256), bf16),
-        in_specs=[VM, VM, VM],
+        in_specs=[VM] * 6,
         out_specs=VM,
         scratch_shapes=[
             pltpu.VMEM((16 * stride, 640), bf16),
             pltpu.VMEM((16 * stride, 512), bf16),
             pltpu.VMEM((16 * stride, 128), f32),
         ],
-        compiler_params=pltpu.CompilerParams(vmem_limit_bytes=20 << 20),
+        compiler_params=pltpu.CompilerParams(vmem_limit_bytes=16 << 20),
         name="convolve",
-    )(block, band, bias)
+    )(block, *cores, band, bias)
 
 
 def place_kernel(own, high, far, low, out, rows):
@@ -427,16 +476,24 @@
     chunk = lax.axis_index("by") * 4 + xi
     left = only(chunk > 0, send(hidden[:, -halo:], y_next, ("frame", "by")))
     right = only(chunk < 15, send(hidden[:, :halo], y_prev, ("frame", "by")))
-    hidden = jnp.concatenate([left, hidden, right], axis=1)
+    first, second = (
+        jnp.concatenate([left[i], hidden[i], right[i]], axis=1)
+        for i in (slice(0, halo), slice(halo, None))
+    )
     x_next = [(i, (i + 1) % 4) for i in range(4)]
     x_prev = [(j, i) for i, j in x_next]
     bx = lax.axis_index("bx")
-    front = only(bx > 0, send(hidden[-halo:], x_next, "bx"))
-    back = only(bx < 3, send(hidden[:halo], x_prev, "bx"))
-    pad = jnp.zeros((16, stride - 32 - 2 * halo, 768), bf16)
-    hidden = jnp.concatenate([jnp.concatenate([front, hidden, back], axis=0), pad], axis=1)
+    front = only(bx > 0, send(second, x_next, "bx"))
+    back = only(bx < 3, send(first, x_prev, "bx"))
     bias = jnp.concatenate([conv_bias, conv_bias], axis=1)
-    out = convolve(hidden.reshape(16 * stride, 768), band, bias)
+
+    def lines(*parts):
+        whole = jnp.concatenate(parts, axis=0)
+        pad = jnp.zeros((whole.shape[0], stride - 32 - 2 * halo, 768), bf16)
+        return jnp.concatenate([whole, pad], axis=1).reshape(-1, 768)
+
+    cores = core(lines(first, second), band, bias)
+    out = convolve(lines(front, first, second, back), cores, band, bias)
     low = send(out[1], up)
     high = send(out[3], down)
     far = send(out[2], x_by(2))

time: 90.9 us -> 90.4 us (level)
  the two profiles are of different devices: /device:TPU:8 before, /device:TPU:64 now
where the time goes in v6:
time: 90.4 us; the launch traced here: 90.3 us
  waiting for transfers between devices  36.6 us (40%)
  starting transfers between devices  31.6 us (35%)
  Pallas kernels  20.8 us (23%)
  other arithmetic  0.94 us (1%)
    ppermute x19, waiting for transfers between devices, send(): return lax.ppermute(v, axis, way)  36.6 us
    ppermute x19, starting transfers between devices, send(): return lax.ppermute(v, axis, way)  31.6 us
    pallas_call x2, Pallas kernels, attend(): pl.pallas_call(functools.partial(attend_kernel, half), out_shape=[jax.Sha...  9.7 us
    pallas_call x1, Pallas kernels, convolve(): pl.pallas_call(conv_kernel, out_shape=jax.ShapeDtypeStruct((4, 64, 256),...  4.57 us
    pallas_call x1, Pallas kernels, core(): pl.pallas_call(core_kernel, out_shape=[jax.ShapeDtypeStruct((stride * (6...  2.25 us
  transfers between devices with their start and end apart: 19, of which 14 were waited for; matrix products, arithmetic and copies ran while one was open for 0% of the time, Pallas kernels for 11%

profile of v6, /device:TPU:64, one launch (start us, length us, event | category | flops | bytes accessed | tf_op | source)
XLA Modules:
  0.0 90.3 jit_solution(14675349547343914839)
XLA Ops:
  0.0 4.8 %attend.3 = (bf16[8,136,128]{2,1,0:T(8,128)(2,1)S(1)}, bf16[8,136,128]{2,1,0:T(8,128)(2,1)S(1)}, bf16[8,136,128]{2,1,0:T(8,128)(2,1)S(1)}, bf16[8,136,128]{2,1,0:T(8,128)(2,1)S(1)}) custom-call(bf16[4,16,512,128]{3,2,1,0:T(8,128)(2,1)} %bitcast.22, bf16[16,512,128]{2,1,0:T(8,128)(2,1)} %bitcast.24, s32[4,16,8,128]{3,2,1,0:T(8,128)} %seen_at.3, ...), custom_call_target="tpu_custom_call" | custom-call | flops 100000000 | bytes 12582912 | tf_op jit(solution)/shard_map/attend/pallas_call | solution.py:134
  4.9 1.6 %collective-permute-start.3 = (bf16[8,136,128]{2,1,0:T(8,128)(2,1)S(1)}, bf16[8,136,128]{2,1,0:T(8,128)(2,1)S(1)}, u32[]{:S(2)}, u32[]{:S(2)}) collective-permute-start(bf16[8,136,128]{2,1,0:T(8,128)(2,1)S(1)} %get-tuple-element.31), channel_id=1, source_target_pairs={{0,16},{16,32},{32,48},{48,0},{64,80},{80,96},{96,112},{112,64},{1... | collective-permute-start | bytes 835592 | tf_op jit(solution)/shard_map/ppermute | solution.py:432
  6.4 4.8 %attend.2 = (bf16[8,136,128]{2,1,0:T(8,128)(2,1)S(1)}, bf16[8,136,128]{2,1,0:T(8,128)(2,1)S(1)}, bf16[8,136,128]{2,1,0:T(8,128)(2,1)S(1)}, bf16[8,136,128]{2,1,0:T(8,128)(2,1)S(1)}) custom-call(bf16[4,16,512,128]{3,2,1,0:T(8,128)(2,1)} %bitcast.23, bf16[16,512,128]{2,1,0:T(8,128)(2,1)} %bitcast.25, s32[4,16,8,128]{3,2,1,0:T(8,128)} %seen_at.3, ...), custom_call_target="tpu_custom_call" | custom-call | flops 100000000 | bytes 12582912 | tf_op jit(solution)/shard_map/attend/pallas_call | solution.py:134
  11.3 1.8 %collective-permute-start.1 = (bf16[8,136,128]{2,1,0:T(8,128)(2,1)S(1)}, bf16[8,136,128]{2,1,0:T(8,128)(2,1)S(1)}, u32[]{:S(2)}, u32[]{:S(2)}) collective-permute-start(bf16[8,136,128]{2,1,0:T(8,128)(2,1)S(1)} %get-tuple-element.27), channel_id=1, source_target_pairs={{0,48},{16,0},{32,16},{48,32},{64,112},{80,64},{96,80},{112,96},{1... | collective-permute-start | bytes 835592 | tf_op jit(solution)/shard_map/ppermute | solution.py:432
  13.1 1.6 %collective-permute-start.5 = (bf16[8,136,128]{2,1,0:T(8,128)(2,1)S(1)}, bf16[8,136,128]{2,1,0:T(8,128)(2,1)S(1)}, u32[]{:S(2)}, u32[]{:S(2)}) collective-permute-start(bf16[8,136,128]{2,1,0:T(8,128)(2,1)S(1)} %get-tuple-element.32), channel_id=1, source_target_pairs={{0,48},{16,0},{32,16},{48,32},{64,112},{80,64},{96,80},{112,96},{1... | collective-permute-start | bytes 835592 | tf_op jit(solution)/shard_map/ppermute | solution.py:432
  14.9 0.6 collective-permute-start.4
  15.5 1.2 %collective-permute-start = (bf16[8,136,128]{2,1,0:T(8,128)(2,1)S(1)}, bf16[8,136,128]{2,1,0:T(8,128)(2,1)S(1)}, u32[]{:S(2)}, u32[]{:S(2)}) collective-permute-start(bf16[8,136,128]{2,1,0:T(8,128)(2,1)S(1)} %get-tuple-element.25), channel_id=1, source_target_pairs={{0,16},{16,32},{32,48},{48,0},{64,80},{80,96},{96,112},{112,64},{1... | collective-permute-start | bytes 835592 | tf_op jit(solution)/shard_map/ppermute | solution.py:432
  16.7 4.2 %collective-permute-done.1.refs_1_ = bf16[8,136,128]{2,1,0:T(8,128)(2,1)S(1)} collective-permute-done((bf16[8,136,128]{2,1,0:T(8,128)(2,1)S(1)}, bf16[8,136,128]{2,1,0:T(8,128)(2,1)S(1)}, u32[]{:S(2)}, u32[]{:S(2)}) %collective-permute-start.1) | collective-permute-done | bytes 278560 | tf_op jit(solution)/shard_map/ppermute | solution.py:432
  21.2 3.0 %collective-permute-start.2 = (bf16[8,136,128]{2,1,0:T(8,128)(2,1)S(1)}, bf16[8,136,128]{2,1,0:T(8,128)(2,1)S(1)}, u32[]{:S(2)}, u32[]{:S(2)}) collective-permute-start(bf16[8,136,128]{2,1,0:T(8,128)(2,1)S(1)} %merge.4), channel_id=1, source_target_pairs={{0,48},{16,0},{32,16},{48,32},{64,112},{80,64},{96,80},{112,96},{1... | collective-permute-start | bytes 835592 | tf_op jit(solution)/shard_map/ppermute | solution.py:432
  24.2 2.7 %collective-permute-done.5.refs_2_ = bf16[8,136,128]{2,1,0:T(8,128)(2,1)S(1)} collective-permute-done((bf16[8,136,128]{2,1,0:T(8,128)(2,1)S(1)}, bf16[8,136,128]{2,1,0:T(8,128)(2,1)S(1)}, u32[]{:S(2)}, u32[]{:S(2)}) %collective-permute-start.5) | collective-permute-done | bytes 278560 | tf_op jit(solution)/shard_map/ppermute | solution.py:432
  27.2 4.7 %collective-permute-start.6 = (bf16[2,136,128]{2,1,0:T(8,128)(2,1)S(1)}, bf16[2,136,128]{2,1,0:T(8,128)(2,1)S(1)}, u32[]{:S(2)}, u32[]{:S(2)}) collective-permute-start(bf16[2,136,128]{2,1,0:T(8,128)(2,1)S(1)} %get-tuple-element.34), channel_id=1, source_target_pairs={{0,64},{16,80},{32,96},{48,112},{64,128},{80,144},{96,160},{112,17... | collective-permute-start | bytes 208904 | tf_op jit(solution)/shard_map/ppermute | solution.py:432
  32.3 1.6 %collective-permute-done.6.came = bf16[2,136,128]{2,1,0:T(8,128)(2,1)S(1)} collective-permute-done((bf16[2,136,128]{2,1,0:T(8,128)(2,1)S(1)}, bf16[2,136,128]{2,1,0:T(8,128)(2,1)S(1)}, u32[]{:S(2)}, u32[]{:S(2)}) %collective-permute-start.6) | collective-permute-done | bytes 69664 | tf_op jit(solution)/shard_map/ppermute | solution.py:432
  34.1 4.7 %collective-permute-start.7 = (bf16[4,136,128]{2,1,0:T(8,128)(2,1)S(1)}, bf16[4,136,128]{2,1,0:T(8,128)(2,1)S(1)}, u32[]{:S(2)}, u32[]{:S(2)}) collective-permute-start(bf16[4,136,128]{2,1,0:T(8,128)(2,1)S(1)} %lift.2), channel_id=1, source_target_pairs={{0,64},{16,80},{32,96},{48,112},{64,128},{80,144},{96,160},{112,17... | collective-permute-start | bytes 417800 | tf_op jit(solution)/shard_map/ppermute | solution.py:432
  39.5 0.9 weights.1
  40.4 1.2 %collective-permute-done.7.low = bf16[4,136,128]{2,1,0:T(8,128)(2,1)S(1)} collective-permute-done((bf16[4,136,128]{2,1,0:T(8,128)(2,1)S(1)}, bf16[4,136,128]{2,1,0:T(8,128)(2,1)S(1)}, u32[]{:S(2)}, u32[]{:S(2)}) %collective-permute-start.7) | collective-permute-done | bytes 139296 | tf_op jit(solution)/shard_map/ppermute | solution.py:432
  41.7 7.5 %collective-permute-done.9.high = bf16[4,136,128]{2,1,0:T(8,128)(2,1)S(1)} collective-permute-done((bf16[4,136,128]{2,1,0:T(8,128)(2,1)S(1)}, bf16[4,136,128]{2,1,0:T(8,128)(2,1)S(1)}, u32[]{:S(2)}, u32[]{:S(2)}) %collective-permute-start.9) | collective-permute-done | bytes 139296 | tf_op jit(solution)/shard_map/ppermute | solution.py:432
  49.2 0.8 finish.1
  50.2 4.1 %collective-permute-start.10 = (bf16[8,32,256]{2,1,0:T(8,128)(2,1)S(1)}, bf16[8,32,256]{2,1,0:T(8,128)(2,1)S(1)}, u32[]{:S(2)}, u32[]{:S(2)}) collective-permute-start(bf16[8,32,256]{2,1,0:T(8,128)(2,1)S(1)} %bitcast.18), channel_id=1, source_target_pairs={{0,64},{16,80},{32,96},{48,112},{64,128},{80,144},{96,160},{112,17... | collective-permute-start | bytes 393224 | tf_op jit(solution)/shard_map/ppermute | solution.py:432
  54.3 3.5 %collective-permute-done.11 = bf16[8,32,256]{2,1,0:T(8,128)(2,1)S(1)} collective-permute-done((bf16[8,32,256]{2,1,0:T(8,128)(2,1)S(1)}, bf16[8,32,256]{2,1,0:T(8,128)(2,1)S(1)}, u32[]{:S(2)}, u32[]{:S(2)}) %collective-permute-start.11) | collective-permute-done | bytes 131104 | tf_op jit(solution)/shard_map/ppermute | solution.py:432
  58.0 2.1 %collective-permute-start.12 = (bf16[8,4,768]{2,1,0:T(4,128)(2,1)S(1)}, bf16[8,4,768]{2,1,0:T(4,128)(2,1)S(1)}, u32[]{:S(2)}, u32[]{:S(2)}) collective-permute-start(bf16[8,4,768]{2,1,0:T(4,128)(2,1)S(1)} %get-tuple-element.45), channel_id=1, source_target_pairs={{0,16},{16,32},{32,48},{48,1},{1,17},{17,33},{33,49},{49,2},{2,18}... | collective-permute-start | bytes 147464 | tf_op jit(solution)/shard_map/ppermute | solution.py:432
  60.1 1.9 %collective-permute-done.13 = bf16[8,4,768]{2,1,0:T(4,128)(2,1)S(1)} collective-permute-done((bf16[8,4,768]{2,1,0:T(4,128)(2,1)S(1)}, bf16[8,4,768]{2,1,0:T(4,128)(2,1)S(1)}, u32[]{:S(2)}, u32[]{:S(2)}) %collective-permute-start.13) | collective-permute-done | bytes 49184 | tf_op jit(solution)/shard_map/ppermute | solution.py:432
  62.1 1.6 %collective-permute-done.12 = bf16[8,4,768]{2,1,0:T(4,128)(2,1)S(1)} collective-permute-done((bf16[8,4,768]{2,1,0:T(4,128)(2,1)S(1)}, bf16[8,4,768]{2,1,0:T(4,128)(2,1)S(1)}, u32[]{:S(2)}, u32[]{:S(2)}) %collective-permute-start.12) | collective-permute-done | bytes 49184 | tf_op jit(solution)/shard_map/ppermute | solution.py:432
  63.9 3.1 %collective-permute-start.15 = (bf16[4,40,768]{2,1,0:T(8,128)(2,1)S(1)}, bf16[4,40,768]{2,1,0:T(8,128)(2,1)S(1)}, u32[]{:S(2)}, u32[]{:S(2)}) collective-permute-start(bf16[4,40,768]{2,1,0:T(8,128)(2,1)S(1)} %pad_maximum_fusion.2), channel_id=1, source_target_pairs={{4,0},{8,4},{12,8},{0,12},{5,1},{9,5},{13,9},{1,13},{6,2},{10,6},{... | collective-permute-start | bytes 737288 | tf_op jit(solution)/shard_map/ppermute | solution.py:432
  67.6 2.2 %core.1 = (bf16[288,640]{1,0:T(8,128)(2,1)S(1)}, bf16[192,512]{1,0:T(8,128)(2,1)S(1)}, bf16[96,384]{1,0:T(8,128)(2,1)S(1)}) custom-call(bf16[384,768]{1,0:T(8,128)(2,1)S(1)} %bitcast.21, bf16[4,3,256,384]{3,2,1,0:T(8,128)(2,1)S(1)} %get-tuple-element.39.band, f32[4,128]{1,0:T(4,128)S(1)} %pad_maximum_fusion.5.bias), custom_call_target="tpu_custom_call" | custom-call | flops 1000000000 | bytes 1000000 | tf_op jit(solution)/shard_map/core/pallas_call | solution.py:359
  69.8 2.3 %collective-permute-done.15 = bf16[4,40,768]{2,1,0:T(8,128)(2,1)S(1)} collective-permute-done((bf16[4,40,768]{2,1,0:T(8,128)(2,1)S(1)}, bf16[4,40,768]{2,1,0:T(8,128)(2,1)S(1)}, u32[]{:S(2)}, u32[]{:S(2)}) %collective-permute-start.15) | collective-permute-done | bytes 245792 | tf_op jit(solution)/shard_map/ppermute | solution.py:432
  72.2 4.3 %collective-permute-done.14 = bf16[4,40,768]{2,1,0:T(8,128)(2,1)S(1)} collective-permute-done((bf16[4,40,768]{2,1,0:T(8,128)(2,1)S(1)}, bf16[4,40,768]{2,1,0:T(8,128)(2,1)S(1)}, u32[]{:S(2)}, u32[]{:S(2)}) %collective-permute-start.14) | collective-permute-done | bytes 245792 | tf_op jit(solution)/shard_map/ppermute | solution.py:432
  76.9 4.6 %convolve.1 = bf16[4,64,256]{2,1,0:T(8,128)(2,1)S(1)} custom-call(bf16[768,768]{1,0:T(8,128)(2,1)S(1)} %bitcast.15, bf16[288,640]{1,0:T(8,128)(2,1)S(1)} %get-tuple-element.40.core0, bf16[192,512]{1,0:T(8,128)(2,1)S(1)} %get-tuple-element.41.core1, bf16[96,384]{1,0:T(8,128)(2,1)S(1)} %get-tuple-element.42.core2, ...), custom_call_target="tpu_custom_call" | custom-call | tf_op jit(solution)/shard_map/convolve/pallas_call | solution.py:395
  81.8 2.3 %collective-permute-start.17 = (bf16[64,256]{1,0:T(8,128)(2,1)S(1)}, bf16[64,256]{1,0:T(8,128)(2,1)S(1)}, u32[]{:S(2)}, u32[]{:S(2)}) collective-permute-start(bf16[64,256]{1,0:T(8,128)(2,1)S(1)} %get-tuple-element.48), channel_id=1, source_target_pairs={{0,32},{16,48},{32,0},{48,16},{64,96},{80,112},{96,64},{112,80},{1... | collective-permute-start | bytes 98312 | tf_op jit(solution)/shard_map/ppermute | solution.py:432
  84.1 1.7 %collective-permute-done.16.high = bf16[64,256]{1,0:T(8,128)(2,1)S(1)} collective-permute-done((bf16[64,256]{1,0:T(8,128)(2,1)S(1)}, bf16[64,256]{1,0:T(8,128)(2,1)S(1)}, u32[]{:S(2)}, u32[]{:S(2)}) %collective-permute-start.16) | collective-permute-done | bytes 32800 | tf_op jit(solution)/shard_map/ppermute | solution.py:432
  85.8 1.4 %collective-permute-done.17.far = bf16[64,256]{1,0:T(8,128)(2,1)S(1)} collective-permute-done((bf16[64,256]{1,0:T(8,128)(2,1)S(1)}, bf16[64,256]{1,0:T(8,128)(2,1)S(1)}, u32[]{:S(2)}, u32[]{:S(2)}) %collective-permute-start.17) | collective-permute-done | bytes 32800 | tf_op jit(solution)/shard_map/ppermute | solution.py:432
  87.3 2.0 %collective-permute-done.18.low = bf16[64,256]{1,0:T(8,128)(2,1)S(1)} collective-permute-done((bf16[64,256]{1,0:T(8,128)(2,1)S(1)}, bf16[64,256]{1,0:T(8,128)(2,1)S(1)}, u32[]{:S(2)}, u32[]{:S(2)}) %collective-permute-start.18) | collective-permute-done | bytes 32800 | tf_op jit(solution)/shard_map/ppermute | solution.py:432
  89.2 1.1 %place.1 = bf16[512,128]{1,0:T(8,128)(2,1)} custom-call(bf16[64,256]{1,0:T(8,128)(2,1)S(1)} %get-tuple-element.50.own, bf16[64,256]{1,0:T(8,128)(2,1)S(1)} %collective-permute-done.16.high, bf16[64,256]{1,0:T(8,128)(2,1)S(1)} %collective-permute-done.17.far, bf16[64,256]{1,0:T(8,128)(2,1)S(1)} %collective-permute-done.18.low), custom_call_target="tpu_custom_call" | custom-call | tf_op jit(solution)/shard_map/place/pallas_call | solution.py:420
  (44 shorter events, 4.0 us)
Async XLA Ops:
  4.9 9.8 %collective-permute-start.3 = (bf16[8,136,128]{2,1,0:T(8,128)(2,1)S(1)}, bf16[8,136,128]{2,1,0:T(8,128)(2,1)S(1)}, u32[]{:S(2)}, u32[]{:S(2)}) collective-permute-start(bf16[8,136,128]{2,1,0:T(8,128)(2,1)S(1)} %get-tuple-element.31), channel_id=1, source_target_pairs={{0,16},{16,32},{32,48},{48,0},{64,80},{80,96},{96,112},{112,64},{1... | collective-permute-start | bytes 835592 | tf_op jit(solution)/shard_map/ppermute | solution.py:432
  11.3 9.6 %collective-permute-start.1 = (bf16[8,136,128]{2,1,0:T(8,128)(2,1)S(1)}, bf16[8,136,128]{2,1,0:T(8,128)(2,1)S(1)}, u32[]{:S(2)}, u32[]{:S(2)}) collective-permute-start(bf16[8,136,128]{2,1,0:T(8,128)(2,1)S(1)} %get-tuple-element.27), channel_id=1, source_target_pairs={{0,48},{16,0},{32,16},{48,32},{64,112},{80,64},{96,80},{112,96},{1... | collective-permute-start | bytes 835592 | tf_op jit(solution)/shard_map/ppermute | solution.py:432
  13.1 13.8 %collective-permute-start.5 = (bf16[8,136,128]{2,1,0:T(8,128)(2,1)S(1)}, bf16[8,136,128]{2,1,0:T(8,128)(2,1)S(1)}, u32[]{:S(2)}, u32[]{:S(2)}) collective-permute-start(bf16[8,136,128]{2,1,0:T(8,128)(2,1)S(1)} %get-tuple-element.32), channel_id=1, source_target_pairs={{0,48},{16,0},{32,16},{48,32},{64,112},{80,64},{96,80},{112,96},{1... | collective-permute-start | bytes 835592 | tf_op jit(solution)/shard_map/ppermute | solution.py:432
  14.9 11.9 %collective-permute-start.4 = (bf16[8,136,128]{2,1,0:T(8,128)(2,1)S(1)}, bf16[8,136,128]{2,1,0:T(8,128)(2,1)S(1)}, u32[]{:S(2)}, u32[]{:S(2)}) collective-permute-start(bf16[8,136,128]{2,1,0:T(8,128)(2,1)S(1)} %merge.6), channel_id=1, source_target_pairs={{0,16},{16,32},{32,48},{48,0},{64,80},{80,96},{96,112},{112,64},{1... | collective-permute-start | bytes 835592 | tf_op jit(solution)/shard_map/ppermute | solution.py:432
  15.5 16.5 %collective-permute-start = (bf16[8,136,128]{2,1,0:T(8,128)(2,1)S(1)}, bf16[8,136,128]{2,1,0:T(8,128)(2,1)S(1)}, u32[]{:S(2)}, u32[]{:S(2)}) collective-permute-start(bf16[8,136,128]{2,1,0:T(8,128)(2,1)S(1)} %get-tuple-element.25), channel_id=1, source_target_pairs={{0,16},{16,32},{32,48},{48,0},{64,80},{80,96},{96,112},{112,64},{1... | collective-permute-start | bytes 835592 | tf_op jit(solution)/shard_map/ppermute | solution.py:432
  21.2 10.8 %collective-permute-start.2 = (bf16[8,136,128]{2,1,0:T(8,128)(2,1)S(1)}, bf16[8,136,128]{2,1,0:T(8,128)(2,1)S(1)}, u32[]{:S(2)}, u32[]{:S(2)}) collective-permute-start(bf16[8,136,128]{2,1,0:T(8,128)(2,1)S(1)} %merge.4), channel_id=1, source_target_pairs={{0,48},{16,0},{32,16},{48,32},{64,112},{80,64},{96,80},{112,96},{1... | collective-permute-start | bytes 835592 | tf_op jit(solution)/shard_map/ppermute | solution.py:432
  26.9 12.6 %copy-start = (bf16[4,3,3,3,64,64]{5,4,3,2,1,0:T(8,128)(2,1)S(1)}, bf16[4,3,3,3,64,64]{5,4,3,2,1,0:T(8,128)(2,1)}, u32[]{:S(2)}) copy-start(bf16[4,3,3,3,64,64]{5,4,3,2,1,0:T(8,128)(2,1)} %param.16) | copy-start | bytes 2654212
  26.9 12.6 %copy-start.1 = (bf16[64,64]{1,0:T(8,128)(2,1)S(1)}, bf16[64,64]{1,0:T(8,128)(2,1)}, u32[]{:S(2)}) copy-start(bf16[64,64]{1,0:T(8,128)(2,1)} %wv.1) | copy-start | bytes 24580
  26.9 12.7 %copy-start.2 = (bf16[64,64]{1,0:T(8,128)(2,1)S(1)}, bf16[64,64]{1,0:T(8,128)(2,1)}, u32[]{:S(2)}) copy-start(bf16[64,64]{1,0:T(8,128)(2,1)} %wo.1) | copy-start | bytes 24580
  27.2 6.7 %collective-permute-start.6 = (bf16[2,136,128]{2,1,0:T(8,128)(2,1)S(1)}, bf16[2,136,128]{2,1,0:T(8,128)(2,1)S(1)}, u32[]{:S(2)}, u32[]{:S(2)}) collective-permute-start(bf16[2,136,128]{2,1,0:T(8,128)(2,1)S(1)} %get-tuple-element.34), channel_id=1, source_target_pairs={{0,64},{16,80},{32,96},{48,112},{64,128},{80,144},{96,160},{112,17... | collective-permute-start | bytes 208904 | tf_op jit(solution)/shard_map/ppermute | solution.py:432
  32.0 7.3 %collective-permute-start.8 = (bf16[2,136,128]{2,1,0:T(8,128)(2,1)S(1)}, bf16[2,136,128]{2,1,0:T(8,128)(2,1)S(1)}, u32[]{:S(2)}, u32[]{:S(2)}) collective-permute-start(bf16[2,136,128]{2,1,0:T(8,128)(2,1)S(1)} %get-tuple-element.36), channel_id=1, source_target_pairs={{64,0},{80,16},{96,32},{112,48},{128,64},{144,80},{160,96},{176,11... | collective-permute-start | bytes 208904 | tf_op jit(solution)/shard_map/ppermute | solution.py:432
  34.1 7.6 %collective-permute-start.7 = (bf16[4,136,128]{2,1,0:T(8,128)(2,1)S(1)}, bf16[4,136,128]{2,1,0:T(8,128)(2,1)S(1)}, u32[]{:S(2)}, u32[]{:S(2)}) collective-permute-start(bf16[4,136,128]{2,1,0:T(8,128)(2,1)S(1)} %lift.2), channel_id=1, source_target_pairs={{0,64},{16,80},{32,96},{48,112},{64,128},{80,144},{96,160},{112,17... | collective-permute-start | bytes 417800 | tf_op jit(solution)/shard_map/ppermute | solution.py:432
  39.4 9.8 %collective-permute-start.9 = (bf16[4,136,128]{2,1,0:T(8,128)(2,1)S(1)}, bf16[4,136,128]{2,1,0:T(8,128)(2,1)S(1)}, u32[]{:S(2)}, u32[]{:S(2)}) collective-permute-start(bf16[4,136,128]{2,1,0:T(8,128)(2,1)S(1)} %lift.3), channel_id=1, source_target_pairs={{64,0},{80,16},{96,32},{112,48},{128,64},{144,80},{160,96},{176,11... | collective-permute-start | bytes 417800 | tf_op jit(solution)/shard_map/ppermute | solution.py:432
  39.5 10.6 %copy-start.3 = (f32[4,64]{1,0:T(4,128)S(1)}, f32[4,64]{1,0:T(4,128)}, u32[]{:S(2)}) copy-start(f32[4,64]{1,0:T(4,128)} %param.17) | copy-start | bytes 3076
  50.0 7.8 %collective-permute-start.11 = (bf16[8,32,256]{2,1,0:T(8,128)(2,1)S(1)}, bf16[8,32,256]{2,1,0:T(8,128)(2,1)S(1)}, u32[]{:S(2)}, u32[]{:S(2)}) collective-permute-start(bf16[8,32,256]{2,1,0:T(8,128)(2,1)S(1)} %bitcast.17), channel_id=1, source_target_pairs={{64,0},{80,16},{96,32},{112,48},{128,64},{144,80},{160,96},{176,11... | collective-permute-start | bytes 393224 | tf_op jit(solution)/shard_map/ppermute | solution.py:432
  50.2 7.6 %collective-permute-start.10 = (bf16[8,32,256]{2,1,0:T(8,128)(2,1)S(1)}, bf16[8,32,256]{2,1,0:T(8,128)(2,1)S(1)}, u32[]{:S(2)}, u32[]{:S(2)}) collective-permute-start(bf16[8,32,256]{2,1,0:T(8,128)(2,1)S(1)} %bitcast.18), channel_id=1, source_target_pairs={{0,64},{16,80},{32,96},{48,112},{64,128},{80,144},{96,160},{112,17... | collective-permute-start | bytes 393224 | tf_op jit(solution)/shard_map/ppermute | solution.py:432
  57.9 4.2 %collective-permute-start.13 = (bf16[8,4,768]{2,1,0:T(4,128)(2,1)S(1)}, bf16[8,4,768]{2,1,0:T(4,128)(2,1)S(1)}, u32[]{:S(2)}, u32[]{:S(2)}) collective-permute-start(bf16[8,4,768]{2,1,0:T(4,128)(2,1)S(1)} %get-tuple-element.46), channel_id=1, source_target_pairs={{16,0},{32,16},{48,32},{1,48},{17,1},{33,17},{49,33},{2,49},{18,2}... | collective-permute-start | bytes 147464 | tf_op jit(solution)/shard_map/ppermute | solution.py:432
  58.0 5.7 %collective-permute-start.12 = (bf16[8,4,768]{2,1,0:T(4,128)(2,1)S(1)}, bf16[8,4,768]{2,1,0:T(4,128)(2,1)S(1)}, u32[]{:S(2)}, u32[]{:S(2)}) collective-permute-start(bf16[8,4,768]{2,1,0:T(4,128)(2,1)S(1)} %get-tuple-element.45), channel_id=1, source_target_pairs={{0,16},{16,32},{32,48},{48,1},{1,17},{17,33},{33,49},{49,2},{2,18}... | collective-permute-start | bytes 147464 | tf_op jit(solution)/shard_map/ppermute | solution.py:432
  63.9 8.3 %collective-permute-start.15 = (bf16[4,40,768]{2,1,0:T(8,128)(2,1)S(1)}, bf16[4,40,768]{2,1,0:T(8,128)(2,1)S(1)}, u32[]{:S(2)}, u32[]{:S(2)}) collective-permute-start(bf16[4,40,768]{2,1,0:T(8,128)(2,1)S(1)} %pad_maximum_fusion.2), channel_id=1, source_target_pairs={{4,0},{8,4},{12,8},{0,12},{5,1},{9,5},{13,9},{1,13},{6,2},{10,6},{... | collective-permute-start | bytes 737288 | tf_op jit(solution)/shard_map/ppermute | solution.py:432
  67.1 9.4 %collective-permute-start.14 = (bf16[4,40,768]{2,1,0:T(8,128)(2,1)S(1)}, bf16[4,40,768]{2,1,0:T(8,128)(2,1)S(1)}, u32[]{:S(2)}, u32[]{:S(2)}) collective-permute-start(bf16[4,40,768]{2,1,0:T(8,128)(2,1)S(1)} %pad_maximum_fusion.1), channel_id=1, source_target_pairs={{0,4},{4,8},{8,12},{12,0},{1,5},{5,9},{9,13},{13,1},{2,6},{6,10},{... | collective-permute-start | bytes 737288 | tf_op jit(solution)/shard_map/ppermute | solution.py:432
  81.5 4.3 %collective-permute-start.16 = (bf16[64,256]{1,0:T(8,128)(2,1)S(1)}, bf16[64,256]{1,0:T(8,128)(2,1)S(1)}, u32[]{:S(2)}, u32[]{:S(2)}) collective-permute-start(bf16[64,256]{1,0:T(8,128)(2,1)S(1)} %get-tuple-element.49), channel_id=1, source_target_pairs={{0,48},{16,0},{32,16},{48,32},{64,112},{80,64},{96,80},{112,96},{1... | collective-permute-start | bytes 98312 | tf_op jit(solution)/shard_map/ppermute | solution.py:432
  81.8 5.4 %collective-permute-start.17 = (bf16[64,256]{1,0:T(8,128)(2,1)S(1)}, bf16[64,256]{1,0:T(8,128)(2,1)S(1)}, u32[]{:S(2)}, u32[]{:S(2)}) collective-permute-start(bf16[64,256]{1,0:T(8,128)(2,1)S(1)} %get-tuple-element.48), channel_id=1, source_target_pairs={{0,32},{16,48},{32,0},{48,16},{64,96},{80,112},{96,64},{112,80},{1... | collective-permute-start | bytes 98312 | tf_op jit(solution)/shard_map/ppermute | solution.py:432
  84.1 5.1 %collective-permute-start.18 = (bf16[64,256]{1,0:T(8,128)(2,1)S(1)}, bf16[64,256]{1,0:T(8,128)(2,1)S(1)}, u32[]{:S(2)}, u32[]{:S(2)}) collective-permute-start(bf16[64,256]{1,0:T(8,128)(2,1)S(1)} %get-tuple-element.47), channel_id=1, source_target_pairs={{0,16},{16,32},{32,48},{48,0},{64,80},{80,96},{96,112},{112,64},{1... | collective-permute-start | bytes 98312 | tf_op jit(solution)/shard_map/ppermute | solution.py:432

commit v7 on v6

--- a/solution.py
+++ b/solution.py
@@ -13,6 +13,11 @@
 stride = 48
 bf16, f32 = jnp.bfloat16, jnp.float32
 VM = pl.BlockSpec(memory_space=pltpu.VMEM)
+
+
+def chunk_of():
+    x, odd = lax.axis_index("frame") % 4, lax.axis_index("by") % 2
+    return x + odd * (3 - 2 * x)
 
 
 def dot(a, b):
@@ -43,9 +48,8 @@
 def attend_kernel(half, feat_at, embed_at, seen_at, wq_at, wk_at, *refs):
     outs, feat, embed, seen, wq, wk, key0, key1, wide0, wide1, sems = refs[:4], *refs[4:]
     steps, frames, n = feat.shape[:3]
-    me = lax.axis_index("frame")
-    zh, xi = me // 4, me % 4
-    turn = (128 - 32 * xi) & 127
+    zh = lax.axis_index("frame") // 4
+    turn = (128 - 32 * chunk_of()) & 127
 
     def copies(s):
         block = 1 + 2 * half + s * n // 4
@@ -306,8 +310,8 @@
 
 
 def row_mask(mask):
-    xi = lax.axis_index("frame") % 4
-    x0, y0 = lax.axis_index("bx") * 8 - halo, lax.axis_index("by") * 128 + xi * 32 - halo
+    x0 = lax.axis_index("bx") * 8 - halo
+    y0 = lax.axis_index("by") * 128 + chunk_of() * 32 - halo
     y = lax.broadcasted_iota(jnp.int32, (stride, 128), 0) + y0
     y_ok = (y >= 0) & (y < 512)
     for x in range(16):
@@ -371,7 +375,7 @@
 
 
 def conv_kernel(block, core0, core1, core2, band, bias, out, buf0, buf1, mask):
-    xi = lax.axis_index("frame") % 4
+    mine, odd = chunk_of(), lax.axis_index("by") % 2
     row_mask(mask)
     src = block
     for layer, (dst, done) in enumerate(((buf0, core0), (buf1, core1), (buf0, core2))):
@@ -388,7 +392,9 @@
         tiles = [h[stride * x : stride * x + 32] for x in range(8)]
         whole = jnp.concatenate(tiles, axis=0).T.astype(bf16)
         for i in range(2):
-            out[(2 * t + i - xi) & 3] = whole[64 * i : 64 * i + 64]
+            goal = 2 * t + i
+            goal = goal + odd * (3 - 2 * goal)
+            out[(goal - mine) & 3] = whole[64 * i : 64 * i + 64]
 
 
 def convolve(block, cores, band, bias):
@@ -408,7 +414,7 @@
 
 
 def place_kernel(own, high, far, low, out, rows):
-    turn = 32 * (lax.axis_index("frame") % 4)
+    turn = 32 * chunk_of()
     parts = [r[...].astype(f32) for r in (own, high, far, low)]
     for x in range(8):
         line = jnp.concatenate([p[:, 32 * x : 32 * x + 32] for p in parts], axis=1)
@@ -428,7 +434,7 @@
     )(own, high, far, low)
 
 
-def send(v, way, axis="frame"):
+def send(v, way, axis=("frame", "by")):
     return lax.ppermute(v, axis, way)
 
 
@@ -438,7 +444,15 @@
 
 def joined(features, voxel_embed, visible, w_query, w_key, w_value, w_out, conv_weight, conv_bias):
     around = range(4)
-    x_by = lambda k: [(4 * z + x, 4 * z + (x + k) % 4) for z in around for x in around]
+
+    def where_is(z, chunk):
+        brick, k = chunk // 4, chunk % 4
+        return (4 * z + (3 - k if brick % 2 else k)) * 4 + brick
+
+    def x_by(r):
+        bases = [(z, 4 * brick, k) for z in around for brick in around for k in around]
+        return [(where_is(z, b + k), where_is(z, b + (k + r) % 4)) for z, b, k in bases]
+
     up, down = x_by(1), x_by(3)
     z_up = [(i, (i + 4) % 16) for i in range(16)]
     z_down = [(j, i) for i, j in z_up]
@@ -455,27 +469,24 @@
     low_a = send(merge([a1, from_low], [8])[0], up)
     high_b = send(merge([b3, from_high], [8])[0], down)
     z1, z2a, z2b = merge([a0, low_a, high_a], [4, 2, 2])
-    from_low = send(z2a, z_up)
-    from_high = send(z2b, z_down)
-    low = send(lift(0, z1, from_low), z_up)
+    from_low = send(z2a, z_up, "frame")
+    from_high = send(z2b, z_down, "frame")
+    low = send(lift(0, z1, from_low), z_up, "frame")
     z3, z0 = merge([b0, low_b, high_b], [4, 4])
-    high = send(lift(2, z3, from_high), z_down)
+    high = send(lift(2, z3, from_high), z_down, "frame")
     hidden = finish(z0, low, high, wide_v, wide_o).reshape(8, 32, 256)
 
     me = lax.axis_index("frame")
-    zh, xi = me // 4, me % 4
-    below = only(zh > 0, send(hidden, z_up))
-    above = only(zh < 3, send(hidden, z_down))
+    zh = me // 4
+    below = only(zh > 0, send(hidden, z_up, "frame"))
+    above = only(zh < 3, send(hidden, z_down, "frame"))
     hidden = jnp.concatenate([below, hidden, above], axis=2)
-
-    def where_is(z, chunk):
-        return (4 * z + chunk % 4) * 4 + chunk // 4
 
     y_next = [(where_is(z, k), where_is(z, (k + 1) % 16)) for z in range(4) for k in range(16)]
     y_prev = [(j, i) for i, j in y_next]
-    chunk = lax.axis_index("by") * 4 + xi
-    left = only(chunk > 0, send(hidden[:, -halo:], y_next, ("frame", "by")))
-    right = only(chunk < 15, send(hidden[:, :halo], y_prev, ("frame", "by")))
+    chunk = lax.axis_index("by") * 4 + chunk_of()
+    left = only(chunk > 0, send(hidden[:, -halo:], y_next))
+    right = only(chunk < 15, send(hidden[:, :halo], y_prev))
     first, second = (
         jnp.concatenate([left[i], hidden[i], right[i]], axis=1)
         for i in (slice(0, halo), slice(halo, None))

time: 90.4 us -> 87.9 us (0.972)
  the two profiles are of different devices: /device:TPU:64 before, /device:TPU:32 now
where the time goes in v7:
time: 87.9 us; the launch traced here: 87.8 us
  waiting for transfers between devices  32.9 us (37%)
  starting transfers between devices  32.8 us (37%)
  Pallas kernels  20.8 us (24%)
  other arithmetic  0.93 us (1%)
    ppermute x19, waiting for transfers between devices, send(): return lax.ppermute(v, axis, way)  32.9 us
    ppermute x19, starting transfers between devices, send(): return lax.ppermute(v, axis, way)  32.8 us
    pallas_call x2, Pallas kernels, attend(): pl.pallas_call(functools.partial(attend_kernel, half), out_shape=[jax.Sha...  9.7 us
    pallas_call x1, Pallas kernels, convolve(): pl.pallas_call(conv_kernel, out_shape=jax.ShapeDtypeStruct((4, 64, 256),...  4.57 us
    pallas_call x1, Pallas kernels, core(): pl.pallas_call(core_kernel, out_shape=[jax.ShapeDtypeStruct((stride * (6...  2.25 us
  transfers between devices with their start and end apart: 19, of which 12 were waited for; matrix products, arithmetic and copies ran while one was open for 0% of the time, Pallas kernels for 11%

profile of v7, /device:TPU:32, one launch (start us, length us, event | category | flops | bytes accessed | tf_op | source)
XLA Modules:
  0.0 87.8 jit_solution(12902394353426320028)
XLA Ops:
  0.0 4.9 %attend.3 = (bf16[8,136,128]{2,1,0:T(8,128)(2,1)S(1)}, bf16[8,136,128]{2,1,0:T(8,128)(2,1)S(1)}, bf16[8,136,128]{2,1,0:T(8,128)(2,1)S(1)}, bf16[8,136,128]{2,1,0:T(8,128)(2,1)S(1)}) custom-call(bf16[4,16,512,128]{3,2,1,0:T(8,128)(2,1)} %bitcast.22, bf16[16,512,128]{2,1,0:T(8,128)(2,1)} %bitcast.24, s32[4,16,8,128]{3,2,1,0:T(8,128)} %seen_at.3, ...), custom_call_target="tpu_custom_call" | custom-call | flops 100000000 | bytes 12582912 | tf_op jit(solution)/shard_map/attend/pallas_call | solution.py:138
  4.9 1.6 %collective-permute-start.3 = (bf16[8,136,128]{2,1,0:T(8,128)(2,1)S(1)}, bf16[8,136,128]{2,1,0:T(8,128)(2,1)S(1)}, u32[]{:S(2)}, u32[]{:S(2)}) collective-permute-start(bf16[8,136,128]{2,1,0:T(8,128)(2,1)S(1)} %get-tuple-element.31), channel_id=1, source_target_pairs={{0,16},{16,32},{32,48},{48,0},{49,33},{33,17},{17,1},{1,49},{2,18}... | collective-permute-start | bytes 835592 | tf_op jit(solution)/shard_map/ppermute | solution.py:438
  6.4 4.9 %attend.2 = (bf16[8,136,128]{2,1,0:T(8,128)(2,1)S(1)}, bf16[8,136,128]{2,1,0:T(8,128)(2,1)S(1)}, bf16[8,136,128]{2,1,0:T(8,128)(2,1)S(1)}, bf16[8,136,128]{2,1,0:T(8,128)(2,1)S(1)}) custom-call(bf16[4,16,512,128]{3,2,1,0:T(8,128)(2,1)} %bitcast.23, bf16[16,512,128]{2,1,0:T(8,128)(2,1)} %bitcast.25, s32[4,16,8,128]{3,2,1,0:T(8,128)} %seen_at.3, ...), custom_call_target="tpu_custom_call" | custom-call | flops 100000000 | bytes 12582912 | tf_op jit(solution)/shard_map/attend/pallas_call | solution.py:138
  11.3 1.8 %collective-permute-start.1 = (bf16[8,136,128]{2,1,0:T(8,128)(2,1)S(1)}, bf16[8,136,128]{2,1,0:T(8,128)(2,1)S(1)}, u32[]{:S(2)}, u32[]{:S(2)}) collective-permute-start(bf16[8,136,128]{2,1,0:T(8,128)(2,1)S(1)} %get-tuple-element.27), channel_id=1, source_target_pairs={{0,48},{16,0},{32,16},{48,32},{49,1},{33,49},{17,33},{1,17},{2,50}... | collective-permute-start | bytes 835592 | tf_op jit(solution)/shard_map/ppermute | solution.py:438
  13.1 1.6 %collective-permute-start.5 = (bf16[8,136,128]{2,1,0:T(8,128)(2,1)S(1)}, bf16[8,136,128]{2,1,0:T(8,128)(2,1)S(1)}, u32[]{:S(2)}, u32[]{:S(2)}) collective-permute-start(bf16[8,136,128]{2,1,0:T(8,128)(2,1)S(1)} %get-tuple-element.32), channel_id=1, source_target_pairs={{0,48},{16,0},{32,16},{48,32},{49,1},{33,49},{17,33},{1,17},{2,50}... | collective-permute-start | bytes 835592 | tf_op jit(solution)/shard_map/ppermute | solution.py:438
  15.8 4.7 %collective-permute-done.1.refs_1_ = bf16[8,136,128]{2,1,0:T(8,128)(2,1)S(1)} collective-permute-done((bf16[8,136,128]{2,1,0:T(8,128)(2,1)S(1)}, bf16[8,136,128]{2,1,0:T(8,128)(2,1)S(1)}, u32[]{:S(2)}, u32[]{:S(2)}) %collective-permute-start.1) | collective-permute-done | bytes 278560 | tf_op jit(solution)/shard_map/ppermute | solution.py:438
  20.8 1.9 %collective-permute-start.2 = (bf16[8,136,128]{2,1,0:T(8,128)(2,1)S(1)}, bf16[8,136,128]{2,1,0:T(8,128)(2,1)S(1)}, u32[]{:S(2)}, u32[]{:S(2)}) collective-permute-start(bf16[8,136,128]{2,1,0:T(8,128)(2,1)S(1)} %merge.4), channel_id=1, source_target_pairs={{0,48},{16,0},{32,16},{48,32},{49,1},{33,49},{17,33},{1,17},{2,50}... | collective-permute-start | bytes 835592 | tf_op jit(solution)/shard_map/ppermute | solution.py:438
  22.7 3.8 %collective-permute-done.5.refs_2_ = bf16[8,136,128]{2,1,0:T(8,128)(2,1)S(1)} collective-permute-done((bf16[8,136,128]{2,1,0:T(8,128)(2,1)S(1)}, bf16[8,136,128]{2,1,0:T(8,128)(2,1)S(1)}, u32[]{:S(2)}, u32[]{:S(2)}) %collective-permute-start.5) | collective-permute-done | bytes 278560 | tf_op jit(solution)/shard_map/ppermute | solution.py:438
  26.8 3.5 %collective-permute-start.6 = (bf16[2,136,128]{2,1,0:T(8,128)(2,1)S(1)}, bf16[2,136,128]{2,1,0:T(8,128)(2,1)S(1)}, u32[]{:S(2)}, u32[]{:S(2)}) collective-permute-start(bf16[2,136,128]{2,1,0:T(8,128)(2,1)S(1)} %get-tuple-element.34), channel_id=1, source_target_pairs={{0,64},{16,80},{32,96},{48,112},{64,128},{80,144},{96,160},{112,17... | collective-permute-start | bytes 208904 | tf_op jit(solution)/shard_map/ppermute | solution.py:438
  30.3 2.2 %collective-permute-start.8 = (bf16[2,136,128]{2,1,0:T(8,128)(2,1)S(1)}, bf16[2,136,128]{2,1,0:T(8,128)(2,1)S(1)}, u32[]{:S(2)}, u32[]{:S(2)}) collective-permute-start(bf16[2,136,128]{2,1,0:T(8,128)(2,1)S(1)} %get-tuple-element.36), channel_id=1, source_target_pairs={{64,0},{80,16},{96,32},{112,48},{128,64},{144,80},{160,96},{176,11... | collective-permute-start | bytes 208904 | tf_op jit(solution)/shard_map/ppermute | solution.py:438
  32.9 2.7 %collective-permute-done.6.came = bf16[2,136,128]{2,1,0:T(8,128)(2,1)S(1)} collective-permute-done((bf16[2,136,128]{2,1,0:T(8,128)(2,1)S(1)}, bf16[2,136,128]{2,1,0:T(8,128)(2,1)S(1)}, u32[]{:S(2)}, u32[]{:S(2)}) %collective-permute-start.6) | collective-permute-done | bytes 69664 | tf_op jit(solution)/shard_map/ppermute | solution.py:438
  35.8 1.0 %collective-permute-start.7 = (bf16[4,136,128]{2,1,0:T(8,128)(2,1)S(1)}, bf16[4,136,128]{2,1,0:T(8,128)(2,1)S(1)}, u32[]{:S(2)}, u32[]{:S(2)}) collective-permute-start(bf16[4,136,128]{2,1,0:T(8,128)(2,1)S(1)} %lift.2), channel_id=1, source_target_pairs={{0,64},{16,80},{32,96},{48,112},{64,128},{80,144},{96,160},{112,17... | collective-permute-start | bytes 417800 | tf_op jit(solution)/shard_map/ppermute | solution.py:438
  37.0 3.3 %collective-permute-start.9 = (bf16[4,136,128]{2,1,0:T(8,128)(2,1)S(1)}, bf16[4,136,128]{2,1,0:T(8,128)(2,1)S(1)}, u32[]{:S(2)}, u32[]{:S(2)}) collective-permute-start(bf16[4,136,128]{2,1,0:T(8,128)(2,1)S(1)} %lift.3), channel_id=1, source_target_pairs={{64,0},{80,16},{96,32},{112,48},{128,64},{144,80},{160,96},{176,11... | collective-permute-start | bytes 417800 | tf_op jit(solution)/shard_map/ppermute | solution.py:438
  40.3 0.9 weights.1
  41.2 3.3 %collective-permute-done.7.low = bf16[4,136,128]{2,1,0:T(8,128)(2,1)S(1)} collective-permute-done((bf16[4,136,128]{2,1,0:T(8,128)(2,1)S(1)}, bf16[4,136,128]{2,1,0:T(8,128)(2,1)S(1)}, u32[]{:S(2)}, u32[]{:S(2)}) %collective-permute-start.7) | collective-permute-done | bytes 139296 | tf_op jit(solution)/shard_map/ppermute | solution.py:438
  44.9 0.8 finish.1
  45.7 3.5 %collective-permute-start.11 = (bf16[8,32,256]{2,1,0:T(8,128)(2,1)S(1)}, bf16[8,32,256]{2,1,0:T(8,128)(2,1)S(1)}, u32[]{:S(2)}, u32[]{:S(2)}) collective-permute-start(bf16[8,32,256]{2,1,0:T(8,128)(2,1)S(1)} %bitcast.17), channel_id=1, source_target_pairs={{64,0},{80,16},{96,32},{112,48},{128,64},{144,80},{160,96},{176,11... | collective-permute-start | bytes 393224 | tf_op jit(solution)/shard_map/ppermute | solution.py:438
  49.2 1.8 %collective-permute-start.10 = (bf16[8,32,256]{2,1,0:T(8,128)(2,1)S(1)}, bf16[8,32,256]{2,1,0:T(8,128)(2,1)S(1)}, u32[]{:S(2)}, u32[]{:S(2)}) collective-permute-start(bf16[8,32,256]{2,1,0:T(8,128)(2,1)S(1)} %bitcast.18), channel_id=1, source_target_pairs={{0,64},{16,80},{32,96},{48,112},{64,128},{80,144},{96,160},{112,17... | collective-permute-start | bytes 393224 | tf_op jit(solution)/shard_map/ppermute | solution.py:438
  51.0 2.9 %collective-permute-done.11 = bf16[8,32,256]{2,1,0:T(8,128)(2,1)S(1)} collective-permute-done((bf16[8,32,256]{2,1,0:T(8,128)(2,1)S(1)}, bf16[8,32,256]{2,1,0:T(8,128)(2,1)S(1)}, u32[]{:S(2)}, u32[]{:S(2)}) %collective-permute-start.11) | collective-permute-done | bytes 131104 | tf_op jit(solution)/shard_map/ppermute | solution.py:438
  53.9 3.1 %collective-permute-done.10 = bf16[8,32,256]{2,1,0:T(8,128)(2,1)S(1)} collective-permute-done((bf16[8,32,256]{2,1,0:T(8,128)(2,1)S(1)}, bf16[8,32,256]{2,1,0:T(8,128)(2,1)S(1)}, u32[]{:S(2)}, u32[]{:S(2)}) %collective-permute-start.10) | collective-permute-done | bytes 131104 | tf_op jit(solution)/shard_map/ppermute | solution.py:438
  57.3 2.1 %collective-permute-start.12 = (bf16[8,4,768]{2,1,0:T(4,128)(2,1)S(1)}, bf16[8,4,768]{2,1,0:T(4,128)(2,1)S(1)}, u32[]{:S(2)}, u32[]{:S(2)}) collective-permute-start(bf16[8,4,768]{2,1,0:T(4,128)(2,1)S(1)} %get-tuple-element.45), channel_id=1, source_target_pairs={{0,16},{16,32},{32,48},{48,49},{49,33},{33,17},{17,1},{1,2},{2,18}... | collective-permute-start | bytes 147464 | tf_op jit(solution)/shard_map/ppermute | solution.py:438
  59.4 1.9 %collective-permute-done.13 = bf16[8,4,768]{2,1,0:T(4,128)(2,1)S(1)} collective-permute-done((bf16[8,4,768]{2,1,0:T(4,128)(2,1)S(1)}, bf16[8,4,768]{2,1,0:T(4,128)(2,1)S(1)}, u32[]{:S(2)}, u32[]{:S(2)}) %collective-permute-start.13) | collective-permute-done | bytes 49184 | tf_op jit(solution)/shard_map/ppermute | solution.py:438
  61.5 3.1 %collective-permute-start.15 = (bf16[4,40,768]{2,1,0:T(8,128)(2,1)S(1)}, bf16[4,40,768]{2,1,0:T(8,128)(2,1)S(1)}, u32[]{:S(2)}, u32[]{:S(2)}) collective-permute-start(bf16[4,40,768]{2,1,0:T(8,128)(2,1)S(1)} %pad_maximum_fusion.2), channel_id=1, source_target_pairs={{4,0},{8,4},{12,8},{0,12},{5,1},{9,5},{13,9},{1,13},{6,2},{10,6},{... | collective-permute-start | bytes 737288 | tf_op jit(solution)/shard_map/ppermute | solution.py:438
  65.2 2.2 %core.1 = (bf16[288,640]{1,0:T(8,128)(2,1)S(1)}, bf16[192,512]{1,0:T(8,128)(2,1)S(1)}, bf16[96,384]{1,0:T(8,128)(2,1)S(1)}) custom-call(bf16[384,768]{1,0:T(8,128)(2,1)S(1)} %bitcast.21, bf16[4,3,256,384]{3,2,1,0:T(8,128)(2,1)S(1)} %get-tuple-element.39.band, f32[4,128]{1,0:T(4,128)S(1)} %pad_maximum_fusion.5.bias), custom_call_target="tpu_custom_call" | custom-call | flops 1000000000 | bytes 1000000 | tf_op jit(solution)/shard_map/core/pallas_call | solution.py:363
  67.5 0.9 %collective-permute-done.15 = bf16[4,40,768]{2,1,0:T(8,128)(2,1)S(1)} collective-permute-done((bf16[4,40,768]{2,1,0:T(8,128)(2,1)S(1)}, bf16[4,40,768]{2,1,0:T(8,128)(2,1)S(1)}, u32[]{:S(2)}, u32[]{:S(2)}) %collective-permute-start.15) | collective-permute-done | bytes 245792 | tf_op jit(solution)/shard_map/ppermute | solution.py:438
  68.4 4.0 %collective-permute-done.14 = bf16[4,40,768]{2,1,0:T(8,128)(2,1)S(1)} collective-permute-done((bf16[4,40,768]{2,1,0:T(8,128)(2,1)S(1)}, bf16[4,40,768]{2,1,0:T(8,128)(2,1)S(1)}, u32[]{:S(2)}, u32[]{:S(2)}) %collective-permute-start.14) | collective-permute-done | bytes 245792 | tf_op jit(solution)/shard_map/ppermute | solution.py:438
  72.8 4.6 %convolve.1 = bf16[4,64,256]{2,1,0:T(8,128)(2,1)S(1)} custom-call(bf16[768,768]{1,0:T(8,128)(2,1)S(1)} %bitcast.15, bf16[288,640]{1,0:T(8,128)(2,1)S(1)} %get-tuple-element.40.core0, bf16[192,512]{1,0:T(8,128)(2,1)S(1)} %get-tuple-element.41.core1, bf16[96,384]{1,0:T(8,128)(2,1)S(1)} %get-tuple-element.42.core2, ...), custom_call_target="tpu_custom_call" | custom-call | tf_op jit(solution)/shard_map/convolve/pallas_call | solution.py:401
  77.4 1.8 %collective-permute-start.16 = (bf16[64,256]{1,0:T(8,128)(2,1)S(1)}, bf16[64,256]{1,0:T(8,128)(2,1)S(1)}, u32[]{:S(2)}, u32[]{:S(2)}) collective-permute-start(bf16[64,256]{1,0:T(8,128)(2,1)S(1)} %get-tuple-element.49), channel_id=1, source_target_pairs={{0,48},{16,0},{32,16},{48,32},{49,1},{33,49},{17,33},{1,17},{2,50}... | collective-permute-start | bytes 98312 | tf_op jit(solution)/shard_map/ppermute | solution.py:438
  79.2 2.4 %collective-permute-start.17 = (bf16[64,256]{1,0:T(8,128)(2,1)S(1)}, bf16[64,256]{1,0:T(8,128)(2,1)S(1)}, u32[]{:S(2)}, u32[]{:S(2)}) collective-permute-start(bf16[64,256]{1,0:T(8,128)(2,1)S(1)} %get-tuple-element.48), channel_id=1, source_target_pairs={{0,32},{16,48},{32,0},{48,16},{49,17},{33,1},{17,49},{1,33},{2,34}... | collective-permute-start | bytes 98312 | tf_op jit(solution)/shard_map/ppermute | solution.py:438
  81.6 3.0 %collective-permute-done.17.far = bf16[64,256]{1,0:T(8,128)(2,1)S(1)} collective-permute-done((bf16[64,256]{1,0:T(8,128)(2,1)S(1)}, bf16[64,256]{1,0:T(8,128)(2,1)S(1)}, u32[]{:S(2)}, u32[]{:S(2)}) %collective-permute-start.17) | collective-permute-done | bytes 32800 | tf_op jit(solution)/shard_map/ppermute | solution.py:438
  84.7 2.1 %collective-permute-done.18.low = bf16[64,256]{1,0:T(8,128)(2,1)S(1)} collective-permute-done((bf16[64,256]{1,0:T(8,128)(2,1)S(1)}, bf16[64,256]{1,0:T(8,128)(2,1)S(1)}, u32[]{:S(2)}, u32[]{:S(2)}) %collective-permute-start.18) | collective-permute-done | bytes 32800 | tf_op jit(solution)/shard_map/ppermute | solution.py:438
  86.7 1.1 %place.1 = bf16[512,128]{1,0:T(8,128)(2,1)} custom-call(bf16[64,256]{1,0:T(8,128)(2,1)S(1)} %get-tuple-element.50.own, bf16[64,256]{1,0:T(8,128)(2,1)S(1)} %collective-permute-done.16.high, bf16[64,256]{1,0:T(8,128)(2,1)S(1)} %collective-permute-done.17.far, bf16[64,256]{1,0:T(8,128)(2,1)S(1)} %collective-permute-done.18.low), custom_call_target="tpu_custom_call" | custom-call | tf_op jit(solution)/shard_map/place/pallas_call | solution.py:426
  (44 shorter events, 4.2 us)
Async XLA Ops:
  4.9 9.8 %collective-permute-start.3 = (bf16[8,136,128]{2,1,0:T(8,128)(2,1)S(1)}, bf16[8,136,128]{2,1,0:T(8,128)(2,1)S(1)}, u32[]{:S(2)}, u32[]{:S(2)}) collective-permute-start(bf16[8,136,128]{2,1,0:T(8,128)(2,1)S(1)} %get-tuple-element.31), channel_id=1, source_target_pairs={{0,16},{16,32},{32,48},{48,0},{49,33},{33,17},{17,1},{1,49},{2,18}... | collective-permute-start | bytes 835592 | tf_op jit(solution)/shard_map/ppermute | solution.py:438
  11.3 9.2 %collective-permute-start.1 = (bf16[8,136,128]{2,1,0:T(8,128)(2,1)S(1)}, bf16[8,136,128]{2,1,0:T(8,128)(2,1)S(1)}, u32[]{:S(2)}, u32[]{:S(2)}) collective-permute-start(bf16[8,136,128]{2,1,0:T(8,128)(2,1)S(1)} %get-tuple-element.27), channel_id=1, source_target_pairs={{0,48},{16,0},{32,16},{48,32},{49,1},{33,49},{17,33},{1,17},{2,50}... | collective-permute-start | bytes 835592 | tf_op jit(solution)/shard_map/ppermute | solution.py:438
  13.1 13.4 %collective-permute-start.5 = (bf16[8,136,128]{2,1,0:T(8,128)(2,1)S(1)}, bf16[8,136,128]{2,1,0:T(8,128)(2,1)S(1)}, u32[]{:S(2)}, u32[]{:S(2)}) collective-permute-start(bf16[8,136,128]{2,1,0:T(8,128)(2,1)S(1)} %get-tuple-element.32), channel_id=1, source_target_pairs={{0,48},{16,0},{32,16},{48,32},{49,1},{33,49},{17,33},{1,17},{2,50}... | collective-permute-start | bytes 835592 | tf_op jit(solution)/shard_map/ppermute | solution.py:438
  14.9 11.5 %collective-permute-start.4 = (bf16[8,136,128]{2,1,0:T(8,128)(2,1)S(1)}, bf16[8,136,128]{2,1,0:T(8,128)(2,1)S(1)}, u32[]{:S(2)}, u32[]{:S(2)}) collective-permute-start(bf16[8,136,128]{2,1,0:T(8,128)(2,1)S(1)} %merge.6), channel_id=1, source_target_pairs={{0,16},{16,32},{32,48},{48,0},{49,33},{33,17},{17,1},{1,49},{2,18}... | collective-permute-start | bytes 835592 | tf_op jit(solution)/shard_map/ppermute | solution.py:438
  15.5 17.1 %collective-permute-start = (bf16[8,136,128]{2,1,0:T(8,128)(2,1)S(1)}, bf16[8,136,128]{2,1,0:T(8,128)(2,1)S(1)}, u32[]{:S(2)}, u32[]{:S(2)}) collective-permute-start(bf16[8,136,128]{2,1,0:T(8,128)(2,1)S(1)} %get-tuple-element.25), channel_id=1, source_target_pairs={{0,16},{16,32},{32,48},{48,0},{49,33},{33,17},{17,1},{1,49},{2,18}... | collective-permute-start | bytes 835592 | tf_op jit(solution)/shard_map/ppermute | solution.py:438
  20.8 11.8 %collective-permute-start.2 = (bf16[8,136,128]{2,1,0:T(8,128)(2,1)S(1)}, bf16[8,136,128]{2,1,0:T(8,128)(2,1)S(1)}, u32[]{:S(2)}, u32[]{:S(2)}) collective-permute-start(bf16[8,136,128]{2,1,0:T(8,128)(2,1)S(1)} %merge.4), channel_id=1, source_target_pairs={{0,48},{16,0},{32,16},{48,32},{49,1},{33,49},{17,33},{1,17},{2,50}... | collective-permute-start | bytes 835592 | tf_op jit(solution)/shard_map/ppermute | solution.py:438
  26.5 13.8 %copy-start = (bf16[4,3,3,3,64,64]{5,4,3,2,1,0:T(8,128)(2,1)S(1)}, bf16[4,3,3,3,64,64]{5,4,3,2,1,0:T(8,128)(2,1)}, u32[]{:S(2)}) copy-start(bf16[4,3,3,3,64,64]{5,4,3,2,1,0:T(8,128)(2,1)} %param.16) | copy-start | bytes 2654212
  26.5 13.8 %copy-start.1 = (bf16[64,64]{1,0:T(8,128)(2,1)S(1)}, bf16[64,64]{1,0:T(8,128)(2,1)}, u32[]{:S(2)}) copy-start(bf16[64,64]{1,0:T(8,128)(2,1)} %wv.1) | copy-start | bytes 24580
  26.5 13.8 %copy-start.2 = (bf16[64,64]{1,0:T(8,128)(2,1)S(1)}, bf16[64,64]{1,0:T(8,128)(2,1)}, u32[]{:S(2)}) copy-start(bf16[64,64]{1,0:T(8,128)(2,1)} %wo.1) | copy-start | bytes 24580
  26.8 8.8 %collective-permute-start.6 = (bf16[2,136,128]{2,1,0:T(8,128)(2,1)S(1)}, bf16[2,136,128]{2,1,0:T(8,128)(2,1)S(1)}, u32[]{:S(2)}, u32[]{:S(2)}) collective-permute-start(bf16[2,136,128]{2,1,0:T(8,128)(2,1)S(1)} %get-tuple-element.34), channel_id=1, source_target_pairs={{0,64},{16,80},{32,96},{48,112},{64,128},{80,144},{96,160},{112,17... | collective-permute-start | bytes 208904 | tf_op jit(solution)/shard_map/ppermute | solution.py:438
  30.3 6.5 %collective-permute-start.8 = (bf16[2,136,128]{2,1,0:T(8,128)(2,1)S(1)}, bf16[2,136,128]{2,1,0:T(8,128)(2,1)S(1)}, u32[]{:S(2)}, u32[]{:S(2)}) collective-permute-start(bf16[2,136,128]{2,1,0:T(8,128)(2,1)S(1)} %get-tuple-element.36), channel_id=1, source_target_pairs={{64,0},{80,16},{96,32},{112,48},{128,64},{144,80},{160,96},{176,11... | collective-permute-start | bytes 208904 | tf_op jit(solution)/shard_map/ppermute | solution.py:438
  35.8 8.7 %collective-permute-start.7 = (bf16[4,136,128]{2,1,0:T(8,128)(2,1)S(1)}, bf16[4,136,128]{2,1,0:T(8,128)(2,1)S(1)}, u32[]{:S(2)}, u32[]{:S(2)}) collective-permute-start(bf16[4,136,128]{2,1,0:T(8,128)(2,1)S(1)} %lift.2), channel_id=1, source_target_pairs={{0,64},{16,80},{32,96},{48,112},{64,128},{80,144},{96,160},{112,17... | collective-permute-start | bytes 417800 | tf_op jit(solution)/shard_map/ppermute | solution.py:438
  37.0 7.9 %collective-permute-start.9 = (bf16[4,136,128]{2,1,0:T(8,128)(2,1)S(1)}, bf16[4,136,128]{2,1,0:T(8,128)(2,1)S(1)}, u32[]{:S(2)}, u32[]{:S(2)}) collective-permute-start(bf16[4,136,128]{2,1,0:T(8,128)(2,1)S(1)} %lift.3), channel_id=1, source_target_pairs={{64,0},{80,16},{96,32},{112,48},{128,64},{144,80},{160,96},{176,11... | collective-permute-start | bytes 417800 | tf_op jit(solution)/shard_map/ppermute | solution.py:438
  40.3 8.9 %copy-start.3 = (f32[4,64]{1,0:T(4,128)S(1)}, f32[4,64]{1,0:T(4,128)}, u32[]{:S(2)}) copy-start(f32[4,64]{1,0:T(4,128)} %param.17) | copy-start | bytes 3076
  45.7 8.3 %collective-permute-start.11 = (bf16[8,32,256]{2,1,0:T(8,128)(2,1)S(1)}, bf16[8,32,256]{2,1,0:T(8,128)(2,1)S(1)}, u32[]{:S(2)}, u32[]{:S(2)}) collective-permute-start(bf16[8,32,256]{2,1,0:T(8,128)(2,1)S(1)} %bitcast.17), channel_id=1, source_target_pairs={{64,0},{80,16},{96,32},{112,48},{128,64},{144,80},{160,96},{176,11... | collective-permute-start | bytes 393224 | tf_op jit(solution)/shard_map/ppermute | solution.py:438
  49.2 7.8 %collective-permute-start.10 = (bf16[8,32,256]{2,1,0:T(8,128)(2,1)S(1)}, bf16[8,32,256]{2,1,0:T(8,128)(2,1)S(1)}, u32[]{:S(2)}, u32[]{:S(2)}) collective-permute-start(bf16[8,32,256]{2,1,0:T(8,128)(2,1)S(1)} %bitcast.18), channel_id=1, source_target_pairs={{0,64},{16,80},{32,96},{48,112},{64,128},{80,144},{96,160},{112,17... | collective-permute-start | bytes 393224 | tf_op jit(solution)/shard_map/ppermute | solution.py:438
  57.1 4.2 %collective-permute-start.13 = (bf16[8,4,768]{2,1,0:T(4,128)(2,1)S(1)}, bf16[8,4,768]{2,1,0:T(4,128)(2,1)S(1)}, u32[]{:S(2)}, u32[]{:S(2)}) collective-permute-start(bf16[8,4,768]{2,1,0:T(4,128)(2,1)S(1)} %get-tuple-element.46), channel_id=1, source_target_pairs={{16,0},{32,16},{48,32},{49,48},{33,49},{17,33},{1,17},{2,1},{18,2}... | collective-permute-start | bytes 147464 | tf_op jit(solution)/shard_map/ppermute | solution.py:438
  57.3 4.1 %collective-permute-start.12 = (bf16[8,4,768]{2,1,0:T(4,128)(2,1)S(1)}, bf16[8,4,768]{2,1,0:T(4,128)(2,1)S(1)}, u32[]{:S(2)}, u32[]{:S(2)}) collective-permute-start(bf16[8,4,768]{2,1,0:T(4,128)(2,1)S(1)} %get-tuple-element.45), channel_id=1, source_target_pairs={{0,16},{16,32},{32,48},{48,49},{49,33},{33,17},{17,1},{1,2},{2,18}... | collective-permute-start | bytes 147464 | tf_op jit(solution)/shard_map/ppermute | solution.py:438
  61.5 6.8 %collective-permute-start.15 = (bf16[4,40,768]{2,1,0:T(8,128)(2,1)S(1)}, bf16[4,40,768]{2,1,0:T(8,128)(2,1)S(1)}, u32[]{:S(2)}, u32[]{:S(2)}) collective-permute-start(bf16[4,40,768]{2,1,0:T(8,128)(2,1)S(1)} %pad_maximum_fusion.2), channel_id=1, source_target_pairs={{4,0},{8,4},{12,8},{0,12},{5,1},{9,5},{13,9},{1,13},{6,2},{10,6},{... | collective-permute-start | bytes 737288 | tf_op jit(solution)/shard_map/ppermute | solution.py:438
  64.7 7.7 %collective-permute-start.14 = (bf16[4,40,768]{2,1,0:T(8,128)(2,1)S(1)}, bf16[4,40,768]{2,1,0:T(8,128)(2,1)S(1)}, u32[]{:S(2)}, u32[]{:S(2)}) collective-permute-start(bf16[4,40,768]{2,1,0:T(8,128)(2,1)S(1)} %pad_maximum_fusion.1), channel_id=1, source_target_pairs={{0,4},{4,8},{8,12},{12,0},{1,5},{5,9},{9,13},{13,1},{2,6},{6,10},{... | collective-permute-start | bytes 737288 | tf_op jit(solution)/shard_map/ppermute | solution.py:438
  77.4 4.2 %collective-permute-start.16 = (bf16[64,256]{1,0:T(8,128)(2,1)S(1)}, bf16[64,256]{1,0:T(8,128)(2,1)S(1)}, u32[]{:S(2)}, u32[]{:S(2)}) collective-permute-start(bf16[64,256]{1,0:T(8,128)(2,1)S(1)} %get-tuple-element.49), channel_id=1, source_target_pairs={{0,48},{16,0},{32,16},{48,32},{49,1},{33,49},{17,33},{1,17},{2,50}... | collective-permute-start | bytes 98312 | tf_op jit(solution)/shard_map/ppermute | solution.py:438
  79.2 5.4 %collective-permute-start.17 = (bf16[64,256]{1,0:T(8,128)(2,1)S(1)}, bf16[64,256]{1,0:T(8,128)(2,1)S(1)}, u32[]{:S(2)}, u32[]{:S(2)}) collective-permute-start(bf16[64,256]{1,0:T(8,128)(2,1)S(1)} %get-tuple-element.48), channel_id=1, source_target_pairs={{0,32},{16,48},{32,0},{48,16},{49,17},{33,1},{17,49},{1,33},{2,34}... | collective-permute-start | bytes 98312 | tf_op jit(solution)/shard_map/ppermute | solution.py:438
  81.6 5.1 %collective-permute-start.18 = (bf16[64,256]{1,0:T(8,128)(2,1)S(1)}, bf16[64,256]{1,0:T(8,128)(2,1)S(1)}, u32[]{:S(2)}, u32[]{:S(2)}) collective-permute-start(bf16[64,256]{1,0:T(8,128)(2,1)S(1)} %get-tuple-element.47), channel_id=1, source_target_pairs={{0,16},{16,32},{32,48},{48,0},{49,33},{33,17},{17,1},{1,49},{2,18}... | collective-permute-start | bytes 98312 | tf_op jit(solution)/shard_map/ppermute | solution.py:438

commit v8 on v6

--- a/solution.py
+++ b/solution.py
@@ -40,16 +40,15 @@
     return hi, mid, m - hi - mid
 
 
-def attend_kernel(half, feat_at, embed_at, seen_at, wq_at, wk_at, *refs):
+def attend_kernel(ahead, feat_at, embed_at, seen_at, wq_at, wk_at, *refs):
     outs, feat, embed, seen, wq, wk, key0, key1, wide0, wide1, sems = refs[:4], *refs[4:]
     steps, frames, n = feat.shape[:3]
     me = lax.axis_index("frame")
     zh, xi = me // 4, me % 4
-    turn = (128 - 32 * xi) & 127
+    turn = (128 - 32 * zh) & 127
 
     def copies(s):
-        block = 1 + 2 * half + s * n // 4
-        z = pl.ds(((block + zh) & 3) * 4 + s * n % 4, n)
+        z = pl.ds(((xi + ahead[s // 2]) & 3) * 4 + s % 2 * n, n)
         return [
             pltpu.make_async_copy(embed_at.at[z], embed.at[s], sems.at[s, 0]),
             pltpu.make_async_copy(feat_at.at[:, z], feat.at[s], sems.at[s, 1]),
@@ -102,8 +101,10 @@
 
         def put(g, tiles):
             tiles = [pltpu.roll(t, turn, 1) for t in tiles]
-            for out, tile in zip(outs, lane_blocks(tiles)):
-                out[s * n + p, 8 * g : 8 * g + 8, :] = tile.astype(bf16)
+            for q, tile in enumerate(lane_blocks(tiles)):
+                unit = (q + 1) % 2 * 4 + s % 2 * n + p
+                out = outs[s // 2 * 2 + (0 if q in (1, 2) else 1)]
+                out[unit, 8 * g : 8 * g + 8, :] = tile.astype(bf16)
 
         for g in range(16):
             rows = slice(32 * g, 32 * g + 32)
@@ -124,7 +125,7 @@
             plane(s, p)
 
 
-def attend(half, feat, embed, visible, w_query, w_key):
+def attend(ahead, feat, embed, visible, w_query, w_key):
     frames, planes, rows = feat.shape[:3]
     c = w_key.shape[0]
     n = 2
@@ -132,7 +133,7 @@
     steps = count // n
     hbm = pl.BlockSpec(memory_space=pltpu.HBM)
     return pl.pallas_call(
-        functools.partial(attend_kernel, half),
+        functools.partial(attend_kernel, ahead),
         out_shape=[jax.ShapeDtypeStruct((count, 136, 128), bf16)] * 4,
         in_specs=[hbm] * 5,
         out_specs=[VM] * 4,
@@ -306,8 +307,8 @@
 
 
 def row_mask(mask):
-    xi = lax.axis_index("frame") % 4
-    x0, y0 = lax.axis_index("bx") * 8 - halo, lax.axis_index("by") * 128 + xi * 32 - halo
+    zh = lax.axis_index("frame") // 4
+    x0, y0 = lax.axis_index("bx") * 8 - halo, lax.axis_index("by") * 128 + zh * 32 - halo
     y = lax.broadcasted_iota(jnp.int32, (stride, 128), 0) + y0
     y_ok = (y >= 0) & (y < 512)
     for x in range(16):
@@ -329,7 +330,7 @@
 
 
 def keep(h, dst, shift, lines, t, layer, mask):
-    z0 = lax.axis_index("frame") // 4 * 4 - halo
+    z0 = lax.axis_index("frame") % 4 * 4 - halo
     lane = lax.broadcasted_iota(jnp.int32, (1, 128), 1)
     z = z0 + layer + 1 + 2 * t + lane // 64
     z_ok = jnp.where((z >= 0) & (z < 16), 1.0, 0.0)
@@ -371,7 +372,7 @@
 
 
 def conv_kernel(block, core0, core1, core2, band, bias, out, buf0, buf1, mask):
-    xi = lax.axis_index("frame") % 4
+    zh = lax.axis_index("frame") // 4
     row_mask(mask)
     src = block
     for layer, (dst, done) in enumerate(((buf0, core0), (buf1, core1), (buf0, core2))):
@@ -388,7 +389,7 @@
         tiles = [h[stride * x : stride * x + 32] for x in range(8)]
         whole = jnp.concatenate(tiles, axis=0).T.astype(bf16)
         for i in range(2):
-            out[(2 * t + i - xi) & 3] = whole[64 * i : 64 * i + 64]
+            out[(2 * t + i - zh) & 3] = whole[64 * i : 64 * i + 64]
 
 
 def convolve(block, cores, band, bias):
@@ -445,35 +446,35 @@
     frames, planes, c = features.shape[:3]
     feat = features.reshape(frames, planes, c * 8, 128)
     embed = voxel_embed.reshape(planes, c * 8, 128)
-    a0, a1, a2, a3 = attend(0, feat, embed, visible, w_query, w_key)
-    from_low = send(a2, up)
-    high_a = send(a3, down)
-    b0, b1, b2, b3 = attend(1, feat, embed, visible, w_query, w_key)
+    s2a, s2b, s1a, s1b = attend((2, 1), feat, embed, visible, w_query, w_key)
+    from_low = send(s2a, up)
+    from_high = send(s2b, down)
+    s3a, s3b, s0a, s0b = attend((3, 0), feat, embed, visible, w_query, w_key)
     band, wide_v, wide_o = weights(conv_weight, w_value, w_out)
-    from_high = send(b2, down)
-    low_b = send(b1, up)
-    low_a = send(merge([a1, from_low], [8])[0], up)
-    high_b = send(merge([b3, from_high], [8])[0], down)
-    z1, z2a, z2b = merge([a0, low_a, high_a], [4, 2, 2])
+    high_a = send(s3a, down)
+    low_a = send(merge([s1a, from_low], [8])[0], up)
+    high_b = send(merge([s3b, from_high], [8])[0], down)
+    low_b = send(s1b, up)
+    z1, z2a, z2b = merge([s0a, low_a, high_a], [4, 2, 2])
     from_low = send(z2a, z_up)
     from_high = send(z2b, z_down)
     low = send(lift(0, z1, from_low), z_up)
-    z3, z0 = merge([b0, low_b, high_b], [4, 4])
+    z3, z0 = merge([s0b, low_b, high_b], [4, 4])
     high = send(lift(2, z3, from_high), z_down)
     hidden = finish(z0, low, high, wide_v, wide_o).reshape(8, 32, 256)
 
     me = lax.axis_index("frame")
     zh, xi = me // 4, me % 4
-    below = only(zh > 0, send(hidden, z_up))
-    above = only(zh < 3, send(hidden, z_down))
+    below = only(xi > 0, send(hidden, up))
+    above = only(xi < 3, send(hidden, down))
     hidden = jnp.concatenate([below, hidden, above], axis=2)
 
-    def where_is(z, chunk):
-        return (4 * z + chunk % 4) * 4 + chunk // 4
-
-    y_next = [(where_is(z, k), where_is(z, (k + 1) % 16)) for z in range(4) for k in range(16)]
+    def where_is(x, chunk):
+        return (4 * (chunk % 4) + x) * 4 + chunk // 4
+
+    y_next = [(where_is(x, k), where_is(x, (k + 1) % 16)) for x in around for k in range(16)]
     y_prev = [(j, i) for i, j in y_next]
-    chunk = lax.axis_index("by") * 4 + xi
+    chunk = lax.axis_index("by") * 4 + zh
     left = only(chunk > 0, send(hidden[:, -halo:], y_next, ("frame", "by")))
     right = only(chunk < 15, send(hidden[:, :halo], y_prev, ("frame", "by")))
     first, second = (
@@ -494,10 +495,11 @@
 
     cores = core(lines(first, second), band, bias)
     out = convolve(lines(front, first, second, back), cores, band, bias)
-    low = send(out[1], up)
-    high = send(out[3], down)
-    far = send(out[2], x_by(2))
-    return place(out[0], high, far, low).reshape(1, c, 8, 128)
+    pieces = [
+        send(out[r], [(4 * z + x, 4 * x + (z + r) % 4) for z in around for x in around])
+        for r in around
+    ]
+    return place(pieces[0], pieces[3], pieces[2], pieces[1]).reshape(1, c, 8, 128)
 
 
 def solution(mesh):

time: 90.4 us -> 97.2 us (1.075)
  the two profiles are of different devices: /device:TPU:64 before, /device:TPU:2 now
where the time goes in v8:
time: 97.2 us; the launch traced here: 97.1 us
  starting transfers between devices  40 us (41%)
  waiting for transfers between devices  35.1 us (36%)
  Pallas kernels  20.8 us (21%)
    ppermute x20, starting transfers between devices, send(): return lax.ppermute(v, axis, way)  40 us
    ppermute x20, waiting for transfers between devices, send(): return lax.ppermute(v, axis, way)  35.1 us
    pallas_call x2, Pallas kernels, attend(): pl.pallas_call(functools.partial(attend_kernel, ahead), out_shape=[jax.Sh...  9.7 us
    pallas_call x1, Pallas kernels, convolve(): pl.pallas_call(conv_kernel, out_shape=jax.ShapeDtypeStruct((4, 64, 256),...  4.58 us
    pallas_call x1, Pallas kernels, core(): pl.pallas_call(core_kernel, out_shape=[jax.ShapeDtypeStruct((stride * (6...  2.24 us
  transfers between devices with their start and end apart: 20, of which 13 were waited for; matrix products, arithmetic and copies ran while one was open for 0% of the time, Pallas kernels for 10%

profile of v8, /device:TPU:2, one launch (start us, length us, event | category | flops | bytes accessed | tf_op | source)
XLA Modules:
  0.0 97.1 jit_solution(14265860512046161657)
XLA Ops:
  0.0 4.9 %attend.3 = (bf16[8,136,128]{2,1,0:T(8,128)(2,1)S(1)}, bf16[8,136,128]{2,1,0:T(8,128)(2,1)S(1)}, bf16[8,136,128]{2,1,0:T(8,128)(2,1)S(1)}, bf16[8,136,128]{2,1,0:T(8,128)(2,1)S(1)}) custom-call(bf16[4,16,512,128]{3,2,1,0:T(8,128)(2,1)} %bitcast.22, bf16[16,512,128]{2,1,0:T(8,128)(2,1)} %bitcast.24, s32[4,16,8,128]{3,2,1,0:T(8,128)} %seen_at.3, ...), custom_call_target="tpu_custom_call" | custom-call | flops 100000000 | bytes 12582912 | tf_op jit(solution)/shard_map/attend/pallas_call | solution.py:135
  4.9 1.6 %collective-permute-start.3 = (bf16[8,136,128]{2,1,0:T(8,128)(2,1)S(1)}, bf16[8,136,128]{2,1,0:T(8,128)(2,1)S(1)}, u32[]{:S(2)}, u32[]{:S(2)}) collective-permute-start(bf16[8,136,128]{2,1,0:T(8,128)(2,1)S(1)} %get-tuple-element.31), channel_id=1, source_target_pairs={{0,16},{16,32},{32,48},{48,0},{64,80},{80,96},{96,112},{112,64},{1... | collective-permute-start | bytes 835592 | tf_op jit(solution)/shard_map/ppermute | solution.py:433
  6.4 0.8 collective-permute-start.1
  7.3 4.8 %attend.2 = (bf16[8,136,128]{2,1,0:T(8,128)(2,1)S(1)}, bf16[8,136,128]{2,1,0:T(8,128)(2,1)S(1)}, bf16[8,136,128]{2,1,0:T(8,128)(2,1)S(1)}, bf16[8,136,128]{2,1,0:T(8,128)(2,1)S(1)}) custom-call(bf16[4,16,512,128]{3,2,1,0:T(8,128)(2,1)} %bitcast.23, bf16[16,512,128]{2,1,0:T(8,128)(2,1)} %bitcast.25, s32[4,16,8,128]{3,2,1,0:T(8,128)} %seen_at.3, ...), custom_call_target="tpu_custom_call" | custom-call | flops 100000000 | bytes 12582912 | tf_op jit(solution)/shard_map/attend/pallas_call | solution.py:135
  12.1 3.2 %collective-permute-start.5 = (bf16[8,136,128]{2,1,0:T(8,128)(2,1)S(1)}, bf16[8,136,128]{2,1,0:T(8,128)(2,1)S(1)}, u32[]{:S(2)}, u32[]{:S(2)}) collective-permute-start(bf16[8,136,128]{2,1,0:T(8,128)(2,1)S(1)} %get-tuple-element.32), channel_id=1, source_target_pairs={{0,48},{16,0},{32,16},{48,32},{64,112},{80,64},{96,80},{112,96},{1... | collective-permute-start | bytes 835592 | tf_op jit(solution)/shard_map/ppermute | solution.py:433
  16.6 1.5 %collective-permute-start.2 = (bf16[8,136,128]{2,1,0:T(8,128)(2,1)S(1)}, bf16[8,136,128]{2,1,0:T(8,128)(2,1)S(1)}, u32[]{:S(2)}, u32[]{:S(2)}) collective-permute-start(bf16[8,136,128]{2,1,0:T(8,128)(2,1)S(1)} %merge.4), channel_id=1, source_target_pairs={{0,48},{16,0},{32,16},{48,32},{64,112},{80,64},{96,80},{112,96},{1... | collective-permute-start | bytes 835592 | tf_op jit(solution)/shard_map/ppermute | solution.py:433
  18.2 3.9 %collective-permute-done.5.refs_2_ = bf16[8,136,128]{2,1,0:T(8,128)(2,1)S(1)} collective-permute-done((bf16[8,136,128]{2,1,0:T(8,128)(2,1)S(1)}, bf16[8,136,128]{2,1,0:T(8,128)(2,1)S(1)}, u32[]{:S(2)}, u32[]{:S(2)}) %collective-permute-start.5) | collective-permute-done | bytes 278560 | tf_op jit(solution)/shard_map/ppermute | solution.py:433
  22.0 2.4 %collective-permute-done.4.refs_1_ = bf16[8,136,128]{2,1,0:T(8,128)(2,1)S(1)} collective-permute-done((bf16[8,136,128]{2,1,0:T(8,128)(2,1)S(1)}, bf16[8,136,128]{2,1,0:T(8,128)(2,1)S(1)}, u32[]{:S(2)}, u32[]{:S(2)}) %collective-permute-start.4) | collective-permute-done | bytes 278560 | tf_op jit(solution)/shard_map/ppermute | solution.py:433
  24.8 2.6 %collective-permute-start.6 = (bf16[2,136,128]{2,1,0:T(8,128)(2,1)S(1)}, bf16[2,136,128]{2,1,0:T(8,128)(2,1)S(1)}, u32[]{:S(2)}, u32[]{:S(2)}) collective-permute-start(bf16[2,136,128]{2,1,0:T(8,128)(2,1)S(1)} %get-tuple-element.34), channel_id=1, source_target_pairs={{0,64},{16,80},{32,96},{48,112},{64,128},{80,144},{96,160},{112,17... | collective-permute-start | bytes 208904 | tf_op jit(solution)/shard_map/ppermute | solution.py:433
  27.4 3.1 %collective-permute-start.8 = (bf16[2,136,128]{2,1,0:T(8,128)(2,1)S(1)}, bf16[2,136,128]{2,1,0:T(8,128)(2,1)S(1)}, u32[]{:S(2)}, u32[]{:S(2)}) collective-permute-start(bf16[2,136,128]{2,1,0:T(8,128)(2,1)S(1)} %get-tuple-element.36), channel_id=1, source_target_pairs={{64,0},{80,16},{96,32},{112,48},{128,64},{144,80},{160,96},{176,11... | collective-permute-start | bytes 208904 | tf_op jit(solution)/shard_map/ppermute | solution.py:433
  30.9 1.9 %collective-permute-done.6.came = bf16[2,136,128]{2,1,0:T(8,128)(2,1)S(1)} collective-permute-done((bf16[2,136,128]{2,1,0:T(8,128)(2,1)S(1)}, bf16[2,136,128]{2,1,0:T(8,128)(2,1)S(1)}, u32[]{:S(2)}, u32[]{:S(2)}) %collective-permute-start.6) | collective-permute-done | bytes 69664 | tf_op jit(solution)/shard_map/ppermute | solution.py:433
  33.0 1.7 %collective-permute-start.7 = (bf16[4,136,128]{2,1,0:T(8,128)(2,1)S(1)}, bf16[4,136,128]{2,1,0:T(8,128)(2,1)S(1)}, u32[]{:S(2)}, u32[]{:S(2)}) collective-permute-start(bf16[4,136,128]{2,1,0:T(8,128)(2,1)S(1)} %lift.2), channel_id=1, source_target_pairs={{0,64},{16,80},{32,96},{48,112},{64,128},{80,144},{96,160},{112,17... | collective-permute-start | bytes 417800 | tf_op jit(solution)/shard_map/ppermute | solution.py:433
  35.1 2.5 %collective-permute-start.9 = (bf16[4,136,128]{2,1,0:T(8,128)(2,1)S(1)}, bf16[4,136,128]{2,1,0:T(8,128)(2,1)S(1)}, u32[]{:S(2)}, u32[]{:S(2)}) collective-permute-start(bf16[4,136,128]{2,1,0:T(8,128)(2,1)S(1)} %lift.3), channel_id=1, source_target_pairs={{64,0},{80,16},{96,32},{112,48},{128,64},{144,80},{160,96},{176,11... | collective-permute-start | bytes 417800 | tf_op jit(solution)/shard_map/ppermute | solution.py:433
  37.7 0.9 weights.1
  38.5 1.8 %collective-permute-done.7.low = bf16[4,136,128]{2,1,0:T(8,128)(2,1)S(1)} collective-permute-done((bf16[4,136,128]{2,1,0:T(8,128)(2,1)S(1)}, bf16[4,136,128]{2,1,0:T(8,128)(2,1)S(1)}, u32[]{:S(2)}, u32[]{:S(2)}) %collective-permute-start.7) | collective-permute-done | bytes 139296 | tf_op jit(solution)/shard_map/ppermute | solution.py:433
  40.3 4.0 %collective-permute-done.9.high = bf16[4,136,128]{2,1,0:T(8,128)(2,1)S(1)} collective-permute-done((bf16[4,136,128]{2,1,0:T(8,128)(2,1)S(1)}, bf16[4,136,128]{2,1,0:T(8,128)(2,1)S(1)}, u32[]{:S(2)}, u32[]{:S(2)}) %collective-permute-start.9) | collective-permute-done | bytes 139296 | tf_op jit(solution)/shard_map/ppermute | solution.py:433
  45.2 2.9 %collective-permute-start.11 = (bf16[8,32,256]{2,1,0:T(8,128)(2,1)S(1)}, bf16[8,32,256]{2,1,0:T(8,128)(2,1)S(1)}, u32[]{:S(2)}, u32[]{:S(2)}) collective-permute-start(bf16[8,32,256]{2,1,0:T(8,128)(2,1)S(1)} %bitcast.17), channel_id=1, source_target_pairs={{0,48},{16,0},{32,16},{48,32},{64,112},{80,64},{96,80},{112,96},{1... | collective-permute-start | bytes 393224 | tf_op jit(solution)/shard_map/ppermute | solution.py:433
  48.2 2.4 %collective-permute-done.11 = bf16[8,32,256]{2,1,0:T(8,128)(2,1)S(1)} collective-permute-done((bf16[8,32,256]{2,1,0:T(8,128)(2,1)S(1)}, bf16[8,32,256]{2,1,0:T(8,128)(2,1)S(1)}, u32[]{:S(2)}, u32[]{:S(2)}) %collective-permute-start.11) | collective-permute-done | bytes 131104 | tf_op jit(solution)/shard_map/ppermute | solution.py:433
  50.6 2.5 %collective-permute-done.10 = bf16[8,32,256]{2,1,0:T(8,128)(2,1)S(1)} collective-permute-done((bf16[8,32,256]{2,1,0:T(8,128)(2,1)S(1)}, bf16[8,32,256]{2,1,0:T(8,128)(2,1)S(1)}, u32[]{:S(2)}, u32[]{:S(2)}) %collective-permute-start.10) | collective-permute-done | bytes 131104 | tf_op jit(solution)/shard_map/ppermute | solution.py:433
  53.3 5.0 %collective-permute-start.12 = (bf16[8,4,768]{2,1,0:T(4,128)(2,1)S(1)}, bf16[8,4,768]{2,1,0:T(4,128)(2,1)S(1)}, u32[]{:S(2)}, u32[]{:S(2)}) collective-permute-start(bf16[8,4,768]{2,1,0:T(4,128)(2,1)S(1)} %get-tuple-element.45), channel_id=1, source_target_pairs={{0,64},{64,128},{128,192},{192,1},{1,65},{65,129},{129,193},{193,2... | collective-permute-start | bytes 147464 | tf_op jit(solution)/shard_map/ppermute | solution.py:433
  58.3 1.9 %collective-permute-done.13 = bf16[8,4,768]{2,1,0:T(4,128)(2,1)S(1)} collective-permute-done((bf16[8,4,768]{2,1,0:T(4,128)(2,1)S(1)}, bf16[8,4,768]{2,1,0:T(4,128)(2,1)S(1)}, u32[]{:S(2)}, u32[]{:S(2)}) %collective-permute-start.13) | collective-permute-done | bytes 49184 | tf_op jit(solution)/shard_map/ppermute | solution.py:433
  60.5 3.1 %collective-permute-start.15 = (bf16[4,40,768]{2,1,0:T(8,128)(2,1)S(1)}, bf16[4,40,768]{2,1,0:T(8,128)(2,1)S(1)}, u32[]{:S(2)}, u32[]{:S(2)}) collective-permute-start(bf16[4,40,768]{2,1,0:T(8,128)(2,1)S(1)} %pad_maximum_fusion.2), channel_id=1, source_target_pairs={{4,0},{8,4},{12,8},{0,12},{5,1},{9,5},{13,9},{1,13},{6,2},{10,6},{... | collective-permute-start | bytes 737288 | tf_op jit(solution)/shard_map/ppermute | solution.py:433
  64.2 2.2 %core.1 = (bf16[288,640]{1,0:T(8,128)(2,1)S(1)}, bf16[192,512]{1,0:T(8,128)(2,1)S(1)}, bf16[96,384]{1,0:T(8,128)(2,1)S(1)}) custom-call(bf16[384,768]{1,0:T(8,128)(2,1)S(1)} %bitcast.21, bf16[4,3,256,384]{3,2,1,0:T(8,128)(2,1)S(1)} %get-tuple-element.39.band, f32[4,128]{1,0:T(4,128)S(1)} %pad_maximum_fusion.5.bias), custom_call_target="tpu_custom_call" | custom-call | flops 1000000000 | bytes 1000000 | tf_op jit(solution)/shard_map/core/pallas_call | solution.py:360
  66.4 3.3 %collective-permute-done.15 = bf16[4,40,768]{2,1,0:T(8,128)(2,1)S(1)} collective-permute-done((bf16[4,40,768]{2,1,0:T(8,128)(2,1)S(1)}, bf16[4,40,768]{2,1,0:T(8,128)(2,1)S(1)}, u32[]{:S(2)}, u32[]{:S(2)}) %collective-permute-start.15) | collective-permute-done | bytes 245792 | tf_op jit(solution)/shard_map/ppermute | solution.py:433
  69.7 3.8 %collective-permute-done.14 = bf16[4,40,768]{2,1,0:T(8,128)(2,1)S(1)} collective-permute-done((bf16[4,40,768]{2,1,0:T(8,128)(2,1)S(1)}, bf16[4,40,768]{2,1,0:T(8,128)(2,1)S(1)}, u32[]{:S(2)}, u32[]{:S(2)}) %collective-permute-start.14) | collective-permute-done | bytes 245792 | tf_op jit(solution)/shard_map/ppermute | solution.py:433
  73.8 4.6 %convolve.1 = bf16[4,64,256]{2,1,0:T(8,128)(2,1)S(1)} custom-call(bf16[768,768]{1,0:T(8,128)(2,1)S(1)} %bitcast.15, bf16[288,640]{1,0:T(8,128)(2,1)S(1)} %get-tuple-element.40.core0, bf16[192,512]{1,0:T(8,128)(2,1)S(1)} %get-tuple-element.41.core1, bf16[96,384]{1,0:T(8,128)(2,1)S(1)} %get-tuple-element.42.core2, ...), custom_call_target="tpu_custom_call" | custom-call | tf_op jit(solution)/shard_map/convolve/pallas_call | solution.py:396
  78.4 4.8 %collective-permute-start.16 = (bf16[64,256]{1,0:T(8,128)(2,1)S(1)}, bf16[64,256]{1,0:T(8,128)(2,1)S(1)}, u32[]{:S(2)}, u32[]{:S(2)}) collective-permute-start(bf16[64,256]{1,0:T(8,128)(2,1)S(1)} %get-tuple-element.50), channel_id=1, source_target_pairs={{0,0},{16,64},{32,128},{48,192},{64,16},{80,80},{96,144},{112,208}... | collective-permute-start | bytes 98312 | tf_op jit(solution)/shard_map/ppermute | solution.py:433
  83.3 4.0 %collective-permute-start.17 = (bf16[64,256]{1,0:T(8,128)(2,1)S(1)}, bf16[64,256]{1,0:T(8,128)(2,1)S(1)}, u32[]{:S(2)}, u32[]{:S(2)}) collective-permute-start(bf16[64,256]{1,0:T(8,128)(2,1)S(1)} %get-tuple-element.49), channel_id=1, source_target_pairs={{0,48},{16,112},{32,176},{48,240},{64,0},{80,64},{96,128},{112,192... | collective-permute-start | bytes 98312 | tf_op jit(solution)/shard_map/ppermute | solution.py:433
  87.3 1.5 %collective-permute-start.18 = (bf16[64,256]{1,0:T(8,128)(2,1)S(1)}, bf16[64,256]{1,0:T(8,128)(2,1)S(1)}, u32[]{:S(2)}, u32[]{:S(2)}) collective-permute-start(bf16[64,256]{1,0:T(8,128)(2,1)S(1)} %get-tuple-element.48), channel_id=1, source_target_pairs={{0,32},{16,96},{32,160},{48,224},{64,48},{80,112},{96,176},{112,24... | collective-permute-start | bytes 98312 | tf_op jit(solution)/shard_map/ppermute | solution.py:433
  89.2 2.8 %collective-permute-done.17.high = bf16[64,256]{1,0:T(8,128)(2,1)S(1)} collective-permute-done((bf16[64,256]{1,0:T(8,128)(2,1)S(1)}, bf16[64,256]{1,0:T(8,128)(2,1)S(1)}, u32[]{:S(2)}, u32[]{:S(2)}) %collective-permute-start.17) | collective-permute-done | bytes 32800 | tf_op jit(solution)/shard_map/ppermute | solution.py:433
  92.1 4.0 %collective-permute-done.18.far = bf16[64,256]{1,0:T(8,128)(2,1)S(1)} collective-permute-done((bf16[64,256]{1,0:T(8,128)(2,1)S(1)}, bf16[64,256]{1,0:T(8,128)(2,1)S(1)}, u32[]{:S(2)}, u32[]{:S(2)}) %collective-permute-start.18) | collective-permute-done | bytes 32800 | tf_op jit(solution)/shard_map/ppermute | solution.py:433
  96.1 1.1 %place.1 = bf16[512,128]{1,0:T(8,128)(2,1)} custom-call(bf16[64,256]{1,0:T(8,128)(2,1)S(1)} %collective-permute-done.16.own, bf16[64,256]{1,0:T(8,128)(2,1)S(1)} %collective-permute-done.17.high, bf16[64,256]{1,0:T(8,128)(2,1)S(1)} %collective-permute-done.18.far, bf16[64,256]{1,0:T(8,128)(2,1)S(1)} %collective-permute-done.19.low), custom_call_target="tpu_custom_call" | custom-call | tf_op jit(solution)/shard_map/place/pallas_call | solution.py:421
  (46 shorter events, 5.3 us)
Async XLA Ops:
  4.9 10.5 %collective-permute-start.3 = (bf16[8,136,128]{2,1,0:T(8,128)(2,1)S(1)}, bf16[8,136,128]{2,1,0:T(8,128)(2,1)S(1)}, u32[]{:S(2)}, u32[]{:S(2)}) collective-permute-start(bf16[8,136,128]{2,1,0:T(8,128)(2,1)S(1)} %get-tuple-element.31), channel_id=1, source_target_pairs={{0,16},{16,32},{32,48},{48,0},{64,80},{80,96},{96,112},{112,64},{1... | collective-permute-start | bytes 835592 | tf_op jit(solution)/shard_map/ppermute | solution.py:433
  6.4 9.9 %collective-permute-start.1 = (bf16[8,136,128]{2,1,0:T(8,128)(2,1)S(1)}, bf16[8,136,128]{2,1,0:T(8,128)(2,1)S(1)}, u32[]{:S(2)}, u32[]{:S(2)}) collective-permute-start(bf16[8,136,128]{2,1,0:T(8,128)(2,1)S(1)} %get-tuple-element.27), channel_id=1, source_target_pairs={{0,48},{16,0},{32,16},{48,32},{64,112},{80,64},{96,80},{112,96},{1... | collective-permute-start | bytes 835592 | tf_op jit(solution)/shard_map/ppermute | solution.py:433
  12.1 9.9 %collective-permute-start.5 = (bf16[8,136,128]{2,1,0:T(8,128)(2,1)S(1)}, bf16[8,136,128]{2,1,0:T(8,128)(2,1)S(1)}, u32[]{:S(2)}, u32[]{:S(2)}) collective-permute-start(bf16[8,136,128]{2,1,0:T(8,128)(2,1)S(1)} %get-tuple-element.32), channel_id=1, source_target_pairs={{0,48},{16,0},{32,16},{48,32},{64,112},{80,64},{96,80},{112,96},{1... | collective-permute-start | bytes 835592 | tf_op jit(solution)/shard_map/ppermute | solution.py:433
  15.6 8.8 %collective-permute-start.4 = (bf16[8,136,128]{2,1,0:T(8,128)(2,1)S(1)}, bf16[8,136,128]{2,1,0:T(8,128)(2,1)S(1)}, u32[]{:S(2)}, u32[]{:S(2)}) collective-permute-start(bf16[8,136,128]{2,1,0:T(8,128)(2,1)S(1)} %merge.6), channel_id=1, source_target_pairs={{0,16},{16,32},{32,48},{48,0},{64,80},{80,96},{96,112},{112,64},{1... | collective-permute-start | bytes 835592 | tf_op jit(solution)/shard_map/ppermute | solution.py:433
  15.7 14.8 %collective-permute-start = (bf16[8,136,128]{2,1,0:T(8,128)(2,1)S(1)}, bf16[8,136,128]{2,1,0:T(8,128)(2,1)S(1)}, u32[]{:S(2)}, u32[]{:S(2)}) collective-permute-start(bf16[8,136,128]{2,1,0:T(8,128)(2,1)S(1)} %get-tuple-element.25), channel_id=1, source_target_pairs={{0,16},{16,32},{32,48},{48,0},{64,80},{80,96},{96,112},{112,64},{1... | collective-permute-start | bytes 835592 | tf_op jit(solution)/shard_map/ppermute | solution.py:433
  16.6 13.9 %collective-permute-start.2 = (bf16[8,136,128]{2,1,0:T(8,128)(2,1)S(1)}, bf16[8,136,128]{2,1,0:T(8,128)(2,1)S(1)}, u32[]{:S(2)}, u32[]{:S(2)}) collective-permute-start(bf16[8,136,128]{2,1,0:T(8,128)(2,1)S(1)} %merge.4), channel_id=1, source_target_pairs={{0,48},{16,0},{32,16},{48,32},{64,112},{80,64},{96,80},{112,96},{1... | collective-permute-start | bytes 835592 | tf_op jit(solution)/shard_map/ppermute | solution.py:433
  24.4 13.2 %copy-start = (bf16[4,3,3,3,64,64]{5,4,3,2,1,0:T(8,128)(2,1)S(1)}, bf16[4,3,3,3,64,64]{5,4,3,2,1,0:T(8,128)(2,1)}, u32[]{:S(2)}) copy-start(bf16[4,3,3,3,64,64]{5,4,3,2,1,0:T(8,128)(2,1)} %param.16) | copy-start | bytes 2654212
  24.4 13.2 %copy-start.1 = (bf16[64,64]{1,0:T(8,128)(2,1)S(1)}, bf16[64,64]{1,0:T(8,128)(2,1)}, u32[]{:S(2)}) copy-start(bf16[64,64]{1,0:T(8,128)(2,1)} %wv.1) | copy-start | bytes 24580
  24.4 13.2 %copy-start.2 = (bf16[64,64]{1,0:T(8,128)(2,1)S(1)}, bf16[64,64]{1,0:T(8,128)(2,1)}, u32[]{:S(2)}) copy-start(bf16[64,64]{1,0:T(8,128)(2,1)} %wo.1) | copy-start | bytes 24580
  24.8 8.0 %collective-permute-start.6 = (bf16[2,136,128]{2,1,0:T(8,128)(2,1)S(1)}, bf16[2,136,128]{2,1,0:T(8,128)(2,1)S(1)}, u32[]{:S(2)}, u32[]{:S(2)}) collective-permute-start(bf16[2,136,128]{2,1,0:T(8,128)(2,1)S(1)} %get-tuple-element.34), channel_id=1, source_target_pairs={{0,64},{16,80},{32,96},{48,112},{64,128},{80,144},{96,160},{112,17... | collective-permute-start | bytes 208904 | tf_op jit(solution)/shard_map/ppermute | solution.py:433
  27.4 7.5 %collective-permute-start.8 = (bf16[2,136,128]{2,1,0:T(8,128)(2,1)S(1)}, bf16[2,136,128]{2,1,0:T(8,128)(2,1)S(1)}, u32[]{:S(2)}, u32[]{:S(2)}) collective-permute-start(bf16[2,136,128]{2,1,0:T(8,128)(2,1)S(1)} %get-tuple-element.36), channel_id=1, source_target_pairs={{64,0},{80,16},{96,32},{112,48},{128,64},{144,80},{160,96},{176,11... | collective-permute-start | bytes 208904 | tf_op jit(solution)/shard_map/ppermute | solution.py:433
  33.0 7.3 %collective-permute-start.7 = (bf16[4,136,128]{2,1,0:T(8,128)(2,1)S(1)}, bf16[4,136,128]{2,1,0:T(8,128)(2,1)S(1)}, u32[]{:S(2)}, u32[]{:S(2)}) collective-permute-start(bf16[4,136,128]{2,1,0:T(8,128)(2,1)S(1)} %lift.2), channel_id=1, source_target_pairs={{0,64},{16,80},{32,96},{48,112},{64,128},{80,144},{96,160},{112,17... | collective-permute-start | bytes 417800 | tf_op jit(solution)/shard_map/ppermute | solution.py:433
  35.1 9.3 %collective-permute-start.9 = (bf16[4,136,128]{2,1,0:T(8,128)(2,1)S(1)}, bf16[4,136,128]{2,1,0:T(8,128)(2,1)S(1)}, u32[]{:S(2)}, u32[]{:S(2)}) collective-permute-start(bf16[4,136,128]{2,1,0:T(8,128)(2,1)S(1)} %lift.3), channel_id=1, source_target_pairs={{64,0},{80,16},{96,32},{112,48},{128,64},{144,80},{160,96},{176,11... | collective-permute-start | bytes 417800 | tf_op jit(solution)/shard_map/ppermute | solution.py:433
  37.6 10.4 %copy-start.3 = (f32[4,64]{1,0:T(4,128)S(1)}, f32[4,64]{1,0:T(4,128)}, u32[]{:S(2)}) copy-start(f32[4,64]{1,0:T(4,128)} %param.17) | copy-start | bytes 3076
  45.2 5.4 %collective-permute-start.11 = (bf16[8,32,256]{2,1,0:T(8,128)(2,1)S(1)}, bf16[8,32,256]{2,1,0:T(8,128)(2,1)S(1)}, u32[]{:S(2)}, u32[]{:S(2)}) collective-permute-start(bf16[8,32,256]{2,1,0:T(8,128)(2,1)S(1)} %bitcast.17), channel_id=1, source_target_pairs={{0,48},{16,0},{32,16},{48,32},{64,112},{80,64},{96,80},{112,96},{1... | collective-permute-start | bytes 393224 | tf_op jit(solution)/shard_map/ppermute | solution.py:433
  48.1 5.0 %collective-permute-start.10 = (bf16[8,32,256]{2,1,0:T(8,128)(2,1)S(1)}, bf16[8,32,256]{2,1,0:T(8,128)(2,1)S(1)}, u32[]{:S(2)}, u32[]{:S(2)}) collective-permute-start(bf16[8,32,256]{2,1,0:T(8,128)(2,1)S(1)} %bitcast.18), channel_id=1, source_target_pairs={{0,16},{16,32},{32,48},{48,0},{64,80},{80,96},{96,112},{112,64},{1... | collective-permute-start | bytes 393224 | tf_op jit(solution)/shard_map/ppermute | solution.py:433
  53.2 7.1 %collective-permute-start.13 = (bf16[8,4,768]{2,1,0:T(4,128)(2,1)S(1)}, bf16[8,4,768]{2,1,0:T(4,128)(2,1)S(1)}, u32[]{:S(2)}, u32[]{:S(2)}) collective-permute-start(bf16[8,4,768]{2,1,0:T(4,128)(2,1)S(1)} %get-tuple-element.46), channel_id=1, source_target_pairs={{64,0},{128,64},{192,128},{1,192},{65,1},{129,65},{193,129},{2,193... | collective-permute-start | bytes 147464 | tf_op jit(solution)/shard_map/ppermute | solution.py:433
  53.3 7.0 %collective-permute-start.12 = (bf16[8,4,768]{2,1,0:T(4,128)(2,1)S(1)}, bf16[8,4,768]{2,1,0:T(4,128)(2,1)S(1)}, u32[]{:S(2)}, u32[]{:S(2)}) collective-permute-start(bf16[8,4,768]{2,1,0:T(4,128)(2,1)S(1)} %get-tuple-element.45), channel_id=1, source_target_pairs={{0,64},{64,128},{128,192},{192,1},{1,65},{65,129},{129,193},{193,2... | collective-permute-start | bytes 147464 | tf_op jit(solution)/shard_map/ppermute | solution.py:433
  60.5 9.2 %collective-permute-start.15 = (bf16[4,40,768]{2,1,0:T(8,128)(2,1)S(1)}, bf16[4,40,768]{2,1,0:T(8,128)(2,1)S(1)}, u32[]{:S(2)}, u32[]{:S(2)}) collective-permute-start(bf16[4,40,768]{2,1,0:T(8,128)(2,1)S(1)} %pad_maximum_fusion.2), channel_id=1, source_target_pairs={{4,0},{8,4},{12,8},{0,12},{5,1},{9,5},{13,9},{1,13},{6,2},{10,6},{... | collective-permute-start | bytes 737288 | tf_op jit(solution)/shard_map/ppermute | solution.py:433
  63.7 9.8 %collective-permute-start.14 = (bf16[4,40,768]{2,1,0:T(8,128)(2,1)S(1)}, bf16[4,40,768]{2,1,0:T(8,128)(2,1)S(1)}, u32[]{:S(2)}, u32[]{:S(2)}) collective-permute-start(bf16[4,40,768]{2,1,0:T(8,128)(2,1)S(1)} %pad_maximum_fusion.1), channel_id=1, source_target_pairs={{0,4},{4,8},{8,12},{12,0},{1,5},{5,9},{9,13},{13,1},{2,6},{6,10},{... | collective-permute-start | bytes 737288 | tf_op jit(solution)/shard_map/ppermute | solution.py:433
  78.4 10.8 %collective-permute-start.16 = (bf16[64,256]{1,0:T(8,128)(2,1)S(1)}, bf16[64,256]{1,0:T(8,128)(2,1)S(1)}, u32[]{:S(2)}, u32[]{:S(2)}) collective-permute-start(bf16[64,256]{1,0:T(8,128)(2,1)S(1)} %get-tuple-element.50), channel_id=1, source_target_pairs={{0,0},{16,64},{32,128},{48,192},{64,16},{80,80},{96,144},{112,208}... | collective-permute-start | bytes 98312 | tf_op jit(solution)/shard_map/ppermute | solution.py:433
  83.3 8.8 %collective-permute-start.17 = (bf16[64,256]{1,0:T(8,128)(2,1)S(1)}, bf16[64,256]{1,0:T(8,128)(2,1)S(1)}, u32[]{:S(2)}, u32[]{:S(2)}) collective-permute-start(bf16[64,256]{1,0:T(8,128)(2,1)S(1)} %get-tuple-element.49), channel_id=1, source_target_pairs={{0,48},{16,112},{32,176},{48,240},{64,0},{80,64},{96,128},{112,192... | collective-permute-start | bytes 98312 | tf_op jit(solution)/shard_map/ppermute | solution.py:433
  87.3 8.8 %collective-permute-start.18 = (bf16[64,256]{1,0:T(8,128)(2,1)S(1)}, bf16[64,256]{1,0:T(8,128)(2,1)S(1)}, u32[]{:S(2)}, u32[]{:S(2)}) collective-permute-start(bf16[64,256]{1,0:T(8,128)(2,1)S(1)} %get-tuple-element.48), channel_id=1, source_target_pairs={{0,32},{16,96},{32,160},{48,224},{64,48},{80,112},{96,176},{112,24... | collective-permute-start | bytes 98312 | tf_op jit(solution)/shard_map/ppermute | solution.py:433
  88.8 7.3 %collective-permute-start.19 = (bf16[64,256]{1,0:T(8,128)(2,1)S(1)}, bf16[64,256]{1,0:T(8,128)(2,1)S(1)}, u32[]{:S(2)}, u32[]{:S(2)}) collective-permute-start(bf16[64,256]{1,0:T(8,128)(2,1)S(1)} %get-tuple-element.47), channel_id=1, source_target_pairs={{0,16},{16,80},{32,144},{48,208},{64,32},{80,96},{96,160},{112,224... | collective-permute-start | bytes 98312 | tf_op jit(solution)/shard_map/ppermute | solution.py:433

commit v9 on v6

--- a/solution.py
+++ b/solution.py
@@ -434,6 +434,13 @@
 
 def only(inside, v):
     return jnp.where(inside, v, jnp.zeros_like(v))
+
+
+def sides(place, from_even, from_odd):
+    is_odd = place % 2 == 1
+    before = jnp.where(is_odd, from_even, from_odd)
+    after = jnp.where(is_odd, from_odd, from_even)
+    return only(place > 0, before), only(place < 3, after)
 
 
 def joined(features, voxel_embed, visible, w_query, w_key, w_value, w_out, conv_weight, conv_bias):
@@ -462,10 +469,12 @@
     high = send(lift(2, z3, from_high), z_down)
     hidden = finish(z0, low, high, wide_v, wide_o).reshape(8, 32, 256)
 
+    even = {i: i ^ 1 for i in range(4)}
+    odd = {0: 0, 1: 2, 2: 1, 3: 3}
     me = lax.axis_index("frame")
     zh, xi = me // 4, me % 4
-    below = only(zh > 0, send(hidden, z_up))
-    above = only(zh < 3, send(hidden, z_down))
+    z_pairs = [[(4 * z + x, 4 * p[z] + x) for z in around for x in around] for p in (even, odd)]
+    below, above = sides(zh, send(hidden, z_pairs[0]), send(hidden, z_pairs[1]))
     hidden = jnp.concatenate([below, hidden, above], axis=2)
 
     def where_is(z, chunk):
@@ -480,11 +489,13 @@
         jnp.concatenate([left[i], hidden[i], right[i]], axis=1)
         for i in (slice(0, halo), slice(halo, None))
     )
-    x_next = [(i, (i + 1) % 4) for i in range(4)]
-    x_prev = [(j, i) for i, j in x_next]
     bx = lax.axis_index("bx")
-    front = only(bx > 0, send(second, x_next, "bx"))
-    back = only(bx < 3, send(first, x_prev, "bx"))
+    is_odd = bx % 2 == 1
+    front, back = sides(
+        bx,
+        send(jnp.where(is_odd, first, second), list(even.items()), "bx"),
+        send(jnp.where(is_odd, second, first), list(odd.items()), "bx"),
+    )
     bias = jnp.concatenate([conv_bias, conv_bias], axis=1)
 
     def lines(*parts):

time: 90.4 us -> 90.1 us (level)
  the two profiles are of different devices: /device:TPU:64 before, /device:TPU:80 now
where the time goes in v9:
time: 90.1 us; the launch traced here: 89.9 us
  waiting for transfers between devices  38.2 us (42%)
  starting transfers between devices  29.5 us (33%)
  Pallas kernels  20.8 us (23%)
  other arithmetic  0.96 us (1%)
    ppermute x19, waiting for transfers between devices, send(): return lax.ppermute(v, axis, way)  38.2 us
    ppermute x19, starting transfers between devices, send(): return lax.ppermute(v, axis, way)  29.5 us
    pallas_call x2, Pallas kernels, attend(): pl.pallas_call(functools.partial(attend_kernel, half), out_shape=[jax.Sha...  9.71 us
    pallas_call x1, Pallas kernels, convolve(): pl.pallas_call(conv_kernel, out_shape=jax.ShapeDtypeStruct((4, 64, 256),...  4.57 us
    pallas_call x1, Pallas kernels, core(): pl.pallas_call(core_kernel, out_shape=[jax.ShapeDtypeStruct((stride * (6...  2.25 us
  transfers between devices with their start and end apart: 19, of which 15 were waited for; matrix products, arithmetic and copies ran while one was open for 0% of the time, Pallas kernels for 11%

profile of v9, /device:TPU:80, one launch (start us, length us, event | category | flops | bytes accessed | tf_op | source)
XLA Modules:
  0.0 89.9 jit_solution(124057189400314595)
XLA Ops:
  0.0 4.9 %attend.3 = (bf16[8,136,128]{2,1,0:T(8,128)(2,1)S(1)}, bf16[8,136,128]{2,1,0:T(8,128)(2,1)S(1)}, bf16[8,136,128]{2,1,0:T(8,128)(2,1)S(1)}, bf16[8,136,128]{2,1,0:T(8,128)(2,1)S(1)}) custom-call(bf16[4,16,512,128]{3,2,1,0:T(8,128)(2,1)} %bitcast.22, bf16[16,512,128]{2,1,0:T(8,128)(2,1)} %bitcast.24, s32[4,16,8,128]{3,2,1,0:T(8,128)} %seen_at.3, ...), custom_call_target="tpu_custom_call" | custom-call | flops 100000000 | bytes 12582912 | tf_op jit(solution)/shard_map/attend/pallas_call | solution.py:134
  4.9 1.6 %collective-permute-start.3 = (bf16[8,136,128]{2,1,0:T(8,128)(2,1)S(1)}, bf16[8,136,128]{2,1,0:T(8,128)(2,1)S(1)}, u32[]{:S(2)}, u32[]{:S(2)}) collective-permute-start(bf16[8,136,128]{2,1,0:T(8,128)(2,1)S(1)} %get-tuple-element.31), channel_id=1, source_target_pairs={{0,16},{16,32},{32,48},{48,0},{64,80},{80,96},{96,112},{112,64},{1... | collective-permute-start | bytes 835592 | tf_op jit(solution)/shard_map/ppermute | solution.py:432
  6.4 4.9 %attend.2 = (bf16[8,136,128]{2,1,0:T(8,128)(2,1)S(1)}, bf16[8,136,128]{2,1,0:T(8,128)(2,1)S(1)}, bf16[8,136,128]{2,1,0:T(8,128)(2,1)S(1)}, bf16[8,136,128]{2,1,0:T(8,128)(2,1)S(1)}) custom-call(bf16[4,16,512,128]{3,2,1,0:T(8,128)(2,1)} %bitcast.23, bf16[16,512,128]{2,1,0:T(8,128)(2,1)} %bitcast.25, s32[4,16,8,128]{3,2,1,0:T(8,128)} %seen_at.3, ...), custom_call_target="tpu_custom_call" | custom-call | flops 100000000 | bytes 12582912 | tf_op jit(solution)/shard_map/attend/pallas_call | solution.py:134
  11.3 1.8 %collective-permute-start.1 = (bf16[8,136,128]{2,1,0:T(8,128)(2,1)S(1)}, bf16[8,136,128]{2,1,0:T(8,128)(2,1)S(1)}, u32[]{:S(2)}, u32[]{:S(2)}) collective-permute-start(bf16[8,136,128]{2,1,0:T(8,128)(2,1)S(1)} %get-tuple-element.27), channel_id=1, source_target_pairs={{0,48},{16,0},{32,16},{48,32},{64,112},{80,64},{96,80},{112,96},{1... | collective-permute-start | bytes 835592 | tf_op jit(solution)/shard_map/ppermute | solution.py:432
  13.1 1.5 %collective-permute-start.5 = (bf16[8,136,128]{2,1,0:T(8,128)(2,1)S(1)}, bf16[8,136,128]{2,1,0:T(8,128)(2,1)S(1)}, u32[]{:S(2)}, u32[]{:S(2)}) collective-permute-start(bf16[8,136,128]{2,1,0:T(8,128)(2,1)S(1)} %get-tuple-element.32), channel_id=1, source_target_pairs={{0,48},{16,0},{32,16},{48,32},{64,112},{80,64},{96,80},{112,96},{1... | collective-permute-start | bytes 835592 | tf_op jit(solution)/shard_map/ppermute | solution.py:432
  15.5 1.2 %collective-permute-start = (bf16[8,136,128]{2,1,0:T(8,128)(2,1)S(1)}, bf16[8,136,128]{2,1,0:T(8,128)(2,1)S(1)}, u32[]{:S(2)}, u32[]{:S(2)}) collective-permute-start(bf16[8,136,128]{2,1,0:T(8,128)(2,1)S(1)} %get-tuple-element.25), channel_id=1, source_target_pairs={{0,16},{16,32},{32,48},{48,0},{64,80},{80,96},{96,112},{112,64},{1... | collective-permute-start | bytes 835592 | tf_op jit(solution)/shard_map/ppermute | solution.py:432
  16.7 4.2 %collective-permute-done.1.refs_1_ = bf16[8,136,128]{2,1,0:T(8,128)(2,1)S(1)} collective-permute-done((bf16[8,136,128]{2,1,0:T(8,128)(2,1)S(1)}, bf16[8,136,128]{2,1,0:T(8,128)(2,1)S(1)}, u32[]{:S(2)}, u32[]{:S(2)}) %collective-permute-start.1) | collective-permute-done | bytes 278560 | tf_op jit(solution)/shard_map/ppermute | solution.py:432
  21.2 3.0 %collective-permute-start.2 = (bf16[8,136,128]{2,1,0:T(8,128)(2,1)S(1)}, bf16[8,136,128]{2,1,0:T(8,128)(2,1)S(1)}, u32[]{:S(2)}, u32[]{:S(2)}) collective-permute-start(bf16[8,136,128]{2,1,0:T(8,128)(2,1)S(1)} %merge.4), channel_id=1, source_target_pairs={{0,48},{16,0},{32,16},{48,32},{64,112},{80,64},{96,80},{112,96},{1... | collective-permute-start | bytes 835592 | tf_op jit(solution)/shard_map/ppermute | solution.py:432
  24.2 2.7 %collective-permute-done.5.refs_2_ = bf16[8,136,128]{2,1,0:T(8,128)(2,1)S(1)} collective-permute-done((bf16[8,136,128]{2,1,0:T(8,128)(2,1)S(1)}, bf16[8,136,128]{2,1,0:T(8,128)(2,1)S(1)}, u32[]{:S(2)}, u32[]{:S(2)}) %collective-permute-start.5) | collective-permute-done | bytes 278560 | tf_op jit(solution)/shard_map/ppermute | solution.py:432
  27.2 4.7 %collective-permute-start.6 = (bf16[2,136,128]{2,1,0:T(8,128)(2,1)S(1)}, bf16[2,136,128]{2,1,0:T(8,128)(2,1)S(1)}, u32[]{:S(2)}, u32[]{:S(2)}) collective-permute-start(bf16[2,136,128]{2,1,0:T(8,128)(2,1)S(1)} %get-tuple-element.34), channel_id=1, source_target_pairs={{0,64},{16,80},{32,96},{48,112},{64,128},{80,144},{96,160},{112,17... | collective-permute-start | bytes 208904 | tf_op jit(solution)/shard_map/ppermute | solution.py:432
  32.3 1.6 %collective-permute-done.6.came = bf16[2,136,128]{2,1,0:T(8,128)(2,1)S(1)} collective-permute-done((bf16[2,136,128]{2,1,0:T(8,128)(2,1)S(1)}, bf16[2,136,128]{2,1,0:T(8,128)(2,1)S(1)}, u32[]{:S(2)}, u32[]{:S(2)}) %collective-permute-start.6) | collective-permute-done | bytes 69664 | tf_op jit(solution)/shard_map/ppermute | solution.py:432
  34.1 4.7 %collective-permute-start.7 = (bf16[4,136,128]{2,1,0:T(8,128)(2,1)S(1)}, bf16[4,136,128]{2,1,0:T(8,128)(2,1)S(1)}, u32[]{:S(2)}, u32[]{:S(2)}) collective-permute-start(bf16[4,136,128]{2,1,0:T(8,128)(2,1)S(1)} %lift.2), channel_id=1, source_target_pairs={{0,64},{16,80},{32,96},{48,112},{64,128},{80,144},{96,160},{112,17... | collective-permute-start | bytes 417800 | tf_op jit(solution)/shard_map/ppermute | solution.py:432
  39.5 0.9 weights.1
  40.4 1.2 %collective-permute-done.7.low = bf16[4,136,128]{2,1,0:T(8,128)(2,1)S(1)} collective-permute-done((bf16[4,136,128]{2,1,0:T(8,128)(2,1)S(1)}, bf16[4,136,128]{2,1,0:T(8,128)(2,1)S(1)}, u32[]{:S(2)}, u32[]{:S(2)}) %collective-permute-start.7) | collective-permute-done | bytes 139296 | tf_op jit(solution)/shard_map/ppermute | solution.py:432
  41.7 6.5 %collective-permute-done.9.high = bf16[4,136,128]{2,1,0:T(8,128)(2,1)S(1)} collective-permute-done((bf16[4,136,128]{2,1,0:T(8,128)(2,1)S(1)}, bf16[4,136,128]{2,1,0:T(8,128)(2,1)S(1)}, u32[]{:S(2)}, u32[]{:S(2)}) %collective-permute-start.9) | collective-permute-done | bytes 139296 | tf_op jit(solution)/shard_map/ppermute | solution.py:432
  49.0 1.9 %collective-permute-start.11 = (bf16[8,32,256]{2,1,0:T(8,128)(2,1)S(1)}, bf16[8,32,256]{2,1,0:T(8,128)(2,1)S(1)}, u32[]{:S(2)}, u32[]{:S(2)}) collective-permute-start(bf16[8,32,256]{2,1,0:T(8,128)(2,1)S(1)} %bitcast.18), channel_id=1, source_target_pairs={{0,0},{16,16},{32,32},{48,48},{64,128},{80,144},{96,160},{112,176}... | collective-permute-start | bytes 393224 | tf_op jit(solution)/shard_map/ppermute | solution.py:432
  51.1 3.8 %collective-permute-done.10 = bf16[8,32,256]{2,1,0:T(8,128)(2,1)S(1)} collective-permute-done((bf16[8,32,256]{2,1,0:T(8,128)(2,1)S(1)}, bf16[8,32,256]{2,1,0:T(8,128)(2,1)S(1)}, u32[]{:S(2)}, u32[]{:S(2)}) %collective-permute-start.10) | collective-permute-done | bytes 131104 | tf_op jit(solution)/shard_map/ppermute | solution.py:432
  54.9 3.8 %collective-permute-done.11 = bf16[8,32,256]{2,1,0:T(8,128)(2,1)S(1)} collective-permute-done((bf16[8,32,256]{2,1,0:T(8,128)(2,1)S(1)}, bf16[8,32,256]{2,1,0:T(8,128)(2,1)S(1)}, u32[]{:S(2)}, u32[]{:S(2)}) %collective-permute-start.11) | collective-permute-done | bytes 131104 | tf_op jit(solution)/shard_map/ppermute | solution.py:432
  59.0 2.1 %collective-permute-start.12 = (bf16[8,4,768]{2,1,0:T(4,128)(2,1)S(1)}, bf16[8,4,768]{2,1,0:T(4,128)(2,1)S(1)}, u32[]{:S(2)}, u32[]{:S(2)}) collective-permute-start(bf16[8,4,768]{2,1,0:T(4,128)(2,1)S(1)} %get-tuple-element.49), channel_id=1, source_target_pairs={{0,16},{16,32},{32,48},{48,1},{1,17},{17,33},{33,49},{49,2},{2,18}... | collective-permute-start | bytes 147464 | tf_op jit(solution)/shard_map/ppermute | solution.py:432
  61.1 1.9 %collective-permute-done.13 = bf16[8,4,768]{2,1,0:T(4,128)(2,1)S(1)} collective-permute-done((bf16[8,4,768]{2,1,0:T(4,128)(2,1)S(1)}, bf16[8,4,768]{2,1,0:T(4,128)(2,1)S(1)}, u32[]{:S(2)}, u32[]{:S(2)}) %collective-permute-start.13) | collective-permute-done | bytes 49184 | tf_op jit(solution)/shard_map/ppermute | solution.py:432
  63.1 1.6 %collective-permute-done.12 = bf16[8,4,768]{2,1,0:T(4,128)(2,1)S(1)} collective-permute-done((bf16[8,4,768]{2,1,0:T(4,128)(2,1)S(1)}, bf16[8,4,768]{2,1,0:T(4,128)(2,1)S(1)}, u32[]{:S(2)}, u32[]{:S(2)}) %collective-permute-start.12) | collective-permute-done | bytes 49184 | tf_op jit(solution)/shard_map/ppermute | solution.py:432
  65.0 1.4 %collective-permute-start.14 = (bf16[4,40,768]{2,1,0:T(8,128)(2,1)S(1)}, bf16[4,40,768]{2,1,0:T(8,128)(2,1)S(1)}, u32[]{:S(2)}, u32[]{:S(2)}) collective-permute-start(bf16[4,40,768]{2,1,0:T(8,128)(2,1)S(1)} %get-tuple-element.45), channel_id=1, source_target_pairs={{0,4},{4,0},{8,12},{12,8},{1,5},{5,1},{9,13},{13,9},{2,6},{6,2},{1... | collective-permute-start | bytes 737288 | tf_op jit(solution)/shard_map/ppermute | solution.py:432
  66.3 2.1 %collective-permute-start.15 = (bf16[4,40,768]{2,1,0:T(8,128)(2,1)S(1)}, bf16[4,40,768]{2,1,0:T(8,128)(2,1)S(1)}, u32[]{:S(2)}, u32[]{:S(2)}) collective-permute-start(bf16[4,40,768]{2,1,0:T(8,128)(2,1)S(1)} %get-tuple-element.46), channel_id=1, source_target_pairs={{0,0},{4,8},{8,4},{12,12},{1,1},{5,9},{9,5},{13,13},{2,2},{6,10},{... | collective-permute-start | bytes 737288 | tf_op jit(solution)/shard_map/ppermute | solution.py:432
  68.6 2.3 %core.1 = (bf16[288,640]{1,0:T(8,128)(2,1)S(1)}, bf16[192,512]{1,0:T(8,128)(2,1)S(1)}, bf16[96,384]{1,0:T(8,128)(2,1)S(1)}) custom-call(bf16[384,768]{1,0:T(8,128)(2,1)S(1)} %bitcast.21, bf16[4,3,256,384]{3,2,1,0:T(8,128)(2,1)S(1)} %get-tuple-element.39.band, f32[4,128]{1,0:T(4,128)S(1)} %pad_maximum_fusion.5.bias), custom_call_target="tpu_custom_call" | custom-call | flops 1000000000 | bytes 1000000 | tf_op jit(solution)/shard_map/core/pallas_call | solution.py:359
  70.9 1.8 %collective-permute-done.14 = bf16[4,40,768]{2,1,0:T(8,128)(2,1)S(1)} collective-permute-done((bf16[4,40,768]{2,1,0:T(8,128)(2,1)S(1)}, bf16[4,40,768]{2,1,0:T(8,128)(2,1)S(1)}, u32[]{:S(2)}, u32[]{:S(2)}) %collective-permute-start.14) | collective-permute-done | bytes 245792 | tf_op jit(solution)/shard_map/ppermute | solution.py:432
  72.7 3.4 %collective-permute-done.15 = bf16[4,40,768]{2,1,0:T(8,128)(2,1)S(1)} collective-permute-done((bf16[4,40,768]{2,1,0:T(8,128)(2,1)S(1)}, bf16[4,40,768]{2,1,0:T(8,128)(2,1)S(1)}, u32[]{:S(2)}, u32[]{:S(2)}) %collective-permute-start.15) | collective-permute-done | bytes 245792 | tf_op jit(solution)/shard_map/ppermute | solution.py:432
  76.5 4.6 %convolve.1 = bf16[4,64,256]{2,1,0:T(8,128)(2,1)S(1)} custom-call(bf16[768,768]{1,0:T(8,128)(2,1)S(1)} %bitcast.15, bf16[288,640]{1,0:T(8,128)(2,1)S(1)} %get-tuple-element.40.core0, bf16[192,512]{1,0:T(8,128)(2,1)S(1)} %get-tuple-element.41.core1, bf16[96,384]{1,0:T(8,128)(2,1)S(1)} %get-tuple-element.42.core2, ...), custom_call_target="tpu_custom_call" | custom-call | tf_op jit(solution)/shard_map/convolve/pallas_call | solution.py:395
  81.5 2.3 %collective-permute-start.17 = (bf16[64,256]{1,0:T(8,128)(2,1)S(1)}, bf16[64,256]{1,0:T(8,128)(2,1)S(1)}, u32[]{:S(2)}, u32[]{:S(2)}) collective-permute-start(bf16[64,256]{1,0:T(8,128)(2,1)S(1)} %get-tuple-element.54), channel_id=1, source_target_pairs={{0,32},{16,48},{32,0},{48,16},{64,96},{80,112},{96,64},{112,80},{1... | collective-permute-start | bytes 98312 | tf_op jit(solution)/shard_map/ppermute | solution.py:432
  83.7 1.7 %collective-permute-done.16.high = bf16[64,256]{1,0:T(8,128)(2,1)S(1)} collective-permute-done((bf16[64,256]{1,0:T(8,128)(2,1)S(1)}, bf16[64,256]{1,0:T(8,128)(2,1)S(1)}, u32[]{:S(2)}, u32[]{:S(2)}) %collective-permute-start.16) | collective-permute-done | bytes 32800 | tf_op jit(solution)/shard_map/ppermute | solution.py:432
  85.5 1.4 %collective-permute-done.17.far = bf16[64,256]{1,0:T(8,128)(2,1)S(1)} collective-permute-done((bf16[64,256]{1,0:T(8,128)(2,1)S(1)}, bf16[64,256]{1,0:T(8,128)(2,1)S(1)}, u32[]{:S(2)}, u32[]{:S(2)}) %collective-permute-start.17) | collective-permute-done | bytes 32800 | tf_op jit(solution)/shard_map/ppermute | solution.py:432
  86.9 2.0 %collective-permute-done.18.low = bf16[64,256]{1,0:T(8,128)(2,1)S(1)} collective-permute-done((bf16[64,256]{1,0:T(8,128)(2,1)S(1)}, bf16[64,256]{1,0:T(8,128)(2,1)S(1)}, u32[]{:S(2)}, u32[]{:S(2)}) %collective-permute-start.18) | collective-permute-done | bytes 32800 | tf_op jit(solution)/shard_map/ppermute | solution.py:432
  88.9 1.1 %place.1 = bf16[512,128]{1,0:T(8,128)(2,1)} custom-call(bf16[64,256]{1,0:T(8,128)(2,1)S(1)} %get-tuple-element.56.own, bf16[64,256]{1,0:T(8,128)(2,1)S(1)} %collective-permute-done.16.high, bf16[64,256]{1,0:T(8,128)(2,1)S(1)} %collective-permute-done.17.far, bf16[64,256]{1,0:T(8,128)(2,1)S(1)} %collective-permute-done.18.low), custom_call_target="tpu_custom_call" | custom-call | tf_op jit(solution)/shard_map/place/pallas_call | solution.py:420
  (41 shorter events, 5.1 us)
Async XLA Ops:
  4.9 9.8 %collective-permute-start.3 = (bf16[8,136,128]{2,1,0:T(8,128)(2,1)S(1)}, bf16[8,136,128]{2,1,0:T(8,128)(2,1)S(1)}, u32[]{:S(2)}, u32[]{:S(2)}) collective-permute-start(bf16[8,136,128]{2,1,0:T(8,128)(2,1)S(1)} %get-tuple-element.31), channel_id=1, source_target_pairs={{0,16},{16,32},{32,48},{48,0},{64,80},{80,96},{96,112},{112,64},{1... | collective-permute-start | bytes 835592 | tf_op jit(solution)/shard_map/ppermute | solution.py:432
  11.3 9.6 %collective-permute-start.1 = (bf16[8,136,128]{2,1,0:T(8,128)(2,1)S(1)}, bf16[8,136,128]{2,1,0:T(8,128)(2,1)S(1)}, u32[]{:S(2)}, u32[]{:S(2)}) collective-permute-start(bf16[8,136,128]{2,1,0:T(8,128)(2,1)S(1)} %get-tuple-element.27), channel_id=1, source_target_pairs={{0,48},{16,0},{32,16},{48,32},{64,112},{80,64},{96,80},{112,96},{1... | collective-permute-start | bytes 835592 | tf_op jit(solution)/shard_map/ppermute | solution.py:432
  13.1 13.8 %collective-permute-start.5 = (bf16[8,136,128]{2,1,0:T(8,128)(2,1)S(1)}, bf16[8,136,128]{2,1,0:T(8,128)(2,1)S(1)}, u32[]{:S(2)}, u32[]{:S(2)}) collective-permute-start(bf16[8,136,128]{2,1,0:T(8,128)(2,1)S(1)} %get-tuple-element.32), channel_id=1, source_target_pairs={{0,48},{16,0},{32,16},{48,32},{64,112},{80,64},{96,80},{112,96},{1... | collective-permute-start | bytes 835592 | tf_op jit(solution)/shard_map/ppermute | solution.py:432
  14.9 11.9 %collective-permute-start.4 = (bf16[8,136,128]{2,1,0:T(8,128)(2,1)S(1)}, bf16[8,136,128]{2,1,0:T(8,128)(2,1)S(1)}, u32[]{:S(2)}, u32[]{:S(2)}) collective-permute-start(bf16[8,136,128]{2,1,0:T(8,128)(2,1)S(1)} %merge.6), channel_id=1, source_target_pairs={{0,16},{16,32},{32,48},{48,0},{64,80},{80,96},{96,112},{112,64},{1... | collective-permute-start | bytes 835592 | tf_op jit(solution)/shard_map/ppermute | solution.py:432
  15.5 16.5 %collective-permute-start = (bf16[8,136,128]{2,1,0:T(8,128)(2,1)S(1)}, bf16[8,136,128]{2,1,0:T(8,128)(2,1)S(1)}, u32[]{:S(2)}, u32[]{:S(2)}) collective-permute-start(bf16[8,136,128]{2,1,0:T(8,128)(2,1)S(1)} %get-tuple-element.25), channel_id=1, source_target_pairs={{0,16},{16,32},{32,48},{48,0},{64,80},{80,96},{96,112},{112,64},{1... | collective-permute-start | bytes 835592 | tf_op jit(solution)/shard_map/ppermute | solution.py:432
  21.2 10.8 %collective-permute-start.2 = (bf16[8,136,128]{2,1,0:T(8,128)(2,1)S(1)}, bf16[8,136,128]{2,1,0:T(8,128)(2,1)S(1)}, u32[]{:S(2)}, u32[]{:S(2)}) collective-permute-start(bf16[8,136,128]{2,1,0:T(8,128)(2,1)S(1)} %merge.4), channel_id=1, source_target_pairs={{0,48},{16,0},{32,16},{48,32},{64,112},{80,64},{96,80},{112,96},{1... | collective-permute-start | bytes 835592 | tf_op jit(solution)/shard_map/ppermute | solution.py:432
  26.9 12.6 %copy-start = (bf16[4,3,3,3,64,64]{5,4,3,2,1,0:T(8,128)(2,1)S(1)}, bf16[4,3,3,3,64,64]{5,4,3,2,1,0:T(8,128)(2,1)}, u32[]{:S(2)}) copy-start(bf16[4,3,3,3,64,64]{5,4,3,2,1,0:T(8,128)(2,1)} %param.16) | copy-start | bytes 2654212
  26.9 12.6 %copy-start.1 = (bf16[64,64]{1,0:T(8,128)(2,1)S(1)}, bf16[64,64]{1,0:T(8,128)(2,1)}, u32[]{:S(2)}) copy-start(bf16[64,64]{1,0:T(8,128)(2,1)} %wv.1) | copy-start | bytes 24580
  26.9 12.6 %copy-start.2 = (bf16[64,64]{1,0:T(8,128)(2,1)S(1)}, bf16[64,64]{1,0:T(8,128)(2,1)}, u32[]{:S(2)}) copy-start(bf16[64,64]{1,0:T(8,128)(2,1)} %wo.1) | copy-start | bytes 24580
  27.2 6.7 %collective-permute-start.6 = (bf16[2,136,128]{2,1,0:T(8,128)(2,1)S(1)}, bf16[2,136,128]{2,1,0:T(8,128)(2,1)S(1)}, u32[]{:S(2)}, u32[]{:S(2)}) collective-permute-start(bf16[2,136,128]{2,1,0:T(8,128)(2,1)S(1)} %get-tuple-element.34), channel_id=1, source_target_pairs={{0,64},{16,80},{32,96},{48,112},{64,128},{80,144},{96,160},{112,17... | collective-permute-start | bytes 208904 | tf_op jit(solution)/shard_map/ppermute | solution.py:432
  32.0 7.3 %collective-permute-start.8 = (bf16[2,136,128]{2,1,0:T(8,128)(2,1)S(1)}, bf16[2,136,128]{2,1,0:T(8,128)(2,1)S(1)}, u32[]{:S(2)}, u32[]{:S(2)}) collective-permute-start(bf16[2,136,128]{2,1,0:T(8,128)(2,1)S(1)} %get-tuple-element.36), channel_id=1, source_target_pairs={{64,0},{80,16},{96,32},{112,48},{128,64},{144,80},{160,96},{176,11... | collective-permute-start | bytes 208904 | tf_op jit(solution)/shard_map/ppermute | solution.py:432
  34.1 7.6 %collective-permute-start.7 = (bf16[4,136,128]{2,1,0:T(8,128)(2,1)S(1)}, bf16[4,136,128]{2,1,0:T(8,128)(2,1)S(1)}, u32[]{:S(2)}, u32[]{:S(2)}) collective-permute-start(bf16[4,136,128]{2,1,0:T(8,128)(2,1)S(1)} %lift.2), channel_id=1, source_target_pairs={{0,64},{16,80},{32,96},{48,112},{64,128},{80,144},{96,160},{112,17... | collective-permute-start | bytes 417800 | tf_op jit(solution)/shard_map/ppermute | solution.py:432
  39.4 8.7 %collective-permute-start.9 = (bf16[4,136,128]{2,1,0:T(8,128)(2,1)S(1)}, bf16[4,136,128]{2,1,0:T(8,128)(2,1)S(1)}, u32[]{:S(2)}, u32[]{:S(2)}) collective-permute-start(bf16[4,136,128]{2,1,0:T(8,128)(2,1)S(1)} %lift.3), channel_id=1, source_target_pairs={{64,0},{80,16},{96,32},{112,48},{128,64},{144,80},{160,96},{176,11... | collective-permute-start | bytes 417800 | tf_op jit(solution)/shard_map/ppermute | solution.py:432
  39.5 11.5 %copy-start.3 = (f32[4,64]{1,0:T(4,128)S(1)}, f32[4,64]{1,0:T(4,128)}, u32[]{:S(2)}) copy-start(f32[4,64]{1,0:T(4,128)} %param.17) | copy-start | bytes 3076
  48.9 6.0 %collective-permute-start.10 = (bf16[8,32,256]{2,1,0:T(8,128)(2,1)S(1)}, bf16[8,32,256]{2,1,0:T(8,128)(2,1)S(1)}, u32[]{:S(2)}, u32[]{:S(2)}) collective-permute-start(bf16[8,32,256]{2,1,0:T(8,128)(2,1)S(1)} %bitcast.17), channel_id=1, source_target_pairs={{0,64},{16,80},{32,96},{48,112},{64,0},{80,16},{96,32},{112,48},{1... | collective-permute-start | bytes 393224 | tf_op jit(solution)/shard_map/ppermute | solution.py:432
  49.0 9.7 %collective-permute-start.11 = (bf16[8,32,256]{2,1,0:T(8,128)(2,1)S(1)}, bf16[8,32,256]{2,1,0:T(8,128)(2,1)S(1)}, u32[]{:S(2)}, u32[]{:S(2)}) collective-permute-start(bf16[8,32,256]{2,1,0:T(8,128)(2,1)S(1)} %bitcast.18), channel_id=1, source_target_pairs={{0,0},{16,16},{32,32},{48,48},{64,128},{80,144},{96,160},{112,176}... | collective-permute-start | bytes 393224 | tf_op jit(solution)/shard_map/ppermute | solution.py:432
  58.9 4.2 %collective-permute-start.13 = (bf16[8,4,768]{2,1,0:T(4,128)(2,1)S(1)}, bf16[8,4,768]{2,1,0:T(4,128)(2,1)S(1)}, u32[]{:S(2)}, u32[]{:S(2)}) collective-permute-start(bf16[8,4,768]{2,1,0:T(4,128)(2,1)S(1)} %get-tuple-element.50), channel_id=1, source_target_pairs={{16,0},{32,16},{48,32},{1,48},{17,1},{33,17},{49,33},{2,49},{18,2}... | collective-permute-start | bytes 147464 | tf_op jit(solution)/shard_map/ppermute | solution.py:432
  59.0 5.7 %collective-permute-start.12 = (bf16[8,4,768]{2,1,0:T(4,128)(2,1)S(1)}, bf16[8,4,768]{2,1,0:T(4,128)(2,1)S(1)}, u32[]{:S(2)}, u32[]{:S(2)}) collective-permute-start(bf16[8,4,768]{2,1,0:T(4,128)(2,1)S(1)} %get-tuple-element.49), channel_id=1, source_target_pairs={{0,16},{16,32},{32,48},{48,1},{1,17},{17,33},{33,49},{49,2},{2,18}... | collective-permute-start | bytes 147464 | tf_op jit(solution)/shard_map/ppermute | solution.py:432
  65.0 7.7 %collective-permute-start.14 = (bf16[4,40,768]{2,1,0:T(8,128)(2,1)S(1)}, bf16[4,40,768]{2,1,0:T(8,128)(2,1)S(1)}, u32[]{:S(2)}, u32[]{:S(2)}) collective-permute-start(bf16[4,40,768]{2,1,0:T(8,128)(2,1)S(1)} %get-tuple-element.45), channel_id=1, source_target_pairs={{0,4},{4,0},{8,12},{12,8},{1,5},{5,1},{9,13},{13,9},{2,6},{6,2},{1... | collective-permute-start | bytes 737288 | tf_op jit(solution)/shard_map/ppermute | solution.py:432
  66.3 9.8 %collective-permute-start.15 = (bf16[4,40,768]{2,1,0:T(8,128)(2,1)S(1)}, bf16[4,40,768]{2,1,0:T(8,128)(2,1)S(1)}, u32[]{:S(2)}, u32[]{:S(2)}) collective-permute-start(bf16[4,40,768]{2,1,0:T(8,128)(2,1)S(1)} %get-tuple-element.46), channel_id=1, source_target_pairs={{0,0},{4,8},{8,4},{12,12},{1,1},{5,9},{9,5},{13,13},{2,2},{6,10},{... | collective-permute-start | bytes 737288 | tf_op jit(solution)/shard_map/ppermute | solution.py:432
  81.1 4.3 %collective-permute-start.16 = (bf16[64,256]{1,0:T(8,128)(2,1)S(1)}, bf16[64,256]{1,0:T(8,128)(2,1)S(1)}, u32[]{:S(2)}, u32[]{:S(2)}) collective-permute-start(bf16[64,256]{1,0:T(8,128)(2,1)S(1)} %get-tuple-element.55), channel_id=1, source_target_pairs={{0,48},{16,0},{32,16},{48,32},{64,112},{80,64},{96,80},{112,96},{1... | collective-permute-start | bytes 98312 | tf_op jit(solution)/shard_map/ppermute | solution.py:432
  81.5 5.4 %collective-permute-start.17 = (bf16[64,256]{1,0:T(8,128)(2,1)S(1)}, bf16[64,256]{1,0:T(8,128)(2,1)S(1)}, u32[]{:S(2)}, u32[]{:S(2)}) collective-permute-start(bf16[64,256]{1,0:T(8,128)(2,1)S(1)} %get-tuple-element.54), channel_id=1, source_target_pairs={{0,32},{16,48},{32,0},{48,16},{64,96},{80,112},{96,64},{112,80},{1... | collective-permute-start | bytes 98312 | tf_op jit(solution)/shard_map/ppermute | solution.py:432
  83.7 5.1 %collective-permute-start.18 = (bf16[64,256]{1,0:T(8,128)(2,1)S(1)}, bf16[64,256]{1,0:T(8,128)(2,1)S(1)}, u32[]{:S(2)}, u32[]{:S(2)}) collective-permute-start(bf16[64,256]{1,0:T(8,128)(2,1)S(1)} %get-tuple-element.53), channel_id=1, source_target_pairs={{0,16},{16,32},{32,48},{48,0},{64,80},{80,96},{96,112},{112,64},{1... | collective-permute-start | bytes 98312 | tf_op jit(solution)/shard_map/ppermute | solution.py:432
